TPU v7x, 32 devices: a whole 2x2x4 slice. The times are simulated.
32 devices in a mesh: row: 4 (over z), ctx: 8 (over y, x, core).
Axes of the slice: x: 2, y: 2, z: 4, core: 2. Of those that a mesh axis runs over, the one named last changes fastest.
Arguments:
- inputs: bfloat16 [8, 2048, 2048], P('row', 'ctx'), may hold values from -6 to 6
- doc_len: int32 [8, 16], P('row'), may hold values from 0 to 2048, as said below
- w_query: bfloat16 [2048, 2048], P(('row', 'ctx')), may hold values from -0.125 to 0.125
- w_key: bfloat16 [2048, 2048], P(('row', 'ctx')), may hold values from -0.125 to 0.125
- w_value: bfloat16 [2048, 2048], P(('row', 'ctx')), may hold values from -0.125 to 0.125
- w_out: bfloat16 [2048, 2048], P(('row', 'ctx')), may hold values from -0.125 to 0.125
- w_up: bfloat16 [2048, 8192], P(('row', 'ctx')), may hold values from -0.125 to 0.125
- w_down: bfloat16 [8192, 2048], P(('row', 'ctx')), may hold values from -0.0625 to 0.0625
- gain_attn: bfloat16 [2048], P(('row', 'ctx')), may hold values from 0.099609375 to 1.8984375
- gain_attn_sub: bfloat16 [2048], P(('row', 'ctx')), may hold values from 0.099609375 to 1.8984375
- gain_ffn: bfloat16 [2048], P(('row', 'ctx')), may hold values from 0.099609375 to 1.8984375
- gain_ffn_sub: bfloat16 [8192], P(('row', 'ctx')), may hold values from 0.099609375 to 1.8984375
- out_cotangent: bfloat16 [8, 2048, 2048], P('row', 'ctx'), may hold values from -6 to 6
Outputs:
- output: bfloat16 [8, 2048, 2048], P('row', 'ctx')
- input_grad: float32 [8, 2048, 2048], P('row', 'ctx')
- query_grad: float32 [2048, 2048], P(('row', 'ctx'))
- key_grad: float32 [2048, 2048], P(('row', 'ctx'))
- value_grad: float32 [2048, 2048], P(('row', 'ctx'))
- out_grad: float32 [2048, 2048], P(('row', 'ctx'))
- up_grad: float32 [2048, 8192], P(('row', 'ctx'))
- down_grad: float32 [8192, 2048], P(('row', 'ctx'))
- gain_attn_grad: float32 [2048], P(('row', 'ctx'))
- gain_attn_sub_grad: float32 [2048], P(('row', 'ctx'))
- gain_ffn_grad: float32 [2048], P(('row', 'ctx'))
- gain_ffn_sub_grad: float32 [8192], P(('row', 'ctx'))
Inputs may be any that keep to these rules, and one draw needn't show every extreme that they name: `doc_len`: each row lists the lengths of its documents in order, zeros after the last; a row's lengths add up to at most 2048, the rest of the row is padding; in each aligned block of 2 rows one row, drawn from the seed, holds a single document of 2048 tokens; every other nonzero length is at least max(1, 102).
All inputs are finite; a program needn't handle non-finite values.
Results may differ from a plain program's by a relative error of at most 0.017.
Values may be sent and summed in bfloat16 or wider, within the bound.
A program may use at most 512 MiB of HBM per device.

v0:
```python
import jax
import jax.numpy as jnp
from jax import lax
from jax.sharding import PartitionSpec as P

HEADS = 32
HEAD_DIM = 64
ROW_LEN = 2048
XPOS_BASE = 512


masked_score = -1e30


def norm_gain(values, gain):
    center = values - jnp.mean(values, axis=-1, keepdims=True)
    spread = jnp.mean(center * center, axis=-1, keepdims=True)
    return center * lax.rsqrt(spread + 1e-05) * gain


def gelu_exact(values):
    return jax.nn.gelu(values, approximate=False)


def doc_info(lengths, places):
    doc_ends = jnp.cumsum(lengths, axis=-1)
    passed = doc_ends[..., None, :] <= places[..., :, None]
    doc_ids = jnp.sum(passed.astype(jnp.int32), axis=-1)
    starts = jnp.sum(jnp.where(passed, lengths[..., None, :], 0), axis=-1)
    is_valid = places < doc_ends[..., -1:]
    return (doc_ids, starts, is_valid)


def xpos_tables(relative):
    half_dim = HEAD_DIM // 2
    ladder = jnp.arange(half_dim, dtype=jnp.float32) / half_dim
    angle_rate = jnp.power(10000.0, -ladder)
    decay_base = (ladder + 0.4) / 1.4
    angles = relative[:, None] * angle_rate[None, :]
    factor = jnp.power(decay_base[None, :], (relative[:, None] - ROW_LEN / 2) / XPOS_BASE)
    return (jnp.cos(angles), jnp.sin(angles), factor)


def rotate(values, cosine, sine_part, factor):
    half_dim = HEAD_DIM // 2
    first_half = values[..., :half_dim]
    second = values[..., half_dim:]
    cosine = cosine[:, None, :]
    sine_part = sine_part[:, None, :]
    turned = jnp.concatenate(
        [first_half * cosine - second * sine_part, second * cosine + first_half * sine_part],
        axis=-1,
    )
    return turned * jnp.concatenate([factor, factor], axis=-1)[:, None, :]


def visible(query_pos, key_pos, query_doc, key_doc, key_valid):
    self_pair = query_pos[..., :, None] == key_pos[..., None, :]
    causal = (
        (query_doc[..., :, None] == key_doc[..., None, :])
        & (key_pos[..., None, :] <= query_pos[..., :, None])
        & key_valid[..., None, :]
    )
    return self_pair | causal


def body(
    inputs,
    doc_len,
    w_query,
    w_key,
    w_value,
    w_out,
    w_up,
    w_down,
    gain_attn,
    gain_attn_sub,
    gain_ffn,
    gain_ffn_sub,
    out_cotangent,
):
    row_count, local_len, width = inputs.shape
    row_len = local_len * lax.axis_size("ctx")
    token_count = row_count * local_len
    head_shape = (token_count, HEADS, HEAD_DIM)
    score_scale = HEAD_DIM ** (-0.5)
    block_len = min(512, row_len)
    block_count = row_len // block_len

    def gather_attention():
        return (
            lax.all_gather(w_query, ("row", "ctx"), axis=0, tiled=True),
            lax.all_gather(w_key, ("row", "ctx"), axis=0, tiled=True),
            lax.all_gather(w_value, ("row", "ctx"), axis=0, tiled=True),
            lax.all_gather(w_out, ("row", "ctx"), axis=0, tiled=True),
            lax.all_gather(gain_attn, ("row", "ctx"), axis=0, tiled=True),
            lax.all_gather(gain_attn_sub, ("row", "ctx"), axis=0, tiled=True),
        )

    def gather_ffn():
        return (
            lax.all_gather(w_up, ("row", "ctx"), axis=0, tiled=True),
            lax.all_gather(w_down, ("row", "ctx"), axis=0, tiled=True),
            lax.all_gather(gain_ffn, ("row", "ctx"), axis=0, tiled=True),
            lax.all_gather(gain_ffn_sub, ("row", "ctx"), axis=0, tiled=True),
        )

    attn_full = gather_attention()
    full_query, full_key, full_value, full_out, full_gain_attn, full_gain_sub = attn_full
    tokens_f = inputs.reshape(token_count, width).astype(jnp.float32)
    normed = norm_gain(tokens_f, full_gain_attn.astype(jnp.float32)).astype(jnp.bfloat16)
    query = jnp.dot(normed, full_query, preferred_element_type=jnp.float32)
    key_raw = jnp.dot(normed, full_key, preferred_element_type=jnp.float32)
    value_raw = jnp.dot(normed, full_value, preferred_element_type=jnp.float32)
    places = lax.axis_index("ctx") * local_len + jnp.arange(local_len, dtype=jnp.int32)
    query_places = jnp.broadcast_to(places[None, :], (row_count, local_len))
    query_docs, query_starts, query_valid = doc_info(doc_len, query_places)
    relative = (query_places - query_starts).astype(jnp.float32).reshape(token_count)
    cosine, sine_part, factor = xpos_tables(relative)
    query_rot = rotate(query.reshape(head_shape), cosine, sine_part, factor).astype(jnp.bfloat16)
    query_heads = query_rot.reshape(row_count, local_len, HEADS, HEAD_DIM)
    key_rot = (
        rotate(key_raw.reshape(head_shape), cosine, sine_part, 1.0 / factor)
        .astype(jnp.bfloat16)
        .reshape(row_count, local_len, width)
    )
    value_low = value_raw.astype(jnp.bfloat16).reshape(row_count, local_len, width)

    def gather_keys():
        keys_all, values_all = (
            lax.all_gather(key_rot, "ctx", axis=1, tiled=True),
            lax.all_gather(value_low, "ctx", axis=1, tiled=True),
        )
        return (
            keys_all.reshape(row_count, row_len, HEADS, HEAD_DIM),
            values_all.reshape(row_count, row_len, HEADS, HEAD_DIM),
        )

    def key_block(keys_all, values_all, block_idx):
        begin = block_idx * block_len
        key_part = lax.dynamic_slice_in_dim(keys_all, begin, block_len, 1)
        value_part = lax.dynamic_slice_in_dim(values_all, begin, block_len, 1)
        key_places = jnp.broadcast_to(
            (begin + jnp.arange(block_len, dtype=jnp.int32))[None, :], (row_count, block_len)
        )
        key_docs, key_starts, key_valid = doc_info(doc_len, key_places)
        allowed = visible(query_places, key_places, query_docs, key_docs, key_valid)[:, None]
        scores = (
            jnp.einsum("rqhd,rkhd->rhqk", query_heads, key_part, preferred_element_type=jnp.float32)
            * score_scale
        )
        return (key_part, value_part, allowed, jnp.where(allowed, scores, masked_score))

    keys_first, values_first = gather_keys()
    stat_shape = (row_count, HEADS, local_len)

    def max_pass(block_idx, carry_in):
        run_max, run_sum = carry_in
        key_part, value_part, allowed, scores = key_block(keys_first, values_first, block_idx)
        new_max = jnp.maximum(run_max, jnp.max(scores, axis=-1))
        expo = jnp.where(allowed, jnp.exp(scores - new_max[..., None]), 0.0)
        return (new_max, run_sum * jnp.exp(run_max - new_max) + jnp.sum(expo, axis=-1))

    run_max, run_sum = lax.fori_loop(
        0,
        block_count,
        max_pass,
        (jnp.full(stat_shape, masked_score, jnp.float32), jnp.zeros(stat_shape, jnp.float32)),
    )
    log_total = run_max + jnp.log(run_sum)

    def out_pass(block_idx, running):
        key_part, value_part, allowed, scores = key_block(keys_first, values_first, block_idx)
        soft_low = jnp.where(allowed, jnp.exp(scores - log_total[..., None]), 0.0).astype(
            jnp.bfloat16
        )
        return running + jnp.einsum(
            "rhqk,rkhd->rqhd", soft_low, value_part, preferred_element_type=jnp.float32
        )

    attended = lax.fori_loop(
        0, block_count, out_pass, jnp.zeros((row_count, local_len, HEADS, HEAD_DIM), jnp.float32)
    )
    attended_flat = attended.reshape(token_count, width)
    context = norm_gain(attended_flat, full_gain_sub.astype(jnp.float32)).astype(jnp.bfloat16)
    residual = tokens_f + jnp.dot(context, full_out, preferred_element_type=jnp.float32)
    ffn_full = gather_ffn()
    full_up, full_down, full_gain_ffn, full_gain_fsub = ffn_full
    ffn_input = norm_gain(residual, full_gain_ffn.astype(jnp.float32)).astype(jnp.bfloat16)
    hidden = jnp.dot(ffn_input, full_up, preferred_element_type=jnp.float32)
    activated = gelu_exact(hidden)
    squeezed = norm_gain(activated, full_gain_fsub.astype(jnp.float32)).astype(jnp.bfloat16)
    output = (
        (residual + jnp.dot(squeezed, full_down, preferred_element_type=jnp.float32))
        .astype(jnp.bfloat16)
        .reshape(row_count, local_len, width)
    )
    back_up, back_down, back_gain_ffn, back_gain_fsub = gather_ffn()
    cot_low = out_cotangent.reshape(token_count, width)
    cot_f = cot_low.astype(jnp.float32)
    down_part = jnp.einsum("tf,td->fd", squeezed, cot_low, preferred_element_type=jnp.float32)
    d_squeezed = jnp.einsum("td,fd->tf", cot_low, back_down, preferred_element_type=jnp.float32)
    norm_back_four = jax.vjp(norm_gain, activated, back_gain_fsub.astype(jnp.float32))[1]
    d_activated, gain_four_part = norm_back_four(d_squeezed)
    gelu_back = jax.vjp(gelu_exact, hidden)[1]
    d_hidden = gelu_back(d_activated)[0].astype(jnp.bfloat16)
    up_part = jnp.einsum("td,tf->df", ffn_input, d_hidden, preferred_element_type=jnp.float32)
    d_ffn_input = jnp.einsum("tf,df->td", d_hidden, back_up, preferred_element_type=jnp.float32)
    norm_back_three = jax.vjp(norm_gain, residual, back_gain_ffn.astype(jnp.float32))[1]
    d_resid_part, gain_three_part = norm_back_three(d_ffn_input)
    d_residual = cot_f + d_resid_part
    up_grad, down_grad, gain_ffn_grad, gain_ffn_sub_grad = (
        lax.psum_scatter(up_part, ("row", "ctx"), scatter_dimension=0, tiled=True),
        lax.psum_scatter(down_part, ("row", "ctx"), scatter_dimension=0, tiled=True),
        lax.psum_scatter(gain_three_part, ("row", "ctx"), scatter_dimension=0, tiled=True),
        lax.psum_scatter(gain_four_part, ("row", "ctx"), scatter_dimension=0, tiled=True),
    )
    d_residual_low = d_residual.astype(jnp.bfloat16)
    back_query, back_key, back_value, back_out, back_gain_attn, back_gain_sub = gather_attention()
    out_part = jnp.einsum("td,te->de", context, d_residual_low, preferred_element_type=jnp.float32)
    d_context = jnp.einsum(
        "te,de->td", d_residual_low, back_out, preferred_element_type=jnp.float32
    )
    norm_back_two = jax.vjp(norm_gain, attended_flat, back_gain_sub.astype(jnp.float32))[1]
    d_attended, gain_two_part = norm_back_two(d_context)
    d_att_low = d_attended.astype(jnp.bfloat16).reshape(row_count, local_len, HEADS, HEAD_DIM)
    delta = jnp.sum(d_att_low.astype(jnp.float32) * attended, axis=-1).transpose(0, 2, 1)
    keys_again, values_again = gather_keys()

    def grad_pass(block_idx, carry_in):
        d_query_acc, kv_buffer = carry_in
        key_part, value_part, allowed, scores = key_block(keys_again, values_again, block_idx)
        soft = jnp.where(allowed, jnp.exp(scores - log_total[..., None]), 0.0)
        soft_low = soft.astype(jnp.bfloat16)
        d_value_part = jnp.einsum(
            "rhqk,rqhd->rkhd", soft_low, d_att_low, preferred_element_type=jnp.float32
        )
        d_soft = jnp.einsum(
            "rqhd,rkhd->rhqk", d_att_low, value_part, preferred_element_type=jnp.float32
        )
        d_scores = (soft * (d_soft - delta[..., None])).astype(jnp.bfloat16)
        d_query_acc = (
            d_query_acc
            + jnp.einsum("rhqk,rkhd->rqhd", d_scores, key_part, preferred_element_type=jnp.float32)
            * score_scale
        )
        d_key_part = (
            jnp.einsum("rhqk,rqhd->rkhd", d_scores, query_heads, preferred_element_type=jnp.float32)
            * score_scale
        )
        joined = jnp.concatenate(
            [
                d_key_part.reshape(row_count, block_len, width),
                d_value_part.reshape(row_count, block_len, width),
            ],
            axis=-1,
        )
        kv_buffer = lax.dynamic_update_slice_in_dim(kv_buffer, joined, block_idx * block_len, 1)
        return (d_query_acc, kv_buffer)

    d_query_rot, kv_terms = lax.fori_loop(
        0,
        block_count,
        grad_pass,
        (
            jnp.zeros((row_count, local_len, HEADS, HEAD_DIM), jnp.float32),
            jnp.zeros((row_count, row_len, 2 * width), jnp.float32),
        ),
    )
    kv_shares = lax.psum_scatter(
        kv_terms.astype(jnp.bfloat16), "ctx", scatter_dimension=1, tiled=True
    ).astype(jnp.float32)
    d_key_rot = kv_shares[..., :width].reshape(head_shape)
    d_value_low = kv_shares[..., width:].reshape(token_count, width).astype(jnp.bfloat16)
    query_back = jax.vjp(
        lambda tensor: rotate(tensor, cosine, sine_part, factor), query.reshape(head_shape)
    )[1]
    key_back = jax.vjp(
        lambda tensor: rotate(tensor, cosine, sine_part, 1.0 / factor), key_raw.reshape(head_shape)
    )[1]
    d_query_low = (
        query_back(d_query_rot.reshape(head_shape))[0]
        .reshape(token_count, width)
        .astype(jnp.bfloat16)
    )
    d_key_low = key_back(d_key_rot)[0].reshape(token_count, width).astype(jnp.bfloat16)
    query_part = jnp.einsum("td,te->de", normed, d_query_low, preferred_element_type=jnp.float32)
    key_part_grad = jnp.einsum("td,te->de", normed, d_key_low, preferred_element_type=jnp.float32)
    value_part_grad = jnp.einsum(
        "td,te->de", normed, d_value_low, preferred_element_type=jnp.float32
    )
    d_normed = jnp.einsum("te,de->td", d_query_low, back_query, preferred_element_type=jnp.float32)
    d_normed = d_normed + jnp.einsum(
        "te,de->td", d_key_low, back_key, preferred_element_type=jnp.float32
    )
    d_normed = d_normed + jnp.einsum(
        "te,de->td", d_value_low, back_value, preferred_element_type=jnp.float32
    )
    norm_back_one = jax.vjp(norm_gain, tokens_f, back_gain_attn.astype(jnp.float32))[1]
    d_tokens_part, gain_one_part = norm_back_one(d_normed)
    input_grad = (d_residual + d_tokens_part).reshape(row_count, local_len, width)
    query_grad, key_grad, value_grad, out_grad, gain_attn_grad, gain_attn_sub_grad = (
        lax.psum_scatter(query_part, ("row", "ctx"), scatter_dimension=0, tiled=True),
        lax.psum_scatter(key_part_grad, ("row", "ctx"), scatter_dimension=0, tiled=True),
        lax.psum_scatter(value_part_grad, ("row", "ctx"), scatter_dimension=0, tiled=True),
        lax.psum_scatter(out_part, ("row", "ctx"), scatter_dimension=0, tiled=True),
        lax.psum_scatter(gain_one_part, ("row", "ctx"), scatter_dimension=0, tiled=True),
        lax.psum_scatter(gain_two_part, ("row", "ctx"), scatter_dimension=0, tiled=True),
    )
    return (
        output,
        input_grad,
        query_grad,
        key_grad,
        value_grad,
        out_grad,
        up_grad,
        down_grad,
        gain_attn_grad,
        gain_attn_sub_grad,
        gain_ffn_grad,
        gain_ffn_sub_grad,
    )


def solution(mesh):
    placed = (
        P("row", "ctx", None),
        P("row", None),
        P(("row", "ctx"), None),
        P(("row", "ctx"), None),
        P(("row", "ctx"), None),
        P(("row", "ctx"), None),
        P(("row", "ctx"), None),
        P(("row", "ctx"), None),
        P(("row", "ctx")),
        P(("row", "ctx")),
        P(("row", "ctx")),
        P(("row", "ctx")),
        P("row", "ctx", None),
    )
    return jax.shard_map(
        body,
        mesh=mesh,
        in_specs=placed,
        out_specs=(
            P("row", "ctx", None),
            P("row", "ctx", None),
            P(("row", "ctx"), None),
            P(("row", "ctx"), None),
            P(("row", "ctx"), None),
            P(("row", "ctx"), None),
            P(("row", "ctx"), None),
            P(("row", "ctx"), None),
            P(("row", "ctx")),
            P(("row", "ctx")),
            P(("row", "ctx")),
            P(("row", "ctx")),
        ),
        check_vma=False,
    )
```

profile of v0, /device:TPU:0, one launch (start us, length us, event | category | flops | bytes accessed | tf_op | source)
XLA Modules:
  0.0 3915.6 jit_solution(8952744382972543884)
XLA Ops:
  12.0 42.7 %all-reduce.12 = (bf16[2048]{0:T(1024)(128)(2,1)S(1)}, bf16[2048]{0:T(1024)(128)(2,1)S(1)}, bf16[2048]{0:T(1024)(128)(2,1)S(1)}) all-reduce(bf16[2048]{0:T(1024)(128)(2,1)S(1)} %dynamic-update-slice, bf16[2048]{0:T(1024)(128)(2,1)S(1)} %dynamic-update-slice.1, ...), channel_id=1, replica_groups=mesh['row'=4,'ctx'=8] {'row','ctx'}, use_global_device_ids=true, to_apply=%add.4 | all-reduce | flops 6144 | bytes 24576
  60.0 31.3 all-gather.10.cloned.1.call-done
  105.1 65.2 %all-gather.18.cloned.1.call-done = bf16[2048,2048]{1,0:T(8,128)(2,1)} async-done(((bf16[64,2048]{1,0:T(8,128)(2,1)}), bf16[2048,2048]{1,0:T(8,128)(2,1)}) %all-gather.18.cloned.1.call-update) | async-done | bytes 8388624 | tf_op jit(solution)/shard_map/all_gather | solution.py:92
  182.7 66.6 %all-gather.14.cloned.1.call-done = bf16[2048,2048]{1,0:T(8,128)(2,1)} async-done(((bf16[64,2048]{1,0:T(8,128)(2,1)}), bf16[2048,2048]{1,0:T(8,128)(2,1)}) %all-gather.14.cloned.1.call-update) | async-done | bytes 8388624 | tf_op jit(solution)/shard_map/all_gather | solution.py:93
  283.3 39.6 %all-gather = bf16[32,1,256]{2,1,0:T(2,128)(2,1)S(1)} all-gather(bf16[1,1,256]{2,1,0:T(2,128)(2,1)S(1)} %reshape.594), channel_id=1, replica_groups=mesh['row'=4,'ctx'=8] {'row','ctx'}, dimensions={0}, use_global_device_ids=true | all-gather | bytes 16896 | tf_op jit(solution)/shard_map/all_gather | solution.py:105
  340.2 23.1 copy.108
  363.3 137.6 %all-gather.16.cloned.1.call-done = bf16[2,2048,2048]{1,0,2:T(2,128)(2,1)} async-done(((bf16[2,256,2048]{1,0,2:T(2,128)(2,1)}), bf16[2,2048,2048]{1,0,2:T(2,128)(2,1)}) %all-gather.16.cloned.1.call-update) | async-done | bytes 16777232 | tf_op jit(solution)/shard_map/all_gather | solution.py:131
  500.9 17.5 copy.110
  518.3 127.3 %while.52 = (s32[]{:T(128)}, f32[2,32,256]{2,1,0:T(8,128)S(1)}, f32[2,32,256]{2,1,0:T(8,128)S(1)}, s32[2,256]{1,0:T(2,128)S(1)}, s32[2,16]{0,1:T(8,128)S(1)}, /*...) while((s32[]{:T(128)}, f32[2,32,256]{2,1,0:T(8,128)S(1)}, ...), condition=%wide.region_9.10_spmd.clone, body=%wide.region_5.9_spmd.clone.sunk | while | flops 1142555136 | bytes 75060816 | solution.py:164
  519.1 15.3 fusion.160
  550.4 15.8 fusion.160
  566.3 15.4 select_reduce_fusion.2
  582.6 16.0 fusion.160
  598.6 15.2 select_reduce_fusion.2
  614.6 15.8 fusion.160
  645.7 65.6 %while.53 = (s32[]{:T(128)}, f32[2,256,32,64]{1,3,2,0:T(8,128)}, bf16[2,2048,32,64]{1,3,2,0:T(8,128)(2,1)}, s32[2,256]{1,0:T(2,128)S(1)}, s32[2,16]{0,1:T(8,128)...) while((s32[]{:T(128)}, f32[2,256,32,64]{1,3,2,0:T(8,128)}, ...), condition=%wide.region_12.13_spmd.clone, body=%wide.region_10.12_spmd.clone.sunk | while | flops 2193146368 | bytes 19487832 | solution.py:181
  661.9 15.2 bitcast_add_fusion.5
  677.9 17.1 bitcast_add_fusion.5
  695.8 15.4 bitcast_add_fusion.5
  746.8 30.6 all-gather.22.cloned.1.call-done
  777.3 58.8 %fusion.92 = (f32[512]{0:T(512)S(1)}, f32[512,8192]{1,0:T(8,128)}, f32[512,8192]{1,0:T(8,128)}, f32[512,8192]{1,0:T(8,128)}) fusion(bf16[2048,8192]{1,0:T(8,128)(2,1)} %all-gather.22.cloned.1.call-done, f32[512,2048]{1,0:T(8,128)} %copy-done.7, f32[2048]{0:T(1024)S(1)} %copy-done.30, f32[512]{0:T(512)S(1)} %fusion.78, f32[512]{0:T(512)S(1)} %broadcast_multiply_fusion.4), kind=kOutput, calls=%fused_computation.197 | convolution fusion | flops 17456693248 | bytes 88094720 | tf_op jit(solution)/shard_map/dot_general | solution.py:190
  836.2 137.0 %all-gather.24.cloned.1.call-done = bf16[8192,2048]{1,0:T(8,128)(2,1)} async-done(((bf16[256,2048]{1,0:T(8,128)(2,1)}), bf16[8192,2048]{1,0:T(8,128)(2,1)}) %all-gather.24.cloned.1.call-update) | async-done | bytes 33554448 | tf_op jit(solution)/shard_map/all_gather | solution.py:103
  973.2 27.6 multiply_reduce_fusion.1
  1014.7 27.0 add_convert_fusion
  1041.8 26.4 multiply_reduce_fusion.3
  1109.8 426.3 %while.54 = (s32[]{:T(128)}, f32[2,256,32,64]{1,3,2,0:T(8,128)}, bf16[2,2048,4096]{2,1,0:T(8,128)(2,1)}, bf16[2,2048,32,64]{1,3,2,0:T(8,128)(2,1)}, s32[2,256]{1...) while((s32[]{:T(128)}, f32[2,256,32,64]{1,3,2,0:T(8,128)}, ...), condition=%wide.region_28.29_spmd.clone, body=%wide.region_26.28_spmd.clone.sunk | while | flops 5495112192 | bytes 240080512 | solution.py:261
  1110.2 17.8 fusion.175
  1128.8 21.8 fusion.176
  1162.4 16.3 fusion.177
  1215.8 17.8 fusion.175
  1234.4 21.8 fusion.176
  1269.2 16.3 fusion.177
  1322.6 17.8 fusion.175
  1341.2 21.8 fusion.176
  1376.0 16.3 fusion.177
  1429.3 17.8 fusion.175
  1447.9 21.8 fusion.176
  1482.7 16.3 fusion.177
  1558.0 181.8 %reduce-scatter.8.cloned.1.call-done = bf16[2,256,4096]{2,1,0:T(8,128)(2,1)} async-done(((bf16[2,2048,4096]{2,1,0:T(8,128)(2,1)}), bf16[2,256,4096]{2,1,0:T(8,128)(2,1)}) %reduce-scatter.8.cloned.1.call-update) | async-done | bytes 4194320 | tf_op jit(solution)/shard_map/reduce_scatter | solution.py:270
  1799.3 32.8 fusion.87
  1833.7 34.3 fusion.89
  1868.0 28.0 add_convert_fusion.4
  1930.4 44.5 %all-reduce.11 = (f32[2048]{0:T(1024)S(1)}, f32[2048]{0:T(1024)S(1)}, f32[2048]{0:T(1024)S(1)}, f32[8192]{0:T(1024)S(1)}) all-reduce(f32[2048]{0:T(1024)S(1)} %get-tuple-element.926, f32[2048]{0:T(1024)S(1)} %copy-done.78, f32[2048]{0:T(1024)S(1)} %copy-done.77, ...), channel_id=9, replica_groups=mesh['row'=4,'ctx'=8] {'row','ctx'}, use_global_device_ids=true, to_apply=%region_39.40.clone | all-reduce | flops 14336 | bytes 114688
  1983.8 130.1 %reduce-scatter.10.cloned.1.call-done = f32[64,2048]{1,0:T(8,128)} async-done(((f32[2048,2048]{1,0:T(8,128)}), f32[64,2048]{1,0:T(8,128)}) %reduce-scatter.10.cloned.1.call-update) | async-done | bytes 524304 | tf_op jit(solution)/shard_map/reduce_scatter | solution.py:303
  2113.9 187.1 %reduce-scatter.12.cloned.1.call-done = f32[64,2048]{1,0:T(8,128)} async-done(((f32[2048,2048]{1,0:T(8,128)}), f32[64,2048]{1,0:T(8,128)}) %reduce-scatter.12.cloned.1.call-update) | async-done | bytes 524304 | tf_op jit(solution)/shard_map/reduce_scatter | solution.py:304
  2301.0 188.2 %reduce-scatter.14.cloned.1.call-done = f32[64,2048]{1,0:T(8,128)} async-done(((f32[2048,2048]{1,0:T(8,128)}), f32[64,2048]{1,0:T(8,128)}) %reduce-scatter.14.cloned.1.call-update) | async-done | bytes 524304 | tf_op jit(solution)/shard_map/reduce_scatter | solution.py:305
  2489.2 706.5 %reduce-scatter.18.cloned.1.call-done = f32[64,8192]{1,0:T(8,128)} async-done(((f32[2048,8192]{1,0:T(8,128)}), f32[64,8192]{1,0:T(8,128)}) %reduce-scatter.18.cloned.1.call-update) | async-done | bytes 2097168 | tf_op jit(solution)/shard_map/reduce_scatter | solution.py:213
  3195.8 713.1 %reduce-scatter.20.cloned.1.call-done = f32[256,2048]{1,0:T(8,128)} async-done(((f32[8192,2048]{1,0:T(8,128)}), f32[256,2048]{1,0:T(8,128)}) %reduce-scatter.20.cloned.1.call-update) | async-done | bytes 2097168 | tf_op jit(solution)/shard_map/reduce_scatter | solution.py:214
  (410 shorter events, 557.0 us)
Async XLA Ops:
  7.2 49.5 %copy-start.2 = (bf16[2,256,2048]{2,1,0:T(8,128)(2,1)S(1)}, bf16[2,256,2048]{2,1,0:T(8,128)(2,1)}, u32[]{:S(2)}) copy-start(bf16[2,256,2048]{2,1,0:T(8,128)(2,1)} %param.19) | copy-start | bytes 6291460
  7.2 84.2 %all-gather.10.cloned.1.call-start = ((), (), s32[]{:S(2)}) async-start(), calls=%async_computation.7 | async-start | bytes 8650752 | tf_op jit(solution)/shard_map/all_gather | solution.py:94
  7.9 162.4 %all-gather.18.cloned.1.call-start = ((), (), s32[]{:S(2)}) async-start(), calls=%async_computation.11 | async-start | bytes 8650752 | tf_op jit(solution)/shard_map/all_gather | solution.py:92
  8.7 240.6 %all-gather.14.cloned.1.call-start = ((), (), s32[]{:S(2)}) async-start(), calls=%async_computation.9 | async-start | bytes 8650752 | tf_op jit(solution)/shard_map/all_gather | solution.py:93
  9.4 330.8 %all-gather.12.cloned.1.call-start = ((), (), s32[]{:S(2)}) async-start(), calls=%async_computation.8 | async-start | bytes 18874368 | tf_op jit(solution)/shard_map/all_gather | solution.py:132
  54.8 48.4 %copy-start.47 = (f32[2048]{0:T(1024)}, f32[2048]{0:T(1024)S(1)}, u32[]{:S(2)}) copy-start(f32[2048]{0:T(1024)S(1)} %convert_element_type.186) | copy-start | bytes 24580
  58.0 43.2 %copy-start.52 = (f32[512]{0:T(512)}, f32[512]{0:T(512)S(1)}, u32[]{:S(2)}) copy-start(f32[512]{0:T(512)S(1)} %rsqrt.47) | copy-start | bytes 6148
  58.0 43.2 %copy-start.54 = (f32[1,2,2,128]{3,1,2,0:T(2,128)}, f32[1,2,2,128]{3,1,2,0:T(2,128)S(1)}, u32[]{:S(2)}) copy-start(f32[1,2,2,128]{3,1,2,0:T(2,128)S(1)} %copy.164) | copy-start | bytes 6148
  60.0 41.5 %copy-start.79 = (s32[2,16]{1,0:T(2,128)S(1)}, s32[2,16]{1,0:T(2,128)}, u32[]{:S(2)}) copy-start(s32[2,16]{1,0:T(2,128)} %param.20) | copy-start | bytes 388
  101.2 399.6 %all-gather.16.cloned.1.call-start = ((), (), s32[]{:S(2)}) async-start(), calls=%async_computation.10 | async-start | bytes 18874368 | tf_op jit(solution)/shard_map/all_gather | solution.py:131
  102.8 174.4 %copy-start.28 = (f32[512,64]{0,1:T(8,128)}, f32[512,64]{0,1:T(8,128)S(1)}, u32[]{:S(2)}) copy-start(f32[512,64]{0,1:T(8,128)S(1)} %get-tuple-element.1038) | copy-start | bytes 393220
  103.1 170.5 %copy-start.36 = (f32[512,32]{0,1:T(8,128)}, f32[512,32]{0,1:T(8,128)S(1)}, u32[]{:S(2)}) copy-start(f32[512,32]{0,1:T(8,128)S(1)} %get-tuple-element.1016) | copy-start | bytes 196612
  103.1 170.5 %copy-start.38 = (f32[512,32]{0,1:T(8,128)}, f32[512,32]{0,1:T(8,128)S(1)}, u32[]{:S(2)}) copy-start(f32[512,32]{0,1:T(8,128)S(1)} %get-tuple-element.1017) | copy-start | bytes 196612
  249.3 12.6 copy-start.22
  279.9 43.8 %copy-start.15 = (f32[512,32,32]{0,2,1:T(8,128)S(1)}, f32[512,32,32]{0,2,1:T(8,128)}, u32[]{:S(2)}) copy-start(f32[512,32,32]{0,2,1:T(8,128)} %get-tuple-element.1008) | copy-start | bytes 6291460
  279.9 455.1 %all-gather.20.cloned.1.call-start = ((), (), s32[]{:S(2)}) async-start(), calls=%async_computation.12 | async-start | bytes 8650752 | tf_op jit(solution)/shard_map/all_gather | solution.py:95
  280.5 496.8 %all-gather.22.cloned.1.call-start = ((), (), s32[]{:S(2)}) async-start(), calls=%async_computation.13 | async-start | bytes 34603008 | tf_op jit(solution)/shard_map/all_gather | solution.py:102
  281.3 691.9 %all-gather.24.cloned.1.call-start = ((), (), s32[]{:S(2)}) async-start(), calls=%async_computation.14 | async-start | bytes 34603008 | tf_op jit(solution)/shard_map/all_gather | solution.py:103
  282.0 1457.7 %reduce-scatter.8.cloned.1.call-start = ((), (), s32[]{:S(2)}) async-start(), calls=%async_computation.15 | async-start | bytes 37748736 | tf_op jit(solution)/shard_map/reduce_scatter | solution.py:270
  711.3 9.9 copy-start.40
  743.6 33.7 copy-start.30
  743.6 324.6 %copy-start.32 = (f32[512]{0:T(512)}, f32[512]{0:T(512)S(1)}, u32[]{:S(2)}) copy-start(f32[512]{0:T(512)S(1)} %broadcast_multiply_fusion.4) | copy-start | bytes 6148
  746.7 321.5 %copy-start.34 = (f32[512]{0:T(512)}, f32[512]{0:T(512)S(1)}, u32[]{:S(2)}) copy-start(f32[512]{0:T(512)S(1)} %fusion.78) | copy-start | bytes 6148
  746.7 226.4 %copy-start.12 = (bf16[2,256,2048]{2,1,0:T(8,128)(2,1)S(1)}, bf16[2,256,2048]{2,1,0:T(8,128)(2,1)}, u32[]{:S(2)}) copy-start(bf16[2,256,2048]{2,1,0:T(8,128)(2,1)} %param.31) | copy-start | bytes 6291460
  746.7 226.4 %copy-start.45 = (f32[32,1,256]{2,1,0:T(1,128)S(1)}, f32[32,1,256]{2,1,0:T(1,128)}, u32[]{:S(2)}) copy-start(f32[32,1,256]{2,1,0:T(1,128)} %convert_element_type.218) | copy-start | bytes 98308
  836.1 178.6 %copy-start.59 = (f32[512]{0:T(512)}, f32[512]{0:T(512)S(1)}, u32[]{:S(2)}) copy-start(f32[512]{0:T(512)S(1)} %broadcast_multiply_fusion.3) | copy-start | bytes 6148
  1000.8 14.0 copy-start.61
  1014.7 27.0 copy-start.8
  1041.8 26.4 copy-start.64
  1098.7 11.1 copy-start.1
  1098.7 11.1 copy-start.27
  1098.7 11.1 copy-start.41
  1098.7 11.1 copy-start.44
  1098.7 11.0 copy-start.51
  1536.2 447.6 %reduce-scatter.16.cloned.1.call-start = ((), (), s32[]{:S(2)}) async-start(), calls=%async_computation.19 | async-start | bytes 17301504 | tf_op jit(solution)/shard_map/reduce_scatter | solution.py:306
  1551.3 562.6 %reduce-scatter.10.cloned.1.call-start = ((), (), s32[]{:S(2)}) async-start(), calls=%async_computation.16 | async-start | bytes 17301504 | tf_op jit(solution)/shard_map/reduce_scatter | solution.py:303
  1774.9 526.2 %reduce-scatter.12.cloned.1.call-start = ((), (), s32[]{:S(2)}) async-start(), calls=%async_computation.17 | async-start | bytes 17301504 | tf_op jit(solution)/shard_map/reduce_scatter | solution.py:304
  1787.1 702.1 %reduce-scatter.14.cloned.1.call-start = ((), (), s32[]{:S(2)}) async-start(), calls=%async_computation.18 | async-start | bytes 17301504 | tf_op jit(solution)/shard_map/reduce_scatter | solution.py:305
  1798.6 1397.1 %reduce-scatter.18.cloned.1.call-start = ((), (), s32[]{:S(2)}) async-start(), calls=%async_computation.20 | async-start | bytes 69206016 | tf_op jit(solution)/shard_map/reduce_scatter | solution.py:213
  1832.1 2076.7 %reduce-scatter.20.cloned.1.call-start = ((), (), s32[]{:S(2)}) async-start(), calls=%async_computation.21 | async-start | bytes 69206016 | tf_op jit(solution)/shard_map/reduce_scatter | solution.py:214
  1868.0 28.0 copy-start.19
  1905.9 10.1 copy-start.4
  1905.9 10.1 slice-start
  1905.9 10.1 copy-start.48
  1905.9 10.1 copy-start.55
  1916.0 10.4 copy-start.68
  1916.0 12.4 copy-start.53
  1926.4 50.9 %copy-start.66 = (f32[512]{0:T(512)S(1)}, f32[512]{0:T(512)}, u32[]{:S(2)}) copy-start(f32[512]{0:T(512)} %copy-done.65) | copy-start | bytes 6148
  (49 other events, 188.7 us)
Sparse Core Ops, SparseCore 0:
  10.9 80.4 all-gather.9
  94.2 76.0 all-gather.17
  173.2 76.0 all-gather.13
  251.6 88.5 all-gather.11
  341.9 158.9 all-gather.15
  503.6 77.4 all-gather.19
  583.9 193.3 all-gather.21
  780.2 192.9 all-gather.23
  1536.3 203.4 reduce-scatter.7
  1742.6 182.6 reduce-scatter.15
  1928.3 185.5 reduce-scatter.9
  2116.7 184.2 reduce-scatter.11
  2304.0 185.1 reduce-scatter.13
  2492.1 703.5 reduce-scatter.17
  3198.7 710.1 reduce-scatter.19
where the time goes:
time: 3930 us; the launch traced here: 3920 us
  waiting for transfers between devices  2590 us (66%)
  matrix products  757 us (19%)
  local copies, waits for them, and re-layouts  232 us (6%)
  other arithmetic  190 us (5%)
  blocking collectives  127 us (3%)
    reduce_scatter x1, waiting for transfers between devices, body(): lax.psum_scatter(down_part, ('row', 'ctx'), scatter_dimension=0, tiled=True)  713 us
    reduce_scatter x1, waiting for transfers between devices, body(): lax.psum_scatter(up_part, ('row', 'ctx'), scatter_dimension=0, tiled=True)  707 us
    reduce_scatter x1, waiting for transfers between devices, body(): lax.psum_scatter(value_part_grad, ('row', 'ctx'), scatter_dimension=0, ti...  188 us
    reduce_scatter x1, waiting for transfers between devices, body(): lax.psum_scatter(key_part_grad, ('row', 'ctx'), scatter_dimension=0, tile...  187 us
    reduce_scatter x1, waiting for transfers between devices, body(): lax.psum_scatter(kv_terms.astype(jnp.bfloat16), 'ctx', scatter_dimension=...  182 us
    all_gather x1, waiting for transfers between devices, gather_keys(): lax.all_gather(key_rot, 'ctx', axis=1, tiled=True)  138 us
    all_gather x1, waiting for transfers between devices, gather_ffn(): lax.all_gather(w_down, ('row', 'ctx'), axis=0, tiled=True)  137 us
    dot_general x8, matrix products, key_block(): jnp.einsum('rqhd,rkhd->rhqk', query_heads, key_part, preferred_element_ty...  134 us
  transfers between devices with their start and end apart: 15, of which 13 were waited for; matrix products, arithmetic and copies ran while one was open for 15% of the time, Pallas kernels for 0%

commit v1 on v0

v1 whole, which is shorter than its diff:
```python
import functools
import jax, jax.numpy as jnp
from jax import lax
from jax.experimental import pallas as pl
from jax.experimental.pallas import tpu as pltpu
bf16=jnp.bfloat16; f32=jnp.float32
HEAD_DIM=64
LOG2E=1.4426950408889634
NEG=-1e30

def fwd_kernel(nh, blk, span_ref, qT_ref, kT_ref, vT_ref, lo_ref, o_ref, oT_ref, lse_ref, k_s, qm_s, acc_s, m_s, l_s):
    r=pl.program_id(0); qb=pl.program_id(1)
    n=kT_ref.shape[1]//blk
    W=2*HEAD_DIM
    @pl.when(qb==0)
    def _():
        for c in range(n):
            k_s[pl.ds(c*blk,blk),:]=kT_ref[:,pl.ds(c*blk,blk)].T
    zero=jnp.zeros((HEAD_DIM,blk),bf16)
    for h in range(nh):
        own=h%2
        qm_s[h,pl.ds(own*HEAD_DIM,HEAD_DIM),:]=qT_ref[pl.ds(h*HEAD_DIM,HEAD_DIM),:]
        qm_s[h,pl.ds((1-own)*HEAD_DIM,HEAD_DIM),:]=zero
    acc_s[...]=jnp.zeros_like(acc_s)
    m_s[...]=jnp.full_like(m_s,NEG)
    l_s[...]=jnp.zeros_like(l_s)
    lo=lo_ref[0]
    def step(kb,masked):
        off=pl.multiple_of(kb*blk,blk)
        if masked:
            key=off+lax.broadcasted_iota(jnp.int32,(blk,blk),0)
            qry=qb*blk+lax.broadcasted_iota(jnp.int32,(blk,blk),1)
            ok=(key<=qry)&(key>=lo)
        for h in range(nh):
            kk=k_s[pl.ds(off,blk),pl.ds((h//2)*W,W)]
            s=jnp.dot(kk,qm_s[h],preferred_element_type=f32)*(LOG2E*HEAD_DIM**-0.5)
            if masked: s=jnp.where(ok,s,NEG)
            m0=m_s[h:h+1,:]
            m1=jnp.maximum(m0,jnp.max(s,axis=0,keepdims=True))
            p=jnp.exp2(s-m1)
            al=jnp.exp2(m0-m1)
            m_s[h:h+1,:]=m1
            l_s[h:h+1,:]=l_s[h:h+1,:]*al+jnp.sum(p,axis=0,keepdims=True)
            vv=vT_ref[pl.ds(h*HEAD_DIM,HEAD_DIM),pl.ds(off,blk)]
            sl=pl.ds(h*HEAD_DIM,HEAD_DIM)
            acc_s[sl,:]=acc_s[sl,:]*al+jnp.dot(vv,p.astype(bf16),preferred_element_type=f32)
    loops(span_ref,r,qb,blk,step)
    for h in range(nh):
        l=l_s[h:h+1,:]
        sl=pl.ds(h*HEAD_DIM,HEAD_DIM)
        oT_ref[sl,:]=acc_s[sl,:]/l
        lse_ref[h:h+1,:]=m_s[h:h+1,:]+jnp.log2(l)
    o_ref[...]=oT_ref[...].T.astype(bf16)

def loops(span_ref,r,qb,blk,step):
    k0=span_ref[r,qb,0]
    u0=span_ref[r,qb,1]
    def masked_body(t,c):
        kb=jnp.where(t<u0-k0,k0+t,qb)
        step(kb,True); return c
    def plain(kb,c):
        step(kb,False); return c
    lax.fori_loop(0,u0-k0+1,masked_body,0)
    lax.fori_loop(u0,qb,plain,0)

def bwd_kernel(nh, blk, span_ref, qT_ref, kT_ref, vT_ref, do_ref, oT_ref, lse_ref, lo_ref, dqT_ref, dkT_ref, dvT_ref,
               k_s, v_s, qm_s, dm_s, qn_s, dn_s, acc_s, dk_s, dv_s, p_s, ds_s, dl_s):
    r=pl.program_id(0); qb=pl.program_id(1)
    n=kT_ref.shape[1]//blk
    W=2*HEAD_DIM; scale=HEAD_DIM**-0.5
    @pl.when(qb==0)
    def _():
        for c in range(n):
            k_s[pl.ds(c*blk,blk),:]=kT_ref[:,pl.ds(c*blk,blk)].T
            v_s[pl.ds(c*blk,blk),:]=vT_ref[:,pl.ds(c*blk,blk)].T
        dk_s[...]=jnp.zeros_like(dk_s)
        dv_s[...]=jnp.zeros_like(dv_s)
    zero=jnp.zeros((HEAD_DIM,blk),bf16)
    doT=do_ref[...].T
    q=qT_ref[...].T
    lane=lax.broadcasted_iota(jnp.int32,(blk,W),1)
    prod=doT.astype(f32)*oT_ref[...]
    for h in range(nh):
        own=h%2
        sl=slice(h*HEAD_DIM,(h+1)*HEAD_DIM)
        qm_s[h,pl.ds(own*HEAD_DIM,HEAD_DIM),:]=qT_ref[pl.ds(h*HEAD_DIM,HEAD_DIM),:]
        qm_s[h,pl.ds((1-own)*HEAD_DIM,HEAD_DIM),:]=zero
        dm_s[h,pl.ds(own*HEAD_DIM,HEAD_DIM),:]=doT[sl,:]
        dm_s[h,pl.ds((1-own)*HEAD_DIM,HEAD_DIM),:]=zero
        mine=(lane//HEAD_DIM)==own
        pr=slice((h//2)*W,(h//2)*W+W)
        qn_s[h//2,pl.ds(own*blk,blk),:]=jnp.where(mine,q[:,pr],jnp.zeros((),bf16))
        dn_s[h//2,pl.ds(own*blk,blk),:]=jnp.where(mine,do_ref[:,pr],jnp.zeros((),bf16))
        dl_s[h:h+1,:]=jnp.sum(prod[sl,:],axis=0,keepdims=True)
    acc_s[...]=jnp.zeros_like(acc_s)
    lo=lo_ref[0]
    def step(kb,masked):
        off=pl.multiple_of(kb*blk,blk)
        if masked:
            key=off+lax.broadcasted_iota(jnp.int32,(blk,blk),0)
            qry=qb*blk+lax.broadcasted_iota(jnp.int32,(blk,blk),1)
            ok=(key<=qry)&(key>=lo)
        for g in range(nh//2):
            kk=k_s[pl.ds(off,blk),pl.ds(g*W,W)]
            vv=v_s[pl.ds(off,blk),pl.ds(g*W,W)]
            for own in range(2):
                h=2*g+own
                s=jnp.dot(kk,qm_s[h],preferred_element_type=f32)*(LOG2E*scale)
                p=jnp.exp2(s-lse_ref[h:h+1,:])
                if masked: p=jnp.where(ok,p,0.0)
                dp=jnp.dot(vv,dm_s[h],preferred_element_type=f32)
                ds=(p*(dp-dl_s[h:h+1,:])).astype(bf16)
                p_s[g,:,pl.ds(own*blk,blk)]=p.astype(bf16)
                ds_s[g,:,pl.ds(own*blk,blk)]=ds
                sl=pl.ds(h*HEAD_DIM,HEAD_DIM)
                acc_s[sl,:]+=jnp.dot(kT_ref[sl,pl.ds(off,blk)],ds,preferred_element_type=f32)
            dv_s[pl.ds(off,blk),pl.ds(g*W,W)]+=jnp.dot(p_s[g],dn_s[g],preferred_element_type=f32)
            dk_s[pl.ds(off,blk),pl.ds(g*W,W)]+=jnp.dot(ds_s[g],qn_s[g],preferred_element_type=f32)
    loops(span_ref,r,qb,blk,step)
    dqT_ref[...]=acc_s[...]*scale
    @pl.when(qb==n-1)
    def _():
        for c in range(n):
            dkT_ref[:,pl.ds(c*blk,blk)]=(dk_s[pl.ds(c*blk,blk),:]*scale).T
            dvT_ref[:,pl.ds(c*blk,blk)]=dv_s[pl.ds(c*blk,blk),:].T.astype(bf16)

def spans(lo,blk):
    rows,length=lo.shape
    n=length//blk
    lob=lo.reshape(rows,n,blk)
    first=lob[:,:,0]//blk
    last=(lob[:,:,-1]+blk-1)//blk
    own=jnp.arange(n,dtype=jnp.int32)[None,:]
    return jnp.stack([jnp.minimum(first,own),jnp.minimum(last,own)],axis=-1).astype(jnp.int32)

PARAMS=pltpu.CompilerParams(dimension_semantics=("arbitrary","arbitrary"),vmem_limit_bytes=60*2**20)

def attention_fwd(qT,kT,vT,lo,blk):
    rows,length=lo.shape
    dim,T=qT.shape
    nh=dim//HEAD_DIM; n=length//blk
    return pl.pallas_call(functools.partial(fwd_kernel,nh,blk),
        out_shape=(jax.ShapeDtypeStruct((T,dim),bf16),jax.ShapeDtypeStruct((dim,T),f32),jax.ShapeDtypeStruct((nh,T),f32)),
        grid_spec=pltpu.PrefetchScalarGridSpec(num_scalar_prefetch=1,grid=(rows,n),
            in_specs=[pl.BlockSpec((dim,blk),lambda r,q,s:(0,r*n+q)),
                      pl.BlockSpec((dim,length),lambda r,q,s:(0,r)),
                      pl.BlockSpec((dim,length),lambda r,q,s:(0,r)),
                      pl.BlockSpec((1,1,blk),lambda r,q,s:(r,0,q))],
            out_specs=[pl.BlockSpec((blk,dim),lambda r,q,s:(r*n+q,0)),
                       pl.BlockSpec((dim,blk),lambda r,q,s:(0,r*n+q)),
                       pl.BlockSpec((nh,blk),lambda r,q,s:(0,r*n+q))],
            scratch_shapes=[pltpu.VMEM((length,dim),bf16),pltpu.VMEM((nh,2*HEAD_DIM,blk),bf16),pltpu.VMEM((dim,blk),f32),
                            pltpu.VMEM((8,blk),f32),pltpu.VMEM((8,blk),f32)]),
        compiler_params=PARAMS,name="attention_forward",
        cost_estimate=pl.CostEstimate(flops=2*2*dim*T*length//2*2,bytes_accessed=20*2**20,transcendentals=nh*T*length//2))(spans(lo,blk),qT,kT,vT,lo[:,None,:])

def attention_bwd(qT,kT,vT,do,oT,lse,lo,blk):
    rows,length=lo.shape
    dim,T=qT.shape
    nh=dim//HEAD_DIM; n=length//blk; W=2*HEAD_DIM
    sds=jax.ShapeDtypeStruct
    return pl.pallas_call(functools.partial(bwd_kernel,nh,blk),
        out_shape=(sds((dim,T),f32),sds((dim,T),f32),sds((dim,T),bf16)),
        grid_spec=pltpu.PrefetchScalarGridSpec(num_scalar_prefetch=1,grid=(rows,n),
            in_specs=[pl.BlockSpec((dim,blk),lambda r,q,s:(0,r*n+q)),
                      pl.BlockSpec((dim,length),lambda r,q,s:(0,r)),
                      pl.BlockSpec((dim,length),lambda r,q,s:(0,r)),
                      pl.BlockSpec((blk,dim),lambda r,q,s:(r*n+q,0)),
                      pl.BlockSpec((dim,blk),lambda r,q,s:(0,r*n+q)),
                      pl.BlockSpec((nh,blk),lambda r,q,s:(0,r*n+q)),
                      pl.BlockSpec((1,1,blk),lambda r,q,s:(r,0,q))],
            out_specs=[pl.BlockSpec((dim,blk),lambda r,q,s:(0,r*n+q)),
                       pl.BlockSpec((dim,length),lambda r,q,s:(0,r)),
                       pl.BlockSpec((dim,length),lambda r,q,s:(0,r))],
            scratch_shapes=[pltpu.VMEM((length,dim),bf16),pltpu.VMEM((length,dim),bf16),
                            pltpu.VMEM((nh,W,blk),bf16),pltpu.VMEM((nh,W,blk),bf16),
                            pltpu.VMEM((nh//2,2*blk,W),bf16),pltpu.VMEM((nh//2,2*blk,W),bf16),
                            pltpu.VMEM((dim,blk),f32),pltpu.VMEM((length,dim),f32),pltpu.VMEM((length,dim),f32),
                            pltpu.VMEM((nh//2,blk,2*blk),bf16),pltpu.VMEM((nh//2,blk,2*blk),bf16),
                            pltpu.VMEM((8,blk),f32)]),
        compiler_params=PARAMS,name="attention_backward",
        cost_estimate=pl.CostEstimate(flops=5*2*dim*T*length//2*2,bytes_accessed=40*2**20,transcendentals=nh*T*length//2))(spans(lo,blk),qT,kT,vT,do,oT,lse,lo[:,None,:])


from jax.sharding import PartitionSpec as P

ROW_LEN = 2048
XPOS_BASE = 512
EPS = 1e-5
BOTH = ("row", "ctx")


def standardize(values):
    center = values - jnp.mean(values, axis=-1, keepdims=True)
    spread = jnp.mean(center * center, axis=-1, keepdims=True)
    rstd = lax.rsqrt(spread + EPS)
    return center * rstd, rstd


def standardize_back(hat, rstd, grad):
    return rstd * (grad - jnp.mean(grad, axis=-1, keepdims=True) - hat * jnp.mean(grad * hat, axis=-1, keepdims=True))


def row_places(lengths, row_len):
    places = jnp.arange(row_len, dtype=jnp.int32)
    ends = jnp.cumsum(lengths, axis=-1)
    passed = ends[:, None, :] <= places[None, :, None]
    starts = jnp.sum(jnp.where(passed, lengths[:, None, :], 0), axis=-1)
    valid = places[None, :] < ends[:, -1:]
    lowest = jnp.where(valid, starts, places[None, :]).astype(jnp.int32)
    return (places[None, :] - starts).astype(f32), lowest


def xpos_tables(relative):
    half = HEAD_DIM // 2
    ladder = jnp.arange(half, dtype=f32) / half
    rate = jnp.power(10000.0, -ladder)
    base = (ladder + 0.4) / 1.4
    angles = rate[:, None] * relative[None, :]
    factor = jnp.power(base[:, None], (relative[None, :] - ROW_LEN / 2) / XPOS_BASE)
    return jnp.cos(angles), jnp.sin(angles), factor


def turn(values, cosine, sine, factor):
    dim, tokens = values.shape
    half = HEAD_DIM // 2
    pairs = values.reshape(dim // HEAD_DIM, 2, half, tokens)
    one, two = pairs[:, 0], pairs[:, 1]
    cosine, sine = cosine * factor, sine * factor
    return jnp.stack([one * cosine - two * sine, two * cosine + one * sine], axis=1).reshape(dim, tokens)


def phi_parts(h):
    cdf = 0.5 * (1.0 + lax.erf(h * (2.0**-0.5)))
    pdf = jnp.exp(-0.5 * h * h) * 0.3989422804014327
    return cdf, pdf


def dot(a, b, spec, kind=f32):
    return jnp.einsum(spec, a, b, preferred_element_type=f32).astype(kind)


def gather_ctx(x):
    return lax.all_gather(x, "ctx", axis=1, tiled=True)


def scatter_ctx(x):
    return lax.psum_scatter(x, "ctx", scatter_dimension=1, tiled=True)


def body(inputs, doc_len, w_query, w_key, w_value, w_out, w_up, w_down, gain_attn, gain_attn_sub, gain_ffn,
         gain_ffn_sub, out_cotangent):
    rows, local_len, width = inputs.shape
    n, m = lax.axis_size("ctx"), lax.axis_size("row")
    row_len = local_len * n
    tokens, group = rows * local_len, rows * row_len
    piece = w_query.shape[0]
    heads_dim = width // n
    ff = w_up.shape[1]
    unit = ff // (n * m)
    ff_dev = unit * m
    blk = min(512, row_len)
    mine = lax.axis_index("ctx")
    mine_row = lax.axis_index("row")

    packed = jnp.concatenate([gain_attn, gain_attn_sub, gain_ffn, gain_ffn_sub])
    packed = jnp.pad(packed, (0, -packed.shape[0] % 2048)).reshape(16, -1)
    gains = lax.all_gather(packed, BOTH, axis=0, tiled=True).reshape(n * m, -1).astype(f32)
    g_attn = gains[:, :piece].reshape(width)
    g_sub = gains[:, piece:2 * piece].reshape(width)
    g_ffn = gains[:, 2 * piece:3 * piece].reshape(width)
    g_fsub = lax.dynamic_index_in_dim(gains[:, 3 * piece:3 * piece + unit].reshape(m, n, unit), mine, 1, False).reshape(ff_dev)

    qkv_local = jnp.concatenate([w.reshape(piece, n, heads_dim) for w in (w_query, w_key, w_value)], axis=2)
    qkv_part = lax.all_to_all(qkv_local, "ctx", split_axis=1, concat_axis=0, tiled=True).reshape(n * piece, 3 * heads_dim)
    w_qkv = lax.all_gather(qkv_part, "row", axis=0, tiled=True)
    x_all = gather_ctx(inputs)
    up_local = w_up.reshape(piece, m, n, unit).transpose(0, 2, 1, 3).reshape(piece, n, ff_dev)
    up_part = lax.all_to_all(up_local, "ctx", split_axis=1, concat_axis=0, tiled=True).reshape(n * piece, ff_dev)
    out_all = lax.all_gather(w_out, BOTH, axis=0, tiled=True)
    up_all = lax.all_gather(up_part, "row", axis=0, tiled=True)
    down_all = lax.all_gather(w_down, "row", axis=0, tiled=True)
    dy_all = gather_ctx(out_cotangent).reshape(group, width)

    x_flat = x_all.reshape(group, width).astype(f32)
    x_hat, x_rstd = standardize(x_flat)
    a = (x_hat * g_attn).astype(bf16)
    qkvT = dot(w_qkv, a, "df,td->ft")
    relative, lowest = row_places(doc_len, row_len)
    cosine, sine, factor = xpos_tables(relative.reshape(group))
    inverse = 1.0 / factor
    qT = turn(qkvT[:heads_dim], cosine, sine, factor).astype(bf16)
    kT = turn(qkvT[heads_dim:2 * heads_dim], cosine, sine, inverse).astype(bf16)
    vT = qkvT[2 * heads_dim:].astype(bf16)
    o_heads, oT, lse = attention_fwd(qT, kT, vT, lowest, blk)
    o = lax.all_to_all(o_heads.reshape(rows, row_len, heads_dim), "ctx", split_axis=1, concat_axis=2, tiled=True)
    o = o.reshape(tokens, width).astype(f32)
    o_hat, o_rstd = standardize(o)
    c = (o_hat * g_sub).astype(bf16)
    x_own = inputs.reshape(tokens, width).astype(f32)
    x1 = x_own + dot(c, out_all, "td,de->te")
    x1_hat, x1_rstd = standardize(x1)
    b = (x1_hat * g_ffn).astype(bf16)
    b_all = gather_ctx(b.reshape(rows, local_len, width)).reshape(group, width)

    de = dot(dy_all, down_all, "td,fd->tf")
    h = dot(b_all, up_all, "td,df->tf")
    cdf, pdf = phi_parts(h)
    gel = h * cdf
    d_hat = de * g_fsub
    mean_own = jnp.mean(gel, axis=-1)
    off = gel - mean_own[:, None]
    stats = jnp.stack([mean_own, jnp.sum(off * off, axis=-1), jnp.sum(d_hat, axis=-1), jnp.sum(d_hat * off, axis=-1)])
    stats = lax.all_gather(stats, "ctx", axis=0, tiled=False)
    mean = jnp.mean(stats[:, 0], axis=0)
    shift = stats[:, 0] - mean
    var = (jnp.sum(stats[:, 1], axis=0) + ff_dev * jnp.sum(shift * shift, axis=0)) / ff
    rstd = lax.rsqrt(var + EPS)
    d_mean = jnp.sum(stats[:, 2], axis=0) / ff
    d_corr = rstd * jnp.sum(stats[:, 3] + stats[:, 2] * shift, axis=0) / ff
    hat = (gel - mean[:, None]) * rstd[:, None]
    e = (hat * g_fsub).astype(bf16)
    gain_fsub_part = jnp.sum(de * hat, axis=0)
    d_gel = rstd[:, None] * (d_hat - d_mean[:, None] - hat * d_corr[:, None])
    dh = (d_gel * (cdf + h * pdf)).astype(bf16)
    db_part = dot(dh, up_all, "tf,df->td", bf16)
    db = scatter_ctx(db_part.reshape(rows, row_len, width)).reshape(tokens, width).astype(f32)
    out_part = dot(e, down_all, "tf,fd->td", bf16)
    output = scatter_ctx(out_part.reshape(rows, row_len, width)).reshape(tokens, width).astype(f32)
    output = (x1 + output).astype(bf16).reshape(rows, local_len, width)
    down_part = dot(e, dy_all, "tf,td->fd", bf16)
    down_grad = lax.psum_scatter(down_part, "row", scatter_dimension=0, tiled=True).astype(f32)
    up_grad_part = dot(b_all, dh, "td,tf->df", bf16)
    up_grad_part = lax.psum_scatter(up_grad_part, "row", scatter_dimension=0, tiled=True)
    up_grad = lax.all_to_all(up_grad_part.reshape(n, piece, ff_dev), "ctx", split_axis=0, concat_axis=2, tiled=True)
    up_grad = up_grad.reshape(piece, n, m, unit).transpose(0, 2, 1, 3).reshape(piece, ff).astype(f32)

    dy = out_cotangent.reshape(tokens, width).astype(f32)
    gain_ffn_part = jnp.sum(db * x1_hat, axis=0)
    dx1 = dy + standardize_back(x1_hat, x1_rstd, db * g_ffn)
    dx1b = dx1.astype(bf16)
    dc = dot(dx1b, out_all, "te,de->td")
    gain_sub_part = jnp.sum(dc * o_hat, axis=0)
    d_o = standardize_back(o_hat, o_rstd, dc * g_sub).astype(bf16).reshape(rows, local_len, width)
    do_heads = lax.all_to_all(d_o, "ctx", split_axis=2, concat_axis=1, tiled=True).reshape(group, heads_dim)
    out_grad_part = dot(c, dx1b, "td,te->de", bf16).reshape(m, n, piece, width)
    out_grad = lax.psum_scatter(out_grad_part, "ctx", scatter_dimension=1, tiled=False)
    out_grad = lax.psum_scatter(out_grad, "row", scatter_dimension=0, tiled=False).astype(f32)
    dqT, dkT, dvT = attention_bwd(qT, kT, vT, do_heads, oT, lse, lowest, blk)
    dqT = turn(dqT, cosine, -sine, factor).astype(bf16)
    dkT = turn(dkT, cosine, -sine, inverse).astype(bf16)
    dqkvT = jnp.concatenate([dqT, dkT, dvT], axis=0)
    da_part = dot(dqkvT, w_qkv, "ft,df->td")
    da = scatter_ctx(da_part.astype(bf16).reshape(rows, row_len, width)).reshape(tokens, width).astype(f32)
    gain_attn_part = jnp.sum(da_part * x_hat, axis=0)
    qkv_grad = dot(a, dqkvT, "td,ft->df", bf16)
    qkv_grad = lax.psum_scatter(qkv_grad, "row", scatter_dimension=0, tiled=True)
    qkv_grad = lax.all_to_all(qkv_grad.reshape(n, piece, 3 * heads_dim), "ctx", split_axis=0, concat_axis=2, tiled=True)
    qkv_grad = qkv_grad.reshape(piece, n, 3, heads_dim).astype(f32)
    query_grad, key_grad, value_grad = (qkv_grad[:, :, i].reshape(piece, width) for i in range(3))
    own_hat, own_rstd = standardize(x_own)
    input_grad = (dx1 + standardize_back(own_hat, own_rstd, da * g_attn)).reshape(rows, local_len, width)

    gain_parts = jnp.concatenate([gain_attn_part, gain_sub_part, gain_ffn_part, gain_fsub_part])
    gain_all = lax.all_gather(gain_parts, BOTH, axis=0, tiled=False)
    place = mine_row * n + mine
    wide = jnp.sum(gain_all[:, :3 * width], axis=0).reshape(3, n * m, piece)
    wide = lax.dynamic_index_in_dim(wide, place, 1, False)
    narrow = lax.dynamic_index_in_dim(gain_all[:, 3 * width:].reshape(m, n, m, unit), mine, 1, False)
    narrow = jnp.sum(lax.dynamic_index_in_dim(narrow, mine_row, 1, False), axis=0)
    return (output, input_grad, query_grad, key_grad, value_grad, out_grad, up_grad, down_grad,
            wide[0], wide[1], wide[2], narrow)


def solution(mesh):
    split = P(BOTH, None)
    acts = P("row", "ctx", None)
    gain = P(BOTH)
    return jax.shard_map(
        body,
        mesh=mesh,
        in_specs=(acts, P("row", None)) + (split,) * 6 + (gain,) * 4 + (acts,),
        out_specs=(acts, acts) + (split,) * 6 + (gain,) * 4,
        check_vma=False,
    )
```

time: 3930 us -> 1430 us (0.36)
  waiting for transfers between devices: 2590 us -> 706 us
  matrix products: 757 us -> 252 us
  local copies, waits for them, and re-layouts: 232 us -> 76.2 us
  Pallas kernels: 0 us -> 109 us
  other arithmetic: 190 us -> 107 us
    reduce_scatter x7 -> x8, waiting for transfers between devices: 2110 us -> 361 us  [the longest x3 273 us: scatter_ctx(): return lax.psum_scatter(x, 'ctx', scatter_dimension=1, tiled=True)]
    dot_general x46 -> x12, matrix products: 757 us -> 252 us  [dot(): return jnp.einsum(spec, a, b, preferred_element_type=f32).astype(kind)]
    all_gather x8 -> x7, waiting for transfers between devices: 482 us -> 308 us  [the longest x3 195 us: gather_ctx(): return lax.all_gather(x, 'ctx', axis=1, tiled=True)]
    pallas_call x0 -> x2, Pallas kernels: none -> 109 us  [the longest x1 66.1 us: attention_bwd(): pl.pallas_call(functools.partial(bwd_kernel, nh, blk), out_shape=(sds((di...]
    unnamed x2 -> x0, blocking collectives: 87.3 us -> none
    dynamic_update_slice x8 -> x0, local copies, waits for them, and re-layouts: 79 us -> none  [grad_pass(): lax.dynamic_update_slice_in_dim(kv_buffer, joined, block_idx * block_len, 1)]
    all_gather x1 -> x3, blocking collectives: 39.6 us -> 116 us  [the longest x1 55.7 us: body(): lax.all_gather(packed, BOTH, axis=0, tiled=True).reshape(n * m, -1)]
    reduce_sum x27 -> x16, other arithmetic: 95.4 us -> 59.8 us  [the longest x1 23.8 us: body(): gain_fsub_part = jnp.sum(de * hat, axis=0)]
  transfers between devices with their start and end apart: 15 -> 20, of which waited for: 13 -> 13; matrix products, arithmetic and copies ran while one was open for 15% -> 23% of each run, Pallas kernels for 0% -> 8%
where the time goes in v1:
time: 1430 us; the launch traced here: 1420 us
  waiting for transfers between devices  706 us (49%)
  matrix products  252 us (18%)
  blocking collectives  137 us (10%)
  Pallas kernels  109 us (8%)
  other arithmetic  107 us (7%)
  local copies, waits for them, and re-layouts  76.2 us (5%)
  starting transfers between devices  19.4 us (1%)
  between operations  15 us (1%)
    reduce_scatter x3, waiting for transfers between devices, scatter_ctx(): return lax.psum_scatter(x, 'ctx', scatter_dimension=1, tiled=True)  273 us
    dot_general x12, matrix products, dot(): return jnp.einsum(spec, a, b, preferred_element_type=f32).astype(kind)  252 us
    all_gather x3, waiting for transfers between devices, gather_ctx(): return lax.all_gather(x, 'ctx', axis=1, tiled=True)  195 us
    pallas_call x1, Pallas kernels, attention_bwd(): pl.pallas_call(functools.partial(bwd_kernel, nh, blk), out_shape=(sds((di...  66.1 us
    all_gather x1, blocking collectives, body(): lax.all_gather(packed, BOTH, axis=0, tiled=True).reshape(n * m, -1)  55.7 us
    all_gather x1, waiting for transfers between devices, body(): down_all = lax.all_gather(w_down, 'row', axis=0, tiled=True)  54.8 us
    reduce_scatter x1, waiting for transfers between devices, body(): lax.psum_scatter(qkv_grad, 'row', scatter_dimension=0, tiled=True)  50.9 us
    all_gather x1, blocking collectives, body(): gain_all = lax.all_gather(gain_parts, BOTH, axis=0, tiled=False)  50.4 us
  transfers between devices with their start and end apart: 20, of which 13 were waited for; matrix products, arithmetic and copies ran while one was open for 23% of the time, Pallas kernels for 8%

profile of v1, /device:TPU:0, one launch (start us, length us, event | category | flops | bytes accessed | tf_op | source)
XLA Modules:
  0.0 1422.5 jit_solution(14524164183130783755)
XLA Ops:
  11.3 21.5 %all_to_all.75 = bf16[64,8,768]{2,0,1:T(8,128)(2,1)} all-to-all(bf16[64,8,768]{2,0,1:T(8,128)(2,1)S(1)} %copy.76), channel_id=1, replica_groups=mesh['row'=4,'ctx'=8] {'ctx'}, dimensions={1} | all-to-all | bytes 1572864 | tf_op jit(solution)/shard_map/all_to_all | solution.py:275
  39.9 55.7 %all_gather.38 = bf16[512,128]{1,0:T(8,128)(2,1)S(1)} all-gather(bf16[16,128]{1,0:T(8,128)(2,1)S(1)} %fusion.47), channel_id=1, replica_groups=mesh['row'=4,'ctx'=8] {'row','ctx'}, dimensions={0}, use_global_device_ids=true | all-gather | bytes 135168 | tf_op jit(solution)/shard_map/all_gather | solution.py:268
  97.6 4.7 power_multiply_fusion.3
  103.3 14.3 %all-gather.13.cloned.1.call-done = bf16[2,2048,2048]{2,1,0:T(8,128)(2,1)} async-done(((bf16[2,256,2048]{2,1,0:T(8,128)(2,1)}), bf16[2,2048,2048]{2,1,0:T(8,128)(2,1)}) %all-gather.13.cloned.1.call-update) | async-done | bytes 16777232 | tf_op jit(solution)/shard_map/all_gather | solution.py:244
  117.6 7.1 convert_reduce_fusion
  124.7 4.2 copy-done
  129.0 5.4 multiply_reduce_fusion.1
  134.5 9.4 multiply_convert_fusion
  143.8 38.7 %all-gather.11.cloned.1.call-done = bf16[2048,768]{1,0:T(8,128)(2,1)} async-done(((bf16[512,768]{1,0:T(8,128)(2,1)}), bf16[2048,768]{1,0:T(8,128)(2,1)}) %all-gather.11.cloned.1.call-update) | async-done | bytes 3145744 | tf_op jit(solution)/shard_map/all_gather | solution.py:276
  182.6 20.3 %fusion.66 = f32[768,4096]{1,0:T(8,128)} fusion(bf16[2048,768]{1,0:T(8,128)(2,1)} %all-gather.11.cloned.1.call-done, bf16[4096,2048]{1,0:T(8,128)(2,1)} %multiply_convert_fusion), kind=kOutput, calls=%fused_computation.196 | convolution fusion | flops 12884901888 | bytes 32505856 | tf_op jit(solution)/shard_map/df,td->ft/dot_general | solution.py:240
  206.8 4.0 fusion.63
  215.0 43.0 %attention_forward.1 = (bf16[4096,256]{1,0:T(8,128)(2,1)}, f32[256,4096]{1,0:T(8,128)}, f32[4,4096]{1,0:T(4,128)}) custom-call(s32[2,4,2]{2,1,0:T(4,128)} %pad_add_fusion.span_ref, bf16[256,4096]{1,0:T(8,128)(2,1)} %bitcast.249, bf16[256,4096]{1,0:T(8,128)(2,1)} %bitcast.247, bf16[256,4096]{1,0:T(8,128)(2,1)} %slice.184.vT_ref, ...), custom_call_target="tpu_custom_call" | custom-call | flops 8589934592 | bytes 20971520 | tf_op jit(solution)/shard_map/attention_forward/pallas_call | solution.py:142
  258.0 5.8 copy.77
  267.7 26.5 %all-to-all-done.1 = bf16[2,2048,256]{2,0,1:T(2,128)(2,1)S(1)} async-done(((bf16[2,2048,256]{2,0,1:T(2,128)(2,1)}), bf16[2,2048,256]{2,0,1:T(2,128)(2,1)S(1)}, u32[]{:S(2)}, u32[]{:S(2)}) %all-to-all-start.1) | async-done | bytes 2097184 | tf_op jit(solution)/shard_map/all_to_all | solution.py:296
  298.3 7.7 fusion.20
  311.2 8.5 fusion.65
  323.9 18.8 %all-gather.19.cloned.1.call-done = bf16[2048,1024]{1,0:T(8,128)(2,1)} async-done(((bf16[512,1024]{1,0:T(8,128)(2,1)}), bf16[2048,1024]{1,0:T(8,128)(2,1)}) %all-gather.19.cloned.1.call-update) | async-done | bytes 4194320 | tf_op jit(solution)/shard_map/all_gather | solution.py:281
  342.6 90.7 %all-gather.17.cloned.1.call-done = bf16[2,2048,2048]{2,1,0:T(8,128)(2,1)} async-done(((bf16[2,256,2048]{2,1,0:T(8,128)(2,1)}), bf16[2,2048,2048]{2,1,0:T(8,128)(2,1)}) %all-gather.17.cloned.1.call-update) | async-done | bytes 16777232 | tf_op jit(solution)/shard_map/all_gather | solution.py:244
  433.4 27.4 %fusion.61 = (f32[4096]{0:T(1024)S(1)}, f32[4096,1024]{0,1:T(8,128)}, f32[4096,1024]{0,1:T(8,128)}) fusion(bf16[4096,2048]{1,0:T(8,128)(2,1)} %bitcast.303, bf16[2048,1024]{1,0:T(8,128)(2,1)} %all-gather.19.cloned.1.call-done), kind=kOutput, calls=%fused_computation.191 | convolution fusion | flops 17200836608 | bytes 54542336 | tf_op jit(solution)/shard_map/td,df->tf/dot_general | solution.py:240
  460.8 54.8 %all-gather.23.cloned.1.call-done = bf16[1024,2048]{1,0:T(8,128)(2,1)} async-done(((bf16[256,2048]{1,0:T(8,128)(2,1)}), bf16[1024,2048]{1,0:T(8,128)(2,1)}) %all-gather.23.cloned.1.call-update) | async-done | bytes 4194320 | tf_op jit(solution)/shard_map/all_gather | solution.py:282
  515.6 90.3 %all-gather.21.cloned.1.call-done = bf16[2,2048,2048]{2,1,0:T(8,128)(2,1)} async-done(((bf16[2,256,2048]{2,1,0:T(8,128)(2,1)}), bf16[2,2048,2048]{2,1,0:T(8,128)(2,1)}) %all-gather.21.cloned.1.call-update) | async-done | bytes 16777232 | tf_op jit(solution)/shard_map/all_gather | solution.py:244
  605.9 28.8 %multiply_reduce_fusion.4 = (f32[4096]{0:T(1024)S(1)}, f32[4096]{0:T(1024)S(1)}, f32[4096]{0:T(1024)S(1)}, f32[4096,1024]{0,1:T(8,128)}) fusion(f32[4096,1024]{0,1:T(8,128)} %get-tuple-element.45, f32[4096]{0:T(1024)S(1)} %broadcast_multiply_fusion.2, f32[1024]{0:T(1024)S(1)} %bitcast.281, bf16[4096,2048]{1,0:T(8,128)(2,1)} %bitcast.301, ...), kind=kOutput, calls=%fused_computation.17 | convolution fusion | flops 17209217024 | bytes 54595584 | tf_op jit(solution)/shard_map/td,fd->tf/dot_general | solution.py:240
  634.8 9.8 all-gather.2
  645.5 23.8 %multiply_reduce_fusion.2 = (f32[1024]{0:T(1024)}, bf16[4096,1024]{0,1:T(8,128)(2,1)}) fusion(f32[4096,1024]{0,1:T(8,128)} %get-tuple-element.95, f32[4096,1024]{0,1:T(8,128)} %get-tuple-element.45, f32[4096]{0:T(1024)S(1)} %get-tuple-element.43, f32[4096]{0:T(1024)S(1)} %broadcast_multiply_fusion.1, f32[4096,1024]{0,1:T(8,128)} %get-tuple-element.94, ...), kind=kLoop, calls=%fused_computation.13 | loop fusion | flops 79690752 | bytes 58793984 | tf_op jit(solution)/shard_map/reduce_sum | solution.py:323
  669.3 25.2 %convolution_convert_fusion = bf16[4096,2048]{1,0:T(8,128)(2,1)} fusion(bf16[4096,1024]{0,1:T(8,128)(2,1)} %get-tuple-element.47, bf16[2048,1024]{1,0:T(8,128)(2,1)} %all-gather.19.cloned.1.call-done), kind=kOutput, calls=%fused_computation.19 | convolution fusion | flops 17188257792 | bytes 29360128 | tf_op jit(solution)/shard_map/tf,df->td/dot_general | solution.py:240
  694.6 27.5 %convolution_convert_fusion.1 = bf16[4096,2048]{1,0:T(8,128)(2,1)} fusion(bf16[1024,2048]{1,0:T(8,128)(2,1)} %all-gather.23.cloned.1.call-done, f32[4096,1024]{0,1:T(8,128)} %get-tuple-element.45, f32[4096]{0:T(1024)S(1)} %get-tuple-element.43, f32[4096]{0:T(1024)S(1)} %broadcast_multiply_fusion.1, f32[1024]{0:T(1024)S(1)} %bitcast.283), kind=kOutput, calls=%fused_computation.20 | convolution fusion | flops 17205035008 | bytes 37785600 | tf_op jit(solution)/shard_map/tf,fd->td/dot_general | solution.py:240
  722.1 88.6 %reduce-scatter.11.cloned.1.call-done = bf16[2,256,2048]{2,1,0:T(8,128)(2,1)} async-done(((bf16[2,2048,2048]{2,1,0:T(8,128)(2,1)}), bf16[2,256,2048]{2,1,0:T(8,128)(2,1)}) %reduce-scatter.11.cloned.1.call-update) | async-done | bytes 2097168 | tf_op jit(solution)/shard_map/reduce_scatter | solution.py:248
  813.0 4.8 fusion.18
  817.8 112.5 %reduce-scatter.9.cloned.1.call-done = bf16[2,256,2048]{2,1,0:T(8,128)(2,1)} async-done(((bf16[2,2048,2048]{2,1,0:T(8,128)(2,1)}), bf16[2,256,2048]{2,1,0:T(8,128)(2,1)}) %reduce-scatter.9.cloned.1.call-update) | async-done | bytes 2097168 | tf_op jit(solution)/shard_map/reduce_scatter | solution.py:248
  930.3 5.8 convert_add_fusion
  936.2 7.6 convolution_convert_fusion.2
  943.7 8.2 copy.86
  952.0 23.9 %convolution_convert_fusion.4 = bf16[2048,1024]{1,0:T(8,128)(2,1)} fusion(bf16[4096,2048]{1,0:T(8,128)(2,1)} %bitcast.304, bf16[4096,1024]{0,1:T(8,128)(2,1)} %get-tuple-element.47), kind=kOutput, calls=%fused_computation.68 | convolution fusion | flops 17181966336 | bytes 29360128 | tf_op jit(solution)/shard_map/td,tf->df/dot_general | solution.py:240
  976.0 12.3 multiply_reduce_fusion.6
  997.4 26.7 %convolution_convert_fusion.3 = bf16[1024,2048]{1,0:T(8,128)(2,1)} fusion(bf16[4096,2048]{1,0:T(8,128)(2,1)} %bitcast.302, f32[4096,1024]{0,1:T(8,128)} %get-tuple-element.45, f32[4096]{0:T(1024)S(1)} %get-tuple-element.43, f32[4096]{0:T(1024)S(1)} %broadcast_multiply_fusion.1, f32[1024]{0:T(1024)S(1)} %bitcast.284), kind=kOutput, calls=%fused_computation.67 | convolution fusion | flops 17198743552 | bytes 37785600 | tf_op jit(solution)/shard_map/tf,td->fd/dot_general | solution.py:240
  1024.1 7.7 all-to-all-done.3
  1033.4 4.0 copy.84
  1037.4 66.1 %attention_backward.1 = (f32[256,4096]{1,0:T(8,128)}, f32[256,4096]{1,0:T(8,128)}, bf16[256,4096]{1,0:T(8,128)(2,1)}) custom-call(s32[2,4,2]{2,1,0:T(4,128)} %pad_add_fusion.span_ref, bf16[256,4096]{1,0:T(8,128)(2,1)} %bitcast.250, bf16[256,4096]{1,0:T(8,128)(2,1)} %bitcast.248, bf16[256,4096]{1,0:T(8,128)(2,1)} %slice.184.vT_ref, ...), custom_call_target="tpu_custom_call" | custom-call | flops 21474836480 | bytes 41943040 | tf_op jit(solution)/shard_map/attention_backward/pallas_call | solution.py:162
  1103.5 4.1 subtract_convert_fusion
  1109.4 19.2 %convolution_convert_fusion.5 = bf16[2048,768]{1,0:T(8,128)(2,1)} fusion(bf16[4096,2048]{1,0:T(8,128)(2,1)} %multiply_convert_fusion, bf16[256,4096]{1,0:T(8,128)(2,1)} %get-tuple-element.23, bf16[256,4096]{1,0:T(8,128)(2,1)S(1)} %bitcast.252, bf16[256,4096]{1,0:T(8,128)(2,1)S(1)} %bitcast.254), kind=kOutput, calls=%fused_computation.70 | convolution fusion | flops 12905349120 | bytes 26214400 | tf_op jit(solution)/shard_map/td,ft->df/dot_general | solution.py:240
  1129.3 24.6 %multiply_reduce_fusion = (f32[2048]{0:T(1024)S(1)}, bf16[4096,2048]{1,0:T(8,128)(2,1)}) fusion(bf16[2,2048,2048]{2,1,0:T(8,128)(2,1)} %all-gather.13.cloned.1.call-done, f32[4096]{0:T(1024)S(1)} %bitcast.279, f32[4096]{0:T(1024)S(1)} %bitcast.277, bf16[2048,768]{1,0:T(8,128)(2,1)} %all-gather.11.cloned.1.call-done, ...), kind=kOutput, calls=%fused_computation.2 | convolution fusion | flops 12954105856 | bytes 43032576 | tf_op jit(solution)/shard_map/ft,df->td/dot_general | solution.py:240
  1158.8 36.9 %reduce-scatter.23.cloned.1.call-done = bf16[256,2048]{1,0:T(8,128)(2,1)} async-done(((bf16[1024,2048]{1,0:T(8,128)(2,1)}), bf16[256,2048]{1,0:T(8,128)(2,1)}) %reduce-scatter.23.cloned.1.call-update) | async-done | bytes 1048592 | tf_op jit(solution)/shard_map/reduce_scatter | solution.py:332
  1208.6 50.9 %reduce-scatter.15.cloned.1.call-done = bf16[512,768]{1,0:T(8,128)(2,1)} async-done(((bf16[2048,768]{1,0:T(8,128)(2,1)}), bf16[512,768]{1,0:T(8,128)(2,1)}) %reduce-scatter.15.cloned.1.call-update) | async-done | bytes 786448 | tf_op jit(solution)/shard_map/reduce_scatter | solution.py:357
  1259.5 4.2 all-to-all-start.4
  1263.7 50.4 %all-gather.1 = f32[229376]{0:T(1024)} all-gather(f32[7168]{0:T(1024)S(1)} %pad_maximum_fusion.8), channel_id=3, replica_groups=mesh['row'=4,'ctx'=8] {'row','ctx'}, dimensions={0}, use_global_device_ids=true | all-gather | bytes 946176 | tf_op jit(solution)/shard_map/all_gather | solution.py:365
  1324.2 7.5 slice_reduce_fusion.1
  1336.3 72.2 %reduce-scatter.13.cloned.1.call-done = bf16[2,256,2048]{2,1,0:T(8,128)(2,1)} async-done(((bf16[2,2048,2048]{2,1,0:T(8,128)(2,1)}), bf16[2,256,2048]{2,1,0:T(8,128)(2,1)}) %reduce-scatter.13.cloned.1.call-update) | async-done | bytes 2097168 | tf_op jit(solution)/shard_map/reduce_scatter | solution.py:248
  1411.5 4.3 fusion.11
  (228 shorter events, 91.3 us)
Async XLA Ops:
  7.2 110.4 %all-gather.13.cloned.1.call-start = ((), (), s32[]{:S(2)}) async-start(), calls=%async_computation.15 | async-start | bytes 18874368 | tf_op jit(solution)/shard_map/all_gather | solution.py:244
  7.9 25.6 %copy-start.17 = (bf16[64,8192]{1,0:T(8,128)(2,1)S(1)}, bf16[64,8192]{1,0:T(8,128)(2,1)}, u32[]{:S(2)}) copy-start(bf16[64,8192]{1,0:T(8,128)(2,1)} %param.19) | copy-start | bytes 3145732
  7.9 174.6 %all-gather.11.cloned.1.call-start = ((), (), s32[]{:S(2)}) async-start(), calls=%async_computation.14 | async-start | bytes 3932160 | tf_op jit(solution)/shard_map/all_gather | solution.py:276
  32.8 278.4 %all-gather.15.cloned.1.call-start = ((), (), s32[]{:S(2)}) async-start(), calls=%async_computation.16 | async-start | bytes 8650752 | tf_op jit(solution)/shard_map/all_gather | solution.py:280
  33.5 5.9 copy-start.39
  33.5 6.3 copy-start.40
  33.6 6.3 copy-start.41
  33.6 6.3 copy-start.42
  33.6 6.3 copy-start.43
  35.8 66.4 %all-to-all-start.2 = ((bf16[64,8,1024]{2,0,1:T(8,128)(2,1)}), bf16[64,8,1024]{2,0,1:T(8,128)(2,1)S(1)}, u32[]{:S(2)}, u32[]{:S(2)}) async-start(bf16[64,8,1024]{2,0,1:T(8,128)(2,1)} %reshape.838), calls=%async_computation.2 | async-start | bytes 2097152 | tf_op jit(solution)/shard_map/all_to_all | solution.py:279
  39.4 303.2 %all-gather.19.cloned.1.call-start = ((), (), s32[]{:S(2)}) async-start(), calls=%async_computation.18 | async-start | bytes 5242880 | tf_op jit(solution)/shard_map/all_gather | solution.py:281
  95.8 38.6 %copy-start.20 = (f32[2048]{0:T(1024)}, f32[2048]{0:T(1024)S(1)}, u32[]{:S(2)}) copy-start(f32[2048]{0:T(1024)S(1)} %mul.486) | copy-start | bytes 24580
  102.2 108.5 %copy-start.11 = (f32[32,4096]{1,0:T(8,128)}, f32[32,4096]{1,0:T(8,128)S(1)}, u32[]{:S(2)}) copy-start(f32[32,4096]{1,0:T(8,128)S(1)} %get-tuple-element.77) | copy-start | bytes 1572868
  102.3 110.6 %copy-start.9 = (f32[32,4096]{1,0:T(8,128)}, f32[32,4096]{1,0:T(8,128)S(1)}, u32[]{:S(2)}) copy-start(f32[32,4096]{1,0:T(8,128)S(1)} %get-tuple-element.73) | copy-start | bytes 1572868
  117.6 11.4 copy-start
  124.7 9.7 copy-start.22
  134.4 9.4 copy-start.24
  263.8 30.4 %all-to-all-start.1 = ((bf16[2,2048,256]{2,0,1:T(2,128)(2,1)}), bf16[2,2048,256]{2,0,1:T(2,128)(2,1)S(1)}, u32[]{:S(2)}, u32[]{:S(2)}) async-start(bf16[2,2048,256]{2,0,1:T(2,128)(2,1)} %copy.77), calls=%async_computation.1 | async-start | bytes 4194304 | tf_op jit(solution)/shard_map/all_to_all | solution.py:296
  267.5 165.8 %all-gather.17.cloned.1.call-start = ((), (), s32[]{:S(2)}) async-start(), calls=%async_computation.17 | async-start | bytes 18874368 | tf_op jit(solution)/shard_map/all_gather | solution.py:244
  267.6 52.6 %copy-start.18 = (f32[2048]{0:T(1024)}, f32[2048]{0:T(1024)S(1)}, u32[]{:S(2)}) copy-start(f32[2048]{0:T(1024)S(1)} %mul.517) | copy-start | bytes 24580
  267.7 43.4 %copy-start.31 = (f32[2048]{0:T(1024)}, f32[2048]{0:T(1024)S(1)}, u32[]{:S(2)}) copy-start(f32[2048]{0:T(1024)S(1)} %mul.511) | copy-start | bytes 24580
  298.3 12.8 copy-start.34
  322.4 193.2 %all-gather.23.cloned.1.call-start = ((), (), s32[]{:S(2)}) async-start(), calls=%async_computation.20 | async-start | bytes 5242880 | tf_op jit(solution)/shard_map/all_gather | solution.py:282
  323.0 282.9 %all-gather.21.cloned.1.call-start = ((), (), s32[]{:S(2)}) async-start(), calls=%async_computation.19 | async-start | bytes 18874368 | tf_op jit(solution)/shard_map/all_gather | solution.py:244
  323.7 487.0 %reduce-scatter.11.cloned.1.call-start = ((), (), s32[]{:S(2)}) async-start(), calls=%async_computation.22 | async-start | bytes 18874368 | tf_op jit(solution)/shard_map/reduce_scatter | solution.py:248
  694.5 235.7 %reduce-scatter.9.cloned.1.call-start = ((), (), s32[]{:S(2)}) async-start(), calls=%async_computation.21 | async-start | bytes 18874368 | tf_op jit(solution)/shard_map/reduce_scatter | solution.py:248
  722.1 88.6 %copy-start.19 = (f32[2048]{0:T(1024)S(1)}, f32[2048]{0:T(1024)}, u32[]{:S(2)}) copy-start(f32[2048]{0:T(1024)} %copy-done.18) | copy-start | bytes 24580
  722.1 90.9 %copy-start.27 = (f32[512]{0:T(512)S(1)}, f32[512]{0:T(512)}, u32[]{:S(2)}) copy-start(f32[512]{0:T(512)} %copy-done.26) | copy-start | bytes 6148
  722.1 90.9 %copy-start.29 = (f32[512]{0:T(512)S(1)}, f32[512]{0:T(512)}, u32[]{:S(2)}) copy-start(f32[512]{0:T(512)} %copy-done.28) | copy-start | bytes 6148
  722.1 406.6 %reduce-scatter.17.cloned.1.call-start = ((), (), s32[]{:S(2)}) async-start(), calls=%async_computation.25 | async-start | bytes 9437184 | tf_op jit(solution)/shard_map/reduce_scatter | solution.py:347
  810.7 119.6 %copy-start.4 = (bf16[2,256,2048]{2,1,0:T(8,128)(2,1)S(1)}, bf16[2,256,2048]{2,1,0:T(8,128)(2,1)}, u32[]{:S(2)}) copy-start(bf16[2,256,2048]{2,1,0:T(8,128)(2,1)} %reduce-scatter.11.cloned.1.call-done) | copy-start | bytes 6291460
  930.3 5.9 copy-start.35
  930.3 5.9 copy-start.37
  936.1 7.6 copy-start.5
  952.0 202.0 %reduce-scatter.21.cloned.1.call-start = ((), (), s32[]{:S(2)}) async-start(), calls=%async_computation.27 | async-start | bytes 5242880 | tf_op jit(solution)/shard_map/reduce_scatter | solution.py:334
  976.0 12.3 copy-start.8
  993.7 38.1 %all-to-all-start.3 = ((bf16[2,256,2048]{1,0,2:T(2,128)(2,1)}), bf16[2,256,2048]{1,0,2:T(2,128)(2,1)S(1)}, u32[]{:S(2)}, u32[]{:S(2)}) async-start(bf16[2,256,2048]{1,0,2:T(2,128)(2,1)} %copy.82), calls=%async_computation.5 | async-start | bytes 4194304 | tf_op jit(solution)/shard_map/all_to_all | solution.py:345
  997.3 198.3 %reduce-scatter.23.cloned.1.call-start = ((), (), s32[]{:S(2)}) async-start(), calls=%async_computation.28 | async-start | bytes 5242880 | tf_op jit(solution)/shard_map/reduce_scatter | solution.py:332
  1024.1 235.4 %reduce-scatter.15.cloned.1.call-start = ((), (), s32[]{:S(2)}) async-start(), calls=%async_computation.24 | async-start | bytes 3932160 | tf_op jit(solution)/shard_map/reduce_scatter | solution.py:357
  1037.4 66.1 %copy-start.10 = (f32[32,4096]{1,0:T(8,128)S(1)}, f32[32,4096]{1,0:T(8,128)}, u32[]{:S(2)}) copy-start(f32[32,4096]{1,0:T(8,128)} %copy-done.9) | copy-start | bytes 1572868
  1037.4 66.1 %copy-start.12 = (f32[32,4096]{1,0:T(8,128)S(1)}, f32[32,4096]{1,0:T(8,128)}, u32[]{:S(2)}) copy-start(f32[32,4096]{1,0:T(8,128)} %copy-done.11) | copy-start | bytes 1572868
  1037.4 66.2 %copy-start.15 = (f32[32,4096]{1,0:T(8,128)S(1)}, f32[32,4096]{1,0:T(8,128)}, u32[]{:S(2)}) copy-start(f32[32,4096]{1,0:T(8,128)} %get-tuple-element.71) | copy-start | bytes 1572868
  1037.4 66.2 %copy-start.16 = (f32[32,4096]{1,0:T(8,128)S(1)}, f32[32,4096]{1,0:T(8,128)}, u32[]{:S(2)}) copy-start(f32[32,4096]{1,0:T(8,128)} %get-tuple-element.79) | copy-start | bytes 1572868
  1128.6 205.9 %reduce-scatter.19.cloned.1.call-start = ((), (), s32[]{:S(2)}) async-start(), calls=%async_computation.26 | async-start | bytes 1310720 | tf_op jit(solution)/shard_map/reduce_scatter | solution.py:348
  1129.2 279.3 %reduce-scatter.13.cloned.1.call-start = ((), (), s32[]{:S(2)}) async-start(), calls=%async_computation.23 | async-start | bytes 18874368 | tf_op jit(solution)/shard_map/reduce_scatter | solution.py:248
  1154.0 44.5 %all-to-all-start.5 = ((bf16[8,64,1024]{2,1,0:T(8,128)(2,1)}), bf16[8,64,1024]{2,1,0:T(8,128)(2,1)S(1)}, u32[]{:S(2)}, u32[]{:S(2)}) async-start(bf16[8,64,1024]{2,1,0:T(8,128)(2,1)} %bitcast.263), calls=%async_computation.12 | async-start | bytes 2097152 | tf_op jit(solution)/shard_map/all_to_all | solution.py:335
  1259.5 57.4 %all-to-all-start.4 = ((bf16[8,64,768]{2,1,0:T(8,128)(2,1)}), bf16[8,64,768]{2,1,0:T(8,128)(2,1)}, u32[]{:S(2)}, u32[]{:S(2)}) async-start(bf16[8,64,768]{2,1,0:T(8,128)(2,1)} %bitcast.267), calls=%async_computation.8 | async-start | bytes 1572864 | tf_op jit(solution)/shard_map/all_to_all | solution.py:358
  1324.2 84.3 %copy-start.21 = (f32[2048]{0:T(1024)S(1)}, f32[2048]{0:T(1024)}, u32[]{:S(2)}) copy-start(f32[2048]{0:T(1024)} %copy-done.20) | copy-start | bytes 24580
  (16 other events, 55.0 us)
Sparse Core Ops, SparseCore 0:
  9.9 107.6 all-gather.12
  119.1 63.3 all-gather.10
  185.4 76.1 all-gather.14
  263.1 79.4 all-gather.18
  344.9 88.3 all-gather.16
  434.8 80.7 all-gather.22
  517.5 88.3 all-gather.20
  694.7 115.9 reduce-scatter.10
  814.3 115.9 reduce-scatter.8
  952.1 84.8 reduce-scatter.16
  1039.4 76.7 reduce-scatter.20
  1118.4 77.2 reduce-scatter.22
  1198.6 60.7 reduce-scatter.14
  1261.7 28.6 reduce-scatter.18
  1293.8 114.6 reduce-scatter.12

commit v2 on v1

v2 whole, which is shorter than its diff:
```python
import functools

import jax
import jax.numpy as jnp
from jax import lax
from jax.experimental import pallas as pl
from jax.experimental.pallas import tpu as pltpu
from jax.sharding import PartitionSpec as P

bf16 = jnp.bfloat16
f32 = jnp.float32
HEAD_DIM = 64
HALF = HEAD_DIM // 2
PAIR = 2 * HEAD_DIM
LOG2E = 1.4426950408889634
NEG = -1e30
ROW_LEN = 2048
XPOS_BASE = 512
EPS = 1e-5
BOTH = ("row", "ctx")


def walk(span_ref, qb, step):
    first = span_ref[2 + 2 * (qb)]
    clear = span_ref[3 + 2 * (qb)]

    def edge(t, carry):
        step(jnp.where(t < clear - first, first + t, qb), True)
        return carry

    def plain(kb, carry):
        step(kb, False)
        return carry

    lax.fori_loop(0, clear - first + 1, edge, 0)
    lax.fori_loop(clear, qb, plain, 0)


def allowed(lowest, kb, qb, blk):
    key = kb * blk + lax.broadcasted_iota(jnp.int32, (blk, blk), 0)
    query = qb * blk + lax.broadcasted_iota(jnp.int32, (blk, blk), 1)
    return (key <= query) & (key >= lowest)


def forward_kernel(nh, blk, unit, span_ref, q0_ref, q1_ref, k0_ref, k1_ref, v0_ref, v1_ref, table_ref, lo_ref,
                   o_ref, oT_ref, lse_ref, qT_ref, kT_ref, vT_ref, k_s, qm_s, acc_s, m_s, l_s):
    qb = pl.program_id(0)
    dim = nh * HEAD_DIM
    length = kT_ref.shape[1]
    core, place = span_ref[0], span_ref[1]
    spots = blk // (2 * unit)
    inner = lax.rem(place, spots)

    def turned(values, at, kind):
        cosine = table_ref[2 * kind, :, pl.ds(at, unit)]
        sine = table_ref[2 * kind + 1, :, pl.ds(at, unit)]
        out = []
        for h in range(nh):
            one = values[h * HEAD_DIM:h * HEAD_DIM + HALF]
            two = values[h * HEAD_DIM + HALF:(h + 1) * HEAD_DIM]
            out += [one * cosine - two * sine, two * cosine + one * sine]
        return jnp.concatenate(out, axis=0).astype(bf16)

    @pl.when(qb == 0)
    def _():
        def load(j, carry):
            src = pl.multiple_of((j ^ place) * unit, unit)
            for half, ref, v_ref in ((0, k0_ref, v0_ref), (1, k1_ref, v1_ref)):
                at = pl.multiple_of((2 * j + (core ^ half)) * unit, unit)
                key = turned(ref[:, pl.ds(src, unit)], at, 1)
                kT_ref[:, pl.ds(at, unit)] = key
                k_s[pl.ds(at, unit), :] = key.T
                vT_ref[:, pl.ds(at, unit)] = v_ref[:, pl.ds(src, unit)].astype(bf16)
            return carry

        lax.fori_loop(0, length // (2 * unit), load, 0)

    for u in range(spots):
        src = pl.multiple_of((u ^ inner) * unit, unit)
        for half, ref in ((0, q0_ref), (1, q1_ref)):
            at = pl.multiple_of((2 * u + (core ^ half)) * unit, unit)
            qT_ref[:, pl.ds(at, unit)] = turned(ref[:, pl.ds(src, unit)], pl.multiple_of(qb * blk + at, unit), 0)
    for h in range(nh):
        own = h % 2
        qm_s[h, pl.ds(own * HEAD_DIM, HEAD_DIM), :] = qT_ref[pl.ds(h * HEAD_DIM, HEAD_DIM), :]
        qm_s[h, pl.ds((1 - own) * HEAD_DIM, HEAD_DIM), :] = jnp.zeros((HEAD_DIM, blk), bf16)
    acc_s[...] = jnp.zeros_like(acc_s)
    m_s[...] = jnp.full_like(m_s, NEG)
    l_s[...] = jnp.zeros_like(l_s)
    lowest = lo_ref[...]

    def step(kb, masked):
        at = pl.multiple_of(kb * blk, blk)
        if masked:
            ok = allowed(lowest, kb, qb, blk)
        for h in range(nh):
            rows = pl.ds(h * HEAD_DIM, HEAD_DIM)
            s = jnp.dot(k_s[pl.ds(at, blk), pl.ds((h // 2) * PAIR, PAIR)], qm_s[h], preferred_element_type=f32)
            s = s * (LOG2E * HEAD_DIM**-0.5)
            if masked:
                s = jnp.where(ok, s, NEG)
            before = m_s[h:h + 1, :]
            now = jnp.maximum(before, jnp.max(s, axis=0, keepdims=True))
            p = jnp.exp2(s - now)
            fade = jnp.exp2(before - now)
            m_s[h:h + 1, :] = now
            l_s[h:h + 1, :] = l_s[h:h + 1, :] * fade + jnp.sum(p, axis=0, keepdims=True)
            acc_s[rows, :] = acc_s[rows, :] * fade + jnp.dot(
                vT_ref[rows, pl.ds(at, blk)], p.astype(bf16), preferred_element_type=f32)

    walk(span_ref, qb, step)
    for h in range(nh):
        rows = pl.ds(h * HEAD_DIM, HEAD_DIM)
        oT_ref[rows, :] = acc_s[rows, :] / l_s[h:h + 1, :]
        lse_ref[h:h + 1, :] = m_s[h:h + 1, :] + jnp.log2(l_s[h:h + 1, :])
    o_ref[...] = oT_ref[...].T.astype(bf16)


def backward_kernel(nh, blk, unit, span_ref, qT_ref, kT_ref, vT_ref, do_ref, oT_ref, lse_ref, table_ref, lo_ref,
                    old0_ref, old1_ref, d0_ref, d1_ref, k_s, v_s, qm_s, dm_s, qn_s, dn_s, acc_s, dk_s, dv_s, p_s, ds_s, dl_s):
    qb = pl.program_id(0)
    dim = nh * HEAD_DIM
    length = kT_ref.shape[1]
    count = length // blk
    scale = HEAD_DIM**-0.5
    core, place = span_ref[0], span_ref[1]

    @pl.when(qb == 0)
    def _():
        for c in range(count):
            k_s[pl.ds(c * blk, blk), :] = kT_ref[:, pl.ds(c * blk, blk)].T
            v_s[pl.ds(c * blk, blk), :] = vT_ref[:, pl.ds(c * blk, blk)].T
        dk_s[...] = jnp.zeros_like(dk_s)
        dv_s[...] = jnp.zeros_like(dv_s)

    doT = do_ref[...].T
    q = qT_ref[...].T
    lane = lax.broadcasted_iota(jnp.int32, (blk, PAIR), 1)
    prod = doT.astype(f32) * oT_ref[...]
    for h in range(nh):
        own = h % 2
        rows = slice(h * HEAD_DIM, (h + 1) * HEAD_DIM)
        zero = jnp.zeros((HEAD_DIM, blk), bf16)
        qm_s[h, pl.ds(own * HEAD_DIM, HEAD_DIM), :] = qT_ref[pl.ds(h * HEAD_DIM, HEAD_DIM), :]
        qm_s[h, pl.ds((1 - own) * HEAD_DIM, HEAD_DIM), :] = zero
        dm_s[h, pl.ds(own * HEAD_DIM, HEAD_DIM), :] = doT[rows, :]
        dm_s[h, pl.ds((1 - own) * HEAD_DIM, HEAD_DIM), :] = zero
        mine = (lane // HEAD_DIM) == own
        pair = slice((h // 2) * PAIR, (h // 2) * PAIR + PAIR)
        qn_s[h // 2, pl.ds(own * blk, blk), :] = jnp.where(mine, q[:, pair], jnp.zeros((), bf16))
        dn_s[h // 2, pl.ds(own * blk, blk), :] = jnp.where(mine, do_ref[:, pair], jnp.zeros((), bf16))
        dl_s[h:h + 1, :] = jnp.sum(prod[rows, :], axis=0, keepdims=True)
    acc_s[...] = jnp.zeros_like(acc_s)
    lowest = lo_ref[...]

    def step(kb, masked):
        at = pl.multiple_of(kb * blk, blk)
        if masked:
            ok = allowed(lowest, kb, qb, blk)
        for g in range(nh // 2):
            lanes = pl.ds(g * PAIR, PAIR)
            for own in range(2):
                h = 2 * g + own
                rows = pl.ds(h * HEAD_DIM, HEAD_DIM)
                s = jnp.dot(k_s[pl.ds(at, blk), lanes], qm_s[h], preferred_element_type=f32) * (LOG2E * scale)
                p = jnp.exp2(s - lse_ref[h:h + 1, :])
                if masked:
                    p = jnp.where(ok, p, 0.0)
                dp = jnp.dot(v_s[pl.ds(at, blk), lanes], dm_s[h], preferred_element_type=f32)
                ds = (p * (dp - dl_s[h:h + 1, :])).astype(bf16)
                p_s[g, :, pl.ds(own * blk, blk)] = p.astype(bf16)
                ds_s[g, :, pl.ds(own * blk, blk)] = ds
                acc_s[rows, :] += jnp.dot(kT_ref[rows, pl.ds(at, blk)], ds, preferred_element_type=f32)
            dv_s[pl.ds(at, blk), lanes] += jnp.dot(p_s[g], dn_s[g], preferred_element_type=f32)
            dk_s[pl.ds(at, blk), lanes] += jnp.dot(ds_s[g], qn_s[g], preferred_element_type=f32)

    walk(span_ref, qb, step)

    def turned_back(values, at, size, kind):
        cosine = table_ref[2 * kind, :, pl.ds(at, size)] * scale
        sine = table_ref[2 * kind + 1, :, pl.ds(at, size)] * scale
        out = []
        for h in range(nh):
            one = values[h * HEAD_DIM:h * HEAD_DIM + HALF]
            two = values[h * HEAD_DIM + HALF:(h + 1) * HEAD_DIM]
            out += [one * cosine + two * sine, two * cosine - one * sine]
        return jnp.concatenate(out, axis=0).T.astype(bf16)

    spots = blk // (2 * unit)
    for u in range(spots):
        dst = pl.multiple_of(((qb * spots + u) ^ place) * unit, unit)
        for half, ref in ((0, d0_ref), (1, d1_ref)):
            at = pl.multiple_of((2 * u + (core ^ half)) * unit, unit)
            ref[pl.ds(dst, unit), pl.ds(0, dim)] = turned_back(
                acc_s[:, pl.ds(at, unit)], pl.multiple_of(qb * blk + at, unit), unit, 0)

    @pl.when(qb == count - 1)
    def _():
        def store(j, carry):
            dst = pl.multiple_of((j ^ place) * unit, unit)
            for half, ref in ((0, d0_ref), (1, d1_ref)):
                at = pl.multiple_of((2 * j + (core ^ half)) * unit, unit)
                ref[pl.ds(dst, unit), pl.ds(dim, dim)] = turned_back(dk_s[pl.ds(at, unit), :].T, at, unit, 1)
                ref[pl.ds(dst, unit), pl.ds(2 * dim, dim)] = dv_s[pl.ds(at, unit), :].astype(bf16)
            return carry

        lax.fori_loop(0, length // (2 * unit), store, 0)


PARAMS = pltpu.CompilerParams(dimension_semantics=("arbitrary",), vmem_limit_bytes=60 * 2**20)


def span_of(lowest, blk, core, place):
    count = lowest.shape[0] // blk
    blocks = lowest.reshape(count, blk)
    own = jnp.arange(count, dtype=jnp.int32)
    first = jnp.minimum(blocks[:, 0] // blk, own)
    clear = jnp.minimum((blocks[:, -1] + blk - 1) // blk, own)
    both = jnp.stack([first, clear], axis=-1).reshape(-1)
    return jnp.concatenate([jnp.stack([core, place]), both]).astype(jnp.int32)


def attention_forward(row, half0, half1, table, lowest, span, blk, unit):
    length = lowest.shape[0]
    dim = half0.shape[0] // 3
    nh, count = dim // HEAD_DIM, length // blk
    spots = blk // (2 * unit)
    sds = jax.ShapeDtypeStruct
    pick = pl.BlockSpec((dim, blk // 2), lambda q, s: (0, row * count + (q ^ lax.div(s[1], spots))))
    keys = pl.BlockSpec((dim, length // 2), lambda q, s: (1, row))
    values = pl.BlockSpec((dim, length // 2), lambda q, s: (2, row))
    wide = pl.BlockSpec((dim, length), lambda q, s: (0, 0))
    cut = pl.BlockSpec((dim, blk), lambda q, s: (0, q))
    return pl.pallas_call(
        functools.partial(forward_kernel, nh, blk, unit),
        out_shape=(sds((length, dim), bf16), sds((dim, length), f32), sds((nh, length), f32),
                   sds((dim, length), bf16), sds((dim, length), bf16), sds((dim, length), bf16)),
        grid_spec=pltpu.PrefetchScalarGridSpec(
            num_scalar_prefetch=1, grid=(count,),
            in_specs=[pick, pick, keys, keys, values, values,
                      pl.BlockSpec((4, HALF, length), lambda q, s: (0, 0, 0)),
                      pl.BlockSpec((1, blk), lambda q, s: (0, q))],
            out_specs=[pl.BlockSpec((blk, dim), lambda q, s: (q, 0)), cut,
                       pl.BlockSpec((nh, blk), lambda q, s: (0, q)), cut, wide, wide],
            scratch_shapes=[pltpu.VMEM((length, dim), bf16), pltpu.VMEM((nh, PAIR, blk), bf16), pltpu.VMEM((dim, blk), f32),
                            pltpu.VMEM((8, blk), f32), pltpu.VMEM((8, blk), f32)]),
        compiler_params=PARAMS, name="attention_forward",
        cost_estimate=pl.CostEstimate(flops=4 * 4 * dim * length * length // 2, bytes_accessed=10 * 2**20,
                                      transcendentals=nh * length * length // 2),
    )(span, half0, half1, half0, half1, half0, half1, table, lowest[None, :])


def attention_backward(row, rows, saved, do, table, lowest, span, blk, unit, before):
    oT, lse, qT, kT, vT = saved
    length = lowest.shape[0]
    dim = qT.shape[0]
    nh, count = dim // HEAD_DIM, length // blk
    sds = jax.ShapeDtypeStruct
    cut = pl.BlockSpec((dim, blk), lambda q, s: (0, q))
    wide = pl.BlockSpec((dim, length), lambda q, s: (0, 0))
    grad = pl.BlockSpec((length // 2, 3 * dim), lambda q, s: (row, 0))
    whole = sds((rows * length // 2, 3 * dim), bf16)
    kernel = functools.partial(backward_kernel, nh, blk, unit)
    if before is None:
        def call(span_ref, *refs):
            kernel(span_ref, *refs[:8], None, None, *refs[8:])
    else:
        call = kernel
    return pl.pallas_call(
        call,
        out_shape=(whole, whole),
        grid_spec=pltpu.PrefetchScalarGridSpec(
            num_scalar_prefetch=1, grid=(count,),
            in_specs=[cut, wide, wide, pl.BlockSpec((blk, dim), lambda q, s: (q, 0)), cut,
                      pl.BlockSpec((nh, blk), lambda q, s: (0, q)),
                      pl.BlockSpec((4, HALF, length), lambda q, s: (0, 0, 0)),
                      pl.BlockSpec((1, blk), lambda q, s: (0, q))]
            + ([] if before is None else [pl.BlockSpec(memory_space=pl.ANY)] * 2),
            out_specs=[grad, grad],
            scratch_shapes=[pltpu.VMEM((length, dim), bf16), pltpu.VMEM((length, dim), bf16),
                            pltpu.VMEM((nh, PAIR, blk), bf16), pltpu.VMEM((nh, PAIR, blk), bf16),
                            pltpu.VMEM((nh // 2, 2 * blk, PAIR), bf16), pltpu.VMEM((nh // 2, 2 * blk, PAIR), bf16),
                            pltpu.VMEM((dim, blk), f32), pltpu.VMEM((length, dim), f32), pltpu.VMEM((length, dim), f32),
                            pltpu.VMEM((nh // 2, blk, 2 * blk), bf16), pltpu.VMEM((nh // 2, blk, 2 * blk), bf16),
                            pltpu.VMEM((8, blk), f32)]),
        compiler_params=PARAMS, name="attention_backward",
        input_output_aliases={} if before is None else {9: 0, 10: 1},
        cost_estimate=pl.CostEstimate(flops=10 * 4 * dim * length * length // 2, bytes_accessed=20 * 2**20,
                                      transcendentals=nh * length * length // 2),
    )(span, qT, kT, vT, do, oT, lse, table, lowest[None, :], *(before or ()))


def hat_of(values):
    center = values - jnp.mean(values, axis=-1, keepdims=True)
    rstd = lax.rsqrt(jnp.mean(center * center, axis=-1, keepdims=True) + EPS)
    return center * rstd, rstd


def hat_back(hat, rstd, grad):
    return rstd * (grad - jnp.mean(grad, axis=-1, keepdims=True) - hat * jnp.mean(grad * hat, axis=-1, keepdims=True))


def wide_row(o_ref):
    return jnp.concatenate([o_ref[i] for i in range(o_ref.shape[0])], axis=1).astype(f32)


def middle_forward_kernel(o_ref, x_ref, w_ref, c_ref, x1_ref, b_ref):
    c = hat_of(wide_row(o_ref))[0].astype(bf16)
    c_ref[...] = c
    x1 = x_ref[...].astype(f32) + jnp.dot(c, w_ref[...], preferred_element_type=f32)
    x1_ref[...] = x1
    b_ref[...] = hat_of(x1)[0].astype(bf16)


def middle_forward(o, x, w):
    n, size, dim = o.shape
    width = n * dim
    step = min(128, size)
    sds = jax.ShapeDtypeStruct
    flat = pl.BlockSpec((step, width), lambda t: (t, 0))
    return pl.pallas_call(
        middle_forward_kernel,
        out_shape=(sds((size, width), bf16), sds((size, width), f32), sds((size, width), bf16)),
        grid=(size // step,),
        in_specs=[pl.BlockSpec((n, step, dim), lambda t: (0, t, 0)), flat,
                  pl.BlockSpec((width, width), lambda t: (0, 0))],
        out_specs=(flat, flat, flat),
        compiler_params=PARAMS, name="middle_forward",
        cost_estimate=pl.CostEstimate(flops=2 * size * width * width, bytes_accessed=14 * 2**20, transcendentals=0),
    )(o, x, w)


def middle_backward_kernel(o_ref, x1_ref, db_ref, dy_ref, w_ref, dx_ref, low_ref, do_ref):
    hat, rstd = hat_of(x1_ref[...])
    dx1 = dy_ref[...].astype(f32) + hat_back(hat, rstd, db_ref[...])
    dx_ref[...] = dx1
    low_ref[...] = dx1.astype(bf16)
    dc = jnp.dot(dx1.astype(bf16), w_ref[...], preferred_element_type=f32)
    hat, rstd = hat_of(wide_row(o_ref))
    d_o = hat_back(hat, rstd, dc).astype(bf16)
    dim = do_ref.shape[2]
    for i in range(do_ref.shape[0]):
        do_ref[i] = d_o[:, i * dim:(i + 1) * dim]


def middle_backward(row, o, x1, db, dy, w):
    n, size, dim = o.shape
    width = n * dim
    step = min(128, size)
    sds = jax.ShapeDtypeStruct
    flat = pl.BlockSpec((step, width), lambda t: (t, 0))
    part = pl.BlockSpec((n, step, dim), lambda t: (0, t, 0))
    return pl.pallas_call(
        middle_backward_kernel,
        out_shape=(sds((size, width), f32), sds((size, width), bf16), sds((n, size, dim), bf16)),
        grid=(size // step,),
        in_specs=[part, flat, pl.BlockSpec((step, width), lambda t: (row * (size // step) + t, 0)), flat,
                  pl.BlockSpec((width, width), lambda t: (0, 0))],
        out_specs=(flat, flat, part),
        compiler_params=PARAMS, name="middle_backward",
        cost_estimate=pl.CostEstimate(flops=2 * size * width * width, bytes_accessed=16 * 2**20, transcendentals=0),
    )(o, x1, db, dy, w)


def ways(row, n):
    bits = [1 << k for k in range(1, n.bit_length() - 1)]
    return bits if row % 2 == 0 else bits[::-1]


def product_sum_kernel(n, rows, cols, x0_ref, x1_ref, w_ref, o_ref, part_s, core_s, sum_s, got_s, send_sem, recv_sem):
    mine = lax.axis_index("ctx")
    spots = n // 2
    size = x0_ref.shape[0] // (rows * spots)
    width = w_ref.shape[1]
    barrier = pltpu.get_barrier_semaphore()
    bits = [1] + ways(0, n)
    for bit in bits:
        pl.semaphore_signal(barrier, inc=1, device_id={"ctx": mine ^ bit}, device_id_type=pl.DeviceIdType.MESH)
    pl.semaphore_wait(barrier, len(bits))
    copies = []

    def send(src, dst, bit):
        at = len(copies)
        copy = pltpu.make_async_remote_copy(
            src_ref=src, dst_ref=dst, send_sem=send_sem.at[at], recv_sem=recv_sem.at[at],
            device_id={"ctx": mine ^ bit}, device_id_type=pl.DeviceIdType.MESH)
        copy.start()
        copies.append(copy)
        return copy

    def key(row, k):
        return [-(k & (bit >> 1)) for bit in ways(row, n)]

    orders = []
    for r in range(rows):
        way = [bit >> 1 for bit in ways(r, n)]
        orders.append(sorted(range(spots), key=lambda k: [0 if k & bit else 1 for bit in way]))
    todo = [(r, orders[r][t]) for t in range(spots) for r in range(rows)]
    inbox, slot, slots = {}, {}, 0

    def product(x_ref, r, k, finish):
        begin = (r * spots + k) * size

        @pl.loop(0, width // cols)
        def _(c):
            at = pl.ds(pl.multiple_of(c * cols, cols), cols)
            finish(at, jnp.dot(x_ref[pl.ds(begin, size), :], w_ref[:, at], preferred_element_type=f32))

    def pair(r, k):
        spot = r * spots + k

        def keep(at, value):
            part_s[spot, :, at] = value.astype(bf16)

        product(x1_ref, r, k, keep)
        inbox[r, k] = send(part_s.at[spot], core_s.at[spot], 1)

    def own(r, k):
        spot = r * spots + k
        inbox[r, k].wait_recv()

        def add(at, value):
            sum_s[spot, :, at] = (value + core_s[spot, :, at].astype(f32)).astype(bf16)

        product(x0_ref, r, k, add)

    def pass_on(r, k, stage):
        nonlocal slots
        bit = ways(r, n)[stage]
        if k & (bit >> 1):
            inbox[r, k ^ (bit >> 1), stage] = (send(sum_s.at[r * spots + k], got_s.at[slots], bit), slots)
            slots += 1

    group = max(rows * spots // 2, 1)
    for begin in range(0, len(todo), group):
        for r, k in todo[begin:begin + group]:
            pair(r, k)
        for r, k in todo[begin:begin + group]:
            own(r, k)
            pass_on(r, k, 0)
    stages = len(bits) - 1
    for stage in range(stages):
        for r, k in todo:
            way = [bit >> 1 for bit in ways(r, n)]
            if any(k & bit for bit in way[:stage + 1]):
                continue
            copy, at = inbox[r, k, stage]
            copy.wait_recv()
            spot = r * spots + k
            if stage == stages - 1:
                o_ref[pl.ds(r * size, size), :] = sum_s[spot].astype(f32) + got_s[at].astype(f32)
            else:
                sum_s[spot] = (sum_s[spot].astype(f32) + got_s[at].astype(f32)).astype(bf16)
                pass_on(r, k, stage + 1)
    for copy in copies:
        copy.wait_send()


def product_sum(x0, x1, w, rows, n, collective_id):
    size = x0.shape[0] // (rows * (n // 2))
    width = w.shape[1]
    count = rows * (n // 2)
    moves = count + rows * (n // 2 - 1)
    vmem = pl.BlockSpec(memory_space=pltpu.VMEM)
    flops = 4 * x0.shape[0] * x0.shape[1] * width
    return pl.pallas_call(
        functools.partial(product_sum_kernel, n, rows, min(512, width)),
        out_shape=jax.ShapeDtypeStruct((rows * size, width), f32),
        in_specs=[vmem] * 3, out_specs=vmem,
        scratch_shapes=[pltpu.VMEM((count, size, width), bf16), pltpu.VMEM((count, size, width), bf16),
                        pltpu.VMEM((count, size, width), bf16), pltpu.VMEM((moves - count, size, width), bf16),
                        pltpu.SemaphoreType.DMA((moves,)), pltpu.SemaphoreType.DMA((moves,))],
        compiler_params=pltpu.CompilerParams(collective_id=collective_id, has_side_effects=True, vmem_limit_bytes=60 * 2**20),
        name="product_sum",
        cost_estimate=pl.CostEstimate(flops=4 * flops, bytes_accessed=20 * 2**20, transcendentals=0),
    )(x0, x1, w)


def standardize(values):
    center = values - jnp.mean(values, axis=-1, keepdims=True)
    spread = jnp.mean(center * center, axis=-1, keepdims=True)
    rstd = lax.rsqrt(spread + EPS)
    return center * rstd, rstd


def standardize_back(hat, rstd, grad):
    return rstd * (grad - jnp.mean(grad, axis=-1, keepdims=True) - hat * jnp.mean(grad * hat, axis=-1, keepdims=True))


def row_places(lengths, row_len):
    places = jnp.arange(row_len, dtype=jnp.int32)
    ends = jnp.cumsum(lengths, axis=-1)
    passed = ends[:, None, :] <= places[None, :, None]
    starts = jnp.sum(jnp.where(passed, lengths[:, None, :], 0), axis=-1)
    valid = places[None, :] < ends[:, -1:]
    lowest = jnp.where(valid, starts, places[None, :]).astype(jnp.int32)
    return (places[None, :] - starts).astype(f32), lowest


def xpos_tables(relative):
    ladder = jnp.arange(HALF, dtype=f32) / HALF
    rate = jnp.power(10000.0, -ladder)
    base = (ladder + 0.4) / 1.4
    angles = rate[None, :, None] * relative[:, None, :]
    power = (relative[:, None, :] - ROW_LEN / 2) / XPOS_BASE
    factor = jnp.power(base[None, :, None], power)
    cosine, sine = jnp.cos(angles), jnp.sin(angles)
    return jnp.stack([cosine * factor, sine * factor, cosine / factor, sine / factor], axis=1)


def dot(a, b, spec, kind=f32):
    return jnp.einsum(spec, a, b, preferred_element_type=f32).astype(kind)


def swap(x, bit):
    n = lax.axis_size("ctx")
    return lax.ppermute(x, "ctx", [(i, i ^ bit) for i in range(n)])


def exchange(blocks):
    n = lax.axis_size("ctx")
    mine = lax.axis_index("ctx")
    out = jnp.zeros_like(blocks)
    for bit in range(n):
        block = lax.dynamic_index_in_dim(blocks, mine ^ bit, 0, False)
        block = swap(block, bit) if bit else block
        out = lax.dynamic_update_index_in_dim(out, block, mine ^ bit, 0)
    return out


def after(x, *others):
    return lax.optimization_barrier((x, *others))[0]


def gather_start(x):
    return [{0: x[r]} for r in range(x.shape[0])]


def gather_step(held, step):
    n = lax.axis_size("ctx")
    out = []
    for r, parts in enumerate(held):
        bit = ways(r, n)[step]
        out.append({**parts, **{k | bit: swap(v, bit) for k, v in parts.items()}})
    return out


def gather_steps():
    return lax.axis_size("ctx").bit_length() - 2


def gather_end(held):
    return jnp.concatenate([parts[k] for parts in held for k in sorted(parts)], axis=0)


def gather_half(x):
    held = gather_start(x)
    for step in range(gather_steps()):
        held = gather_step(held, step)
    return gather_end(held)


def plus(a, b, kind=bf16):
    return (a.astype(f32) + b.astype(f32)).astype(kind)


def reduce_start(half0, half1, rows):
    n = lax.axis_size("ctx")
    width = half0.shape[-1]
    both = plus(half0, swap(half1, 1)).reshape(rows, n // 2, -1, width)
    return [{2 * k: both[r, k] for k in range(n // 2)} for r in range(rows)]


def reduce_step(held, step):
    n = lax.axis_size("ctx")
    out = []
    for r, parts in enumerate(held):
        bit = ways(r, n)[step]
        kind = bf16 if len(parts) > 2 else f32
        out.append({k: plus(v, swap(parts[k | bit], bit), kind) for k, v in parts.items() if not k & bit})
    return out


def reduce_end(held):
    return jnp.concatenate([parts[0] for parts in held], axis=0)


def reduce_halves(half0, half1, rows):
    held = reduce_start(half0, half1, rows)
    for step in range(gather_steps()):
        held = reduce_step(held, step)
    return reduce_end(held)


def body(inputs, doc_len, w_query, w_key, w_value, w_out, w_up, w_down, gain_attn, gain_attn_sub, gain_ffn,
         gain_ffn_sub, out_cotangent):
    rows, local_len, width = inputs.shape
    n, m = lax.axis_size("ctx"), lax.axis_size("row")
    row_len = local_len * n
    tokens, half = rows * local_len, rows * row_len // 2
    piece = w_query.shape[0]
    heads_dim = width // n
    ff = w_up.shape[1]
    unit = ff // (n * m)
    ff_dev = unit * m
    blk = min(512, row_len)
    mine = lax.axis_index("ctx")
    core, place = mine & 1, mine >> 1

    def scaled(w, gain):
        return (w.astype(f32) * gain.astype(f32)[:, None]).astype(bf16)

    x_own = inputs.reshape(tokens, width).astype(f32)
    x_hat, x_rstd = standardize(x_own)
    x_low = x_hat.astype(bf16)
    xh0 = gather_half(x_low.reshape(rows, local_len, width))
    xh1 = swap(xh0, 1)

    qkv_local = jnp.concatenate(
        [scaled(w, gain_attn).reshape(piece, n, heads_dim) for w in (w_query, w_key, w_value)], axis=2)
    qkv_part = exchange(qkv_local.transpose(1, 0, 2)).reshape(n * piece, 3 * heads_dim)
    w_qkv = lax.all_gather(qkv_part, "row", axis=0, tiled=True)
    out_all = lax.all_gather(scaled(w_out, gain_attn_sub), BOTH, axis=0, tiled=True)

    relative, lowest = row_places(doc_len, row_len)
    table = xpos_tables(relative)
    span = [span_of(lowest[r], blk, core, place) for r in range(rows)]
    qkv0 = dot(w_qkv, xh0, "df,td->ft")
    qkv1 = dot(w_qkv, xh1, "df,td->ft")
    qkv0, qkv1, w_up_in, cot = lax.optimization_barrier((qkv0, qkv1, w_up, out_cotangent))
    up_local = scaled(w_up_in, gain_ffn).reshape(piece, m, n, unit).transpose(2, 0, 1, 3).reshape(n, piece, ff_dev)
    up_part = lax.all_to_all(up_local, "ctx", split_axis=0, concat_axis=0, tiled=True).reshape(n * piece, ff_dev)
    dy_held = gather_step(gather_start(cot), 0)
    dy_steps = gather_steps()
    saved, o = [], []
    for r in range(rows):
        o_row, *kept = attention_forward(r, qkv0, qkv1, table[r], lowest[r], span[r], blk, local_len)
        if r == 0:
            o_row, kept, qkv0, qkv1, dy_held, out_all = lax.optimization_barrier((o_row, kept, qkv0, qkv1, dy_held, out_all))
            down_all = lax.all_gather(after(scaled(w_down, gain_ffn_sub), out_all), "row", axis=0, tiled=True)
            for step in range(1, dy_steps):
                dy_held = gather_step(dy_held, step)
        if r == rows - 1:
            o_row, o = lax.optimization_barrier((o_row, o))
        saved.append(kept)
        o.append(lax.all_to_all(o_row.reshape(n, local_len, heads_dim), "ctx", split_axis=0, concat_axis=0, tiled=True))
    o, down_all, up_part = lax.optimization_barrier((o, down_all, up_part))
    up_all = lax.all_gather(up_part, "row", axis=0, tiled=True)
    c, x1, b_low = zip(*[middle_forward(o[r], inputs[r], out_all) for r in range(rows)])
    b_low, dy_held = lax.optimization_barrier((b_low, dy_held))
    dy0 = gather_end(dy_held)
    dy1 = swap(dy0, 1)
    b_held = gather_step([{0: v} for v in b_low], 0)
    d_hat0 = dot(dy0, down_all, "td,fd->tf")
    b_held, d_hat0 = lax.optimization_barrier((b_held, d_hat0))
    for step in range(1, gather_steps()):
        b_held = gather_step(b_held, step)
    d_hat1 = dot(dy1, down_all, "td,fd->tf")
    b_held, d_hat1 = lax.optimization_barrier((b_held, d_hat1))
    b0 = gather_end(b_held)
    b1 = swap(b0, 1)

    def activate(b):
        h = dot(b, up_all, "td,df->tf")
        return h, 0.5 * (1.0 + lax.erf(h * (2.0**-0.5)))

    def own_stats(h, cdf, d_hat):
        gel = h * cdf
        mean = jnp.mean(gel, axis=-1)
        off = gel - mean[:, None]
        return jnp.stack([mean, jnp.sum(off * off, axis=-1), jnp.sum(d_hat, axis=-1), jnp.sum(d_hat * off, axis=-1)])

    h0, cdf0 = activate(b0)
    h1, cdf1 = activate(b1)
    stats = jnp.stack([own_stats(h0, cdf0, d_hat0), own_stats(h1, cdf1, d_hat1)], axis=1)
    order = jnp.arange(n // 2, dtype=jnp.int32) ^ place
    halves = jnp.arange(2, dtype=jnp.int32) ^ core

    def reorder(v):
        v = v.reshape(v.shape[0], 2, rows, n // 2, local_len)
        return jnp.take(jnp.take(v, halves, axis=1), order, axis=3).reshape(v.shape[0], 2 * half)

    stats = lax.all_gather(reorder(stats.reshape(4, 2 * half)), "ctx", axis=0, tiled=False)
    mean = jnp.mean(stats[:, 0], axis=0)
    shift = stats[:, 0] - mean
    var = (jnp.sum(stats[:, 1], axis=0) + ff_dev * jnp.sum(shift * shift, axis=0)) / ff
    rstd = lax.rsqrt(var + EPS)
    d_mean = jnp.sum(stats[:, 2], axis=0) / ff
    d_corr = rstd * jnp.sum(stats[:, 3] + stats[:, 2] * shift, axis=0) / ff
    merged = reorder(jnp.stack([mean, rstd, d_mean, d_corr])).reshape(4, 2, half, 1)

    def finish(h, cdf, d_hat, which):
        mean, rstd, d_mean, d_corr = (merged[k, which] for k in range(4))
        hat = (h * cdf - mean) * rstd
        d_gel = rstd * (d_hat - d_mean - hat * d_corr)
        pdf = jnp.exp(-0.5 * h * h) * 0.3989422804014327
        return hat.astype(bf16), (d_gel * (cdf + h * pdf)).astype(bf16)

    e0, dh0 = finish(h0, cdf0, d_hat0, 0)
    e1, dh1 = finish(h1, cdf1, d_hat1, 1)
    down_part = (dot(e0, dy0, "tf,td->fd") + dot(e1, dy1, "tf,td->fd")).astype(bf16)
    up_part = (dot(b0, dh0, "td,tf->df") + dot(b1, dh1, "td,tf->df")).astype(bf16)
    e0, e1, dh0, dh1, down_part, up_part = lax.optimization_barrier((e0, e1, dh0, dh1, down_part, up_part))
    down_sum = lax.psum_scatter(down_part, "row", scatter_dimension=0, tiled=True)
    db = product_sum(dh0, dh1, up_all.T, rows, n, 1)
    e0, e1, db, up_part, down_sum = lax.optimization_barrier((e0, e1, db, up_part, down_sum))
    down_raw = down_sum.astype(f32)
    up_sum = lax.psum_scatter(up_part, "row", scatter_dimension=0, tiled=True)
    ffn = product_sum(e0, e1, down_all, rows, n, 3)
    db, ffn, up_sum = lax.optimization_barrier((db, ffn, up_sum))
    output = (jnp.stack(x1) + ffn.reshape(rows, local_len, width)).astype(bf16)

    out_allT = out_all.T
    dx1, dx1b, d_o = zip(*[middle_backward(r, o[r], x1[r], db, out_cotangent[r], out_allT) for r in range(rows)])
    do_heads = [lax.all_to_all(v, "ctx", split_axis=0, concat_axis=0, tiled=True).reshape(row_len, heads_dim) for v in d_o]
    c_order = jnp.concatenate(c).reshape(tokens, m, n, piece).transpose(0, 2, 1, 3).reshape(tokens, width)
    out_part = dot(c_order, jnp.concatenate(dx1b), "td,te->de", bf16)
    do_heads[0], out_part = lax.optimization_barrier((do_heads[0], out_part))
    out_part = lax.psum_scatter(out_part, "ctx", scatter_dimension=0, tiled=True)
    up_moved = lax.all_to_all(after(up_sum.reshape(n, piece, ff_dev), do_heads[-1]), "ctx", split_axis=0, concat_axis=2, tiled=True)
    grads = None
    for r in range(rows):
        grads = attention_backward(r, rows, saved[r], do_heads[r], table[r], lowest[r], span[r], blk, local_len, grads)
    grads, out_part, up_moved = lax.optimization_barrier((grads, out_part, up_moved))
    d0, d1 = grads
    out_sum = lax.psum_scatter(out_part, "row", scatter_dimension=0, tiled=True)
    qkv_part = (dot(xh0, d0, "td,tf->df") + dot(xh1, d1, "td,tf->df")).astype(bf16)
    d0, d1, qkv_part, out_sum = lax.optimization_barrier((d0, d1, qkv_part, out_sum))
    out_raw = out_sum.astype(f32)
    qkv_part = lax.psum_scatter(qkv_part, "row", scatter_dimension=0, tiled=True)
    da = product_sum(d0, d1, w_qkv.T, rows, n, 2)
    da, qkv_part = lax.optimization_barrier((da, qkv_part))
    up_raw = up_moved.reshape(piece, n, m, unit).transpose(0, 2, 1, 3).reshape(piece, ff).astype(f32)
    qkv_raw = lax.all_to_all(qkv_part.reshape(n, piece, 3 * heads_dim), "ctx", split_axis=0, concat_axis=2, tiled=True)
    qkv_raw = qkv_raw.reshape(piece, n, 3, heads_dim).astype(f32)
    query_raw, key_raw, value_raw = (qkv_raw[:, :, i].reshape(piece, width) for i in range(3))
    input_grad = jnp.stack(dx1) + standardize_back(x_hat, x_rstd, da).reshape(rows, local_len, width)

    def against(w, raw):
        return jnp.sum(w.astype(f32) * raw, axis=-1)

    def grown(raw, gain):
        return raw * gain.astype(f32)[:, None]

    gain_one = against(w_query, query_raw) + against(w_key, key_raw) + against(w_value, value_raw)
    return (output, input_grad, grown(query_raw, gain_attn), grown(key_raw, gain_attn), grown(value_raw, gain_attn),
            grown(out_raw, gain_attn_sub), grown(up_raw, gain_ffn), grown(down_raw, gain_ffn_sub),
            gain_one, against(w_out, out_raw), against(w_up, up_raw), against(w_down, down_raw))


def solution(mesh):
    split = P(BOTH, None)
    acts = P("row", "ctx", None)
    gain = P(BOTH)
    return jax.shard_map(
        body,
        mesh=mesh,
        in_specs=(acts, P("row", None)) + (split,) * 6 + (gain,) * 4 + (acts,),
        out_specs=(acts, acts) + (split,) * 6 + (gain,) * 4,
        check_vma=False,
    )
```

time: 1430 us -> 1060 us (0.74); the launches traced: 1420 us -> 1070 us
  waiting for transfers between devices: 706 us -> 212 us
  Pallas kernels: 109 us -> 409 us
  blocking collectives: 137 us -> 29.2 us
  matrix products: 252 us -> 167 us
  starting transfers between devices: 19.4 us -> 59.8 us
  other arithmetic: 107 us -> 80.2 us
  local copies, waits for them, and re-layouts: 76.2 us -> 94 us
    reduce_scatter x7 -> x3, waiting for transfers between devices: 324 us -> 0.06 us  [the longest x1 0.02 us: body(): lax.psum_scatter(out_part, 'ctx', scatter_dimension=0, tiled=True)]
    pallas_call x2 -> x11, Pallas kernels: 109 us -> 409 us  [the longest x3 264 us: product_sum(): pl.pallas_call(functools.partial(product_sum_kernel, n, rows, min(512, wi...]
    all_gather x5 -> x2, waiting for transfers between devices: 250 us -> 12.6 us  [the longest x1 11.6 us: body(): lax.all_gather(after(scaled(w_down, gain_ffn_sub), out_all), 'row', axis=...]
    ppermute x0 -> x28, waiting for transfers between devices: none -> 127 us  [swap(): return lax.ppermute(x, 'ctx', [(i, i ^ bit) for i in range(n)])]
    all_gather x3 -> x1, blocking collectives: 116 us -> 9.83 us  [body(): lax.all_gather(reorder(stats.reshape(4, 2 * half)), 'ctx', axis=0, tiled=...]
    dot_general x12 -> x13, matrix products: 252 us -> 167 us  [dot(): return jnp.einsum(spec, a, b, preferred_element_type=f32).astype(kind)]
    all_gather x1, waiting for transfers between devices: 38.7 us -> 0.01 us  [body(): w_qkv = lax.all_gather(qkv_part, 'row', axis=0, tiled=True)]
    reduce_scatter x1, waiting for transfers between devices: 36.9 us -> 0.02 us  [body(): lax.psum_scatter(down_part, 'row', scatter_dimension=0, tiled=True)]
  transfers between devices with their start and end apart: 20 -> 43, of which waited for: 13 -> 19; matrix products, arithmetic and copies ran while one was open for 23% -> 18% of each run, Pallas kernels for 8% -> 37%
where the time goes in v2:
time: 1060 us; the launch traced here: 1070 us
  Pallas kernels  409 us (39%)
  waiting for transfers between devices  212 us (20%)
  matrix products  167 us (16%)
  local copies, waits for them, and re-layouts  94 us (9%)
  other arithmetic  80.2 us (8%)
  starting transfers between devices  59.8 us (6%)
  blocking collectives  29.2 us (3%)
  between operations  15.3 us (1%)
    pallas_call x3, Pallas kernels, product_sum(): pl.pallas_call(functools.partial(product_sum_kernel, n, rows, min(512, wi...  264 us
    dot_general x13, matrix products, dot(): return jnp.einsum(spec, a, b, preferred_element_type=f32).astype(kind)  167 us
    ppermute x28, waiting for transfers between devices, swap(): return lax.ppermute(x, 'ctx', [(i, i ^ bit) for i in range(n)])  127 us
    pallas_call x2, Pallas kernels, attention_backward(): pl.pallas_call(call, out_shape=(whole, whole), grid_spec=pltpu.PrefetchSc...  63.7 us
    pallas_call x2, Pallas kernels, attention_forward(): pl.pallas_call(functools.partial(forward_kernel, nh, blk, unit), out_shap...  44.9 us
    unnamed x133, local copies, waits for them, and re-layouts  36.9 us
    ppermute x28, starting transfers between devices, swap(): return lax.ppermute(x, 'ctx', [(i, i ^ bit) for i in range(n)])  27.3 us
    convert_element_type x2, other arithmetic, finish(): return (hat.astype(bf16), (d_gel * (cdf + h * pdf)).astype(bf16))  26.8 us
  transfers between devices with their start and end apart: 43, of which 19 were waited for; matrix products, arithmetic and copies ran while one was open for 18% of the time, Pallas kernels for 37%

profile of v2, /device:TPU:0, one launch (start us, length us, event | category | flops | bytes accessed | tf_op | source)
XLA Modules:
  0.0 1066.8 jit_solution(4319867856137100093)
XLA Ops:
  21.8 5.9 collective-permute-done.4
  37.0 21.7 %collective-permute-done.7 = bf16[256,2048]{1,0:T(8,128)(2,1)S(1)} collective-permute-done((bf16[256,2048]{1,0:T(8,128)(2,1)S(1)}, bf16[256,2048]{1,0:T(8,128)(2,1)S(1)}, u32[]{:S(2)}, u32[]{:S(2)}) %collective-permute-start.7) | collective-permute-done | bytes 1048608 | tf_op jit(solution)/shard_map/ppermute | solution.py:517
  63.4 20.1 %collective-permute-done.8 = bf16[256,2048]{1,0:T(8,128)(2,1)S(1)} collective-permute-done((bf16[256,2048]{1,0:T(8,128)(2,1)S(1)}, bf16[256,2048]{1,0:T(8,128)(2,1)S(1)}, u32[]{:S(2)}, u32[]{:S(2)}) %collective-permute-start.8) | collective-permute-done | bytes 1048608 | tf_op jit(solution)/shard_map/ppermute | solution.py:517
  84.5 20.4 %collective-permute-done.9 = bf16[256,2048]{1,0:T(8,128)(2,1)S(1)} collective-permute-done((bf16[256,2048]{1,0:T(8,128)(2,1)S(1)}, bf16[256,2048]{1,0:T(8,128)(2,1)S(1)}, u32[]{:S(2)}, u32[]{:S(2)}) %collective-permute-start.9) | collective-permute-done | bytes 1048608 | tf_op jit(solution)/shard_map/ppermute | solution.py:517
  120.3 12.8 %fusion.59.q0_ref.k0_ref.v0_ref = f32[768,2048]{1,0:T(8,128)} fusion(bf16[2048,768]{0,1:T(8,128)(2,1)} %all-gather.5.cloned.1.call-done, bf16[2048,2048]{1,0:T(8,128)(2,1)} %constant_dynamic-update-slice_fusion.3), kind=kOutput, calls=%fused_computation.238 | convolution fusion | flops 6442450944 | bytes 17825792 | tf_op jit(solution)/shard_map/df,td->ft/dot_general | solution.py:512
  133.1 11.5 %fusion.60.q1_ref.k1_ref.v1_ref = f32[768,2048]{1,0:T(8,128)} fusion(bf16[2048,768]{0,1:T(8,128)(2,1)S(1)} %copy-done.42, bf16[2048,2048]{1,0:T(8,128)(2,1)} %collective-permute-done.13), kind=kOutput, calls=%fused_computation.239 | convolution fusion | flops 6442450944 | bytes 17825792 | tf_op jit(solution)/shard_map/df,td->ft/dot_general | solution.py:512
  148.3 29.0 %attention_forward.2 = (bf16[2048,256]{1,0:T(8,128)(2,1)}, f32[256,2048]{1,0:T(8,128)}, f32[4,2048]{1,0:T(4,128)}, bf16[256,2048]{1,0:T(8,128)(2,1)}, bf16[256,2...) custom-call(s32[10]{0:T(128)} %pad_add_fusion.4.span_ref, f32[768,2048]{1,0:T(8,128)} %fusion.59.q0_ref.k0_ref.v0_ref, ...), custom_call_target="tpu_custom_call" | custom-call | flops 8589934592 | bytes 10485760 | tf_op jit(solution)/shard_map/attention_forward/pallas_call | solution.py:234
  177.3 5.6 collective-permute-done.14
  193.6 9.6 all-to-all-done.o_ref
  203.2 14.0 %all-to-all-start.2 = ((bf16[8,64,1024]{2,1,0:T(8,128)(2,1)}), bf16[8,64,1024]{2,1,0:T(8,128)(2,1)}, u32[]{:S(2)}, u32[]{:S(2)}) async-start(bf16[8,64,1024]{2,1,0:T(8,128)(2,1)} %reshape.392), calls=%async_computation.2 | async-start | bytes 2097152 | tf_op jit(solution)/shard_map/all_to_all | solution.py:632
  217.9 15.9 %attention_forward.3 = (bf16[2048,256]{1,0:T(8,128)(2,1)}, f32[256,2048]{1,0:T(8,128)}, f32[4,2048]{1,0:T(4,128)}, bf16[256,2048]{1,0:T(8,128)(2,1)}, bf16[256,2...) custom-call(s32[10]{0:T(128)} %pad_add_fusion.2.span_ref, f32[768,2048]{1,0:T(8,128)} %fusion.59.q0_ref.k0_ref.v0_ref, ...), custom_call_target="tpu_custom_call" | custom-call | flops 8589934592 | bytes 10485760 | tf_op jit(solution)/shard_map/attention_forward/pallas_call | solution.py:234
  243.4 10.3 all-to-all-done.1.o_ref
  253.7 11.6 %all-gather.9.cloned.1.call-done.w_ref = bf16[1024,2048]{1,0:T(8,128)(2,1)} async-done(((bf16[256,2048]{1,0:T(8,128)(2,1)}), bf16[1024,2048]{1,0:T(8,128)(2,1)}) %all-gather.9.cloned.1.call-update) | async-done | bytes 4194320 | tf_op jit(solution)/shard_map/all_gather | solution.py:640
  265.3 8.5 middle_forward.3
  273.8 8.5 middle_forward.2
  282.3 15.0 %collective-permute-done.17 = bf16[256,2048]{1,0:T(8,128)(2,1)} collective-permute-done((bf16[256,2048]{1,0:T(8,128)(2,1)}, bf16[256,2048]{1,0:T(8,128)(2,1)}, u32[]{:S(2)}, u32[]{:S(2)}) %collective-permute-start.17) | collective-permute-done | bytes 1048608 | tf_op jit(solution)/shard_map/ppermute | solution.py:517
  317.0 13.2 %fusion.61 = f32[2048,1024]{1,0:T(8,128)} fusion(bf16[2048,2048]{1,0:T(8,128)(2,1)} %constant_dynamic-update-slice_fusion.11, bf16[1024,2048]{1,0:T(8,128)(2,1)S(1)} %copy-done.41), kind=kOutput, calls=%fused_computation.240 | convolution fusion | flops 8589934592 | bytes 20971520 | tf_op jit(solution)/shard_map/td,fd->tf/dot_general | solution.py:512
  332.6 8.1 collective-permute-done.20
  345.8 14.9 %fusion.62 = f32[2048,1024]{1,0:T(8,128)} fusion(bf16[2048,2048]{1,0:T(8,128)(2,1)} %collective-permute-done.26, bf16[1024,2048]{1,0:T(8,128)(2,1)} %all-gather.9.cloned.1.call-done.w_ref), kind=kOutput, calls=%fused_computation.241 | convolution fusion | flops 8589934592 | bytes 20971520 | tf_op jit(solution)/shard_map/td,fd->tf/dot_general | solution.py:512
  360.7 7.1 collective-permute-done.22
  367.8 20.8 %collective-permute-done.23 = bf16[256,2048]{1,0:T(8,128)(2,1)S(1)} collective-permute-done((bf16[256,2048]{1,0:T(8,128)(2,1)}, bf16[256,2048]{1,0:T(8,128)(2,1)S(1)}, u32[]{:S(2)}, u32[]{:S(2)}) %collective-permute-start.23) | collective-permute-done | bytes 1048608 | tf_op jit(solution)/shard_map/ppermute | solution.py:517
  401.2 24.1 %all-gather.11.cloned.1.call-done = bf16[2048,1024]{0,1:T(8,128)(2,1)} async-done(((bf16[512,1024]{0,1:T(8,128)(2,1)}), bf16[2048,1024]{0,1:T(8,128)(2,1)}) %all-gather.11.cloned.1.call-update) | async-done | bytes 4194320 | tf_op jit(solution)/shard_map/all_gather | solution.py:648
  425.3 16.4 %fusion.52 = (f32[2048]{0:T(1024)S(1)}, f32[2048,1024]{1,0:T(8,128)}, f32[2048,1024]{1,0:T(8,128)}) fusion(bf16[2048,2048]{1,0:T(8,128)(2,1)} %constant_dynamic-update-slice_fusion.19, bf16[2048,1024]{0,1:T(8,128)(2,1)} %all-gather.11.cloned.1.call-done), kind=kOutput, calls=%fused_computation.233 | convolution fusion | flops 8600418304 | bytes 29368320 | tf_op jit(solution)/shard_map/td,df->tf/dot_general | solution.py:512
  441.7 16.4 %fusion.54 = (f32[2048]{0:T(1024)S(1)}, f32[2048,1024]{1,0:T(8,128)}, f32[2048,1024]{1,0:T(8,128)}) fusion(bf16[2048,2048]{1,0:T(8,128)(2,1)} %collective-permute-done.27, bf16[2048,1024]{0,1:T(8,128)(2,1)} %all-gather.11.cloned.1.call-done), kind=kOutput, calls=%fused_computation.234 | convolution fusion | flops 8600418304 | bytes 29368320 | tf_op jit(solution)/shard_map/td,df->tf/dot_general | solution.py:512
  458.1 13.0 %multiply_reduce_fusion.1 = (f32[2048]{0:T(1024)S(1)}, f32[2048]{0:T(1024)S(1)}, f32[2048]{0:T(1024)S(1)}, f32[2048]{0:T(1024)S(1)}, f32[2048]{0:T(1024)S(1)}, /*index=5*/f32[2048]{0:T(1024)S(1)}) fusion(f32[2048,1024]{1,0:T(8,128)} %get-tuple-element.289, f32[2048]{0:T(1024)S(1)} %broadcast_multiply_fusion.6, f32[2048,1024]{1,0:T(8,128)} %fusion.62, ...), kind=kLoop, calls=%fused_computation.23 | loop fusion | flops 25153536 | bytes 33619968 | tf_op jit(solution)/shard_map/reduce_sum | solution.py:671
  472.7 9.8 all_gather.19
  485.1 12.6 %fusion.11 = (bf16[2048,1024]{1,0:T(8,128)(2,1)S(1)}, bf16[2048,1024]{1,0:T(8,128)(2,1)}) fusion(f32[2048,1024]{1,0:T(8,128)} %get-tuple-element.361, f32[2048,1024]{1,0:T(8,128)} %fusion.62, f32[2048,1024]{1,0:T(8,128)} %get-tuple-element.289, f32[2048]{0:T(1024)S(1)} %bitcast.240, f32[2048]{0:T(1024)S(1)} %bitcast.239, f32[2048]{0:T(1024)S(1)} %bitcast.241, ...), kind=kLoop, calls=%fused_computation.17 | loop fusion | flops 35651584 | bytes 33587200 | tf_op jit(solution)/shard_map/convert_element_type | solution.py:697
  497.8 14.1 %fusion.5 = (bf16[2048,1024]{1,0:T(8,128)(2,1)S(1)}, bf16[2048,1024]{1,0:T(8,128)(2,1)}) fusion(f32[2048,1024]{1,0:T(8,128)} %get-tuple-element.360, f32[2048,1024]{1,0:T(8,128)} %fusion.61, f32[2048,1024]{1,0:T(8,128)} %get-tuple-element.287, f32[2048]{0:T(1024)S(1)} %bitcast.235, f32[2048]{0:T(1024)S(1)} %bitcast.236, f32[2048]{0:T(1024)S(1)} %bitcast.237, ...), kind=kLoop, calls=%fused_computation.11 | loop fusion | flops 35651584 | bytes 33587200 | tf_op jit(solution)/shard_map/convert_element_type | solution.py:697
  511.9 13.1 %fusion.64 = f32[2048,1024]{1,0:T(8,128)S(1)} fusion(bf16[2048,2048]{1,0:T(8,128)(2,1)} %collective-permute-done.27, bf16[2048,1024]{1,0:T(8,128)(2,1)S(1)} %get-tuple-element.174.x1_ref), kind=kOutput, calls=%fused_computation.243 | convolution fusion | flops 8589934592 | bytes 20971520 | tf_op jit(solution)/shard_map/td,tf->df/dot_general | solution.py:512
  525.0 12.8 %add_convert_fusion = bf16[2048,1024]{1,0:T(8,128)(2,1)} fusion(f32[2048,1024]{1,0:T(8,128)S(1)} %fusion.64, bf16[2048,2048]{1,0:T(8,128)(2,1)} %constant_dynamic-update-slice_fusion.19, bf16[2048,1024]{1,0:T(8,128)(2,1)S(1)} %get-tuple-element.173.x0_ref), kind=kOutput, calls=%fused_computation.18 | convolution fusion | flops 8594128896 | bytes 25165824 | tf_op jit(solution)/shard_map/td,tf->df/dot_general | solution.py:512
  537.8 13.0 %fusion.63 = f32[1024,2048]{1,0:T(8,128)S(1)} fusion(bf16[2048,1024]{1,0:T(8,128)(2,1)} %get-tuple-element.179.x1_ref, bf16[2048,2048]{1,0:T(8,128)(2,1)} %collective-permute-done.26), kind=kOutput, calls=%fused_computation.242 | convolution fusion | flops 8589934592 | bytes 20971520 | tf_op jit(solution)/shard_map/tf,td->fd/dot_general | solution.py:512
  550.8 12.8 %add_convert_fusion.1 = bf16[1024,2048]{1,0:T(8,128)(2,1)} fusion(f32[1024,2048]{1,0:T(8,128)S(1)} %fusion.63, bf16[2048,1024]{1,0:T(8,128)(2,1)S(1)} %copy-done.8, bf16[2048,2048]{1,0:T(8,128)(2,1)} %constant_dynamic-update-slice_fusion.11), kind=kOutput, calls=%fused_computation.19 | convolution fusion | flops 8594128896 | bytes 25165824 | tf_op jit(solution)/shard_map/tf,td->fd/dot_general | solution.py:512
  563.7 89.6 %product_sum.3.db_ref = f32[512,2048]{1,0:T(8,128)} custom-call(bf16[2048,1024]{1,0:T(8,128)(2,1)} %copy-done.10, bf16[2048,1024]{1,0:T(8,128)(2,1)} %copy-done.9, bf16[1024,2048]{1,0:T(8,128)(2,1)} %bitcast.243), custom_call_target="tpu_custom_call" | custom-call | flops 68719476736 | bytes 20971520 | tf_op jit(solution)/shard_map/product_sum/pallas_call | solution.py:466
  654.8 12.5 %copy.186 = bf16[2048,2048]{0,1:T(8,128)(2,1)} copy(bf16[2048,2048]{1,0:T(8,128)(2,1)} %all-gather.7.cloned.1.call-done.w_ref) | data formatting | bytes 16777216 | tf_op jit(solution)/shard_map/optimization_barrier | solution.py:639
  673.1 87.7 %product_sum.4 = f32[512,2048]{1,0:T(8,128)} custom-call(bf16[2048,1024]{1,0:T(8,128)(2,1)} %get-tuple-element.178.x0_ref, bf16[2048,1024]{1,0:T(8,128)(2,1)} %get-tuple-element.179.x1_ref, bf16[1024,2048]{1,0:T(8,128)(2,1)} %all-gather.9.cloned.1.call-done.w_ref), custom_call_target="tpu_custom_call" | custom-call | flops 68719476736 | bytes 20971520 | tf_op jit(solution)/shard_map/product_sum/pallas_call | solution.py:466
  760.8 9.9 middle_backward.2
  774.3 9.9 middle_backward.3
  784.2 8.2 convolution_convert_fusion
  794.0 19.3 %all_to_all.52 = bf16[8,256,256]{2,1,0:T(8,128)(2,1)} all-to-all(bf16[8,256,256]{2,1,0:T(8,128)(2,1)S(1)} %copy-done.23), channel_id=1, replica_groups=mesh['row'=4,'ctx'=8] {'ctx'}, dimensions={0} | all-to-all | bytes 2097152 | tf_op jit(solution)/shard_map/all_to_all | solution.py:715
  816.9 41.0 %attention_backward.2 = (bf16[2048,768]{1,0:T(8,128)(2,1)}, bf16[2048,768]{1,0:T(8,128)(2,1)}) custom-call(s32[10]{0:T(128)} %pad_add_fusion.4.span_ref, bf16[256,2048]{1,0:T(8,128)(2,1)} %get-tuple-element.191.refs_0_, bf16[256,2048]{1,0:T(8,128)(2,1)} %get-tuple-element.192.refs_1_, bf16[256,2048]{1,0:T(8,128)(2,1)} %get-tuple-element.193.refs_2_, ...), custom_call_target="tpu_custom_call" | custom-call | flops 21474836480 | bytes 20971520 | tf_op jit(solution)/shard_map/attention_backward/pallas_call | solution.py:269
  858.0 22.7 %attention_backward.3 = (bf16[2048,768]{1,0:T(8,128)(2,1)}, bf16[2048,768]{1,0:T(8,128)(2,1)}) custom-call(s32[10]{0:T(128)} %pad_add_fusion.2.span_ref, bf16[256,2048]{1,0:T(8,128)(2,1)} %get-tuple-element.185.qT_ref, bf16[256,2048]{1,0:T(8,128)(2,1)} %get-tuple-element.186.kT_ref, ...), custom_call_target="tpu_custom_call", output_to_operand_aliasing={{0}: (9, {}), {1}: (10, {})} | custom-call | flops 21474836480 | bytes 20971520 | tf_op jit(solution)/shard_map/attention_backward/pallas_call | solution.py:269
  880.9 11.1 %fusion.65 = f32[2048,768]{1,0:T(8,128)S(1)} fusion(bf16[2048,2048]{1,0:T(8,128)(2,1)} %collective-permute-done.13, bf16[2048,768]{1,0:T(8,128)(2,1)} %get-tuple-element.213.x1_ref), kind=kOutput, calls=%fused_computation.244 | convolution fusion | flops 6442450944 | bytes 17825792 | tf_op jit(solution)/shard_map/td,tf->df/dot_general | solution.py:512
  892.0 10.7 %add_convert_fusion.2 = bf16[2048,768]{1,0:T(8,128)(2,1)} fusion(f32[2048,768]{1,0:T(8,128)S(1)} %fusion.65, bf16[2048,2048]{1,0:T(8,128)(2,1)} %constant_dynamic-update-slice_fusion.3, bf16[2048,768]{1,0:T(8,128)(2,1)S(1)} %copy-done.46), kind=kOutput, calls=%fused_computation.31 | convolution fusion | flops 6445596672 | bytes 20971520 | tf_op jit(solution)/shard_map/td,tf->df/dot_general | solution.py:512
  902.7 23.2 %reduce-scatter.16.cloned.1.call-done = bf16[64,2048]{1,0:T(8,128)(2,1)} async-done(((bf16[256,2048]{1,0:T(8,128)(2,1)}), bf16[64,2048]{1,0:T(8,128)(2,1)}) %reduce-scatter.16.cloned.1.call-update) | async-done | bytes 262160
  931.8 5.3 fusion.14
  944.6 86.4 %product_sum.5 = f32[512,2048]{1,0:T(8,128)} custom-call(bf16[2048,768]{1,0:T(8,128)(2,1)} %get-tuple-element.212.x0_ref, bf16[2048,768]{1,0:T(8,128)(2,1)} %get-tuple-element.213.x1_ref, bf16[768,2048]{1,0:T(8,128)(2,1)} %bitcast.244), custom_call_target="tpu_custom_call" | custom-call | flops 51539607552 | bytes 20971520 | tf_op jit(solution)/shard_map/product_sum/pallas_call | solution.py:466
  1042.1 5.0 all-to-all-done.6
  1051.9 4.1 slice_reduce_fusion
  (333 shorter events, 162.3 us)
Async XLA Ops:
  7.2 113.1 %all-gather.5.cloned.1.call-start = ((), (), s32[]{:S(2)}) async-start(), calls=%async_computation.12 | async-start | bytes 3932160 | tf_op jit(solution)/shard_map/all_gather | solution.py:622
  13.2 5.4 collective-permute-start
  13.7 7.5 collective-permute-start.1
  16.3 5.5 collective-permute-start.2
  16.5 5.3 collective-permute-start.3
  18.4 9.4 collective-permute-start.4
  18.6 9.2 collective-permute-start.5
  21.2 6.6 collective-permute-start.6
  29.0 155.0 %all-gather.7.cloned.1.call-start = ((), (), s32[]{:S(2)}) async-start(), calls=%async_computation.13 | async-start | bytes 8650752 | tf_op jit(solution)/shard_map/all_gather | solution.py:623
  30.0 235.3 %all-gather.9.cloned.1.call-start = ((), (), s32[]{:S(2)}) async-start(), calls=%async_computation.14 | async-start | bytes 5242880 | tf_op jit(solution)/shard_map/all_gather | solution.py:640
  33.5 77.9 %copy-start.44 = (bf16[256]{0:T(256)(128)(2,1)S(1)}, bf16[256]{0:T(256)(128)(2,1)}, u32[]{:S(2)}) copy-start(bf16[256]{0:T(256)(128)(2,1)} %param.28) | copy-start | bytes 1540
  33.5 25.2 %collective-permute-start.7 = (bf16[256,2048]{1,0:T(8,128)(2,1)S(1)}, bf16[256,2048]{1,0:T(8,128)(2,1)S(1)}, u32[]{:S(2)}, u32[]{:S(2)}) collective-permute-start(bf16[256,2048]{1,0:T(8,128)(2,1)S(1)} %get-tuple-element.306), channel_id=1, source_target_pairs={{0,2},{1,3},{2,0},{3,1},{4,6},{5,7},{6,4},{7,5},{8,10},{9,11},{10,... | collective-permute-start | bytes 3145736 | tf_op jit(solution)/shard_map/ppermute | solution.py:517
  35.0 27.9 %collective-permute-start.11 = (bf16[256,2048]{1,0:T(8,128)(2,1)S(1)}, bf16[256,2048]{1,0:T(8,128)(2,1)S(1)}, u32[]{:S(2)}, u32[]{:S(2)}) collective-permute-start(bf16[256,2048]{1,0:T(8,128)(2,1)S(1)} %get-tuple-element.304), channel_id=1, source_target_pairs={{0,4},{1,5},{2,6},{3,7},{4,0},{5,1},{6,2},{7,3},{8,12},{9,13},{10,... | collective-permute-start | bytes 3145736 | tf_op jit(solution)/shard_map/ppermute | solution.py:517
  36.3 47.2 %collective-permute-start.8 = (bf16[256,2048]{1,0:T(8,128)(2,1)S(1)}, bf16[256,2048]{1,0:T(8,128)(2,1)S(1)}, u32[]{:S(2)}, u32[]{:S(2)}) collective-permute-start(bf16[256,2048]{1,0:T(8,128)(2,1)S(1)} %get-tuple-element.306), channel_id=1, source_target_pairs={{0,4},{1,5},{2,6},{3,7},{4,0},{5,1},{6,2},{7,3},{8,12},{9,13},{10,... | collective-permute-start | bytes 3145736 | tf_op jit(solution)/shard_map/ppermute | solution.py:517
  58.7 46.2 %collective-permute-start.9 = (bf16[256,2048]{1,0:T(8,128)(2,1)S(1)}, bf16[256,2048]{1,0:T(8,128)(2,1)S(1)}, u32[]{:S(2)}, u32[]{:S(2)}) collective-permute-start(bf16[256,2048]{1,0:T(8,128)(2,1)S(1)} %collective-permute-done.7), channel_id=1, source_target_pairs={{0,4},{1,5},{2,6},{3,7},{4,0},{5,1},{6,2},{7,3},{8,12},{9,13},{10,... | collective-permute-start | bytes 3145736 | tf_op jit(solution)/shard_map/ppermute | solution.py:517
  60.3 46.7 %collective-permute-start.10 = (bf16[256,2048]{1,0:T(8,128)(2,1)S(1)}, bf16[256,2048]{1,0:T(8,128)(2,1)S(1)}, u32[]{:S(2)}, u32[]{:S(2)}) collective-permute-start(bf16[256,2048]{1,0:T(8,128)(2,1)S(1)} %get-tuple-element.304), channel_id=1, source_target_pairs={{0,2},{1,3},{2,0},{3,1},{4,6},{5,7},{6,4},{7,5},{8,10},{9,11},{10,... | collective-permute-start | bytes 3145736 | tf_op jit(solution)/shard_map/ppermute | solution.py:517
  62.9 46.3 %collective-permute-start.12 = (bf16[256,2048]{1,0:T(8,128)(2,1)S(1)}, bf16[256,2048]{1,0:T(8,128)(2,1)S(1)}, u32[]{:S(2)}, u32[]{:S(2)}) collective-permute-start(bf16[256,2048]{1,0:T(8,128)(2,1)S(1)} %collective-permute-done.11), channel_id=1, source_target_pairs={{0,2},{1,3},{2,0},{3,1},{4,6},{5,7},{6,4},{7,5},{8,10},{9,11},{10,... | collective-permute-start | bytes 3145736 | tf_op jit(solution)/shard_map/ppermute | solution.py:517
  110.2 22.9 %collective-permute-start.13 = (bf16[2048,2048]{1,0:T(8,128)(2,1)}, bf16[2048,2048]{1,0:T(8,128)(2,1)}, u32[]{:S(2)}, u32[]{:S(2)}) collective-permute-start(bf16[2048,2048]{1,0:T(8,128)(2,1)} %constant_dynamic-update-slice_fusion.3), channel_id=1, source_target_pairs={{0,1},{1,0},{2,3},{3,2},{4,5},{5,4},{6,7},{7,6},{8,9},{9,8},{10,11... | collective-permute-start | bytes 25165832 | tf_op jit(solution)/shard_map/ppermute | solution.py:517
  145.8 37.1 %collective-permute-start.14 = (bf16[256,2048]{1,0:T(8,128)(2,1)}, bf16[256,2048]{1,0:T(8,128)(2,1)}, u32[]{:S(2)}, u32[]{:S(2)}) collective-permute-start(bf16[256,2048]{1,0:T(8,128)(2,1)} %get-tuple-element.147), channel_id=1, source_target_pairs={{0,2},{1,3},{2,0},{3,1},{4,6},{5,7},{6,4},{7,5},{8,10},{9,11},{10,... | collective-permute-start | bytes 3145736 | tf_op jit(solution)/shard_map/ppermute | solution.py:517
  147.1 35.9 %collective-permute-start.15 = (bf16[256,2048]{1,0:T(8,128)(2,1)S(1)}, bf16[256,2048]{1,0:T(8,128)(2,1)}, u32[]{:S(2)}, u32[]{:S(2)}) collective-permute-start(bf16[256,2048]{1,0:T(8,128)(2,1)S(1)} %get-tuple-element.151), channel_id=1, source_target_pairs={{0,4},{1,5},{2,6},{3,7},{4,0},{5,1},{6,2},{7,3},{8,12},{9,13},{10,... | collective-permute-start | bytes 3145736 | tf_op jit(solution)/shard_map/ppermute | solution.py:517
  184.3 18.9 %all-to-all-start = ((bf16[8,256,256]{2,1,0:T(8,128)(2,1)}), bf16[8,256,256]{2,1,0:T(8,128)(2,1)S(1)}, u32[]{:S(2)}, u32[]{:S(2)}) async-start(bf16[8,256,256]{2,1,0:T(8,128)(2,1)} %bitcast.212), calls=%async_computation | async-start | bytes 2097152 | tf_op jit(solution)/shard_map/all_to_all | solution.py:646
  203.2 30.6 %all-to-all-start.2 = ((bf16[8,64,1024]{2,1,0:T(8,128)(2,1)}), bf16[8,64,1024]{2,1,0:T(8,128)(2,1)}, u32[]{:S(2)}, u32[]{:S(2)}) async-start(bf16[8,64,1024]{2,1,0:T(8,128)(2,1)} %reshape.392), calls=%async_computation.2 | async-start | bytes 2097152 | tf_op jit(solution)/shard_map/all_to_all | solution.py:632
  233.8 19.9 %all-to-all-start.1 = ((bf16[8,256,256]{2,1,0:T(8,128)(2,1)}), bf16[8,256,256]{2,1,0:T(8,128)(2,1)S(1)}, u32[]{:S(2)}, u32[]{:S(2)}) async-start(bf16[8,256,256]{2,1,0:T(8,128)(2,1)} %bitcast.213), calls=%async_computation.1 | async-start | bytes 2097152 | tf_op jit(solution)/shard_map/all_to_all | solution.py:646
  237.8 187.5 %all-gather.11.cloned.1.call-start = ((), (), s32[]{:S(2)}) async-start(), calls=%async_computation.15 | async-start | bytes 5242880 | tf_op jit(solution)/shard_map/all_gather | solution.py:648
  237.8 44.5 %collective-permute-start.16 = (bf16[256,2048]{1,0:T(8,128)(2,1)}, bf16[256,2048]{1,0:T(8,128)(2,1)}, u32[]{:S(2)}, u32[]{:S(2)}) collective-permute-start(bf16[256,2048]{1,0:T(8,128)(2,1)} %get-tuple-element.147), channel_id=1, source_target_pairs={{0,4},{1,5},{2,6},{3,7},{4,0},{5,1},{6,2},{7,3},{8,12},{9,13},{10,... | collective-permute-start | bytes 3145736 | tf_op jit(solution)/shard_map/ppermute | solution.py:517
  239.8 57.5 %collective-permute-start.17 = (bf16[256,2048]{1,0:T(8,128)(2,1)}, bf16[256,2048]{1,0:T(8,128)(2,1)}, u32[]{:S(2)}, u32[]{:S(2)}) collective-permute-start(bf16[256,2048]{1,0:T(8,128)(2,1)} %collective-permute-done.14), channel_id=1, source_target_pairs={{0,4},{1,5},{2,6},{3,7},{4,0},{5,1},{6,2},{7,3},{8,12},{9,13},{10,... | collective-permute-start | bytes 3145736 | tf_op jit(solution)/shard_map/ppermute | solution.py:517
  239.9 57.4 %collective-permute-start.18 = (bf16[256,2048]{1,0:T(8,128)(2,1)}, bf16[256,2048]{1,0:T(8,128)(2,1)}, u32[]{:S(2)}, u32[]{:S(2)}) collective-permute-start(bf16[256,2048]{1,0:T(8,128)(2,1)} %copy-done.12), channel_id=1, source_target_pairs={{0,2},{1,3},{2,0},{3,1},{4,6},{5,7},{6,4},{7,5},{8,10},{9,11},{10,... | collective-permute-start | bytes 3145736 | tf_op jit(solution)/shard_map/ppermute | solution.py:517
  241.8 55.5 %collective-permute-start.19 = (bf16[256,2048]{1,0:T(8,128)(2,1)}, bf16[256,2048]{1,0:T(8,128)(2,1)}, u32[]{:S(2)}, u32[]{:S(2)}) collective-permute-start(bf16[256,2048]{1,0:T(8,128)(2,1)} %collective-permute-done.15), channel_id=1, source_target_pairs={{0,2},{1,3},{2,0},{3,1},{4,6},{5,7},{6,4},{7,5},{8,10},{9,11},{10,... | collective-permute-start | bytes 3145736 | tf_op jit(solution)/shard_map/ppermute | solution.py:517
  315.0 30.8 %collective-permute-start.26 = (bf16[2048,2048]{1,0:T(8,128)(2,1)}, bf16[2048,2048]{1,0:T(8,128)(2,1)}, u32[]{:S(2)}, u32[]{:S(2)}) collective-permute-start(bf16[2048,2048]{1,0:T(8,128)(2,1)} %constant_dynamic-update-slice_fusion.11), channel_id=1, source_target_pairs={{0,1},{1,0},{2,3},{3,2},{4,5},{5,4},{6,7},{7,6},{8,9},{9,8},{10,11... | collective-permute-start | bytes 25165832 | tf_op jit(solution)/shard_map/ppermute | solution.py:517
  315.0 25.7 %collective-permute-start.20 = (bf16[256,2048]{1,0:T(8,128)(2,1)S(1)}, bf16[256,2048]{1,0:T(8,128)(2,1)}, u32[]{:S(2)}, u32[]{:S(2)}) collective-permute-start(bf16[256,2048]{1,0:T(8,128)(2,1)S(1)} %copy-done.21), channel_id=1, source_target_pairs={{0,2},{1,3},{2,0},{3,1},{4,6},{5,7},{6,4},{7,5},{8,10},{9,11},{10,... | collective-permute-start | bytes 3145736 | tf_op jit(solution)/shard_map/ppermute | solution.py:517
  316.4 25.3 %collective-permute-start.21 = (bf16[256,2048]{1,0:T(8,128)(2,1)S(1)}, bf16[256,2048]{1,0:T(8,128)(2,1)}, u32[]{:S(2)}, u32[]{:S(2)}) collective-permute-start(bf16[256,2048]{1,0:T(8,128)(2,1)S(1)} %copy-done.20), channel_id=1, source_target_pairs={{0,4},{1,5},{2,6},{3,7},{4,0},{5,1},{6,2},{7,3},{8,12},{9,13},{10,... | collective-permute-start | bytes 3145736 | tf_op jit(solution)/shard_map/ppermute | solution.py:517
  332.5 320.8 %reduce-scatter.8.cloned.1.call-start = ((), (), s32[]{:S(2)}) async-start(), calls=%async_computation.16 | async-start | bytes 5242880 | tf_op jit(solution)/shard_map/reduce_scatter | solution.py:704
  341.7 26.1 %collective-permute-start.22 = (bf16[256,2048]{1,0:T(8,128)(2,1)S(1)}, bf16[256,2048]{1,0:T(8,128)(2,1)S(1)}, u32[]{:S(2)}, u32[]{:S(2)}) collective-permute-start(bf16[256,2048]{1,0:T(8,128)(2,1)S(1)} %copy-done.21), channel_id=1, source_target_pairs={{0,4},{1,5},{2,6},{3,7},{4,0},{5,1},{6,2},{7,3},{8,12},{9,13},{10,... | collective-permute-start | bytes 3145736 | tf_op jit(solution)/shard_map/ppermute | solution.py:517
  342.4 46.2 %collective-permute-start.23 = (bf16[256,2048]{1,0:T(8,128)(2,1)}, bf16[256,2048]{1,0:T(8,128)(2,1)S(1)}, u32[]{:S(2)}, u32[]{:S(2)}) collective-permute-start(bf16[256,2048]{1,0:T(8,128)(2,1)} %collective-permute-done.20), channel_id=1, source_target_pairs={{0,4},{1,5},{2,6},{3,7},{4,0},{5,1},{6,2},{7,3},{8,12},{9,13},{10,... | collective-permute-start | bytes 3145736 | tf_op jit(solution)/shard_map/ppermute | solution.py:517
  343.8 44.8 %collective-permute-start.24 = (bf16[256,2048]{1,0:T(8,128)(2,1)S(1)}, bf16[256,2048]{1,0:T(8,128)(2,1)S(1)}, u32[]{:S(2)}, u32[]{:S(2)}) collective-permute-start(bf16[256,2048]{1,0:T(8,128)(2,1)S(1)} %copy-done.20), channel_id=1, source_target_pairs={{0,2},{1,3},{2,0},{3,1},{4,6},{5,7},{6,4},{7,5},{8,10},{9,11},{10,... | collective-permute-start | bytes 3145736 | tf_op jit(solution)/shard_map/ppermute | solution.py:517
  344.4 45.7 %collective-permute-start.25 = (bf16[256,2048]{1,0:T(8,128)(2,1)}, bf16[256,2048]{1,0:T(8,128)(2,1)S(1)}, u32[]{:S(2)}, u32[]{:S(2)}) collective-permute-start(bf16[256,2048]{1,0:T(8,128)(2,1)} %collective-permute-done.21), channel_id=1, source_target_pairs={{0,2},{1,3},{2,0},{3,1},{4,6},{5,7},{6,4},{7,5},{8,10},{9,11},{10,... | collective-permute-start | bytes 3145736 | tf_op jit(solution)/shard_map/ppermute | solution.py:517
  401.1 40.6 %collective-permute-start.27 = (bf16[2048,2048]{1,0:T(8,128)(2,1)}, bf16[2048,2048]{1,0:T(8,128)(2,1)}, u32[]{:S(2)}, u32[]{:S(2)}) collective-permute-start(bf16[2048,2048]{1,0:T(8,128)(2,1)} %constant_dynamic-update-slice_fusion.19), channel_id=1, source_target_pairs={{0,1},{1,0},{2,3},{3,2},{4,5},{5,4},{6,7},{7,6},{8,9},{9,8},{10,11... | collective-permute-start | bytes 25165832 | tf_op jit(solution)/shard_map/ppermute | solution.py:517
  563.6 197.2 %reduce-scatter.10.cloned.1.call-start = ((), (), s32[]{:S(2)}) async-start(), calls=%async_computation.17 | async-start | bytes 5242880 | tf_op jit(solution)/shard_map/reduce_scatter | solution.py:708
  563.7 89.7 %copy-start.6 = (bf16[2,256,2048]{2,1,0:T(8,128)(2,1)S(1)}, bf16[2,256,2048]{2,1,0:T(8,128)(2,1)}, u32[]{:S(2)}) copy-start(bf16[2,256,2048]{2,1,0:T(8,128)(2,1)} %param.29) | copy-start | bytes 6291460
  770.7 21.7 %all-to-all-start.4 = ((bf16[8,256,256]{2,1,0:T(8,128)(2,1)}), bf16[8,256,256]{2,1,0:T(8,128)(2,1)S(1)}, u32[]{:S(2)}, u32[]{:S(2)}) async-start(bf16[8,256,256]{2,1,0:T(8,128)(2,1)} %get-tuple-element.194), calls=%async_computation.6 | async-start | bytes 2097152 | tf_op jit(solution)/shard_map/all_to_all | solution.py:715
  774.3 106.5 %reduce-scatter.12.cloned.1.call-start = ((), (), s32[]{:S(2)}) async-start(), calls=%async_computation.18 | async-start | bytes 9437184 | tf_op jit(solution)/shard_map/reduce_scatter | solution.py:719
  813.3 67.4 %all-to-all-start.5 = ((bf16[8,64,1024]{2,1,0:T(8,128)(2,1)}), bf16[8,64,1024]{2,1,0:T(8,128)(2,1)S(1)}, u32[]{:S(2)}, u32[]{:S(2)}) async-start(bf16[8,64,1024]{2,1,0:T(8,128)(2,1)} %bitcast.49), calls=%async_computation.8 | async-start | bytes 2097152 | tf_op jit(solution)/shard_map/all_to_all | solution.py:720
  816.9 109.0 %reduce-scatter.16.cloned.1.call-start = ((), (), s32[]{:S(2)}) async-start(), calls=%async_computation.20 | async-start | bytes 1310720
  880.8 150.1 %reduce-scatter.14.cloned.1.call-start = ((), (), s32[]{:S(2)}) async-start(), calls=%async_computation.19 | async-start | bytes 3932160 | tf_op jit(solution)/shard_map/reduce_scatter | solution.py:730
  944.6 90.0 %copy-start.1 = (bf16[2,256,2048]{2,1,0:T(8,128)(2,1)S(1)}, bf16[2,256,2048]{2,1,0:T(8,128)(2,1)}, u32[]{:S(2)}) copy-start(bf16[2,256,2048]{2,1,0:T(8,128)(2,1)} %param.17) | copy-start | bytes 6291460
  944.6 90.0 %copy-start.29 = (f32[1,2,2,128]{3,1,2,0:T(2,128)S(1)}, f32[1,2,2,128]{3,1,2,0:T(2,128)}, u32[]{:S(2)}) copy-start(f32[1,2,2,128]{3,1,2,0:T(2,128)} %copy-done.28) | copy-start | bytes 6148
  944.6 90.0 %copy-start.31 = (f32[1,2,2,128]{3,1,2,0:T(2,128)S(1)}, f32[1,2,2,128]{3,1,2,0:T(2,128)}, u32[]{:S(2)}) copy-start(f32[1,2,2,128]{3,1,2,0:T(2,128)} %copy-done.30) | copy-start | bytes 6148
  1031.0 16.1 %all-to-all-start.6 = ((bf16[8,64,768]{2,1,0:T(8,128)(2,1)}), bf16[8,64,768]{2,1,0:T(8,128)(2,1)S(1)}, u32[]{:S(2)}, u32[]{:S(2)}) async-start(bf16[8,64,768]{2,1,0:T(8,128)(2,1)} %bitcast.221), calls=%async_computation.10 | async-start | bytes 1572864 | tf_op jit(solution)/shard_map/all_to_all | solution.py:734
  (42 other events, 769.7 us)
Sparse Core Ops, SparseCore 0:
  29.1 64.5 all-gather.4
  97.2 86.8 all-gather.6
  185.6 79.6 all-gather.8
  332.6 92.6 all-gather.10
  563.8 74.4 reduce-scatter.7
  653.5 73.9 reduce-scatter.9
  792.5 80.0 reduce-scatter.11
  881.0 44.9 reduce-scatter.15
  928.2 58.9 reduce-scatter.13

commit v3 on v2

--- a/solution.py
+++ b/solution.py
@@ -335,7 +335,7 @@
     dx1 = dy_ref[...].astype(f32) + hat_back(hat, rstd, db_ref[...])
     dx_ref[...] = dx1
     low_ref[...] = dx1.astype(bf16)
-    dc = jnp.dot(dx1.astype(bf16), w_ref[...], preferred_element_type=f32)
+    dc = times_rows(dx1.astype(bf16), w_ref[...])
     hat, rstd = hat_of(wide_row(o_ref))
     d_o = hat_back(hat, rstd, dc).astype(bf16)
     dim = do_ref.shape[2]
@@ -367,11 +367,15 @@
     return bits if row % 2 == 0 else bits[::-1]
 
 
-def product_sum_kernel(n, rows, cols, x0_ref, x1_ref, w_ref, o_ref, part_s, core_s, sum_s, got_s, send_sem, recv_sem):
+def times_rows(a, w):
+    return lax.dot_general(a, w, (((1,), (1,)), ((), ())), preferred_element_type=f32)
+
+
+def product_sum_kernel(n, rows, cols, turned, x0_ref, x1_ref, w_ref, o_ref, part_s, core_s, sum_s, got_s, send_sem, recv_sem):
     mine = lax.axis_index("ctx")
     spots = n // 2
     size = x0_ref.shape[0] // (rows * spots)
-    width = w_ref.shape[1]
+    width = o_ref.shape[1]
     barrier = pltpu.get_barrier_semaphore()
     bits = [1] + ways(0, n)
     for bit in bits:
@@ -404,7 +408,8 @@
         @pl.loop(0, width // cols)
         def _(c):
             at = pl.ds(pl.multiple_of(c * cols, cols), cols)
-            finish(at, jnp.dot(x_ref[pl.ds(begin, size), :], w_ref[:, at], preferred_element_type=f32))
+            x = x_ref[pl.ds(begin, size), :]
+            finish(at, times_rows(x, w_ref[at, :]) if turned else jnp.dot(x, w_ref[:, at], preferred_element_type=f32))
 
     def pair(r, k):
         spot = r * spots + k
@@ -456,15 +461,15 @@
         copy.wait_send()
 
 
-def product_sum(x0, x1, w, rows, n, collective_id):
+def product_sum(x0, x1, w, rows, n, collective_id, turned=False):
     size = x0.shape[0] // (rows * (n // 2))
-    width = w.shape[1]
+    width = w.shape[0 if turned else 1]
     count = rows * (n // 2)
     moves = count + rows * (n // 2 - 1)
     vmem = pl.BlockSpec(memory_space=pltpu.VMEM)
     flops = 4 * x0.shape[0] * x0.shape[1] * width
     return pl.pallas_call(
-        functools.partial(product_sum_kernel, n, rows, min(512, width)),
+        functools.partial(product_sum_kernel, n, rows, min(512, width), turned),
         out_shape=jax.ShapeDtypeStruct((rows * size, width), f32),
         in_specs=[vmem] * 3, out_specs=vmem,
         scratch_shapes=[pltpu.VMEM((count, size, width), bf16), pltpu.VMEM((count, size, width), bf16),
@@ -474,6 +479,158 @@
         name="product_sum",
         cost_estimate=pl.CostEstimate(flops=4 * flops, bytes_accessed=20 * 2**20, transcendentals=0),
     )(x0, x1, w)
+
+
+def gather_product_kernel(n, rows, cols, b_ref, dy0_ref, dy1_ref, up_ref, down_ref, b0_ref, b1_ref, h0_ref, h1_ref, d0_ref, d1_ref,
+                          stat_ref, got_s, d_s, h_s, dy_s, send_sem, recv_sem, dy_sem, b_sem, h_sem, d_sem):
+    mine = lax.axis_index("ctx")
+    spots = n // 2
+    size = b_ref.shape[0] // rows
+    ff = up_ref.shape[1]
+    count = rows * spots
+    barrier = pltpu.get_barrier_semaphore()
+    bits = [1] + ways(0, n)
+    for bit in bits:
+        pl.semaphore_signal(barrier, inc=1, device_id={"ctx": mine ^ bit}, device_id_type=pl.DeviceIdType.MESH)
+    pl.semaphore_wait(barrier, len(bits))
+    sends, locals_, arrival = [], [], {}
+
+    def send(src, half, row, k, bit):
+        at, to = len(sends), half * count + row * spots + k
+        copy = pltpu.make_async_remote_copy(
+            src_ref=src, dst_ref=got_s.at[to], send_sem=send_sem.at[at], recv_sem=recv_sem.at[at],
+            device_id={"ctx": mine ^ bit}, device_id_type=pl.DeviceIdType.MESH)
+        copy.start()
+        sends.append(copy)
+        arrival[half, row, k] = copy
+
+    def held(half, row, k):
+        if half == 0 and k == 0:
+            return b_ref.at[pl.ds(row * size, size), :]
+        return got_s.at[half * count + row * spots + k]
+
+    def onward(row, k):
+        way = ways(row, n)
+        top = max([s for s, bit in enumerate(way) if k & (bit >> 1)], default=-1)
+        for bit in way[top + 1:]:
+            send(held(0, row, k), 0, row, k | (bit >> 1), bit)
+        send(held(0, row, k), 1, row, k, 1)
+
+    for r in range(rows):
+        onward(r, 0)
+
+    def fetch(t, slot):
+        begin = pl.multiple_of(lax.rem(t, count) * size, size)
+
+        @pl.when(t < count)
+        def _():
+            pltpu.make_async_copy(dy0_ref.at[pl.ds(begin, size), :], dy_s.at[slot], dy_sem.at[slot]).start()
+
+        @pl.when(t >= count)
+        def _():
+            pltpu.make_async_copy(dy1_ref.at[pl.ds(begin, size), :], dy_s.at[slot], dy_sem.at[slot]).start()
+
+    fetch(0, 0)
+
+    @pl.loop(0, 2 * count)
+    def _(t):
+        slot = lax.rem(t, 2)
+
+        @pl.when(t + 1 < 2 * count)
+        def _():
+            fetch(t + 1, 1 - slot)
+
+        pltpu.make_async_copy(dy0_ref.at[pl.ds(0, size), :], dy_s.at[slot], dy_sem.at[slot]).wait()
+
+        @pl.loop(0, ff // cols)
+        def _(c):
+            at = pl.ds(pl.multiple_of(c * cols, cols), cols)
+            d_s[t, :, at] = times_rows(dy_s[slot], down_ref[at, :])
+
+    for t in range(2 * count):
+        dst = (d0_ref, d1_ref)[t // count].at[pl.ds((t % count) * size, size), :]
+        copy = pltpu.make_async_copy(d_s.at[t], dst, d_sem.at[t])
+        copy.start()
+        locals_.append(copy)
+
+    outs = []
+    lane = lax.broadcasted_iota(jnp.int32, (32, 128), 1)
+
+    def block(half, row, k):
+        t = half * count + row * spots + k
+        src = held(half, row, k)
+        copy = pltpu.make_async_copy(src, (b0_ref, b1_ref)[half].at[pl.ds((t % count) * size, size), :], b_sem.at[t])
+        copy.start()
+        locals_.append(copy)
+        slot = len(outs) % 2
+        if len(outs) >= 2:
+            outs[-2].wait()
+
+        @pl.loop(0, ff // cols)
+        def _(c):
+            at = pl.ds(pl.multiple_of(c * cols, cols), cols)
+            h_s[slot, :, at] = jnp.dot(src[...], up_ref[:, at], preferred_element_type=f32)
+
+        copy = pltpu.make_async_copy(h_s.at[slot], (h0_ref, h1_ref)[half].at[pl.ds((t % count) * size, size), :], h_sem.at[t])
+        copy.start()
+        outs.append(copy)
+
+        @pl.loop(0, size // 32)
+        def _(c):
+            at = pl.ds(pl.multiple_of(c * 32, 32), 32)
+            h = h_s[slot, at, :]
+            gel = h * (0.5 * (1.0 + lax.erf(h * (2.0**-0.5))))
+            d = d_s[t, at, :]
+            mean = jnp.mean(gel, axis=-1, keepdims=True)
+            off = gel - mean
+            spread = jnp.sum(off * off, axis=-1, keepdims=True)
+            total = jnp.sum(d, axis=-1, keepdims=True)
+            cross = jnp.sum(d * off, axis=-1, keepdims=True)
+            line = jnp.where(lane == 0, mean, jnp.where(lane == 1, spread, jnp.where(lane == 2, total, cross)))
+            stat_ref[pl.ds(pl.multiple_of(t * size + c * 32, 32), 32), :] = line
+
+    order = []
+    for k in range(spots):
+        for r in range(rows):
+            way = ways(r, n)
+            order.append((r, sum((bit >> 1) for s, bit in enumerate(way) if k >> s & 1)))
+    for begin in range(0, len(order), rows):
+        some = order[begin:begin + rows]
+        for r, k in some:
+            if k:
+                arrival[0, r, k].wait_recv()
+                onward(r, k)
+        for r, k in some:
+            block(0, r, k)
+        for r, k in some:
+            arrival[1, r, k].wait_recv()
+            block(1, r, k)
+    for copy in outs[-2:] + locals_:
+        copy.wait()
+    for copy in sends:
+        copy.wait_send()
+
+
+def gather_product(b, dy0, dy1, up, down, rows, n, collective_id):
+    size = b.shape[0] // rows
+    width, ff = up.shape
+    count = rows * (n // 2)
+    half = count * size
+    moves = rows * (n - 1)
+    vmem, here = pl.BlockSpec(memory_space=pltpu.VMEM), pl.BlockSpec(memory_space=pl.ANY)
+    sds = jax.ShapeDtypeStruct
+    return pl.pallas_call(
+        functools.partial(gather_product_kernel, n, rows, min(256, ff)),
+        out_shape=(sds((half, width), bf16),) * 2 + (sds((half, ff), f32),) * 4 + (sds((2 * half, 128), f32),),
+        in_specs=[vmem, here, here, vmem, vmem], out_specs=(here,) * 6 + (vmem,),
+        scratch_shapes=[pltpu.VMEM((2 * count, size, width), bf16), pltpu.VMEM((2 * count, size, ff), f32),
+                        pltpu.VMEM((2, size, ff), f32), pltpu.VMEM((2, size, width), bf16),
+                        pltpu.SemaphoreType.DMA((moves,)), pltpu.SemaphoreType.DMA((moves,)), pltpu.SemaphoreType.DMA((2,))]
+        + [pltpu.SemaphoreType.DMA((2 * count,))] * 3,
+        compiler_params=pltpu.CompilerParams(collective_id=collective_id, has_side_effects=True, vmem_limit_bytes=62 * 2**20),
+        name="gather_product",
+        cost_estimate=pl.CostEstimate(flops=16 * half * width * ff, bytes_accessed=70 * 2**20, transcendentals=0),
+    )(b, dy0, dy1, up, down)
 
 
 def standardize(values):
@@ -650,29 +807,9 @@
     b_low, dy_held = lax.optimization_barrier((b_low, dy_held))
     dy0 = gather_end(dy_held)
     dy1 = swap(dy0, 1)
-    b_held = gather_step([{0: v} for v in b_low], 0)
-    d_hat0 = dot(dy0, down_all, "td,fd->tf")
-    b_held, d_hat0 = lax.optimization_barrier((b_held, d_hat0))
-    for step in range(1, gather_steps()):
-        b_held = gather_step(b_held, step)
-    d_hat1 = dot(dy1, down_all, "td,fd->tf")
-    b_held, d_hat1 = lax.optimization_barrier((b_held, d_hat1))
-    b0 = gather_end(b_held)
-    b1 = swap(b0, 1)
-
-    def activate(b):
-        h = dot(b, up_all, "td,df->tf")
-        return h, 0.5 * (1.0 + lax.erf(h * (2.0**-0.5)))
-
-    def own_stats(h, cdf, d_hat):
-        gel = h * cdf
-        mean = jnp.mean(gel, axis=-1)
-        off = gel - mean[:, None]
-        return jnp.stack([mean, jnp.sum(off * off, axis=-1), jnp.sum(d_hat, axis=-1), jnp.sum(d_hat * off, axis=-1)])
-
-    h0, cdf0 = activate(b0)
-    h1, cdf1 = activate(b1)
-    stats = jnp.stack([own_stats(h0, cdf0, d_hat0), own_stats(h1, cdf1, d_hat1)], axis=1)
+
+    b0, b1, h0, h1, d_hat0, d_hat1, stats = gather_product(jnp.concatenate(b_low), dy0, dy1, up_all, down_all, rows, n, 4)
+    stats = stats[:, :4].T
     order = jnp.arange(n // 2, dtype=jnp.int32) ^ place
     halves = jnp.arange(2, dtype=jnp.int32) ^ core
 
@@ -680,7 +817,7 @@
         v = v.reshape(v.shape[0], 2, rows, n // 2, local_len)
         return jnp.take(jnp.take(v, halves, axis=1), order, axis=3).reshape(v.shape[0], 2 * half)
 
-    stats = lax.all_gather(reorder(stats.reshape(4, 2 * half)), "ctx", axis=0, tiled=False)
+    stats = lax.all_gather(reorder(stats), "ctx", axis=0, tiled=False)
     mean = jnp.mean(stats[:, 0], axis=0)
     shift = stats[:, 0] - mean
     var = (jnp.sum(stats[:, 1], axis=0) + ff_dev * jnp.sum(shift * shift, axis=0)) / ff
@@ -689,20 +826,21 @@
     d_corr = rstd * jnp.sum(stats[:, 3] + stats[:, 2] * shift, axis=0) / ff
     merged = reorder(jnp.stack([mean, rstd, d_mean, d_corr])).reshape(4, 2, half, 1)
 
-    def finish(h, cdf, d_hat, which):
+    def finish(h, d_hat, which):
+        cdf = 0.5 * (1.0 + lax.erf(h * (2.0**-0.5)))
         mean, rstd, d_mean, d_corr = (merged[k, which] for k in range(4))
         hat = (h * cdf - mean) * rstd
         d_gel = rstd * (d_hat - d_mean - hat * d_corr)
         pdf = jnp.exp(-0.5 * h * h) * 0.3989422804014327
         return hat.astype(bf16), (d_gel * (cdf + h * pdf)).astype(bf16)
 
-    e0, dh0 = finish(h0, cdf0, d_hat0, 0)
-    e1, dh1 = finish(h1, cdf1, d_hat1, 1)
+    e0, dh0 = finish(h0, d_hat0, 0)
+    e1, dh1 = finish(h1, d_hat1, 1)
     down_part = (dot(e0, dy0, "tf,td->fd") + dot(e1, dy1, "tf,td->fd")).astype(bf16)
     up_part = (dot(b0, dh0, "td,tf->df") + dot(b1, dh1, "td,tf->df")).astype(bf16)
     e0, e1, dh0, dh1, down_part, up_part = lax.optimization_barrier((e0, e1, dh0, dh1, down_part, up_part))
     down_sum = lax.psum_scatter(down_part, "row", scatter_dimension=0, tiled=True)
-    db = product_sum(dh0, dh1, up_all.T, rows, n, 1)
+    db = product_sum(dh0, dh1, up_all, rows, n, 1, True)
     e0, e1, db, up_part, down_sum = lax.optimization_barrier((e0, e1, db, up_part, down_sum))
     down_raw = down_sum.astype(f32)
     up_sum = lax.psum_scatter(up_part, "row", scatter_dimension=0, tiled=True)
@@ -710,8 +848,7 @@
     db, ffn, up_sum = lax.optimization_barrier((db, ffn, up_sum))
     output = (jnp.stack(x1) + ffn.reshape(rows, local_len, width)).astype(bf16)
 
-    out_allT = out_all.T
-    dx1, dx1b, d_o = zip(*[middle_backward(r, o[r], x1[r], db, out_cotangent[r], out_allT) for r in range(rows)])
+    dx1, dx1b, d_o = zip(*[middle_backward(r, o[r], x1[r], db, out_cotangent[r], out_all) for r in range(rows)])
     do_heads = [lax.all_to_all(v, "ctx", split_axis=0, concat_axis=0, tiled=True).reshape(row_len, heads_dim) for v in d_o]
     c_order = jnp.concatenate(c).reshape(tokens, m, n, piece).transpose(0, 2, 1, 3).reshape(tokens, width)
     out_part = dot(c_order, jnp.concatenate(dx1b), "td,te->de", bf16)
@@ -728,7 +865,7 @@
     d0, d1, qkv_part, out_sum = lax.optimization_barrier((d0, d1, qkv_part, out_sum))
     out_raw = out_sum.astype(f32)
     qkv_part = lax.psum_scatter(qkv_part, "row", scatter_dimension=0, tiled=True)
-    da = product_sum(d0, d1, w_qkv.T, rows, n, 2)
+    da = product_sum(d0, d1, w_qkv, rows, n, 2, True)
     da, qkv_part = lax.optimization_barrier((da, qkv_part))
     up_raw = up_moved.reshape(piece, n, m, unit).transpose(0, 2, 1, 3).reshape(piece, ff).astype(f32)
     qkv_raw = lax.all_to_all(qkv_part.reshape(n, piece, 3 * heads_dim), "ctx", split_axis=0, concat_axis=2, tiled=True)

time: 1060 us -> 1080 us (1.019)
  Pallas kernels: 409 us -> 528 us
  matrix products: 167 us -> 112 us
  other arithmetic: 80.2 us -> 54.7 us
  local copies, waits for them, and re-layouts: 94 us -> 69.1 us
  starting transfers between devices: 59.8 us -> 44.7 us
  waiting for transfers between devices: 212 us -> 223 us
    pallas_call x0 -> x1, Pallas kernels: none -> 96.4 us  [gather_product(): pl.pallas_call(functools.partial(gather_product_kernel, n, rows, min(256,...]
    dot_general x13 -> x9, matrix products: 167 us -> 112 us  [dot(): return jnp.einsum(spec, a, b, preferred_element_type=f32).astype(kind)]
    all_gather x1, waiting for transfers between devices: 24.1 us -> 77.6 us  [body(): up_all = lax.all_gather(up_part, 'row', axis=0, tiled=True)]
    ppermute x28 -> x21, waiting for transfers between devices: 127 us -> 98.8 us  [swap(): return lax.ppermute(x, 'ctx', [(i, i ^ bit) for i in range(n)])]
    unnamed x10 -> x9, waiting for transfers between devices: 23.3 us -> 0.15 us
    optimization_barrier x4 -> x0, local copies, waits for them, and re-layouts: 16.9 us -> none  [the longest x1 12.5 us: body(): lax.optimization_barrier((o_row, kept, qkv0, qkv1, dy_held, out_all))]
    reduce_scatter x0 -> x1, waiting for transfers between devices: none -> 13.3 us  [body(): out_sum = lax.psum_scatter(out_part, 'row', scatter_dimension=0, tiled=True)]
    reduce_sum x1 -> x0, other arithmetic: 13 us -> none  [own_stats(): jnp.sum(off * off, axis=-1)]
  transfers between devices with their start and end apart: 43 -> 36, of which waited for: 19 -> 14; matrix products, arithmetic and copies ran while one was open for 18% -> 11% of each run, Pallas kernels for 37% -> 39%
where the time goes in v3:
time: 1080 us
  Pallas kernels  528 us (49%)
  waiting for transfers between devices  223 us (21%)
  matrix products  112 us (10%)
  local copies, waits for them, and re-layouts  69.1 us (6%)
  other arithmetic  54.7 us (5%)
  starting transfers between devices  44.7 us (4%)
  blocking collectives  28.7 us (3%)
  between operations  15.6 us (1%)
    pallas_call x3, Pallas kernels, product_sum(): pl.pallas_call(functools.partial(product_sum_kernel, n, rows, min(512, wi...  265 us
    dot_general x9, matrix products, dot(): return jnp.einsum(spec, a, b, preferred_element_type=f32).astype(kind)  112 us
    ppermute x21, waiting for transfers between devices, swap(): return lax.ppermute(x, 'ctx', [(i, i ^ bit) for i in range(n)])  98.8 us
    pallas_call x1, Pallas kernels, gather_product(): pl.pallas_call(functools.partial(gather_product_kernel, n, rows, min(256,...  96.4 us
    all_gather x1, waiting for transfers between devices, body(): up_all = lax.all_gather(up_part, 'row', axis=0, tiled=True)  77.6 us
    pallas_call x2, Pallas kernels, attention_backward(): pl.pallas_call(call, out_shape=(whole, whole), grid_spec=pltpu.PrefetchSc...  73.7 us
    pallas_call x2, Pallas kernels, attention_forward(): pl.pallas_call(functools.partial(forward_kernel, nh, blk, unit), out_shap...  51.5 us
    unnamed x138, local copies, waits for them, and re-layouts  30 us
  transfers between devices with their start and end apart: 36, of which 14 were waited for; matrix products, arithmetic and copies ran while one was open for 11% of the time, Pallas kernels for 39%

profile of v3, /device:TPU:0, one launch (start us, length us, event | category | flops | bytes accessed | tf_op | source)
XLA Modules:
  0.0 1076.2 jit_solution(594534859131761586)
XLA Ops:
  20.1 5.9 collective-permute-done.4
  35.0 21.7 %collective-permute-done.7 = bf16[256,2048]{1,0:T(8,128)(2,1)S(1)} collective-permute-done((bf16[256,2048]{1,0:T(8,128)(2,1)S(1)}, bf16[256,2048]{1,0:T(8,128)(2,1)S(1)}, u32[]{:S(2)}, u32[]{:S(2)}) %collective-permute-start.7) | collective-permute-done | bytes 1048608 | tf_op jit(solution)/shard_map/ppermute | solution.py:674
  61.4 20.1 %collective-permute-done.8 = bf16[256,2048]{1,0:T(8,128)(2,1)S(1)} collective-permute-done((bf16[256,2048]{1,0:T(8,128)(2,1)S(1)}, bf16[256,2048]{1,0:T(8,128)(2,1)S(1)}, u32[]{:S(2)}, u32[]{:S(2)}) %collective-permute-start.8) | collective-permute-done | bytes 1048608 | tf_op jit(solution)/shard_map/ppermute | solution.py:674
  82.5 20.4 %collective-permute-done.9 = bf16[256,2048]{1,0:T(8,128)(2,1)S(1)} collective-permute-done((bf16[256,2048]{1,0:T(8,128)(2,1)S(1)}, bf16[256,2048]{1,0:T(8,128)(2,1)S(1)}, u32[]{:S(2)}, u32[]{:S(2)}) %collective-permute-start.9) | collective-permute-done | bytes 1048608 | tf_op jit(solution)/shard_map/ppermute | solution.py:674
  115.4 3.1 slice_bitcast_fusion
  118.5 13.0 %fusion.53.q0_ref.k0_ref.v0_ref = f32[768,2048]{1,0:T(8,128)} fusion(bf16[2048,768]{1,0:T(8,128)(2,1)} %all-gather.5.cloned.1.call-done.w_ref, bf16[2048,2048]{1,0:T(8,128)(2,1)} %constant_dynamic-update-slice_fusion.3), kind=kOutput, calls=%fused_computation.219 | convolution fusion | flops 6442450944 | bytes 17825792 | tf_op jit(solution)/shard_map/df,td->ft/dot_general | solution.py:669
  131.5 11.4 %fusion.54.q1_ref.k1_ref.v1_ref = f32[768,2048]{1,0:T(8,128)} fusion(bf16[2048,768]{1,0:T(8,128)(2,1)S(1)} %copy-done.44, bf16[2048,2048]{1,0:T(8,128)(2,1)} %collective-permute-done.13), kind=kOutput, calls=%fused_computation.220 | convolution fusion | flops 6442450944 | bytes 17825792 | tf_op jit(solution)/shard_map/df,td->ft/dot_general | solution.py:669
  146.6 22.7 %attention_forward.2 = (bf16[2048,256]{1,0:T(8,128)(2,1)}, f32[256,2048]{1,0:T(8,128)}, f32[4,2048]{1,0:T(4,128)}, bf16[256,2048]{1,0:T(8,128)(2,1)}, bf16[256,2...) custom-call(s32[10]{0:T(128)} %pad_add_fusion.4.span_ref, f32[768,2048]{1,0:T(8,128)} %fusion.53.q0_ref.k0_ref.v0_ref, ...), custom_call_target="tpu_custom_call" | custom-call | flops 8589934592 | bytes 10485760 | tf_op jit(solution)/shard_map/attention_forward/pallas_call | solution.py:234
  169.2 11.8 %collective-permute-done.14 = bf16[256,2048]{1,0:T(8,128)(2,1)} collective-permute-done((bf16[256,2048]{1,0:T(8,128)(2,1)}, bf16[256,2048]{1,0:T(8,128)(2,1)}, u32[]{:S(2)}, u32[]{:S(2)}) %collective-permute-start.14) | collective-permute-done | bytes 1048608 | tf_op jit(solution)/shard_map/ppermute | solution.py:674
  182.3 4.0 all-to-all-start
  192.0 9.6 all-to-all-done.o_ref
  201.6 4.3 all-to-all-start.2
  206.5 28.8 %attention_forward.3 = (bf16[2048,256]{1,0:T(8,128)(2,1)}, f32[256,2048]{1,0:T(8,128)}, f32[4,2048]{1,0:T(4,128)}, bf16[256,2048]{1,0:T(8,128)(2,1)}, bf16[256,2...) custom-call(s32[10]{0:T(128)} %pad_add_fusion.2.span_ref, f32[768,2048]{1,0:T(8,128)} %fusion.53.q0_ref.k0_ref.v0_ref, ...), custom_call_target="tpu_custom_call" | custom-call | flops 8589934592 | bytes 10485760 | tf_op jit(solution)/shard_map/attention_forward/pallas_call | solution.py:234
  235.3 4.1 all-to-all-start.1
  245.1 10.3 all-to-all-done.1.o_ref
  255.4 7.9 all-gather.9.cloned.1.call-done.down_ref.w_ref
  263.3 8.5 middle_forward.3
  271.8 8.4 middle_forward.2
  280.2 18.7 %collective-permute-done.17 = bf16[256,2048]{1,0:T(8,128)(2,1)} collective-permute-done((bf16[256,2048]{1,0:T(8,128)(2,1)}, bf16[256,2048]{1,0:T(8,128)(2,1)}, u32[]{:S(2)}, u32[]{:S(2)}) %collective-permute-start.17) | collective-permute-done | bytes 1048608 | tf_op jit(solution)/shard_map/ppermute | solution.py:674
  318.3 77.6 %all-gather.11.cloned.1.call-done.up_ref.w_ref = bf16[2048,1024]{1,0:T(8,128)(2,1)} async-done(((bf16[512,1024]{1,0:T(8,128)(2,1)}), bf16[2048,1024]{1,0:T(8,128)(2,1)}) %all-gather.11.cloned.1.call-update) | async-done | bytes 4194320 | tf_op jit(solution)/shard_map/all_gather | solution.py:805
  395.9 96.4 %gather_product.1 = (bf16[2048,2048]{1,0:T(8,128)(2,1)}, bf16[2048,2048]{1,0:T(8,128)(2,1)}, f32[2048,1024]{1,0:T(8,128)}, f32[2048,1024]{1,0:T(8,128)}, f32[204...) custom-call(bf16[512,2048]{1,0:T(8,128)(2,1)} %pad_maximum_fusion.1.b_ref, ...), custom_call_target="tpu_custom_call" | custom-call | flops 68719476736 | bytes 73400320 | tf_op jit(solution)/shard_map/gather_product/pallas_call | solution.py:622
  496.0 9.3 all_gather.19
  507.9 8.2 fusion.11
  516.2 16.4 %fusion.56 = f32[2048,1024]{1,0:T(8,128)} fusion(bf16[2048,2048]{1,0:T(8,128)(2,1)} %get-tuple-element.156, bf16[2048,1024]{1,0:T(8,128)(2,1)S(1)} %get-tuple-element.160.x1_ref), kind=kOutput, calls=%fused_computation.222 | convolution fusion | flops 8589934592 | bytes 20971520 | tf_op jit(solution)/shard_map/td,tf->df/dot_general | solution.py:669
  532.7 7.3 fusion.5
  540.0 13.1 %fusion.55 = f32[1024,2048]{1,0:T(8,128)S(1)} fusion(bf16[2048,1024]{1,0:T(8,128)(2,1)S(1)} %get-tuple-element.165.x1_ref, bf16[2048,2048]{1,0:T(8,128)(2,1)} %collective-permute-done.20.dy1_ref), kind=kOutput, calls=%fused_computation.221 | convolution fusion | flops 8589934592 | bytes 20971520 | tf_op jit(solution)/shard_map/tf,td->fd/dot_general | solution.py:669
  553.1 13.5 %add_convert_fusion.1 = bf16[1024,2048]{1,0:T(8,128)(2,1)} fusion(f32[1024,2048]{1,0:T(8,128)S(1)} %fusion.55, bf16[2048,1024]{1,0:T(8,128)(2,1)S(1)} %get-tuple-element.164.x0_ref, bf16[2048,2048]{1,0:T(8,128)(2,1)} %constant_dynamic-update-slice_fusion.11.dy0_ref), kind=kOutput, calls=%fused_computation.19 | convolution fusion | flops 8594128896 | bytes 25165824 | tf_op jit(solution)/shard_map/tf,td->fd/dot_general | solution.py:669
  566.6 15.3 %add_convert_fusion = bf16[2048,1024]{1,0:T(8,128)(2,1)} fusion(f32[2048,1024]{1,0:T(8,128)} %fusion.56, bf16[2048,2048]{1,0:T(8,128)(2,1)} %get-tuple-element.155, bf16[2048,1024]{1,0:T(8,128)(2,1)} %get-tuple-element.159.x0_ref), kind=kOutput, calls=%fused_computation.18 | convolution fusion | flops 8594128896 | bytes 25165824 | tf_op jit(solution)/shard_map/td,tf->df/dot_general | solution.py:669
  582.0 90.0 %product_sum.3.db_ref = f32[512,2048]{1,0:T(8,128)} custom-call(bf16[2048,1024]{1,0:T(8,128)(2,1)} %get-tuple-element.159.x0_ref, bf16[2048,1024]{1,0:T(8,128)(2,1)} %copy-done.15, bf16[2048,1024]{1,0:T(8,128)(2,1)} %all-gather.11.cloned.1.call-done.up_ref.w_ref), custom_call_target="tpu_custom_call" | custom-call | flops 68719476736 | bytes 20971520 | tf_op jit(solution)/shard_map/product_sum/pallas_call | solution.py:471
  679.7 87.6 %product_sum.4 = f32[512,2048]{1,0:T(8,128)} custom-call(bf16[2048,1024]{1,0:T(8,128)(2,1)} %copy-done.14, bf16[2048,1024]{1,0:T(8,128)(2,1)} %copy-done.13, bf16[1024,2048]{1,0:T(8,128)(2,1)} %all-gather.9.cloned.1.call-done.down_ref.w_ref), custom_call_target="tpu_custom_call" | custom-call | flops 68719476736 | bytes 20971520 | tf_op jit(solution)/shard_map/product_sum/pallas_call | solution.py:471
  767.3 12.7 %middle_backward.2 = (f32[256,2048]{1,0:T(8,128)}, bf16[256,2048]{1,0:T(8,128)(2,1)}, bf16[8,256,256]{2,1,0:T(8,128)(2,1)}) custom-call(bf16[8,256,256]{2,1,0:T(8,128)(2,1)} %copy-done.3, f32[256,2048]{1,0:T(8,128)} %get-tuple-element.129.x1_ref, f32[512,2048]{1,0:T(8,128)} %product_sum.3.db_ref, bf16[256,2048]{1,0:T(8,128)(2,1)} %get-tuple-element.224.dy_ref, ...), custom_call_target="tpu_custom_call" | custom-call | flops 2147483648 | bytes 16777216 | tf_op jit(solution)/shard_map/middle_backward/pallas_call | solution.py:353
  780.0 3.6 all-to-all-start.4
  783.6 12.7 %middle_backward.3 = (f32[256,2048]{1,0:T(8,128)}, bf16[256,2048]{1,0:T(8,128)(2,1)}, bf16[8,256,256]{2,1,0:T(8,128)(2,1)}) custom-call(bf16[8,256,256]{2,1,0:T(8,128)(2,1)} %copy-done.4, f32[256,2048]{1,0:T(8,128)} %get-tuple-element.131.x1_ref, f32[512,2048]{1,0:T(8,128)} %product_sum.3.db_ref, bf16[256,2048]{1,0:T(8,128)(2,1)} %get-tuple-element.225.dy_ref, ...), custom_call_target="tpu_custom_call" | custom-call | flops 2147483648 | bytes 16777216 | tf_op jit(solution)/shard_map/middle_backward/pallas_call | solution.py:353
  796.2 8.2 convolution_convert_fusion
  806.0 19.3 %all_to_all.52 = bf16[8,256,256]{2,1,0:T(8,128)(2,1)} all-to-all(bf16[8,256,256]{2,1,0:T(8,128)(2,1)S(1)} %copy-done.22), channel_id=1, replica_groups=mesh['row'=4,'ctx'=8] {'ctx'}, dimensions={0} | all-to-all | bytes 2097152 | tf_op jit(solution)/shard_map/all_to_all | solution.py:852
  825.4 3.6 all-to-all-start.5
  829.0 32.3 %attention_backward.2 = (bf16[2048,768]{1,0:T(8,128)(2,1)}, bf16[2048,768]{1,0:T(8,128)(2,1)}) custom-call(s32[10]{0:T(128)} %pad_add_fusion.4.span_ref, bf16[256,2048]{1,0:T(8,128)(2,1)} %get-tuple-element.177.refs_0_, bf16[256,2048]{1,0:T(8,128)(2,1)} %get-tuple-element.178.refs_1_, bf16[256,2048]{1,0:T(8,128)(2,1)} %get-tuple-element.179.refs_2_, ...), custom_call_target="tpu_custom_call" | custom-call | flops 21474836480 | bytes 20971520 | tf_op jit(solution)/shard_map/attention_backward/pallas_call | solution.py:269
  861.3 41.3 %attention_backward.3 = (bf16[2048,768]{1,0:T(8,128)(2,1)}, bf16[2048,768]{1,0:T(8,128)(2,1)}) custom-call(s32[10]{0:T(128)} %pad_add_fusion.2.span_ref, bf16[256,2048]{1,0:T(8,128)(2,1)} %get-tuple-element.171.qT_ref, bf16[256,2048]{1,0:T(8,128)(2,1)} %get-tuple-element.172.kT_ref, ...), custom_call_target="tpu_custom_call", output_to_operand_aliasing={{0}: (9, {}), {1}: (10, {})} | custom-call | flops 21474836480 | bytes 20971520 | tf_op jit(solution)/shard_map/attention_backward/pallas_call | solution.py:269
  902.9 10.8 fusion.57
  913.7 10.6 add_convert_fusion.2
  924.3 13.3 %reduce-scatter.12.cloned.1.call-done = bf16[64,2048]{1,0:T(8,128)(2,1)} async-done(((bf16[256,2048]{1,0:T(8,128)(2,1)}), bf16[64,2048]{1,0:T(8,128)(2,1)}) %reduce-scatter.12.cloned.1.call-update) | async-done | bytes 262160 | tf_op jit(solution)/shard_map/reduce_scatter | solution.py:863
  937.6 4.0 fusion.18
  941.6 4.1 fusion.14
  953.0 87.1 %product_sum.5 = f32[512,2048]{1,0:T(8,128)} custom-call(bf16[2048,768]{1,0:T(8,128)(2,1)} %get-tuple-element.198.x0_ref, bf16[2048,768]{1,0:T(8,128)(2,1)} %get-tuple-element.199.x1_ref, bf16[2048,768]{1,0:T(8,128)(2,1)} %all-gather.5.cloned.1.call-done.w_ref), custom_call_target="tpu_custom_call" | custom-call | flops 51539607552 | bytes 20971520 | tf_op jit(solution)/shard_map/product_sum/pallas_call | solution.py:471
  1040.1 3.6 all-to-all-start.6
  1043.7 3.3 fusion.49
  1052.1 4.1 all-to-all-done.6
  1061.1 4.1 slice_reduce_fusion
  (305 shorter events, 112.7 us)
Async XLA Ops:
  7.2 111.3 %all-gather.5.cloned.1.call-start = ((), (), s32[]{:S(2)}) async-start(), calls=%async_computation.12 | async-start | bytes 3932160 | tf_op jit(solution)/shard_map/all_gather | solution.py:779
  9.6 17.5 %copy-start.45 = (bf16[64]{0:T(256)(128)(2,1)S(1)}, bf16[64]{0:T(256)(128)(2,1)}, u32[]{:S(2)}) copy-start(bf16[64]{0:T(256)(128)(2,1)} %param.26) | copy-start | bytes 388
  9.6 17.5 %copy-start.19 = (bf16[64,2048]{1,0:T(8,128)(2,1)S(1)}, bf16[64,2048]{1,0:T(8,128)(2,1)}, u32[]{:S(2)}) copy-start(bf16[64,2048]{1,0:T(8,128)(2,1)} %param.22) | copy-start | bytes 786436
  9.6 18.4 %copy-start = (bf16[2,256,2048]{2,1,0:T(8,128)(2,1)S(1)}, bf16[2,256,2048]{2,1,0:T(8,128)(2,1)}, u32[]{:S(2)}) copy-start(bf16[2,256,2048]{2,1,0:T(8,128)(2,1)} %param.17) | copy-start | bytes 6291460
  11.5 5.4 collective-permute-start
  12.0 7.5 collective-permute-start.1
  14.6 5.5 collective-permute-start.2
  14.8 5.3 collective-permute-start.3
  16.6 9.4 collective-permute-start.4
  16.8 9.2 collective-permute-start.5
  19.5 6.6 collective-permute-start.6
  27.0 155.1 %all-gather.7.cloned.1.call-start = ((), (), s32[]{:S(2)}) async-start(), calls=%async_computation.13 | async-start | bytes 8650752 | tf_op jit(solution)/shard_map/all_gather | solution.py:780
  27.9 235.4 %all-gather.9.cloned.1.call-start = ((), (), s32[]{:S(2)}) async-start(), calls=%async_computation.14 | async-start | bytes 5242880 | tf_op jit(solution)/shard_map/all_gather | solution.py:797
  31.5 25.2 %collective-permute-start.7 = (bf16[256,2048]{1,0:T(8,128)(2,1)S(1)}, bf16[256,2048]{1,0:T(8,128)(2,1)S(1)}, u32[]{:S(2)}, u32[]{:S(2)}) collective-permute-start(bf16[256,2048]{1,0:T(8,128)(2,1)S(1)} %get-tuple-element.234), channel_id=1, source_target_pairs={{0,2},{1,3},{2,0},{3,1},{4,6},{5,7},{6,4},{7,5},{8,10},{9,11},{10,... | collective-permute-start | bytes 3145736 | tf_op jit(solution)/shard_map/ppermute | solution.py:674
  32.9 27.9 %collective-permute-start.11 = (bf16[256,2048]{1,0:T(8,128)(2,1)S(1)}, bf16[256,2048]{1,0:T(8,128)(2,1)S(1)}, u32[]{:S(2)}, u32[]{:S(2)}) collective-permute-start(bf16[256,2048]{1,0:T(8,128)(2,1)S(1)} %get-tuple-element.232), channel_id=1, source_target_pairs={{0,4},{1,5},{2,6},{3,7},{4,0},{5,1},{6,2},{7,3},{8,12},{9,13},{10,... | collective-permute-start | bytes 3145736 | tf_op jit(solution)/shard_map/ppermute | solution.py:674
  34.3 47.2 %collective-permute-start.8 = (bf16[256,2048]{1,0:T(8,128)(2,1)S(1)}, bf16[256,2048]{1,0:T(8,128)(2,1)S(1)}, u32[]{:S(2)}, u32[]{:S(2)}) collective-permute-start(bf16[256,2048]{1,0:T(8,128)(2,1)S(1)} %get-tuple-element.234), channel_id=1, source_target_pairs={{0,4},{1,5},{2,6},{3,7},{4,0},{5,1},{6,2},{7,3},{8,12},{9,13},{10,... | collective-permute-start | bytes 3145736 | tf_op jit(solution)/shard_map/ppermute | solution.py:674
  56.7 46.2 %collective-permute-start.9 = (bf16[256,2048]{1,0:T(8,128)(2,1)S(1)}, bf16[256,2048]{1,0:T(8,128)(2,1)S(1)}, u32[]{:S(2)}, u32[]{:S(2)}) collective-permute-start(bf16[256,2048]{1,0:T(8,128)(2,1)S(1)} %collective-permute-done.7), channel_id=1, source_target_pairs={{0,4},{1,5},{2,6},{3,7},{4,0},{5,1},{6,2},{7,3},{8,12},{9,13},{10,... | collective-permute-start | bytes 3145736 | tf_op jit(solution)/shard_map/ppermute | solution.py:674
  58.3 46.8 %collective-permute-start.10 = (bf16[256,2048]{1,0:T(8,128)(2,1)S(1)}, bf16[256,2048]{1,0:T(8,128)(2,1)S(1)}, u32[]{:S(2)}, u32[]{:S(2)}) collective-permute-start(bf16[256,2048]{1,0:T(8,128)(2,1)S(1)} %get-tuple-element.232), channel_id=1, source_target_pairs={{0,2},{1,3},{2,0},{3,1},{4,6},{5,7},{6,4},{7,5},{8,10},{9,11},{10,... | collective-permute-start | bytes 3145736 | tf_op jit(solution)/shard_map/ppermute | solution.py:674
  60.8 46.4 %collective-permute-start.12 = (bf16[256,2048]{1,0:T(8,128)(2,1)S(1)}, bf16[256,2048]{1,0:T(8,128)(2,1)S(1)}, u32[]{:S(2)}, u32[]{:S(2)}) collective-permute-start(bf16[256,2048]{1,0:T(8,128)(2,1)S(1)} %collective-permute-done.11), channel_id=1, source_target_pairs={{0,2},{1,3},{2,0},{3,1},{4,6},{5,7},{6,4},{7,5},{8,10},{9,11},{10,... | collective-permute-start | bytes 3145736 | tf_op jit(solution)/shard_map/ppermute | solution.py:674
  108.3 23.1 %collective-permute-start.13 = (bf16[2048,2048]{1,0:T(8,128)(2,1)}, bf16[2048,2048]{1,0:T(8,128)(2,1)}, u32[]{:S(2)}, u32[]{:S(2)}) collective-permute-start(bf16[2048,2048]{1,0:T(8,128)(2,1)} %constant_dynamic-update-slice_fusion.3), channel_id=1, source_target_pairs={{0,1},{1,0},{2,3},{3,2},{4,5},{5,4},{6,7},{7,6},{8,9},{9,8},{10,11... | collective-permute-start | bytes 25165832 | tf_op jit(solution)/shard_map/ppermute | solution.py:674
  144.0 25.2 %copy-start.10 = (bf16[256,2048]{1,0:T(8,128)(2,1)}, bf16[256,2048]{1,0:T(8,128)(2,1)S(1)}, u32[]{:S(2)}) copy-start(bf16[256,2048]{1,0:T(8,128)(2,1)S(1)} %get-tuple-element.144) | copy-start | bytes 3145732
  144.0 37.0 %collective-permute-start.14 = (bf16[256,2048]{1,0:T(8,128)(2,1)}, bf16[256,2048]{1,0:T(8,128)(2,1)}, u32[]{:S(2)}, u32[]{:S(2)}) collective-permute-start(bf16[256,2048]{1,0:T(8,128)(2,1)} %get-tuple-element.140), channel_id=1, source_target_pairs={{0,2},{1,3},{2,0},{3,1},{4,6},{5,7},{6,4},{7,5},{8,10},{9,11},{10,... | collective-permute-start | bytes 3145736 | tf_op jit(solution)/shard_map/ppermute | solution.py:674
  145.2 35.9 %collective-permute-start.15 = (bf16[256,2048]{1,0:T(8,128)(2,1)S(1)}, bf16[256,2048]{1,0:T(8,128)(2,1)}, u32[]{:S(2)}, u32[]{:S(2)}) collective-permute-start(bf16[256,2048]{1,0:T(8,128)(2,1)S(1)} %get-tuple-element.144), channel_id=1, source_target_pairs={{0,4},{1,5},{2,6},{3,7},{4,0},{5,1},{6,2},{7,3},{8,12},{9,13},{10,... | collective-permute-start | bytes 3145736 | tf_op jit(solution)/shard_map/ppermute | solution.py:674
  146.6 35.7 %copy-start.47 = (bf16[64]{0:T(256)(128)(2,1)S(1)}, bf16[64]{0:T(256)(128)(2,1)}, u32[]{:S(2)}) copy-start(bf16[64]{0:T(256)(128)(2,1)} %param.27) | copy-start | bytes 388
  182.3 19.3 %all-to-all-start = ((bf16[8,256,256]{2,1,0:T(8,128)(2,1)}), bf16[8,256,256]{2,1,0:T(8,128)(2,1)S(1)}, u32[]{:S(2)}, u32[]{:S(2)}) async-start(bf16[8,256,256]{2,1,0:T(8,128)(2,1)} %bitcast.205), calls=%async_computation | async-start | bytes 2097152 | tf_op jit(solution)/shard_map/all_to_all | solution.py:803
  201.6 33.7 %copy-start.3 = (bf16[8,256,256]{2,1,0:T(8,128)(2,1)}, bf16[8,256,256]{2,1,0:T(8,128)(2,1)S(1)}, u32[]{:S(2)}) copy-start(bf16[8,256,256]{2,1,0:T(8,128)(2,1)S(1)} %all-to-all-done.o_ref) | copy-start | bytes 3145732
  201.6 33.7 %all-to-all-start.2 = ((bf16[8,64,1024]{2,1,0:T(8,128)(2,1)}), bf16[8,64,1024]{2,1,0:T(8,128)(2,1)}, u32[]{:S(2)}, u32[]{:S(2)}) async-start(bf16[8,64,1024]{2,1,0:T(8,128)(2,1)} %reshape.347), calls=%async_computation.2 | async-start | bytes 2097152 | tf_op jit(solution)/shard_map/all_to_all | solution.py:789
  235.3 20.1 %all-to-all-start.1 = ((bf16[8,256,256]{2,1,0:T(8,128)(2,1)}), bf16[8,256,256]{2,1,0:T(8,128)(2,1)S(1)}, u32[]{:S(2)}, u32[]{:S(2)}) async-start(bf16[8,256,256]{2,1,0:T(8,128)(2,1)} %bitcast.206), calls=%async_computation.1 | async-start | bytes 2097152 | tf_op jit(solution)/shard_map/all_to_all | solution.py:803
  239.4 156.4 %all-gather.11.cloned.1.call-start = ((), (), s32[]{:S(2)}) async-start(), calls=%async_computation.15 | async-start | bytes 5242880 | tf_op jit(solution)/shard_map/all_gather | solution.py:805
  239.5 40.7 %collective-permute-start.16 = (bf16[256,2048]{1,0:T(8,128)(2,1)}, bf16[256,2048]{1,0:T(8,128)(2,1)}, u32[]{:S(2)}, u32[]{:S(2)}) collective-permute-start(bf16[256,2048]{1,0:T(8,128)(2,1)} %get-tuple-element.140), channel_id=1, source_target_pairs={{0,4},{1,5},{2,6},{3,7},{4,0},{5,1},{6,2},{7,3},{8,12},{9,13},{10,... | collective-permute-start | bytes 3145736 | tf_op jit(solution)/shard_map/ppermute | solution.py:674
  241.5 57.5 %collective-permute-start.17 = (bf16[256,2048]{1,0:T(8,128)(2,1)}, bf16[256,2048]{1,0:T(8,128)(2,1)}, u32[]{:S(2)}, u32[]{:S(2)}) collective-permute-start(bf16[256,2048]{1,0:T(8,128)(2,1)} %collective-permute-done.14), channel_id=1, source_target_pairs={{0,4},{1,5},{2,6},{3,7},{4,0},{5,1},{6,2},{7,3},{8,12},{9,13},{10,... | collective-permute-start | bytes 3145736 | tf_op jit(solution)/shard_map/ppermute | solution.py:674
  241.6 57.4 %collective-permute-start.18 = (bf16[256,2048]{1,0:T(8,128)(2,1)}, bf16[256,2048]{1,0:T(8,128)(2,1)}, u32[]{:S(2)}, u32[]{:S(2)}) collective-permute-start(bf16[256,2048]{1,0:T(8,128)(2,1)} %copy-done.10), channel_id=1, source_target_pairs={{0,2},{1,3},{2,0},{3,1},{4,6},{5,7},{6,4},{7,5},{8,10},{9,11},{10,... | collective-permute-start | bytes 3145736 | tf_op jit(solution)/shard_map/ppermute | solution.py:674
  243.5 55.5 %collective-permute-start.19 = (bf16[256,2048]{1,0:T(8,128)(2,1)}, bf16[256,2048]{1,0:T(8,128)(2,1)}, u32[]{:S(2)}, u32[]{:S(2)}) collective-permute-start(bf16[256,2048]{1,0:T(8,128)(2,1)} %collective-permute-done.15), channel_id=1, source_target_pairs={{0,2},{1,3},{2,0},{3,1},{4,6},{5,7},{6,4},{7,5},{8,10},{9,11},{10,... | collective-permute-start | bytes 3145736 | tf_op jit(solution)/shard_map/ppermute | solution.py:674
  316.6 79.2 %collective-permute-start.20 = (bf16[2048,2048]{1,0:T(8,128)(2,1)}, bf16[2048,2048]{1,0:T(8,128)(2,1)}, u32[]{:S(2)}, u32[]{:S(2)}) collective-permute-start(bf16[2048,2048]{1,0:T(8,128)(2,1)} %constant_dynamic-update-slice_fusion.11.dy0_ref), channel_id=1, source_target_pairs={{0,1},{1,0},{2,3},{3,2},{4,5},{5,4},{6,7},{7,6},{8,9},{9,8},{10,11... | collective-permute-start | bytes 25165832 | tf_op jit(solution)/shard_map/ppermute | solution.py:674
  316.7 355.3 %reduce-scatter.6.cloned.1.call-start = ((), (), s32[]{:S(2)}) async-start(), calls=%async_computation.16 | async-start | bytes 5242880 | tf_op jit(solution)/shard_map/reduce_scatter | solution.py:842
  516.2 23.8 %copy-start.13 = (bf16[2048,1024]{1,0:T(8,128)(2,1)}, bf16[2048,1024]{1,0:T(8,128)(2,1)S(1)}, u32[]{:S(2)}) copy-start(bf16[2048,1024]{1,0:T(8,128)(2,1)S(1)} %get-tuple-element.165.x1_ref) | copy-start | bytes 12582916
  581.9 185.4 %reduce-scatter.8.cloned.1.call-start = ((), (), s32[]{:S(2)}) async-start(), calls=%async_computation.17 | async-start | bytes 5242880 | tf_op jit(solution)/shard_map/reduce_scatter | solution.py:846
  780.0 24.5 %all-to-all-start.4 = ((bf16[8,256,256]{2,1,0:T(8,128)(2,1)}), bf16[8,256,256]{2,1,0:T(8,128)(2,1)S(1)}, u32[]{:S(2)}, u32[]{:S(2)}) async-start(bf16[8,256,256]{2,1,0:T(8,128)(2,1)} %get-tuple-element.180), calls=%async_computation.6 | async-start | bytes 2097152 | tf_op jit(solution)/shard_map/all_to_all | solution.py:852
  783.5 119.2 %reduce-scatter.10.cloned.1.call-start = ((), (), s32[]{:S(2)}) async-start(), calls=%async_computation.18 | async-start | bytes 9437184 | tf_op jit(solution)/shard_map/reduce_scatter | solution.py:856
  825.4 77.3 %all-to-all-start.5 = ((bf16[8,64,1024]{2,1,0:T(8,128)(2,1)}), bf16[8,64,1024]{2,1,0:T(8,128)(2,1)S(1)}, u32[]{:S(2)}, u32[]{:S(2)}) async-start(bf16[8,64,1024]{2,1,0:T(8,128)(2,1)} %bitcast.49), calls=%async_computation.8 | async-start | bytes 2097152 | tf_op jit(solution)/shard_map/all_to_all | solution.py:857
  829.0 108.6 %reduce-scatter.12.cloned.1.call-start = ((), (), s32[]{:S(2)}) async-start(), calls=%async_computation.19 | async-start | bytes 1310720 | tf_op jit(solution)/shard_map/reduce_scatter | solution.py:863
  902.8 137.2 %reduce-scatter.14.cloned.1.call-start = ((), (), s32[]{:S(2)}) async-start(), calls=%async_computation.20 | async-start | bytes 3932160 | tf_op jit(solution)/shard_map/reduce_scatter | solution.py:867
  913.7 23.9 %copy-start.39 = (f32[256]{0:T(256)S(1)}, f32[256]{0:T(256)}, u32[]{:S(2)}) copy-start(f32[256]{0:T(256)} %copy-done.38) | copy-start | bytes 3076
  924.3 17.3 %copy-start.7 = (f32[256,2048]{1,0:T(8,128)S(1)}, f32[256,2048]{1,0:T(8,128)}, u32[]{:S(2)}) copy-start(f32[256,2048]{1,0:T(8,128)} %get-tuple-element.131.x1_ref) | copy-start | bytes 6291460
  952.9 90.7 %copy-start.1 = (bf16[2,256,2048]{2,1,0:T(8,128)(2,1)S(1)}, bf16[2,256,2048]{2,1,0:T(8,128)(2,1)}, u32[]{:S(2)}) copy-start(bf16[2,256,2048]{2,1,0:T(8,128)(2,1)} %param.17) | copy-start | bytes 6291460
  952.9 90.7 %copy-start.32 = (f32[1,2,2,128]{3,1,2,0:T(2,128)S(1)}, f32[1,2,2,128]{3,1,2,0:T(2,128)}, u32[]{:S(2)}) copy-start(f32[1,2,2,128]{3,1,2,0:T(2,128)} %copy-done.31) | copy-start | bytes 6148
  953.0 90.7 %copy-start.34 = (f32[1,2,2,128]{3,1,2,0:T(2,128)S(1)}, f32[1,2,2,128]{3,1,2,0:T(2,128)}, u32[]{:S(2)}) copy-start(f32[1,2,2,128]{3,1,2,0:T(2,128)} %copy-done.33) | copy-start | bytes 6148
  1040.1 16.1 %all-to-all-start.6 = ((bf16[8,64,768]{2,1,0:T(8,128)(2,1)}), bf16[8,64,768]{2,1,0:T(8,128)(2,1)S(1)}, u32[]{:S(2)}, u32[]{:S(2)}) async-start(bf16[8,64,768]{2,1,0:T(8,128)(2,1)} %bitcast.214), calls=%async_computation.11 | async-start | bytes 1572864 | tf_op jit(solution)/shard_map/all_to_all | solution.py:871
  (41 other events, 259.5 us)
Sparse Core Ops, SparseCore 0:
  27.1 64.5 all-gather.4
  95.2 86.8 all-gather.6
  183.7 79.6 all-gather.8
  316.8 79.0 all-gather.10
  582.0 74.3 reduce-scatter.5
  672.1 73.9 reduce-scatter.7
  804.6 80.3 reduce-scatter.9
  902.9 34.5 reduce-scatter.11
  939.9 58.8 reduce-scatter.13

commit v4 on v3

--- a/solution.py
+++ b/solution.py
@@ -371,8 +371,32 @@
     return lax.dot_general(a, w, (((1,), (1,)), ((), ())), preferred_element_type=f32)
 
 
-def product_sum_kernel(n, rows, cols, turned, x0_ref, x1_ref, w_ref, o_ref, part_s, core_s, sum_s, got_s, send_sem, recv_sem):
+def weight_copies(all_ref, kind, dst_ref, sems, first=0):
+    m, lines, ff = all_ref.shape
+    unit = ff // m
+    pieces = dst_ref.shape[1 if kind == "down" else 0] // ff
+    depth = lines - unit * pieces
+    copies = []
+    for r in range(m):
+        if kind == "up":
+            moves = [(all_ref.at[r, pl.ds(0, depth), :], dst_ref.at[pl.ds(r * depth, depth), :])]
+        else:
+            moves = [(all_ref.at[r, pl.ds(depth + q * unit, unit), :],
+                      dst_ref.at[pl.ds(r * unit, unit), pl.ds(q * ff, ff)]) for q in range(pieces)]
+        for src, dst in moves:
+            copies.append(pltpu.make_async_copy(src, dst, sems.at[first + len(copies)]))
+    for copy in copies:
+        copy.start()
+    return copies
+
+
+def product_sum_kernel(n, rows, cols, turned, kind, x0_ref, x1_ref, w_ref, o_ref, part_s, core_s, sum_s, got_s, send_sem, recv_sem,
+                       *own_w):
     mine = lax.axis_index("ctx")
+    loads = []
+    if kind:
+        loads = weight_copies(w_ref, kind, *own_w)
+        w_ref = own_w[0]
     spots = n // 2
     size = x0_ref.shape[0] // (rows * spots)
     width = o_ref.shape[1]
@@ -381,6 +405,8 @@
     for bit in bits:
         pl.semaphore_signal(barrier, inc=1, device_id={"ctx": mine ^ bit}, device_id_type=pl.DeviceIdType.MESH)
     pl.semaphore_wait(barrier, len(bits))
+    for copy in loads:
+        copy.wait()
     copies = []
 
     def send(src, dst, bit):
@@ -461,32 +487,36 @@
         copy.wait_send()
 
 
-def product_sum(x0, x1, w, rows, n, collective_id, turned=False):
+def product_sum(x0, x1, w, rows, n, collective_id, turned=False, kind=None, wide=None):
     size = x0.shape[0] // (rows * (n // 2))
-    width = w.shape[0 if turned else 1]
+    depth = x0.shape[1]
+    width = wide if kind else w.shape[0 if turned else 1]
     count = rows * (n // 2)
     moves = count + rows * (n // 2 - 1)
     vmem = pl.BlockSpec(memory_space=pltpu.VMEM)
     flops = 4 * x0.shape[0] * x0.shape[1] * width
     return pl.pallas_call(
-        functools.partial(product_sum_kernel, n, rows, min(512, width), turned),
+        functools.partial(product_sum_kernel, n, rows, min(512, width), turned, kind),
         out_shape=jax.ShapeDtypeStruct((rows * size, width), f32),
-        in_specs=[vmem] * 3, out_specs=vmem,
+        in_specs=[vmem, vmem, pl.BlockSpec(memory_space=pl.ANY) if kind else vmem], out_specs=vmem,
         scratch_shapes=[pltpu.VMEM((count, size, width), bf16), pltpu.VMEM((count, size, width), bf16),
                         pltpu.VMEM((count, size, width), bf16), pltpu.VMEM((moves - count, size, width), bf16),
-                        pltpu.SemaphoreType.DMA((moves,)), pltpu.SemaphoreType.DMA((moves,))],
+                        pltpu.SemaphoreType.DMA((moves,)), pltpu.SemaphoreType.DMA((moves,))]
+        + ([pltpu.VMEM((width, depth) if turned else (depth, width), bf16), pltpu.SemaphoreType.DMA((64,))] if kind else []),
         compiler_params=pltpu.CompilerParams(collective_id=collective_id, has_side_effects=True, vmem_limit_bytes=60 * 2**20),
         name="product_sum",
         cost_estimate=pl.CostEstimate(flops=4 * flops, bytes_accessed=20 * 2**20, transcendentals=0),
     )(x0, x1, w)
 
 
-def gather_product_kernel(n, rows, cols, b_ref, dy0_ref, dy1_ref, up_ref, down_ref, b0_ref, b1_ref, h0_ref, h1_ref, d0_ref, d1_ref,
-                          stat_ref, got_s, d_s, h_s, dy_s, send_sem, recv_sem, dy_sem, b_sem, h_sem, d_sem):
+def gather_product_kernel(n, rows, cols, b_ref, dy0_ref, dy1_ref, w_ref, b0_ref, b1_ref, h0_ref, h1_ref, d0_ref, d1_ref,
+                          stat_ref, up_ref, down_ref, got_s, d_s, h_s, dy_s, w_sem, send_sem, recv_sem, dy_sem, b_sem, h_sem, d_sem):
     mine = lax.axis_index("ctx")
     spots = n // 2
     size = b_ref.shape[0] // rows
     ff = up_ref.shape[1]
+    loads = weight_copies(w_ref, "down", down_ref, w_sem)
+    loads_up = weight_copies(w_ref, "up", up_ref, w_sem, len(loads))
     count = rows * spots
     barrier = pltpu.get_barrier_semaphore()
     bits = [1] + ways(0, n)
@@ -531,6 +561,8 @@
             pltpu.make_async_copy(dy1_ref.at[pl.ds(begin, size), :], dy_s.at[slot], dy_sem.at[slot]).start()
 
     fetch(0, 0)
+    for copy in loads:
+        copy.wait()
 
     @pl.loop(0, 2 * count)
     def _(t):
@@ -553,6 +585,8 @@
         copy.start()
         locals_.append(copy)
 
+    for copy in loads_up:
+        copy.wait()
     outs = []
     lane = lax.broadcasted_iota(jnp.int32, (32, 128), 1)
 
@@ -611,9 +645,9 @@
         copy.wait_send()
 
 
-def gather_product(b, dy0, dy1, up, down, rows, n, collective_id):
+def gather_product(b, dy0, dy1, weights, rows, n, collective_id):
     size = b.shape[0] // rows
-    width, ff = up.shape
+    width, ff = b.shape[1], weights.shape[2]
     count = rows * (n // 2)
     half = count * size
     moves = rows * (n - 1)
@@ -622,15 +656,16 @@
     return pl.pallas_call(
         functools.partial(gather_product_kernel, n, rows, min(256, ff)),
         out_shape=(sds((half, width), bf16),) * 2 + (sds((half, ff), f32),) * 4 + (sds((2 * half, 128), f32),),
-        in_specs=[vmem, here, here, vmem, vmem], out_specs=(here,) * 6 + (vmem,),
-        scratch_shapes=[pltpu.VMEM((2 * count, size, width), bf16), pltpu.VMEM((2 * count, size, ff), f32),
-                        pltpu.VMEM((2, size, ff), f32), pltpu.VMEM((2, size, width), bf16),
+        in_specs=[vmem, here, here, here], out_specs=(here,) * 6 + (vmem,),
+        scratch_shapes=[pltpu.VMEM((width, ff), bf16), pltpu.VMEM((ff, width), bf16),
+                        pltpu.VMEM((2 * count, size, width), bf16), pltpu.VMEM((2 * count, size, ff), f32),
+                        pltpu.VMEM((2, size, ff), f32), pltpu.VMEM((2, size, width), bf16), pltpu.SemaphoreType.DMA((64,)),
                         pltpu.SemaphoreType.DMA((moves,)), pltpu.SemaphoreType.DMA((moves,)), pltpu.SemaphoreType.DMA((2,))]
         + [pltpu.SemaphoreType.DMA((2 * count,))] * 3,
         compiler_params=pltpu.CompilerParams(collective_id=collective_id, has_side_effects=True, vmem_limit_bytes=62 * 2**20),
         name="gather_product",
         cost_estimate=pl.CostEstimate(flops=16 * half * width * ff, bytes_accessed=70 * 2**20, transcendentals=0),
-    )(b, dy0, dy1, up, down)
+    )(b, dy0, dy1, weights)
 
 
 def standardize(values):
@@ -770,13 +805,22 @@
     x_own = inputs.reshape(tokens, width).astype(f32)
     x_hat, x_rstd = standardize(x_own)
     x_low = x_hat.astype(bf16)
-    xh0 = gather_half(x_low.reshape(rows, local_len, width))
-    xh1 = swap(xh0, 1)
+    x_held = gather_step(gather_start(x_low.reshape(rows, local_len, width)), 0)
 
     qkv_local = jnp.concatenate(
         [scaled(w, gain_attn).reshape(piece, n, heads_dim) for w in (w_query, w_key, w_value)], axis=2)
     qkv_part = exchange(qkv_local.transpose(1, 0, 2)).reshape(n * piece, 3 * heads_dim)
+    x_held, qkv_part = lax.optimization_barrier((x_held, qkv_part))
     w_qkv = lax.all_gather(qkv_part, "row", axis=0, tiled=True)
+    up_local = scaled(after(w_up, qkv_part), gain_ffn).reshape(piece, m, n, unit).transpose(2, 0, 1, 3).reshape(n, piece, ff_dev)
+    up_part = lax.all_to_all(up_local, "ctx", split_axis=0, concat_axis=0, tiled=True).reshape(n * piece, ff_dev)
+    for step in range(1, gather_steps()):
+        x_held = gather_step(x_held, step)
+    xh0 = gather_end(x_held)
+    xh0, up_part = lax.optimization_barrier((xh0, up_part))
+    xh1 = swap(xh0, 1)
+    down_local = scaled(w_down, gain_ffn_sub)
+    ffn_local = jnp.concatenate([up_part] + [down_local[:, q:q + ff_dev] for q in range(0, width, ff_dev)], axis=0)
     out_all = lax.all_gather(scaled(w_out, gain_attn_sub), BOTH, axis=0, tiled=True)
 
     relative, lowest = row_places(doc_len, row_len)
@@ -784,9 +828,7 @@
     span = [span_of(lowest[r], blk, core, place) for r in range(rows)]
     qkv0 = dot(w_qkv, xh0, "df,td->ft")
     qkv1 = dot(w_qkv, xh1, "df,td->ft")
-    qkv0, qkv1, w_up_in, cot = lax.optimization_barrier((qkv0, qkv1, w_up, out_cotangent))
-    up_local = scaled(w_up_in, gain_ffn).reshape(piece, m, n, unit).transpose(2, 0, 1, 3).reshape(n, piece, ff_dev)
-    up_part = lax.all_to_all(up_local, "ctx", split_axis=0, concat_axis=0, tiled=True).reshape(n * piece, ff_dev)
+    qkv0, qkv1, cot = lax.optimization_barrier((qkv0, qkv1, out_cotangent))
     dy_held = gather_step(gather_start(cot), 0)
     dy_steps = gather_steps()
     saved, o = [], []
@@ -794,21 +836,19 @@
         o_row, *kept = attention_forward(r, qkv0, qkv1, table[r], lowest[r], span[r], blk, local_len)
         if r == 0:
             o_row, kept, qkv0, qkv1, dy_held, out_all = lax.optimization_barrier((o_row, kept, qkv0, qkv1, dy_held, out_all))
-            down_all = lax.all_gather(after(scaled(w_down, gain_ffn_sub), out_all), "row", axis=0, tiled=True)
+            ffn_all = lax.all_gather(after(ffn_local, out_all), "row", axis=0, tiled=False)
             for step in range(1, dy_steps):
                 dy_held = gather_step(dy_held, step)
         if r == rows - 1:
             o_row, o = lax.optimization_barrier((o_row, o))
         saved.append(kept)
         o.append(lax.all_to_all(o_row.reshape(n, local_len, heads_dim), "ctx", split_axis=0, concat_axis=0, tiled=True))
-    o, down_all, up_part = lax.optimization_barrier((o, down_all, up_part))
-    up_all = lax.all_gather(up_part, "row", axis=0, tiled=True)
     c, x1, b_low = zip(*[middle_forward(o[r], inputs[r], out_all) for r in range(rows)])
     b_low, dy_held = lax.optimization_barrier((b_low, dy_held))
     dy0 = gather_end(dy_held)
     dy1 = swap(dy0, 1)
 
-    b0, b1, h0, h1, d_hat0, d_hat1, stats = gather_product(jnp.concatenate(b_low), dy0, dy1, up_all, down_all, rows, n, 4)
+    b0, b1, h0, h1, d_hat0, d_hat1, stats = gather_product(jnp.concatenate(b_low), dy0, dy1, ffn_all, rows, n, 4)
     stats = stats[:, :4].T
     order = jnp.arange(n // 2, dtype=jnp.int32) ^ place
     halves = jnp.arange(2, dtype=jnp.int32) ^ core
@@ -840,35 +880,35 @@
     up_part = (dot(b0, dh0, "td,tf->df") + dot(b1, dh1, "td,tf->df")).astype(bf16)
     e0, e1, dh0, dh1, down_part, up_part = lax.optimization_barrier((e0, e1, dh0, dh1, down_part, up_part))
     down_sum = lax.psum_scatter(down_part, "row", scatter_dimension=0, tiled=True)
-    db = product_sum(dh0, dh1, up_all, rows, n, 1, True)
-    e0, e1, db, up_part, down_sum = lax.optimization_barrier((e0, e1, db, up_part, down_sum))
+    db = product_sum(dh0, dh1, ffn_all, rows, n, 1, True, "up", width)
+    db, up_part, down_sum = lax.optimization_barrier((db, up_part, down_sum))
     down_raw = down_sum.astype(f32)
     up_sum = lax.psum_scatter(up_part, "row", scatter_dimension=0, tiled=True)
-    ffn = product_sum(e0, e1, down_all, rows, n, 3)
-    db, ffn, up_sum = lax.optimization_barrier((db, ffn, up_sum))
-    output = (jnp.stack(x1) + ffn.reshape(rows, local_len, width)).astype(bf16)
 
     dx1, dx1b, d_o = zip(*[middle_backward(r, o[r], x1[r], db, out_cotangent[r], out_all) for r in range(rows)])
     do_heads = [lax.all_to_all(v, "ctx", split_axis=0, concat_axis=0, tiled=True).reshape(row_len, heads_dim) for v in d_o]
     c_order = jnp.concatenate(c).reshape(tokens, m, n, piece).transpose(0, 2, 1, 3).reshape(tokens, width)
     out_part = dot(c_order, jnp.concatenate(dx1b), "td,te->de", bf16)
     do_heads[0], out_part = lax.optimization_barrier((do_heads[0], out_part))
+    grads = attention_backward(0, rows, saved[0], do_heads[0], table[0], lowest[0], span[0], blk, local_len, None)
+    grads, do_heads, up_sum, out_part = lax.optimization_barrier((grads, do_heads, up_sum, out_part))
     out_part = lax.psum_scatter(out_part, "ctx", scatter_dimension=0, tiled=True)
-    up_moved = lax.all_to_all(after(up_sum.reshape(n, piece, ff_dev), do_heads[-1]), "ctx", split_axis=0, concat_axis=2, tiled=True)
-    grads = None
-    for r in range(rows):
+    up_moved = lax.all_to_all(up_sum.reshape(n, piece, ff_dev), "ctx", split_axis=0, concat_axis=2, tiled=True)
+    for r in range(1, rows):
         grads = attention_backward(r, rows, saved[r], do_heads[r], table[r], lowest[r], span[r], blk, local_len, grads)
-    grads, out_part, up_moved = lax.optimization_barrier((grads, out_part, up_moved))
     d0, d1 = grads
-    out_sum = lax.psum_scatter(out_part, "row", scatter_dimension=0, tiled=True)
     qkv_part = (dot(xh0, d0, "td,tf->df") + dot(xh1, d1, "td,tf->df")).astype(bf16)
-    d0, d1, qkv_part, out_sum = lax.optimization_barrier((d0, d1, qkv_part, out_sum))
-    out_raw = out_sum.astype(f32)
+    d0, d1, qkv_part, out_part, up_moved = lax.optimization_barrier((d0, d1, qkv_part, out_part, up_moved))
     qkv_part = lax.psum_scatter(qkv_part, "row", scatter_dimension=0, tiled=True)
     da = product_sum(d0, d1, w_qkv, rows, n, 2, True)
-    da, qkv_part = lax.optimization_barrier((da, qkv_part))
+    e0, e1, da, qkv_part, out_part = lax.optimization_barrier((e0, e1, da, qkv_part, out_part))
+    out_raw = lax.psum_scatter(out_part, "row", scatter_dimension=0, tiled=True).astype(f32)
     up_raw = up_moved.reshape(piece, n, m, unit).transpose(0, 2, 1, 3).reshape(piece, ff).astype(f32)
     qkv_raw = lax.all_to_all(qkv_part.reshape(n, piece, 3 * heads_dim), "ctx", split_axis=0, concat_axis=2, tiled=True)
+
+    ffn = product_sum(e0, e1, ffn_all, rows, n, 3, False, "down", width)
+    ffn, out_raw, qkv_raw = lax.optimization_barrier((ffn, out_raw, qkv_raw))
+    output = (jnp.stack(x1) + ffn.reshape(rows, local_len, width)).astype(bf16)
     qkv_raw = qkv_raw.reshape(piece, n, 3, heads_dim).astype(f32)
     query_raw, key_raw, value_raw = (qkv_raw[:, :, i].reshape(piece, width) for i in range(3))
     input_grad = jnp.stack(dx1) + standardize_back(x_hat, x_rstd, da).reshape(rows, local_len, width)

time: 1080 us -> 1020 us (0.944)
  waiting for transfers between devices: 223 us -> 176 us
  blocking collectives: 28.7 us -> 9.65 us
    all_gather x2 -> x1, waiting for transfers between devices: 85.6 us -> 35.1 us  [body(): lax.all_gather(after(ffn_local, out_all), 'row', axis=0, tiled=False)]
    all_gather x1, waiting for transfers between devices: 0.97 us -> 22.5 us  [body(): lax.all_gather(scaled(w_out, gain_attn_sub), BOTH, axis=0, tiled=True)]
    all_to_all x1 -> x0, blocking collectives: 19.3 us -> none  [body(): lax.all_to_all(v, 'ctx', split_axis=0, concat_axis=0, tiled=True)]
    all_to_all x2, waiting for transfers between devices: 19.9 us -> 1.74 us  [body(): lax.all_to_all(o_row.reshape(n, local_len, heads_dim), 'ctx', split_axis=...]
    reduce_scatter x1, waiting for transfers between devices: 13.3 us -> 0.02 us  [body(): lax.psum_scatter(out_part, 'row', scatter_dimension=0, tiled=True)]
    reduce_scatter x1, waiting for transfers between devices: 0.02 us -> 11.1 us  [body(): lax.psum_scatter(out_part, 'ctx', scatter_dimension=0, tiled=True)]
    unnamed x138 -> x165, local copies, waits for them, and re-layouts: 30 us -> 32.5 us
  transfers between devices with their start and end apart: 36 -> 36, of which waited for: 14 -> 15; matrix products, arithmetic and copies ran while one was open for 11% -> 12% of each run, Pallas kernels for 39% -> 43%
where the time goes in v4:
time: 1020 us; the launch traced here: 1010 us
  Pallas kernels  530 us (52%)
  waiting for transfers between devices  176 us (17%)
  matrix products  111 us (11%)
  local copies, waits for them, and re-layouts  65.3 us (6%)
  other arithmetic  53.1 us (5%)
  starting transfers between devices  50 us (5%)
  between operations  16 us (2%)
    pallas_call x3, Pallas kernels, product_sum(): pl.pallas_call(functools.partial(product_sum_kernel, n, rows, min(512, wi...  267 us
    dot_general x9, matrix products, dot(): return jnp.einsum(spec, a, b, preferred_element_type=f32).astype(kind)  111 us
    ppermute x21, waiting for transfers between devices, swap(): return lax.ppermute(x, 'ctx', [(i, i ^ bit) for i in range(n)])  100 us
    pallas_call x1, Pallas kernels, gather_product(): pl.pallas_call(functools.partial(gather_product_kernel, n, rows, min(256,...  95.2 us
    pallas_call x2, Pallas kernels, attention_backward(): pl.pallas_call(call, out_shape=(whole, whole), grid_spec=pltpu.PrefetchSc...  73.7 us
    pallas_call x2, Pallas kernels, attention_forward(): pl.pallas_call(functools.partial(forward_kernel, nh, blk, unit), out_shap...  52 us
    all_gather x1, waiting for transfers between devices, body(): lax.all_gather(after(ffn_local, out_all), 'row', axis=0, tiled=False)  35.1 us
    unnamed x165, local copies, waits for them, and re-layouts  32.5 us
  transfers between devices with their start and end apart: 36, of which 15 were waited for; matrix products, arithmetic and copies ran while one was open for 12% of the time, Pallas kernels for 43%

profile of v4, /device:TPU:0, one launch (start us, length us, event | category | flops | bytes accessed | tf_op | source)
XLA Modules:
  0.0 1010.7 jit_solution(11021696990765555059)
XLA Ops:
  18.9 2.6 collective-permute-start.7
  25.5 23.6 %collective-permute-done.8 = bf16[64,768]{1,0:T(8,128)(2,1)S(1)} collective-permute-done((bf16[64,768]{1,0:T(8,128)(2,1)S(1)}, bf16[64,768]{1,0:T(8,128)(2,1)S(1)}, u32[]{:S(2)}, u32[]{:S(2)}) %collective-permute-start.8) | collective-permute-done | bytes 98336 | tf_op jit(solution)/shard_map/ppermute | solution.py:709
  61.8 4.4 all-to-all-start
  68.8 10.4 %collective-permute-done.9 = bf16[256,2048]{1,0:T(8,128)(2,1)} collective-permute-done((bf16[256,2048]{1,0:T(8,128)(2,1)}, bf16[256,2048]{1,0:T(8,128)(2,1)}, u32[]{:S(2)}, u32[]{:S(2)}) %collective-permute-start.9) | collective-permute-done | bytes 1048608 | tf_op jit(solution)/shard_map/ppermute | solution.py:709
  81.5 20.1 %collective-permute-done.10 = bf16[256,2048]{1,0:T(8,128)(2,1)} collective-permute-done((bf16[256,2048]{1,0:T(8,128)(2,1)}, bf16[256,2048]{1,0:T(8,128)(2,1)}, u32[]{:S(2)}, u32[]{:S(2)}) %collective-permute-start.10) | collective-permute-done | bytes 1048608 | tf_op jit(solution)/shard_map/ppermute | solution.py:709
  110.9 3.9 all-to-all-done
  117.7 3.1 power_multiply_fusion.3
  122.5 13.6 %fusion.54.q0_ref.k0_ref.v0_ref = f32[768,2048]{1,0:T(8,128)} fusion(bf16[2048,768]{1,0:T(8,128)(2,1)} %all-gather.5.cloned.1.call-done.w_ref, bf16[2048,2048]{1,0:T(8,128)(2,1)} %constant_dynamic-update-slice_fusion.3), kind=kOutput, calls=%fused_computation.221 | convolution fusion | flops 6442450944 | bytes 17825792 | tf_op jit(solution)/shard_map/df,td->ft/dot_general | solution.py:704
  136.1 10.9 %fusion.55.q1_ref.k1_ref.v1_ref = f32[768,2048]{1,0:T(8,128)} fusion(bf16[2048,768]{1,0:T(8,128)(2,1)S(1)} %copy-done.55, bf16[2048,2048]{1,0:T(8,128)(2,1)} %collective-permute-done.13), kind=kOutput, calls=%fused_computation.222 | convolution fusion | flops 6442450944 | bytes 17825792 | tf_op jit(solution)/shard_map/df,td->ft/dot_general | solution.py:704
  150.8 2.7 pad_maximum_fusion.2
  153.5 28.8 %attention_forward.2 = (bf16[2048,256]{1,0:T(8,128)(2,1)}, f32[256,2048]{1,0:T(8,128)}, f32[4,2048]{1,0:T(4,128)}, bf16[256,2048]{1,0:T(8,128)(2,1)}, bf16[256,2...) custom-call(s32[10]{0:T(128)} %pad_add_fusion.4.span_ref, f32[768,2048]{1,0:T(8,128)} %fusion.54.q0_ref.k0_ref.v0_ref, ...), custom_call_target="tpu_custom_call" | custom-call | flops 8589934592 | bytes 10485760 | tf_op jit(solution)/shard_map/attention_forward/pallas_call | solution.py:234
  182.6 22.5 %all-gather.7.cloned.1.call-done.w_ref = bf16[2048,2048]{1,0:T(8,128)(2,1)} async-done(((bf16[64,2048]{1,0:T(8,128)(2,1)}), bf16[2048,2048]{1,0:T(8,128)(2,1)}) %all-gather.7.cloned.1.call-update) | async-done | bytes 8388624 | tf_op jit(solution)/shard_map/all_gather | solution.py:824
  205.1 3.7 all-to-all-start.1
  209.7 23.2 %attention_forward.3 = (bf16[2048,256]{1,0:T(8,128)(2,1)}, f32[256,2048]{1,0:T(8,128)}, f32[4,2048]{1,0:T(4,128)}, bf16[256,2048]{1,0:T(8,128)(2,1)}, bf16[256,2...) custom-call(s32[10]{0:T(128)} %pad_add_fusion.2.span_ref, f32[768,2048]{1,0:T(8,128)} %fusion.54.q0_ref.k0_ref.v0_ref, ...), custom_call_target="tpu_custom_call" | custom-call | flops 8589934592 | bytes 10485760 | tf_op jit(solution)/shard_map/attention_forward/pallas_call | solution.py:234
  232.8 4.3 all-to-all-start.2
  242.9 8.5 middle_forward.2
  253.1 8.5 middle_forward.3
  261.6 13.0 %collective-permute-done.16 = bf16[256,2048]{1,0:T(8,128)(2,1)} collective-permute-done((bf16[256,2048]{1,0:T(8,128)(2,1)}, bf16[256,2048]{1,0:T(8,128)(2,1)}, u32[]{:S(2)}, u32[]{:S(2)}) %collective-permute-start.16) | collective-permute-done | bytes 1048608 | tf_op jit(solution)/shard_map/ppermute | solution.py:709
  274.6 22.0 %collective-permute-done.17 = bf16[256,2048]{1,0:T(8,128)(2,1)} collective-permute-done((bf16[256,2048]{1,0:T(8,128)(2,1)}, bf16[256,2048]{1,0:T(8,128)(2,1)}, u32[]{:S(2)}, u32[]{:S(2)}) %collective-permute-start.17) | collective-permute-done | bytes 1048608 | tf_op jit(solution)/shard_map/ppermute | solution.py:709
  310.4 9.4 collective-permute-done.20.dy1_ref
  319.8 35.1 %all-gather.9.cloned.1.call-done = bf16[4096,1024]{1,0:T(8,128)(2,1)} async-done(((bf16[1024,1024]{1,0:T(8,128)(2,1)}), bf16[4096,1024]{1,0:T(8,128)(2,1)}) %all-gather.9.cloned.1.call-update) | async-done | bytes 8388624 | tf_op jit(solution)/shard_map/all_gather | solution.py:839
  354.8 95.2 %gather_product.1 = (bf16[2048,2048]{1,0:T(8,128)(2,1)}, bf16[2048,2048]{1,0:T(8,128)(2,1)}, f32[2048,1024]{1,0:T(8,128)}, f32[2048,1024]{1,0:T(8,128)}, f32[204...) custom-call(bf16[512,2048]{1,0:T(8,128)(2,1)} %pad_maximum_fusion.1.b_ref, ...), custom_call_target="tpu_custom_call" | custom-call | flops 68719476736 | bytes 73400320 | tf_op jit(solution)/shard_map/gather_product/pallas_call | solution.py:656
  453.8 9.6 all_gather.19
  466.0 8.0 fusion.11
  474.1 16.4 %fusion.57 = f32[2048,1024]{1,0:T(8,128)} fusion(bf16[2048,2048]{1,0:T(8,128)(2,1)} %get-tuple-element.164, bf16[2048,1024]{1,0:T(8,128)(2,1)S(1)} %get-tuple-element.174.x1_ref), kind=kOutput, calls=%fused_computation.224 | convolution fusion | flops 8589934592 | bytes 20971520 | tf_op jit(solution)/shard_map/td,tf->df/dot_general | solution.py:704
  490.5 7.3 fusion.5
  497.8 13.2 %fusion.56 = f32[1024,2048]{1,0:T(8,128)S(1)} fusion(bf16[2048,1024]{1,0:T(8,128)(2,1)S(1)} %get-tuple-element.205.x1_ref, bf16[2048,2048]{1,0:T(8,128)(2,1)} %collective-permute-done.20.dy1_ref), kind=kOutput, calls=%fused_computation.223 | convolution fusion | flops 8589934592 | bytes 20971520 | tf_op jit(solution)/shard_map/tf,td->fd/dot_general | solution.py:704
  511.0 11.2 %add_convert_fusion.1 = bf16[1024,2048]{1,0:T(8,128)(2,1)} fusion(f32[1024,2048]{1,0:T(8,128)S(1)} %fusion.56, bf16[2048,1024]{1,0:T(8,128)(2,1)S(1)} %get-tuple-element.204.x0_ref, bf16[2048,2048]{1,0:T(8,128)(2,1)S(1)} %bitcast.219), kind=kOutput, calls=%fused_computation.19 | convolution fusion | flops 8594128896 | bytes 25165824 | tf_op jit(solution)/shard_map/tf,td->fd/dot_general | solution.py:704
  522.3 15.3 %add_convert_fusion = bf16[2048,1024]{1,0:T(8,128)(2,1)} fusion(f32[2048,1024]{1,0:T(8,128)} %fusion.57, bf16[2048,2048]{1,0:T(8,128)(2,1)} %get-tuple-element.163, bf16[2048,1024]{1,0:T(8,128)(2,1)} %get-tuple-element.173.x0_ref), kind=kOutput, calls=%fused_computation.18 | convolution fusion | flops 8594128896 | bytes 25165824 | tf_op jit(solution)/shard_map/td,tf->df/dot_general | solution.py:704
  537.6 90.8 %product_sum.3.db_ref = f32[512,2048]{1,0:T(8,128)} custom-call(bf16[2048,1024]{1,0:T(8,128)(2,1)} %get-tuple-element.173.x0_ref, bf16[2048,1024]{1,0:T(8,128)(2,1)} %copy-done.20, bf16[4,1024,1024]{2,1,0:T(8,128)(2,1)} %bitcast.242), custom_call_target="tpu_custom_call" | custom-call | flops 68719476736 | bytes 20971520 | tf_op jit(solution)/shard_map/product_sum/pallas_call | solution.py:498
  636.2 12.6 %middle_backward.2 = (f32[256,2048]{1,0:T(8,128)}, bf16[256,2048]{1,0:T(8,128)(2,1)}, bf16[8,256,256]{2,1,0:T(8,128)(2,1)}) custom-call(bf16[8,256,256]{2,1,0:T(8,128)(2,1)} %copy-done.3, f32[256,2048]{1,0:T(8,128)} %get-tuple-element.137.x1_ref, f32[512,2048]{1,0:T(8,128)} %product_sum.3.db_ref, bf16[256,2048]{1,0:T(8,128)(2,1)} %get-tuple-element.235.dy_ref, ...), custom_call_target="tpu_custom_call" | custom-call | flops 2147483648 | bytes 16777216 | tf_op jit(solution)/shard_map/middle_backward/pallas_call | solution.py:353
  648.8 4.0 all-to-all-start.3
  652.8 12.7 %middle_backward.3 = (f32[256,2048]{1,0:T(8,128)}, bf16[256,2048]{1,0:T(8,128)(2,1)}, bf16[8,256,256]{2,1,0:T(8,128)(2,1)}) custom-call(bf16[8,256,256]{2,1,0:T(8,128)(2,1)} %all-to-all-done.2.o_ref, f32[256,2048]{1,0:T(8,128)} %get-tuple-element.139.x1_ref, f32[512,2048]{1,0:T(8,128)} %product_sum.3.db_ref, bf16[256,2048]{1,0:T(8,128)(2,1)} %get-tuple-element.234.dy_ref, ...), custom_call_target="tpu_custom_call" | custom-call | flops 2147483648 | bytes 16777216 | tf_op jit(solution)/shard_map/middle_backward/pallas_call | solution.py:353
  665.4 8.3 convolution_convert_fusion
  673.7 4.2 all-to-all-start.4
  678.0 40.8 %attention_backward.2 = (bf16[2048,768]{1,0:T(8,128)(2,1)}, bf16[2048,768]{1,0:T(8,128)(2,1)}) custom-call(s32[10]{0:T(128)} %pad_add_fusion.4.span_ref, bf16[256,2048]{1,0:T(8,128)(2,1)} %get-tuple-element.170.refs_0_, bf16[256,2048]{1,0:T(8,128)(2,1)} %get-tuple-element.171.refs_1_, bf16[256,2048]{1,0:T(8,128)(2,1)} %get-tuple-element.172.refs_2_, ...), custom_call_target="tpu_custom_call" | custom-call | flops 21474836480 | bytes 20971520 | tf_op jit(solution)/shard_map/attention_backward/pallas_call | solution.py:269
  719.7 4.1 all-to-all-start.5
  723.9 32.9 %attention_backward.3 = (bf16[2048,768]{1,0:T(8,128)(2,1)}, bf16[2048,768]{1,0:T(8,128)(2,1)}) custom-call(s32[10]{0:T(128)} %pad_add_fusion.2.span_ref, bf16[256,2048]{1,0:T(8,128)(2,1)} %get-tuple-element.167.qT_ref, bf16[256,2048]{1,0:T(8,128)(2,1)} %get-tuple-element.168.kT_ref, ...), custom_call_target="tpu_custom_call", output_to_operand_aliasing={{0}: (9, {}), {1}: (10, {})} | custom-call | flops 21474836480 | bytes 20971520 | tf_op jit(solution)/shard_map/attention_backward/pallas_call | solution.py:269
  756.8 10.8 %fusion.58 = f32[2048,768]{1,0:T(8,128)S(1)} fusion(bf16[2048,2048]{1,0:T(8,128)(2,1)} %collective-permute-done.13, bf16[2048,768]{1,0:T(8,128)(2,1)} %get-tuple-element.201.x1_ref), kind=kOutput, calls=%fused_computation.225 | convolution fusion | flops 6442450944 | bytes 17825792 | tf_op jit(solution)/shard_map/td,tf->df/dot_general | solution.py:704
  767.7 10.9 %add_convert_fusion.2 = bf16[2048,768]{1,0:T(8,128)(2,1)} fusion(f32[2048,768]{1,0:T(8,128)S(1)} %fusion.58, bf16[2048,2048]{1,0:T(8,128)(2,1)} %constant_dynamic-update-slice_fusion.3, bf16[2048,768]{1,0:T(8,128)(2,1)S(1)} %copy-done.59), kind=kOutput, calls=%fused_computation.27 | convolution fusion | flops 6445596672 | bytes 20971520 | tf_op jit(solution)/shard_map/td,tf->df/dot_general | solution.py:704
  778.7 11.1 %reduce-scatter.10.cloned.1.call-done = bf16[256,2048]{1,0:T(8,128)(2,1)} async-done(((bf16[2048,2048]{1,0:T(8,128)(2,1)}), bf16[256,2048]{1,0:T(8,128)(2,1)}) %reduce-scatter.10.cloned.1.call-update) | async-done | bytes 1048592 | tf_op jit(solution)/shard_map/reduce_scatter | solution.py:895
  789.9 3.6 fusion.18
  799.1 86.5 %product_sum.4 = f32[512,2048]{1,0:T(8,128)} custom-call(bf16[2048,768]{1,0:T(8,128)(2,1)} %get-tuple-element.200.x0_ref, bf16[2048,768]{1,0:T(8,128)(2,1)} %get-tuple-element.201.x1_ref, bf16[2048,768]{1,0:T(8,128)(2,1)} %all-gather.5.cloned.1.call-done.w_ref), custom_call_target="tpu_custom_call" | custom-call | flops 51539607552 | bytes 20971520 | tf_op jit(solution)/shard_map/product_sum/pallas_call | solution.py:498
  885.6 3.6 all-to-all-start.6
  889.9 90.0 %product_sum.5 = f32[512,2048]{1,0:T(8,128)} custom-call(bf16[2048,1024]{1,0:T(8,128)(2,1)} %copy-done.19, bf16[2048,1024]{1,0:T(8,128)(2,1)} %copy-done.18, bf16[4,1024,1024]{2,1,0:T(8,128)(2,1)} %bitcast.243), custom_call_target="tpu_custom_call" | custom-call | flops 68719476736 | bytes 20971520 | tf_op jit(solution)/shard_map/product_sum/pallas_call | solution.py:498
  980.0 3.3 fusion.49
  985.6 2.8 maximum_add_fusion.1
  991.9 4.1 slice_reduce_fusion
  (333 shorter events, 107.2 us)
Async XLA Ops:
  7.2 115.3 %all-gather.5.cloned.1.call-start = ((), (), s32[]{:S(2)}) async-start(), calls=%async_computation.12 | async-start | bytes 3932160 | tf_op jit(solution)/shard_map/all_gather | solution.py:814
  11.4 7.4 collective-permute-start.2
  12.0 9.5 collective-permute-start.3
  14.6 7.6 collective-permute-start.4
  14.8 7.9 collective-permute-start.5
  16.6 7.9 collective-permute-start.6
  18.4 33.0 %copy-start.56 = (bf16[64]{0:T(256)(128)(2,1)S(1)}, bf16[64]{0:T(256)(128)(2,1)}, u32[]{:S(2)}) copy-start(bf16[64]{0:T(256)(128)(2,1)} %param.26) | copy-start | bytes 388
  18.4 33.6 %copy-start.32 = (bf16[64,2048]{1,0:T(8,128)(2,1)S(1)}, bf16[64,2048]{1,0:T(8,128)(2,1)}, u32[]{:S(2)}) copy-start(bf16[64,2048]{1,0:T(8,128)(2,1)} %param.22) | copy-start | bytes 786436
  18.4 34.4 %copy-start.57 = (bf16[64]{0:T(256)(128)(2,1)S(1)}, bf16[64]{0:T(256)(128)(2,1)}, u32[]{:S(2)}) copy-start(bf16[64]{0:T(256)(128)(2,1)} %param.27) | copy-start | bytes 388
  18.7 31.0 %copy-start.13 = (bf16[256,2048]{1,0:T(8,128)(2,1)}, bf16[256,2048]{1,0:T(8,128)(2,1)S(1)}, u32[]{:S(2)}) copy-start(bf16[256,2048]{1,0:T(8,128)(2,1)S(1)} %get-tuple-element.116) | copy-start | bytes 3145732
  18.7 40.6 %copy-start.9 = (bf16[64,8192]{1,0:T(8,128)(2,1)S(1)}, bf16[64,8192]{1,0:T(8,128)(2,1)}, u32[]{:S(2)}) copy-start(bf16[64,8192]{1,0:T(8,128)(2,1)} %param.23) | copy-start | bytes 3145732
  18.9 6.6 collective-permute-start.7
  21.5 27.6 %collective-permute-start = (bf16[256,2048]{1,0:T(8,128)(2,1)S(1)}, bf16[256,2048]{1,0:T(8,128)(2,1)S(1)}, u32[]{:S(2)}, u32[]{:S(2)}) collective-permute-start(bf16[256,2048]{1,0:T(8,128)(2,1)S(1)} %get-tuple-element.116), channel_id=1, source_target_pairs={{0,2},{1,3},{2,0},{3,1},{4,6},{5,7},{6,4},{7,5},{8,10},{9,11},{10,... | collective-permute-start | bytes 3145736 | tf_op jit(solution)/shard_map/ppermute | solution.py:709
  22.1 27.5 %collective-permute-start.1 = (bf16[256,2048]{1,0:T(8,128)(2,1)S(1)}, bf16[256,2048]{1,0:T(8,128)(2,1)S(1)}, u32[]{:S(2)}, u32[]{:S(2)}) collective-permute-start(bf16[256,2048]{1,0:T(8,128)(2,1)S(1)} %get-tuple-element.118), channel_id=1, source_target_pairs={{0,4},{1,5},{2,6},{3,7},{4,0},{5,1},{6,2},{7,3},{8,12},{9,13},{10,... | collective-permute-start | bytes 3145736 | tf_op jit(solution)/shard_map/ppermute | solution.py:709
  22.6 26.4 %collective-permute-start.8 = (bf16[64,768]{1,0:T(8,128)(2,1)S(1)}, bf16[64,768]{1,0:T(8,128)(2,1)S(1)}, u32[]{:S(2)}, u32[]{:S(2)}) collective-permute-start(bf16[64,768]{1,0:T(8,128)(2,1)S(1)} %bitcast.223), channel_id=1, source_target_pairs={{0,7},{1,6},{2,5},{3,4},{4,3},{5,2},{6,1},{7,0},{8,15},{9,14},{10,... | collective-permute-start | bytes 294920 | tf_op jit(solution)/shard_map/ppermute | solution.py:709
  51.3 153.8 %all-gather.7.cloned.1.call-start = ((), (), s32[]{:S(2)}) async-start(), calls=%async_computation.13 | async-start | bytes 8650752 | tf_op jit(solution)/shard_map/all_gather | solution.py:824
  52.8 26.4 %collective-permute-start.9 = (bf16[256,2048]{1,0:T(8,128)(2,1)}, bf16[256,2048]{1,0:T(8,128)(2,1)}, u32[]{:S(2)}, u32[]{:S(2)}) collective-permute-start(bf16[256,2048]{1,0:T(8,128)(2,1)} %copy-done.13), channel_id=1, source_target_pairs={{0,4},{1,5},{2,6},{3,7},{4,0},{5,1},{6,2},{7,3},{8,12},{9,13},{10,... | collective-permute-start | bytes 3145736 | tf_op jit(solution)/shard_map/ppermute | solution.py:709
  54.6 47.0 %collective-permute-start.10 = (bf16[256,2048]{1,0:T(8,128)(2,1)}, bf16[256,2048]{1,0:T(8,128)(2,1)}, u32[]{:S(2)}, u32[]{:S(2)}) collective-permute-start(bf16[256,2048]{1,0:T(8,128)(2,1)} %copy-done.29), channel_id=1, source_target_pairs={{0,4},{1,5},{2,6},{3,7},{4,0},{5,1},{6,2},{7,3},{8,12},{9,13},{10,... | collective-permute-start | bytes 3145736 | tf_op jit(solution)/shard_map/ppermute | solution.py:709
  54.9 50.2 %collective-permute-start.11 = (bf16[256,2048]{1,0:T(8,128)(2,1)}, bf16[256,2048]{1,0:T(8,128)(2,1)}, u32[]{:S(2)}, u32[]{:S(2)}) collective-permute-start(bf16[256,2048]{1,0:T(8,128)(2,1)} %copy-done.11), channel_id=1, source_target_pairs={{0,2},{1,3},{2,0},{3,1},{4,6},{5,7},{6,4},{7,5},{8,10},{9,11},{10,... | collective-permute-start | bytes 3145736 | tf_op jit(solution)/shard_map/ppermute | solution.py:709
  56.6 52.0 %collective-permute-start.12 = (bf16[256,2048]{1,0:T(8,128)(2,1)}, bf16[256,2048]{1,0:T(8,128)(2,1)}, u32[]{:S(2)}, u32[]{:S(2)}) collective-permute-start(bf16[256,2048]{1,0:T(8,128)(2,1)} %copy-done.27), channel_id=1, source_target_pairs={{0,2},{1,3},{2,0},{3,1},{4,6},{5,7},{6,4},{7,5},{8,10},{9,11},{10,... | collective-permute-start | bytes 3145736 | tf_op jit(solution)/shard_map/ppermute | solution.py:709
  61.8 42.3 %copy-start.12 = (bf16[256,2048]{1,0:T(8,128)(2,1)S(1)}, bf16[256,2048]{1,0:T(8,128)(2,1)}, u32[]{:S(2)}) copy-start(bf16[256,2048]{1,0:T(8,128)(2,1)} %copy-done.11) | copy-start | bytes 3145732
  61.8 53.1 %all-to-all-start = ((bf16[8,64,1024]{2,1,0:T(8,128)(2,1)}), bf16[8,64,1024]{2,1,0:T(8,128)(2,1)}, u32[]{:S(2)}, u32[]{:S(2)}) async-start(bf16[8,64,1024]{2,1,0:T(8,128)(2,1)} %reshape.342), calls=%async_computation | async-start | bytes 2097152 | tf_op jit(solution)/shard_map/all_to_all | solution.py:816
  66.1 288.7 %all-gather.9.cloned.1.call-start = ((), (), s32[]{:S(2)}) async-start(), calls=%async_computation.19 | async-start | bytes 10485760 | tf_op jit(solution)/shard_map/all_gather | solution.py:839
  68.8 38.7 %copy-start.28 = (bf16[256,2048]{1,0:T(8,128)(2,1)S(1)}, bf16[256,2048]{1,0:T(8,128)(2,1)}, u32[]{:S(2)}) copy-start(bf16[256,2048]{1,0:T(8,128)(2,1)} %copy-done.27) | copy-start | bytes 3145732
  114.8 21.2 %collective-permute-start.13 = (bf16[2048,2048]{1,0:T(8,128)(2,1)}, bf16[2048,2048]{1,0:T(8,128)(2,1)}, u32[]{:S(2)}, u32[]{:S(2)}) collective-permute-start(bf16[2048,2048]{1,0:T(8,128)(2,1)} %constant_dynamic-update-slice_fusion.3), channel_id=1, source_target_pairs={{0,1},{1,0},{2,3},{3,2},{4,5},{5,4},{6,7},{7,6},{8,9},{9,8},{10,11... | collective-permute-start | bytes 25165832 | tf_op jit(solution)/shard_map/ppermute | solution.py:709
  148.2 34.1 %copy-start.14 = (bf16[256,2048]{1,0:T(8,128)(2,1)}, bf16[256,2048]{1,0:T(8,128)(2,1)S(1)}, u32[]{:S(2)}) copy-start(bf16[256,2048]{1,0:T(8,128)(2,1)S(1)} %get-tuple-element.152) | copy-start | bytes 3145732
  148.2 34.4 %collective-permute-start.14 = (bf16[256,2048]{1,0:T(8,128)(2,1)}, bf16[256,2048]{1,0:T(8,128)(2,1)}, u32[]{:S(2)}, u32[]{:S(2)}) collective-permute-start(bf16[256,2048]{1,0:T(8,128)(2,1)} %get-tuple-element.148), channel_id=1, source_target_pairs={{0,2},{1,3},{2,0},{3,1},{4,6},{5,7},{6,4},{7,5},{8,10},{9,11},{10,... | collective-permute-start | bytes 3145736 | tf_op jit(solution)/shard_map/ppermute | solution.py:709
  148.8 33.8 %collective-permute-start.15 = (bf16[256,2048]{1,0:T(8,128)(2,1)S(1)}, bf16[256,2048]{1,0:T(8,128)(2,1)}, u32[]{:S(2)}, u32[]{:S(2)}) collective-permute-start(bf16[256,2048]{1,0:T(8,128)(2,1)S(1)} %get-tuple-element.152), channel_id=1, source_target_pairs={{0,4},{1,5},{2,6},{3,7},{4,0},{5,1},{6,2},{7,3},{8,12},{9,13},{10,... | collective-permute-start | bytes 3145736 | tf_op jit(solution)/shard_map/ppermute | solution.py:709
  205.1 27.7 %all-to-all-start.1 = ((bf16[8,256,256]{2,1,0:T(8,128)(2,1)}), bf16[8,256,256]{2,1,0:T(8,128)(2,1)S(1)}, u32[]{:S(2)}, u32[]{:S(2)}) async-start(bf16[8,256,256]{2,1,0:T(8,128)(2,1)} %bitcast.208), calls=%async_computation.1 | async-start | bytes 2097152 | tf_op jit(solution)/shard_map/all_to_all | solution.py:845
  232.8 20.3 %all-to-all-start.2 = ((bf16[8,256,256]{2,1,0:T(8,128)(2,1)}), bf16[8,256,256]{2,1,0:T(8,128)(2,1)}, u32[]{:S(2)}, u32[]{:S(2)}) async-start(bf16[8,256,256]{2,1,0:T(8,128)(2,1)} %bitcast.209), calls=%async_computation.2 | async-start | bytes 2097152 | tf_op jit(solution)/shard_map/all_to_all | solution.py:845
  237.1 391.4 %reduce-scatter.6.cloned.1.call-start = ((), (), s32[]{:S(2)}) async-start(), calls=%async_computation.14 | async-start | bytes 5242880 | tf_op jit(solution)/shard_map/reduce_scatter | solution.py:882
  237.2 37.5 %collective-permute-start.16 = (bf16[256,2048]{1,0:T(8,128)(2,1)}, bf16[256,2048]{1,0:T(8,128)(2,1)}, u32[]{:S(2)}, u32[]{:S(2)}) collective-permute-start(bf16[256,2048]{1,0:T(8,128)(2,1)} %get-tuple-element.148), channel_id=1, source_target_pairs={{0,4},{1,5},{2,6},{3,7},{4,0},{5,1},{6,2},{7,3},{8,12},{9,13},{10,... | collective-permute-start | bytes 3145736 | tf_op jit(solution)/shard_map/ppermute | solution.py:709
  239.3 57.3 %collective-permute-start.17 = (bf16[256,2048]{1,0:T(8,128)(2,1)}, bf16[256,2048]{1,0:T(8,128)(2,1)}, u32[]{:S(2)}, u32[]{:S(2)}) collective-permute-start(bf16[256,2048]{1,0:T(8,128)(2,1)} %collective-permute-done.14), channel_id=1, source_target_pairs={{0,4},{1,5},{2,6},{3,7},{4,0},{5,1},{6,2},{7,3},{8,12},{9,13},{10,... | collective-permute-start | bytes 3145736 | tf_op jit(solution)/shard_map/ppermute | solution.py:709
  239.3 57.3 %collective-permute-start.18 = (bf16[256,2048]{1,0:T(8,128)(2,1)}, bf16[256,2048]{1,0:T(8,128)(2,1)}, u32[]{:S(2)}, u32[]{:S(2)}) collective-permute-start(bf16[256,2048]{1,0:T(8,128)(2,1)} %copy-done.14), channel_id=1, source_target_pairs={{0,2},{1,3},{2,0},{3,1},{4,6},{5,7},{6,4},{7,5},{8,10},{9,11},{10,... | collective-permute-start | bytes 3145736 | tf_op jit(solution)/shard_map/ppermute | solution.py:709
  241.3 55.4 %collective-permute-start.19 = (bf16[256,2048]{1,0:T(8,128)(2,1)}, bf16[256,2048]{1,0:T(8,128)(2,1)}, u32[]{:S(2)}, u32[]{:S(2)}) collective-permute-start(bf16[256,2048]{1,0:T(8,128)(2,1)} %collective-permute-done.15), channel_id=1, source_target_pairs={{0,2},{1,3},{2,0},{3,1},{4,6},{5,7},{6,4},{7,5},{8,10},{9,11},{10,... | collective-permute-start | bytes 3145736 | tf_op jit(solution)/shard_map/ppermute | solution.py:709
  306.4 13.4 %collective-permute-start.20 = (bf16[2048,2048]{1,0:T(8,128)(2,1)S(1)}, bf16[2048,2048]{1,0:T(8,128)(2,1)}, u32[]{:S(2)}, u32[]{:S(2)}) collective-permute-start(bf16[2048,2048]{1,0:T(8,128)(2,1)S(1)} %constant_dynamic-update-slice_fusion.11.dy0_ref), channel_id=1, source_target_pairs={{0,1},{1,0},{2,3},{3,2},{4,5},{5,4},{6,7},{7,6},{8,9},{9,8},{10,11... | collective-permute-start | bytes 25165832 | tf_op jit(solution)/shard_map/ppermute | solution.py:709
  474.0 23.8 %copy-start.18 = (bf16[2048,1024]{1,0:T(8,128)(2,1)}, bf16[2048,1024]{1,0:T(8,128)(2,1)S(1)}, u32[]{:S(2)}) copy-start(bf16[2048,1024]{1,0:T(8,128)(2,1)S(1)} %get-tuple-element.205.x1_ref) | copy-start | bytes 12582916
  537.6 181.2 %reduce-scatter.8.cloned.1.call-start = ((), (), s32[]{:S(2)}) async-start(), calls=%async_computation.15 | async-start | bytes 5242880 | tf_op jit(solution)/shard_map/reduce_scatter | solution.py:886
  648.8 24.9 %all-to-all-start.3 = ((bf16[8,256,256]{2,1,0:T(8,128)(2,1)}), bf16[8,256,256]{2,1,0:T(8,128)(2,1)S(1)}, u32[]{:S(2)}, u32[]{:S(2)}) async-start(bf16[8,256,256]{2,1,0:T(8,128)(2,1)} %get-tuple-element.178), calls=%async_computation.4 | async-start | bytes 2097152 | tf_op jit(solution)/shard_map/all_to_all | solution.py:889
  673.7 45.0 %all-to-all-start.4 = ((bf16[8,256,256]{2,1,0:T(8,128)(2,1)}), bf16[8,256,256]{2,1,0:T(8,128)(2,1)S(1)}, u32[]{:S(2)}, u32[]{:S(2)}) async-start(bf16[8,256,256]{2,1,0:T(8,128)(2,1)} %get-tuple-element.188), calls=%async_computation.5 | async-start | bytes 2097152 | tf_op jit(solution)/shard_map/all_to_all | solution.py:889
  677.9 111.9 %reduce-scatter.10.cloned.1.call-start = ((), (), s32[]{:S(2)}) async-start(), calls=%async_computation.16 | async-start | bytes 9437184 | tf_op jit(solution)/shard_map/reduce_scatter | solution.py:895
  719.7 58.9 %all-to-all-start.5 = ((bf16[8,64,1024]{2,1,0:T(8,128)(2,1)}), bf16[8,64,1024]{2,1,0:T(8,128)(2,1)S(1)}, u32[]{:S(2)}, u32[]{:S(2)}) async-start(bf16[8,64,1024]{2,1,0:T(8,128)(2,1)} %bitcast.47), calls=%async_computation.8 | async-start | bytes 2097152 | tf_op jit(solution)/shard_map/all_to_all | solution.py:896
  723.9 161.7 %reduce-scatter.12.cloned.1.call-start = ((), (), s32[]{:S(2)}) async-start(), calls=%async_computation.17 | async-start | bytes 3932160 | tf_op jit(solution)/shard_map/reduce_scatter | solution.py:902
  885.6 102.8 %all-to-all-start.6 = ((bf16[8,64,768]{2,1,0:T(8,128)(2,1)}), bf16[8,64,768]{2,1,0:T(8,128)(2,1)S(1)}, u32[]{:S(2)}, u32[]{:S(2)}) async-start(bf16[8,64,768]{2,1,0:T(8,128)(2,1)} %bitcast.217), calls=%async_computation.11 | async-start | bytes 1572864 | tf_op jit(solution)/shard_map/all_to_all | solution.py:907
  889.1 99.4 %reduce-scatter.14.cloned.1.call-start = ((), (), s32[]{:S(2)}) async-start(), calls=%async_computation.18 | async-start | bytes 1310720 | tf_op jit(solution)/shard_map/reduce_scatter | solution.py:905
  889.9 90.0 %copy-start.1 = (bf16[2,256,2048]{2,1,0:T(8,128)(2,1)S(1)}, bf16[2,256,2048]{2,1,0:T(8,128)(2,1)}, u32[]{:S(2)}) copy-start(bf16[2,256,2048]{2,1,0:T(8,128)(2,1)} %param.17) | copy-start | bytes 6291460
  889.9 90.0 %copy-start.43 = (f32[1,2,2,128]{3,1,2,0:T(2,128)S(1)}, f32[1,2,2,128]{3,1,2,0:T(2,128)}, u32[]{:S(2)}) copy-start(f32[1,2,2,128]{3,1,2,0:T(2,128)} %copy-done.42) | copy-start | bytes 6148
  889.9 90.0 %copy-start.45 = (f32[1,2,2,128]{3,1,2,0:T(2,128)S(1)}, f32[1,2,2,128]{3,1,2,0:T(2,128)}, u32[]{:S(2)}) copy-start(f32[1,2,2,128]{3,1,2,0:T(2,128)} %copy-done.44) | copy-start | bytes 6148
  (54 other events, 372.9 us)
Sparse Core Ops, SparseCore 0:
  51.4 64.9 all-gather.4
  119.9 85.1 all-gather.6
  206.7 148.0 all-gather.8
  537.7 74.0 reduce-scatter.5
  628.6 73.9 reduce-scatter.7
  718.9 70.8 reduce-scatter.9
  792.2 60.2 reduce-scatter.11
  892.4 28.5 reduce-scatter.13

commit v5 on v4

--- a/solution.py
+++ b/solution.py
@@ -737,6 +737,25 @@
     return out
 
 
+def gather_own(held, step):
+    n = lax.axis_size("ctx")
+    out = []
+    for r, parts in enumerate(held):
+        bit = ways(r, n)[step]
+        out.append({**parts, bit: swap(parts[0], bit)})
+    return out
+
+
+def gather_rest(held, step):
+    n = lax.axis_size("ctx")
+    out = []
+    for r, parts in enumerate(held):
+        bit = ways(r, n)[step]
+        moved = {k | bit: swap(v, bit) for k, v in parts.items() if k and not k & bit}
+        out.append({**parts, **moved})
+    return out
+
+
 def gather_steps():
     return lax.axis_size("ctx").bit_length() - 2
 
@@ -810,7 +829,6 @@
     qkv_local = jnp.concatenate(
         [scaled(w, gain_attn).reshape(piece, n, heads_dim) for w in (w_query, w_key, w_value)], axis=2)
     qkv_part = exchange(qkv_local.transpose(1, 0, 2)).reshape(n * piece, 3 * heads_dim)
-    x_held, qkv_part = lax.optimization_barrier((x_held, qkv_part))
     w_qkv = lax.all_gather(qkv_part, "row", axis=0, tiled=True)
     up_local = scaled(after(w_up, qkv_part), gain_ffn).reshape(piece, m, n, unit).transpose(2, 0, 1, 3).reshape(n, piece, ff_dev)
     up_part = lax.all_to_all(up_local, "ctx", split_axis=0, concat_axis=0, tiled=True).reshape(n * piece, ff_dev)
@@ -837,10 +855,12 @@
         if r == 0:
             o_row, kept, qkv0, qkv1, dy_held, out_all = lax.optimization_barrier((o_row, kept, qkv0, qkv1, dy_held, out_all))
             ffn_all = lax.all_gather(after(ffn_local, out_all), "row", axis=0, tiled=False)
-            for step in range(1, dy_steps):
+            dy_held = gather_own(dy_held, 1)
+        if r == rows - 1:
+            o_row, o, dy_held = lax.optimization_barrier((o_row, o, dy_held))
+            dy_held = gather_rest(dy_held, 1)
+            for step in range(2, dy_steps):
                 dy_held = gather_step(dy_held, step)
-        if r == rows - 1:
-            o_row, o = lax.optimization_barrier((o_row, o))
         saved.append(kept)
         o.append(lax.all_to_all(o_row.reshape(n, local_len, heads_dim), "ctx", split_axis=0, concat_axis=0, tiled=True))
     c, x1, b_low = zip(*[middle_forward(o[r], inputs[r], out_all) for r in range(rows)])

time: 1020 us -> 1000 us (0.980)
  waiting for transfers between devices: 176 us -> 152 us
    all_gather x1, waiting for transfers between devices: 22.5 us -> 0.02 us  [body(): lax.all_gather(scaled(w_out, gain_attn_sub), BOTH, axis=0, tiled=True)]
    all_gather x1, waiting for transfers between devices: 35.1 us -> 46.9 us  [body(): lax.all_gather(after(ffn_local, out_all), 'row', axis=0, tiled=False)]
    ppermute x21, waiting for transfers between devices: 100 us -> 89.3 us  [swap(): return lax.ppermute(x, 'ctx', [(i, i ^ bit) for i in range(n)])]
    unnamed x165 -> x150, local copies, waits for them, and re-layouts: 32.5 us -> 33.1 us
  transfers between devices with their start and end apart: 36 -> 36, of which waited for: 15 -> 11; matrix products, arithmetic and copies ran while one was open for 12% -> 13% of each run, Pallas kernels for 43% -> 44%
where the time goes in v5:
time: 1000 us; the launch traced here: 996 us
  Pallas kernels  536 us (54%)
  waiting for transfers between devices  152 us (15%)
  matrix products  110 us (11%)
  local copies, waits for them, and re-layouts  66.6 us (7%)
  other arithmetic  53.2 us (5%)
  starting transfers between devices  51.8 us (5%)
  between operations  15.9 us (2%)
    pallas_call x3, Pallas kernels, product_sum(): pl.pallas_call(functools.partial(product_sum_kernel, n, rows, min(512, wi...  267 us
    dot_general x9, matrix products, dot(): return jnp.einsum(spec, a, b, preferred_element_type=f32).astype(kind)  110 us
    pallas_call x1, Pallas kernels, gather_product(): pl.pallas_call(functools.partial(gather_product_kernel, n, rows, min(256,...  95.2 us
    ppermute x21, waiting for transfers between devices, swap(): return lax.ppermute(x, 'ctx', [(i, i ^ bit) for i in range(n)])  89.3 us
    pallas_call x2, Pallas kernels, attention_backward(): pl.pallas_call(call, out_shape=(whole, whole), grid_spec=pltpu.PrefetchSc...  77.4 us
    pallas_call x2, Pallas kernels, attention_forward(): pl.pallas_call(functools.partial(forward_kernel, nh, blk, unit), out_shap...  54.4 us
    all_gather x1, waiting for transfers between devices, body(): lax.all_gather(after(ffn_local, out_all), 'row', axis=0, tiled=False)  46.9 us
    unnamed x150, local copies, waits for them, and re-layouts  33.1 us
  transfers between devices with their start and end apart: 36, of which 11 were waited for; matrix products, arithmetic and copies ran while one was open for 13% of the time, Pallas kernels for 44%

profile of v5, /device:TPU:0, one launch (start us, length us, event | category | flops | bytes accessed | tf_op | source)
XLA Modules:
  0.0 996.0 jit_solution(4645707234812551139)
XLA Ops:
  12.0 2.6 collective-permute-start.1
  16.8 2.6 collective-permute-start.5
  20.1 5.9 collective-permute-done.4
  37.5 20.8 %collective-permute-done.7 = bf16[256,2048]{1,0:T(8,128)(2,1)} collective-permute-done((bf16[256,2048]{1,0:T(8,128)(2,1)}, bf16[256,2048]{1,0:T(8,128)(2,1)}, u32[]{:S(2)}, u32[]{:S(2)}) %collective-permute-start.7) | collective-permute-done | bytes 1048608 | tf_op jit(solution)/shard_map/ppermute | solution.py:709
  62.1 3.6 all-to-all-start
  68.4 16.3 %collective-permute-done.11 = bf16[256,2048]{1,0:T(8,128)(2,1)} collective-permute-done((bf16[256,2048]{1,0:T(8,128)(2,1)}, bf16[256,2048]{1,0:T(8,128)(2,1)}, u32[]{:S(2)}, u32[]{:S(2)}) %collective-permute-start.11) | collective-permute-done | bytes 1048608 | tf_op jit(solution)/shard_map/ppermute | solution.py:709
  89.5 24.2 %collective-permute-done.9 = bf16[256,2048]{1,0:T(8,128)(2,1)} collective-permute-done((bf16[256,2048]{1,0:T(8,128)(2,1)}, bf16[256,2048]{1,0:T(8,128)(2,1)}, u32[]{:S(2)}, u32[]{:S(2)}) %collective-permute-start.9) | collective-permute-done | bytes 1048608 | tf_op jit(solution)/shard_map/ppermute | solution.py:709
  126.9 3.1 power_multiply_fusion.3
  131.7 13.2 %fusion.54.q0_ref.k0_ref.v0_ref = f32[768,2048]{1,0:T(8,128)} fusion(bf16[2048,768]{1,0:T(8,128)(2,1)} %all-gather.5.cloned.1.call-done.w_ref, bf16[2048,2048]{1,0:T(8,128)(2,1)} %constant_dynamic-update-slice_fusion.3), kind=kOutput, calls=%fused_computation.221 | convolution fusion | flops 6442450944 | bytes 17825792 | tf_op jit(solution)/shard_map/df,td->ft/dot_general | solution.py:704
  144.8 11.1 %fusion.55.q1_ref.k1_ref.v1_ref = f32[768,2048]{1,0:T(8,128)} fusion(bf16[2048,768]{1,0:T(8,128)(2,1)S(1)} %copy-done.48, bf16[2048,2048]{1,0:T(8,128)(2,1)} %collective-permute-done.13), kind=kOutput, calls=%fused_computation.222 | convolution fusion | flops 6442450944 | bytes 17825792 | tf_op jit(solution)/shard_map/df,td->ft/dot_general | solution.py:704
  161.7 28.8 %attention_forward.2 = (bf16[2048,256]{1,0:T(8,128)(2,1)}, f32[256,2048]{1,0:T(8,128)}, f32[4,2048]{1,0:T(4,128)}, bf16[256,2048]{1,0:T(8,128)(2,1)}, bf16[256,2...) custom-call(s32[10]{0:T(128)} %pad_add_fusion.4.span_ref, f32[768,2048]{1,0:T(8,128)} %fusion.54.q0_ref.k0_ref.v0_ref, ...), custom_call_target="tpu_custom_call" | custom-call | flops 8589934592 | bytes 10485760 | tf_op jit(solution)/shard_map/attention_forward/pallas_call | solution.py:234
  192.7 3.7 all-to-all-start.1
  197.2 25.5 %attention_forward.3 = (bf16[2048,256]{1,0:T(8,128)(2,1)}, f32[256,2048]{1,0:T(8,128)}, f32[4,2048]{1,0:T(4,128)}, bf16[256,2048]{1,0:T(8,128)(2,1)}, bf16[256,2...) custom-call(s32[10]{0:T(128)} %pad_add_fusion.2.span_ref, f32[768,2048]{1,0:T(8,128)} %fusion.54.q0_ref.k0_ref.v0_ref, ...), custom_call_target="tpu_custom_call" | custom-call | flops 8589934592 | bytes 10485760 | tf_op jit(solution)/shard_map/attention_forward/pallas_call | solution.py:234
  222.8 5.5 all-to-all-done.1.o_ref
  228.3 4.3 all-to-all-start.2
  237.4 8.5 middle_forward.2
  245.9 2.6 all-to-all-done.2.o_ref
  248.5 8.4 middle_forward.3
  256.9 12.6 %collective-permute-done.18 = bf16[256,2048]{1,0:T(8,128)(2,1)} collective-permute-done((bf16[256,2048]{1,0:T(8,128)(2,1)}, bf16[256,2048]{1,0:T(8,128)(2,1)}, u32[]{:S(2)}, u32[]{:S(2)}) %collective-permute-start.18) | collective-permute-done | bytes 1048608 | tf_op jit(solution)/shard_map/ppermute | solution.py:709
  284.4 9.4 collective-permute-done.20.dy1_ref
  293.8 46.9 %all-gather.9.cloned.1.call-done = bf16[4096,1024]{1,0:T(8,128)(2,1)} async-done(((bf16[1024,1024]{1,0:T(8,128)(2,1)}), bf16[4096,1024]{1,0:T(8,128)(2,1)}) %all-gather.9.cloned.1.call-update) | async-done | bytes 8388624 | tf_op jit(solution)/shard_map/all_gather | solution.py:857
  340.7 95.2 %gather_product.1 = (bf16[2048,2048]{1,0:T(8,128)(2,1)}, bf16[2048,2048]{1,0:T(8,128)(2,1)}, f32[2048,1024]{1,0:T(8,128)}, f32[2048,1024]{1,0:T(8,128)}, f32[204...) custom-call(bf16[512,2048]{1,0:T(8,128)(2,1)} %pad_maximum_fusion.1.b_ref, ...), custom_call_target="tpu_custom_call" | custom-call | flops 68719476736 | bytes 73400320 | tf_op jit(solution)/shard_map/gather_product/pallas_call | solution.py:656
  439.7 9.6 all_gather.19
  451.9 8.0 fusion.11
  460.0 16.5 %fusion.57 = f32[2048,1024]{1,0:T(8,128)} fusion(bf16[2048,2048]{1,0:T(8,128)(2,1)} %get-tuple-element.166, bf16[2048,1024]{1,0:T(8,128)(2,1)S(1)} %get-tuple-element.176.x1_ref), kind=kOutput, calls=%fused_computation.224 | convolution fusion | flops 8589934592 | bytes 20971520 | tf_op jit(solution)/shard_map/td,tf->df/dot_general | solution.py:704
  476.5 7.3 fusion.5
  483.8 13.2 %fusion.56 = f32[1024,2048]{1,0:T(8,128)S(1)} fusion(bf16[2048,1024]{1,0:T(8,128)(2,1)S(1)} %get-tuple-element.207.x1_ref, bf16[2048,2048]{1,0:T(8,128)(2,1)} %collective-permute-done.20.dy1_ref), kind=kOutput, calls=%fused_computation.223 | convolution fusion | flops 8589934592 | bytes 20971520 | tf_op jit(solution)/shard_map/tf,td->fd/dot_general | solution.py:704
  497.0 11.2 %add_convert_fusion.1 = bf16[1024,2048]{1,0:T(8,128)(2,1)} fusion(f32[1024,2048]{1,0:T(8,128)S(1)} %fusion.56, bf16[2048,1024]{1,0:T(8,128)(2,1)S(1)} %get-tuple-element.206.x0_ref, bf16[2048,2048]{1,0:T(8,128)(2,1)S(1)} %bitcast.220), kind=kOutput, calls=%fused_computation.19 | convolution fusion | flops 8594128896 | bytes 25165824 | tf_op jit(solution)/shard_map/tf,td->fd/dot_general | solution.py:704
  508.2 15.3 %add_convert_fusion = bf16[2048,1024]{1,0:T(8,128)(2,1)} fusion(f32[2048,1024]{1,0:T(8,128)} %fusion.57, bf16[2048,2048]{1,0:T(8,128)(2,1)} %get-tuple-element.165, bf16[2048,1024]{1,0:T(8,128)(2,1)} %get-tuple-element.175.x0_ref), kind=kOutput, calls=%fused_computation.18 | convolution fusion | flops 8594128896 | bytes 25165824 | tf_op jit(solution)/shard_map/td,tf->df/dot_general | solution.py:704
  523.6 90.8 %product_sum.3.db_ref = f32[512,2048]{1,0:T(8,128)} custom-call(bf16[2048,1024]{1,0:T(8,128)(2,1)} %get-tuple-element.175.x0_ref, bf16[2048,1024]{1,0:T(8,128)(2,1)} %copy-done.16, bf16[4,1024,1024]{2,1,0:T(8,128)(2,1)} %bitcast.243), custom_call_target="tpu_custom_call" | custom-call | flops 68719476736 | bytes 20971520 | tf_op jit(solution)/shard_map/product_sum/pallas_call | solution.py:498
  622.1 12.7 %middle_backward.2 = (f32[256,2048]{1,0:T(8,128)}, bf16[256,2048]{1,0:T(8,128)(2,1)}, bf16[8,256,256]{2,1,0:T(8,128)(2,1)}) custom-call(bf16[8,256,256]{2,1,0:T(8,128)(2,1)} %copy-done.5, f32[256,2048]{1,0:T(8,128)} %get-tuple-element.137.x1_ref, f32[512,2048]{1,0:T(8,128)} %product_sum.3.db_ref, bf16[256,2048]{1,0:T(8,128)(2,1)} %get-tuple-element.237.dy_ref, ...), custom_call_target="tpu_custom_call" | custom-call | flops 2147483648 | bytes 16777216 | tf_op jit(solution)/shard_map/middle_backward/pallas_call | solution.py:353
  634.8 4.0 all-to-all-start.3
  638.7 12.7 %middle_backward.3 = (f32[256,2048]{1,0:T(8,128)}, bf16[256,2048]{1,0:T(8,128)(2,1)}, bf16[8,256,256]{2,1,0:T(8,128)(2,1)}) custom-call(bf16[8,256,256]{2,1,0:T(8,128)(2,1)} %all-to-all-done.2.o_ref, f32[256,2048]{1,0:T(8,128)} %get-tuple-element.139.x1_ref, f32[512,2048]{1,0:T(8,128)} %product_sum.3.db_ref, bf16[256,2048]{1,0:T(8,128)(2,1)} %get-tuple-element.236.dy_ref, ...), custom_call_target="tpu_custom_call" | custom-call | flops 2147483648 | bytes 16777216 | tf_op jit(solution)/shard_map/middle_backward/pallas_call | solution.py:353
  651.4 8.3 convolution_convert_fusion
  659.7 4.2 all-to-all-start.4
  664.0 40.8 %attention_backward.2 = (bf16[2048,768]{1,0:T(8,128)(2,1)}, bf16[2048,768]{1,0:T(8,128)(2,1)}) custom-call(s32[10]{0:T(128)} %pad_add_fusion.4.span_ref, bf16[256,2048]{1,0:T(8,128)(2,1)} %get-tuple-element.172.refs_0_, bf16[256,2048]{1,0:T(8,128)(2,1)} %get-tuple-element.173.refs_1_, bf16[256,2048]{1,0:T(8,128)(2,1)} %get-tuple-element.174.refs_2_, ...), custom_call_target="tpu_custom_call" | custom-call | flops 21474836480 | bytes 20971520 | tf_op jit(solution)/shard_map/attention_backward/pallas_call | solution.py:269
  705.7 4.2 all-to-all-start.5
  709.9 36.6 %attention_backward.3 = (bf16[2048,768]{1,0:T(8,128)(2,1)}, bf16[2048,768]{1,0:T(8,128)(2,1)}) custom-call(s32[10]{0:T(128)} %pad_add_fusion.2.span_ref, bf16[256,2048]{1,0:T(8,128)(2,1)} %get-tuple-element.169.qT_ref, bf16[256,2048]{1,0:T(8,128)(2,1)} %get-tuple-element.170.kT_ref, ...), custom_call_target="tpu_custom_call", output_to_operand_aliasing={{0}: (9, {}), {1}: (10, {})} | custom-call | flops 21474836480 | bytes 20971520 | tf_op jit(solution)/shard_map/attention_backward/pallas_call | solution.py:269
  746.5 10.6 %fusion.58 = f32[2048,768]{1,0:T(8,128)S(1)} fusion(bf16[2048,2048]{1,0:T(8,128)(2,1)} %collective-permute-done.13, bf16[2048,768]{1,0:T(8,128)(2,1)} %get-tuple-element.203.x1_ref), kind=kOutput, calls=%fused_computation.225 | convolution fusion | flops 6442450944 | bytes 17825792 | tf_op jit(solution)/shard_map/td,tf->df/dot_general | solution.py:704
  757.1 10.9 %add_convert_fusion.2 = bf16[2048,768]{1,0:T(8,128)(2,1)} fusion(f32[2048,768]{1,0:T(8,128)S(1)} %fusion.58, bf16[2048,2048]{1,0:T(8,128)(2,1)} %constant_dynamic-update-slice_fusion.3, bf16[2048,768]{1,0:T(8,128)(2,1)S(1)} %copy-done.52), kind=kOutput, calls=%fused_computation.27 | convolution fusion | flops 6445596672 | bytes 20971520 | tf_op jit(solution)/shard_map/td,tf->df/dot_general | solution.py:704
  768.1 7.0 reduce-scatter.10.cloned.1.call-done
  775.1 3.6 fusion.18
  784.4 86.5 %product_sum.4 = f32[512,2048]{1,0:T(8,128)} custom-call(bf16[2048,768]{1,0:T(8,128)(2,1)} %get-tuple-element.202.x0_ref, bf16[2048,768]{1,0:T(8,128)(2,1)} %get-tuple-element.203.x1_ref, bf16[2048,768]{1,0:T(8,128)(2,1)} %all-gather.5.cloned.1.call-done.w_ref), custom_call_target="tpu_custom_call" | custom-call | flops 51539607552 | bytes 20971520 | tf_op jit(solution)/shard_map/product_sum/pallas_call | solution.py:498
  870.9 3.6 all-to-all-start.6
  875.2 90.0 %product_sum.5 = f32[512,2048]{1,0:T(8,128)} custom-call(bf16[2048,1024]{1,0:T(8,128)(2,1)} %copy-done.15, bf16[2048,1024]{1,0:T(8,128)(2,1)} %copy-done.14, bf16[4,1024,1024]{2,1,0:T(8,128)(2,1)} %bitcast.244), custom_call_target="tpu_custom_call" | custom-call | flops 68719476736 | bytes 20971520 | tf_op jit(solution)/shard_map/product_sum/pallas_call | solution.py:498
  965.2 3.3 fusion.49
  970.9 2.8 maximum_add_fusion.1
  977.2 4.1 slice_reduce_fusion
  (318 shorter events, 107.9 us)
Async XLA Ops:
  7.2 124.5 %all-gather.5.cloned.1.call-start = ((), (), s32[]{:S(2)}) async-start(), calls=%async_computation.12 | async-start | bytes 3932160 | tf_op jit(solution)/shard_map/all_gather | solution.py:832
  9.6 17.5 %copy-start = (bf16[2,256,2048]{2,1,0:T(8,128)(2,1)S(1)}, bf16[2,256,2048]{2,1,0:T(8,128)(2,1)}, u32[]{:S(2)}) copy-start(bf16[2,256,2048]{2,1,0:T(8,128)(2,1)} %param.17) | copy-start | bytes 6291460
  11.4 5.4 collective-permute-start
  12.0 7.5 collective-permute-start.1
  14.6 5.5 collective-permute-start.2
  14.8 5.3 collective-permute-start.3
  16.6 9.4 collective-permute-start.4
  16.8 9.2 collective-permute-start.5
  19.5 6.6 collective-permute-start.6
  27.0 163.6 %all-gather.7.cloned.1.call-start = ((), (), s32[]{:S(2)}) async-start(), calls=%async_computation.13 | async-start | bytes 8650752 | tf_op jit(solution)/shard_map/all_gather | solution.py:842
  28.2 31.4 %copy-start.11 = (bf16[64,8192]{1,0:T(8,128)(2,1)S(1)}, bf16[64,8192]{1,0:T(8,128)(2,1)}, u32[]{:S(2)}) copy-start(bf16[64,8192]{1,0:T(8,128)(2,1)} %param.23) | copy-start | bytes 3145732
  32.0 26.3 %collective-permute-start.7 = (bf16[256,2048]{1,0:T(8,128)(2,1)}, bf16[256,2048]{1,0:T(8,128)(2,1)}, u32[]{:S(2)}, u32[]{:S(2)}) collective-permute-start(bf16[256,2048]{1,0:T(8,128)(2,1)} %get-tuple-element.246), channel_id=1, source_target_pairs={{0,2},{1,3},{2,0},{3,1},{4,6},{5,7},{6,4},{7,5},{8,10},{9,11},{10,... | collective-permute-start | bytes 3145736 | tf_op jit(solution)/shard_map/ppermute | solution.py:709
  34.9 52.3 %collective-permute-start.8 = (bf16[256,2048]{1,0:T(8,128)(2,1)}, bf16[256,2048]{1,0:T(8,128)(2,1)}, u32[]{:S(2)}, u32[]{:S(2)}) collective-permute-start(bf16[256,2048]{1,0:T(8,128)(2,1)} %get-tuple-element.246), channel_id=1, source_target_pairs={{0,4},{1,5},{2,6},{3,7},{4,0},{5,1},{6,2},{7,3},{8,12},{9,13},{10,... | collective-permute-start | bytes 3145736 | tf_op jit(solution)/shard_map/ppermute | solution.py:709
  36.2 80.8 %collective-permute-start.10 = (bf16[256,2048]{1,0:T(8,128)(2,1)}, bf16[256,2048]{1,0:T(8,128)(2,1)}, u32[]{:S(2)}, u32[]{:S(2)}) collective-permute-start(bf16[256,2048]{1,0:T(8,128)(2,1)} %get-tuple-element.244), channel_id=1, source_target_pairs={{0,2},{1,3},{2,0},{3,1},{4,6},{5,7},{6,4},{7,5},{8,10},{9,11},{10,... | collective-permute-start | bytes 3145736 | tf_op jit(solution)/shard_map/ppermute | solution.py:709
  36.8 48.0 %collective-permute-start.11 = (bf16[256,2048]{1,0:T(8,128)(2,1)}, bf16[256,2048]{1,0:T(8,128)(2,1)}, u32[]{:S(2)}, u32[]{:S(2)}) collective-permute-start(bf16[256,2048]{1,0:T(8,128)(2,1)} %get-tuple-element.244), channel_id=1, source_target_pairs={{0,4},{1,5},{2,6},{3,7},{4,0},{5,1},{6,2},{7,3},{8,12},{9,13},{10,... | collective-permute-start | bytes 3145736 | tf_op jit(solution)/shard_map/ppermute | solution.py:709
  37.5 22.6 %copy-start.46 = (f32[64]{0:T(128)}, f32[64]{0:T(128)S(1)}, u32[]{:S(2)}) copy-start(f32[64]{0:T(128)S(1)} %convert_element_type.150) | copy-start | bytes 772
  58.4 55.4 %collective-permute-start.9 = (bf16[256,2048]{1,0:T(8,128)(2,1)}, bf16[256,2048]{1,0:T(8,128)(2,1)}, u32[]{:S(2)}, u32[]{:S(2)}) collective-permute-start(bf16[256,2048]{1,0:T(8,128)(2,1)} %collective-permute-done.7), channel_id=1, source_target_pairs={{0,4},{1,5},{2,6},{3,7},{4,0},{5,1},{6,2},{7,3},{8,12},{9,13},{10,... | collective-permute-start | bytes 3145736 | tf_op jit(solution)/shard_map/ppermute | solution.py:709
  62.1 60.7 %all-to-all-start = ((bf16[8,64,1024]{2,1,0:T(8,128)(2,1)}), bf16[8,64,1024]{2,1,0:T(8,128)(2,1)S(1)}, u32[]{:S(2)}, u32[]{:S(2)}) async-start(bf16[8,64,1024]{2,1,0:T(8,128)(2,1)} %reshape.342), calls=%async_computation | async-start | bytes 2097152 | tf_op jit(solution)/shard_map/all_to_all | solution.py:834
  65.6 275.1 %all-gather.9.cloned.1.call-start = ((), (), s32[]{:S(2)}) async-start(), calls=%async_computation.19 | async-start | bytes 10485760 | tf_op jit(solution)/shard_map/all_gather | solution.py:857
  66.0 50.1 %copy-start.4 = (bf16[512,2048]{1,0:T(8,128)(2,1)S(1)}, bf16[512,2048]{1,0:T(8,128)(2,1)}, u32[]{:S(2)}) copy-start(bf16[512,2048]{1,0:T(8,128)(2,1)} %copy-done.3) | copy-start | bytes 6291460
  84.8 37.0 %collective-permute-start.12 = (bf16[256,2048]{1,0:T(8,128)(2,1)}, bf16[256,2048]{1,0:T(8,128)(2,1)S(1)}, u32[]{:S(2)}, u32[]{:S(2)}) collective-permute-start(bf16[256,2048]{1,0:T(8,128)(2,1)} %collective-permute-done.11), channel_id=1, source_target_pairs={{0,2},{1,3},{2,0},{3,1},{4,6},{5,7},{6,4},{7,5},{8,10},{9,11},{10,... | collective-permute-start | bytes 3145736 | tf_op jit(solution)/shard_map/ppermute | solution.py:709
  122.8 22.0 %collective-permute-start.13 = (bf16[2048,2048]{1,0:T(8,128)(2,1)}, bf16[2048,2048]{1,0:T(8,128)(2,1)}, u32[]{:S(2)}, u32[]{:S(2)}) collective-permute-start(bf16[2048,2048]{1,0:T(8,128)(2,1)} %constant_dynamic-update-slice_fusion.3), channel_id=1, source_target_pairs={{0,1},{1,0},{2,3},{3,2},{4,5},{5,4},{6,7},{7,6},{8,9},{9,8},{10,11... | collective-permute-start | bytes 25165832 | tf_op jit(solution)/shard_map/ppermute | solution.py:709
  157.4 33.1 %collective-permute-start.14 = (bf16[256,2048]{1,0:T(8,128)(2,1)}, bf16[256,2048]{1,0:T(8,128)(2,1)}, u32[]{:S(2)}, u32[]{:S(2)}) collective-permute-start(bf16[256,2048]{1,0:T(8,128)(2,1)} %get-tuple-element.150), channel_id=1, source_target_pairs={{0,2},{1,3},{2,0},{3,1},{4,6},{5,7},{6,4},{7,5},{8,10},{9,11},{10,... | collective-permute-start | bytes 3145736 | tf_op jit(solution)/shard_map/ppermute | solution.py:709
  158.4 32.2 %collective-permute-start.15 = (bf16[256,2048]{1,0:T(8,128)(2,1)}, bf16[256,2048]{1,0:T(8,128)(2,1)}, u32[]{:S(2)}, u32[]{:S(2)}) collective-permute-start(bf16[256,2048]{1,0:T(8,128)(2,1)} %get-tuple-element.154), channel_id=1, source_target_pairs={{0,4},{1,5},{2,6},{3,7},{4,0},{5,1},{6,2},{7,3},{8,12},{9,13},{10,... | collective-permute-start | bytes 3145736 | tf_op jit(solution)/shard_map/ppermute | solution.py:709
  190.6 37.7 %collective-permute-start.16 = (bf16[256,2048]{1,0:T(8,128)(2,1)}, bf16[256,2048]{1,0:T(8,128)(2,1)}, u32[]{:S(2)}, u32[]{:S(2)}) collective-permute-start(bf16[256,2048]{1,0:T(8,128)(2,1)} %get-tuple-element.150), channel_id=1, source_target_pairs={{0,4},{1,5},{2,6},{3,7},{4,0},{5,1},{6,2},{7,3},{8,12},{9,13},{10,... | collective-permute-start | bytes 3145736 | tf_op jit(solution)/shard_map/ppermute | solution.py:709
  191.6 36.6 %collective-permute-start.17 = (bf16[256,2048]{1,0:T(8,128)(2,1)}, bf16[256,2048]{1,0:T(8,128)(2,1)}, u32[]{:S(2)}, u32[]{:S(2)}) collective-permute-start(bf16[256,2048]{1,0:T(8,128)(2,1)} %get-tuple-element.154), channel_id=1, source_target_pairs={{0,2},{1,3},{2,0},{3,1},{4,6},{5,7},{6,4},{7,5},{8,10},{9,11},{10,... | collective-permute-start | bytes 3145736 | tf_op jit(solution)/shard_map/ppermute | solution.py:709
  192.7 35.5 %all-to-all-start.1 = ((bf16[8,256,256]{2,1,0:T(8,128)(2,1)}), bf16[8,256,256]{2,1,0:T(8,128)(2,1)S(1)}, u32[]{:S(2)}, u32[]{:S(2)}) async-start(bf16[8,256,256]{2,1,0:T(8,128)(2,1)} %bitcast.208), calls=%async_computation.1 | async-start | bytes 2097152 | tf_op jit(solution)/shard_map/all_to_all | solution.py:865
  228.3 20.2 %all-to-all-start.2 = ((bf16[8,256,256]{2,1,0:T(8,128)(2,1)}), bf16[8,256,256]{2,1,0:T(8,128)(2,1)}, u32[]{:S(2)}, u32[]{:S(2)}) async-start(bf16[8,256,256]{2,1,0:T(8,128)(2,1)} %bitcast.211), calls=%async_computation.2 | async-start | bytes 2097152 | tf_op jit(solution)/shard_map/all_to_all | solution.py:865
  232.6 381.9 %reduce-scatter.6.cloned.1.call-start = ((), (), s32[]{:S(2)}) async-start(), calls=%async_computation.14 | async-start | bytes 5242880 | tf_op jit(solution)/shard_map/reduce_scatter | solution.py:902
  232.6 36.9 %collective-permute-start.18 = (bf16[256,2048]{1,0:T(8,128)(2,1)}, bf16[256,2048]{1,0:T(8,128)(2,1)}, u32[]{:S(2)}, u32[]{:S(2)}) collective-permute-start(bf16[256,2048]{1,0:T(8,128)(2,1)} %collective-permute-done.14), channel_id=1, source_target_pairs={{0,4},{1,5},{2,6},{3,7},{4,0},{5,1},{6,2},{7,3},{8,12},{9,13},{10,... | collective-permute-start | bytes 3145736 | tf_op jit(solution)/shard_map/ppermute | solution.py:709
  234.5 35.1 %collective-permute-start.19 = (bf16[256,2048]{1,0:T(8,128)(2,1)}, bf16[256,2048]{1,0:T(8,128)(2,1)}, u32[]{:S(2)}, u32[]{:S(2)}) collective-permute-start(bf16[256,2048]{1,0:T(8,128)(2,1)} %collective-permute-done.15), channel_id=1, source_target_pairs={{0,2},{1,3},{2,0},{3,1},{4,6},{5,7},{6,4},{7,5},{8,10},{9,11},{10,... | collective-permute-start | bytes 3145736 | tf_op jit(solution)/shard_map/ppermute | solution.py:709
  280.4 13.4 %collective-permute-start.20 = (bf16[2048,2048]{1,0:T(8,128)(2,1)S(1)}, bf16[2048,2048]{1,0:T(8,128)(2,1)}, u32[]{:S(2)}, u32[]{:S(2)}) collective-permute-start(bf16[2048,2048]{1,0:T(8,128)(2,1)S(1)} %constant_dynamic-update-slice_fusion.11.dy0_ref), channel_id=1, source_target_pairs={{0,1},{1,0},{2,3},{3,2},{4,5},{5,4},{6,7},{7,6},{8,9},{9,8},{10,11... | collective-permute-start | bytes 25165832 | tf_op jit(solution)/shard_map/ppermute | solution.py:709
  459.9 16.6 %copy-start.16 = (bf16[2048,1024]{1,0:T(8,128)(2,1)}, bf16[2048,1024]{1,0:T(8,128)(2,1)S(1)}, u32[]{:S(2)}) copy-start(bf16[2048,1024]{1,0:T(8,128)(2,1)S(1)} %get-tuple-element.176.x1_ref) | copy-start | bytes 12582916
  459.9 23.9 %copy-start.14 = (bf16[2048,1024]{1,0:T(8,128)(2,1)}, bf16[2048,1024]{1,0:T(8,128)(2,1)S(1)}, u32[]{:S(2)}) copy-start(bf16[2048,1024]{1,0:T(8,128)(2,1)S(1)} %get-tuple-element.207.x1_ref) | copy-start | bytes 12582916
  459.9 16.5 %slice-start = ((s8[8388608]{0:T(1024)(128)(4,1)}), s8[4194304]{0:T(1024)(128)(4,1)S(1)}, s32[]{:S(2)}) async-start(s8[8388608]{0:T(1024)(128)(4,1)} %bitcast.178), calls=%async_computation.20 | async-start | bytes 8388608
  459.9 16.5 %slice-start.2 = ((s8[8388608]{0:T(1024)(128)(4,1)}), s8[4194304]{0:T(1024)(128)(4,1)S(1)}, s32[]{:S(2)}) async-start(s8[8388608]{0:T(1024)(128)(4,1)} %bitcast.180), calls=%async_computation.22 | async-start | bytes 8388608
  476.5 20.5 %slice-start.4 = ((s8[8388608]{0:T(1024)(128)(4,1)}), s8[4194304]{0:T(1024)(128)(4,1)S(1)}, s32[]{:S(2)}) async-start(s8[8388608]{0:T(1024)(128)(4,1)} %bitcast.219), calls=%async_computation.24 | async-start | bytes 8388608
  523.5 181.2 %reduce-scatter.8.cloned.1.call-start = ((), (), s32[]{:S(2)}) async-start(), calls=%async_computation.15 | async-start | bytes 5242880 | tf_op jit(solution)/shard_map/reduce_scatter | solution.py:906
  634.8 24.9 %all-to-all-start.3 = ((bf16[8,256,256]{2,1,0:T(8,128)(2,1)}), bf16[8,256,256]{2,1,0:T(8,128)(2,1)S(1)}, u32[]{:S(2)}, u32[]{:S(2)}) async-start(bf16[8,256,256]{2,1,0:T(8,128)(2,1)} %get-tuple-element.180), calls=%async_computation.4 | async-start | bytes 2097152 | tf_op jit(solution)/shard_map/all_to_all | solution.py:909
  659.7 45.0 %all-to-all-start.4 = ((bf16[8,256,256]{2,1,0:T(8,128)(2,1)}), bf16[8,256,256]{2,1,0:T(8,128)(2,1)S(1)}, u32[]{:S(2)}, u32[]{:S(2)}) async-start(bf16[8,256,256]{2,1,0:T(8,128)(2,1)} %get-tuple-element.190), calls=%async_computation.5 | async-start | bytes 2097152 | tf_op jit(solution)/shard_map/all_to_all | solution.py:909
  663.9 111.2 %reduce-scatter.10.cloned.1.call-start = ((), (), s32[]{:S(2)}) async-start(), calls=%async_computation.16 | async-start | bytes 9437184 | tf_op jit(solution)/shard_map/reduce_scatter | solution.py:915
  705.7 62.3 %all-to-all-start.5 = ((bf16[8,64,1024]{2,1,0:T(8,128)(2,1)}), bf16[8,64,1024]{2,1,0:T(8,128)(2,1)S(1)}, u32[]{:S(2)}, u32[]{:S(2)}) async-start(bf16[8,64,1024]{2,1,0:T(8,128)(2,1)} %bitcast.47), calls=%async_computation.8 | async-start | bytes 2097152 | tf_op jit(solution)/shard_map/all_to_all | solution.py:916
  709.9 161.0 %reduce-scatter.12.cloned.1.call-start = ((), (), s32[]{:S(2)}) async-start(), calls=%async_computation.17 | async-start | bytes 3932160 | tf_op jit(solution)/shard_map/reduce_scatter | solution.py:922
  870.9 102.8 %all-to-all-start.6 = ((bf16[8,64,768]{2,1,0:T(8,128)(2,1)}), bf16[8,64,768]{2,1,0:T(8,128)(2,1)S(1)}, u32[]{:S(2)}, u32[]{:S(2)}) async-start(bf16[8,64,768]{2,1,0:T(8,128)(2,1)} %bitcast.218), calls=%async_computation.11 | async-start | bytes 1572864 | tf_op jit(solution)/shard_map/all_to_all | solution.py:927
  874.4 99.3 %reduce-scatter.14.cloned.1.call-start = ((), (), s32[]{:S(2)}) async-start(), calls=%async_computation.18 | async-start | bytes 1310720 | tf_op jit(solution)/shard_map/reduce_scatter | solution.py:925
  875.2 90.0 %copy-start.1 = (bf16[2,256,2048]{2,1,0:T(8,128)(2,1)S(1)}, bf16[2,256,2048]{2,1,0:T(8,128)(2,1)}, u32[]{:S(2)}) copy-start(bf16[2,256,2048]{2,1,0:T(8,128)(2,1)} %param.17) | copy-start | bytes 6291460
  875.2 90.0 %copy-start.36 = (f32[1,2,2,128]{3,1,2,0:T(2,128)S(1)}, f32[1,2,2,128]{3,1,2,0:T(2,128)}, u32[]{:S(2)}) copy-start(f32[1,2,2,128]{3,1,2,0:T(2,128)} %copy-done.35) | copy-start | bytes 6148
  875.2 90.0 %copy-start.38 = (f32[1,2,2,128]{3,1,2,0:T(2,128)S(1)}, f32[1,2,2,128]{3,1,2,0:T(2,128)}, u32[]{:S(2)}) copy-start(f32[1,2,2,128]{3,1,2,0:T(2,128)} %copy-done.37) | copy-start | bytes 6148
  (47 other events, 281.4 us)
Sparse Core Ops, SparseCore 0:
  27.1 64.5 all-gather.4
  95.2 77.6 all-gather.6
  190.7 149.9 all-gather.8
  523.7 74.0 reduce-scatter.5
  614.6 73.9 reduce-scatter.7
  704.9 70.1 reduce-scatter.9
  777.5 60.2 reduce-scatter.11
  877.7 28.5 reduce-scatter.13

commit v6 on v5

--- a/solution.py
+++ b/solution.py
@@ -846,15 +846,15 @@
     span = [span_of(lowest[r], blk, core, place) for r in range(rows)]
     qkv0 = dot(w_qkv, xh0, "df,td->ft")
     qkv1 = dot(w_qkv, xh1, "df,td->ft")
-    qkv0, qkv1, cot = lax.optimization_barrier((qkv0, qkv1, out_cotangent))
+    qkv0, qkv1, cot, out_all = lax.optimization_barrier((qkv0, qkv1, out_cotangent, out_all))
+    ffn_all = lax.all_gather(after(ffn_local, out_all), "row", axis=0, tiled=False)
     dy_held = gather_step(gather_start(cot), 0)
     dy_steps = gather_steps()
     saved, o = [], []
     for r in range(rows):
         o_row, *kept = attention_forward(r, qkv0, qkv1, table[r], lowest[r], span[r], blk, local_len)
         if r == 0:
-            o_row, kept, qkv0, qkv1, dy_held, out_all = lax.optimization_barrier((o_row, kept, qkv0, qkv1, dy_held, out_all))
-            ffn_all = lax.all_gather(after(ffn_local, out_all), "row", axis=0, tiled=False)
+            o_row, kept, qkv0, qkv1, dy_held = lax.optimization_barrier((o_row, kept, qkv0, qkv1, dy_held))
             dy_held = gather_own(dy_held, 1)
         if r == rows - 1:
             o_row, o, dy_held = lax.optimization_barrier((o_row, o, dy_held))

time: 1000 us -> 991 us (level)
  waiting for transfers between devices: 152 us -> 130 us
  Pallas kernels: 536 us -> 546 us
    all_gather x1, waiting for transfers between devices: 46.9 us -> 16.7 us  [body(): lax.all_gather(after(ffn_local, out_all), 'row', axis=0, tiled=False)]
    all_gather x1, waiting for transfers between devices: 0.02 us -> 18.2 us  [body(): lax.all_gather(scaled(w_out, gain_attn_sub), BOTH, axis=0, tiled=True)]
    unnamed x150 -> x148, local copies, waits for them, and re-layouts: 33.1 us -> 31.3 us
  transfers between devices with their start and end apart: 36 -> 36, of which waited for: 11 -> 12; matrix products, arithmetic and copies ran while one was open for 13% -> 13% of each run, Pallas kernels for 44% -> 46%
where the time goes in v6:
time: 991 us; the launch traced here: 985 us
  Pallas kernels  546 us (55%)
  waiting for transfers between devices  130 us (13%)
  matrix products  111 us (11%)
  local copies, waits for them, and re-layouts  66.7 us (7%)
  other arithmetic  53.2 us (5%)
  starting transfers between devices  52.4 us (5%)
  between operations  15.9 us (2%)
    pallas_call x3, Pallas kernels, product_sum(): pl.pallas_call(functools.partial(product_sum_kernel, n, rows, min(512, wi...  268 us
    dot_general x9, matrix products, dot(): return jnp.einsum(spec, a, b, preferred_element_type=f32).astype(kind)  111 us
    pallas_call x1, Pallas kernels, gather_product(): pl.pallas_call(functools.partial(gather_product_kernel, n, rows, min(256,...  95.2 us
    ppermute x21, waiting for transfers between devices, swap(): return lax.ppermute(x, 'ctx', [(i, i ^ bit) for i in range(n)])  88.4 us
    pallas_call x2, Pallas kernels, attention_backward(): pl.pallas_call(call, out_shape=(whole, whole), grid_spec=pltpu.PrefetchSc...  83.2 us
    pallas_call x2, Pallas kernels, attention_forward(): pl.pallas_call(functools.partial(forward_kernel, nh, blk, unit), out_shap...  57.9 us
    unnamed x148, local copies, waits for them, and re-layouts  31.3 us
    pallas_call x2, Pallas kernels, middle_backward(): pl.pallas_call(middle_backward_kernel, out_shape=(sds((size, width), f32)...  25.3 us
  transfers between devices with their start and end apart: 36, of which 12 were waited for; matrix products, arithmetic and copies ran while one was open for 13% of the time, Pallas kernels for 46%

profile of v6, /device:TPU:0, one launch (start us, length us, event | category | flops | bytes accessed | tf_op | source)
XLA Modules:
  0.0 985.3 jit_solution(16132374749092911841)
XLA Ops:
  12.0 2.6 collective-permute-start.1
  16.8 2.6 collective-permute-start.5
  20.1 5.9 collective-permute-done.4
  35.9 22.3 %collective-permute-done.7 = bf16[256,2048]{1,0:T(8,128)(2,1)} collective-permute-done((bf16[256,2048]{1,0:T(8,128)(2,1)}, bf16[256,2048]{1,0:T(8,128)(2,1)}, u32[]{:S(2)}, u32[]{:S(2)}) %collective-permute-start.7) | collective-permute-done | bytes 1048608 | tf_op jit(solution)/shard_map/ppermute | solution.py:709
  61.8 3.6 all-to-all-start
  68.2 13.8 %collective-permute-done.11 = bf16[256,2048]{1,0:T(8,128)(2,1)} collective-permute-done((bf16[256,2048]{1,0:T(8,128)(2,1)}, bf16[256,2048]{1,0:T(8,128)(2,1)}, u32[]{:S(2)}, u32[]{:S(2)}) %collective-permute-start.11) | collective-permute-done | bytes 1048608 | tf_op jit(solution)/shard_map/ppermute | solution.py:709
  82.1 3.2 collective-permute-start.12
  87.6 24.4 %collective-permute-done.9 = bf16[256,2048]{1,0:T(8,128)(2,1)} collective-permute-done((bf16[256,2048]{1,0:T(8,128)(2,1)}, bf16[256,2048]{1,0:T(8,128)(2,1)}, u32[]{:S(2)}, u32[]{:S(2)}) %collective-permute-start.9) | collective-permute-done | bytes 1048608 | tf_op jit(solution)/shard_map/ppermute | solution.py:709
  125.3 3.1 power_multiply_fusion.3
  130.1 13.3 %fusion.54.q0_ref.k0_ref.v0_ref = f32[768,2048]{1,0:T(8,128)} fusion(bf16[2048,768]{1,0:T(8,128)(2,1)} %all-gather.5.cloned.1.call-done.w_ref, bf16[2048,2048]{1,0:T(8,128)(2,1)} %constant_dynamic-update-slice_fusion.3), kind=kOutput, calls=%fused_computation.221 | convolution fusion | flops 6442450944 | bytes 17825792 | tf_op jit(solution)/shard_map/df,td->ft/dot_general | solution.py:704
  143.4 11.3 %fusion.55.q1_ref.k1_ref.v1_ref = f32[768,2048]{1,0:T(8,128)} fusion(bf16[2048,768]{1,0:T(8,128)(2,1)S(1)} %copy-done.47, bf16[2048,2048]{1,0:T(8,128)(2,1)} %collective-permute-done.13), kind=kOutput, calls=%fused_computation.222 | convolution fusion | flops 6442450944 | bytes 17825792 | tf_op jit(solution)/shard_map/df,td->ft/dot_general | solution.py:704
  154.7 18.2 %all-gather.7.cloned.1.call-done.w_ref = bf16[2048,2048]{1,0:T(8,128)(2,1)} async-done(((bf16[64,2048]{1,0:T(8,128)(2,1)}), bf16[2048,2048]{1,0:T(8,128)(2,1)}) %all-gather.7.cloned.1.call-update) | async-done | bytes 8388624 | tf_op jit(solution)/shard_map/all_gather | solution.py:842
  172.9 3.3 slice_bitcast_fusion.6
  180.3 28.8 %attention_forward.2 = (bf16[2048,256]{1,0:T(8,128)(2,1)}, f32[256,2048]{1,0:T(8,128)}, f32[4,2048]{1,0:T(4,128)}, bf16[256,2048]{1,0:T(8,128)(2,1)}, bf16[256,2...) custom-call(s32[10]{0:T(128)} %pad_add_fusion.4.span_ref, f32[768,2048]{1,0:T(8,128)} %fusion.54.q0_ref.k0_ref.v0_ref, ...), custom_call_target="tpu_custom_call" | custom-call | flops 8589934592 | bytes 10485760 | tf_op jit(solution)/shard_map/attention_forward/pallas_call | solution.py:234
  211.2 3.7 all-to-all-start.1
  215.7 29.1 %attention_forward.3 = (bf16[2048,256]{1,0:T(8,128)(2,1)}, f32[256,2048]{1,0:T(8,128)}, f32[4,2048]{1,0:T(4,128)}, bf16[256,2048]{1,0:T(8,128)(2,1)}, bf16[256,2...) custom-call(s32[10]{0:T(128)} %pad_add_fusion.2.span_ref, f32[768,2048]{1,0:T(8,128)} %fusion.54.q0_ref.k0_ref.v0_ref, ...), custom_call_target="tpu_custom_call" | custom-call | flops 8589934592 | bytes 10485760 | tf_op jit(solution)/shard_map/attention_forward/pallas_call | solution.py:234
  246.5 4.2 all-to-all-start.2
  255.7 8.5 middle_forward.2
  266.7 8.5 middle_forward.3
  275.2 12.5 %collective-permute-done.18 = bf16[256,2048]{1,0:T(8,128)(2,1)} collective-permute-done((bf16[256,2048]{1,0:T(8,128)(2,1)}, bf16[256,2048]{1,0:T(8,128)(2,1)}, u32[]{:S(2)}, u32[]{:S(2)}) %collective-permute-start.18) | collective-permute-done | bytes 1048608 | tf_op jit(solution)/shard_map/ppermute | solution.py:709
  302.6 9.4 collective-permute-done.20.dy1_ref
  312.0 16.7 %all-gather.9.cloned.1.call-done = bf16[4096,1024]{1,0:T(8,128)(2,1)} async-done(((bf16[1024,1024]{1,0:T(8,128)(2,1)}), bf16[4096,1024]{1,0:T(8,128)(2,1)}) %all-gather.9.cloned.1.call-update) | async-done | bytes 8388624 | tf_op jit(solution)/shard_map/all_gather | solution.py:850
  328.7 95.2 %gather_product.1 = (bf16[2048,2048]{1,0:T(8,128)(2,1)}, bf16[2048,2048]{1,0:T(8,128)(2,1)}, f32[2048,1024]{1,0:T(8,128)}, f32[2048,1024]{1,0:T(8,128)}, f32[204...) custom-call(bf16[512,2048]{1,0:T(8,128)(2,1)} %pad_maximum_fusion.1.b_ref, ...), custom_call_target="tpu_custom_call" | custom-call | flops 68719476736 | bytes 73400320 | tf_op jit(solution)/shard_map/gather_product/pallas_call | solution.py:656
  427.6 9.7 all_gather.19
  439.9 8.0 fusion.11
  447.9 16.4 %fusion.57 = f32[2048,1024]{1,0:T(8,128)} fusion(bf16[2048,2048]{1,0:T(8,128)(2,1)} %get-tuple-element.166, bf16[2048,1024]{1,0:T(8,128)(2,1)S(1)} %get-tuple-element.176.x1_ref), kind=kOutput, calls=%fused_computation.224 | convolution fusion | flops 8589934592 | bytes 20971520 | tf_op jit(solution)/shard_map/td,tf->df/dot_general | solution.py:704
  464.4 7.3 fusion.5
  471.7 13.2 %fusion.56 = f32[1024,2048]{1,0:T(8,128)S(1)} fusion(bf16[2048,1024]{1,0:T(8,128)(2,1)S(1)} %get-tuple-element.207.x1_ref, bf16[2048,2048]{1,0:T(8,128)(2,1)} %collective-permute-done.20.dy1_ref), kind=kOutput, calls=%fused_computation.223 | convolution fusion | flops 8589934592 | bytes 20971520 | tf_op jit(solution)/shard_map/tf,td->fd/dot_general | solution.py:704
  484.9 11.2 %add_convert_fusion.1 = bf16[1024,2048]{1,0:T(8,128)(2,1)} fusion(f32[1024,2048]{1,0:T(8,128)S(1)} %fusion.56, bf16[2048,1024]{1,0:T(8,128)(2,1)S(1)} %get-tuple-element.206.x0_ref, bf16[2048,2048]{1,0:T(8,128)(2,1)S(1)} %bitcast.220), kind=kOutput, calls=%fused_computation.19 | convolution fusion | flops 8594128896 | bytes 25165824 | tf_op jit(solution)/shard_map/tf,td->fd/dot_general | solution.py:704
  496.1 15.3 %add_convert_fusion = bf16[2048,1024]{1,0:T(8,128)(2,1)} fusion(f32[2048,1024]{1,0:T(8,128)} %fusion.57, bf16[2048,2048]{1,0:T(8,128)(2,1)} %get-tuple-element.165, bf16[2048,1024]{1,0:T(8,128)(2,1)} %get-tuple-element.175.x0_ref), kind=kOutput, calls=%fused_computation.18 | convolution fusion | flops 8594128896 | bytes 25165824 | tf_op jit(solution)/shard_map/td,tf->df/dot_general | solution.py:704
  511.5 90.8 %product_sum.3.db_ref = f32[512,2048]{1,0:T(8,128)} custom-call(bf16[2048,1024]{1,0:T(8,128)(2,1)} %get-tuple-element.175.x0_ref, bf16[2048,1024]{1,0:T(8,128)(2,1)} %copy-done.15, bf16[4,1024,1024]{2,1,0:T(8,128)(2,1)} %bitcast.243), custom_call_target="tpu_custom_call" | custom-call | flops 68719476736 | bytes 20971520 | tf_op jit(solution)/shard_map/product_sum/pallas_call | solution.py:498
  610.0 12.7 %middle_backward.2 = (f32[256,2048]{1,0:T(8,128)}, bf16[256,2048]{1,0:T(8,128)(2,1)}, bf16[8,256,256]{2,1,0:T(8,128)(2,1)}) custom-call(bf16[8,256,256]{2,1,0:T(8,128)(2,1)} %copy-done.5, f32[256,2048]{1,0:T(8,128)} %get-tuple-element.137.x1_ref, f32[512,2048]{1,0:T(8,128)} %product_sum.3.db_ref, bf16[256,2048]{1,0:T(8,128)(2,1)} %get-tuple-element.237.dy_ref, ...), custom_call_target="tpu_custom_call" | custom-call | flops 2147483648 | bytes 16777216 | tf_op jit(solution)/shard_map/middle_backward/pallas_call | solution.py:353
  622.7 4.0 all-to-all-start.3
  626.7 12.6 %middle_backward.3 = (f32[256,2048]{1,0:T(8,128)}, bf16[256,2048]{1,0:T(8,128)(2,1)}, bf16[8,256,256]{2,1,0:T(8,128)(2,1)}) custom-call(bf16[8,256,256]{2,1,0:T(8,128)(2,1)} %all-to-all-done.2.o_ref, f32[256,2048]{1,0:T(8,128)} %get-tuple-element.139.x1_ref, f32[512,2048]{1,0:T(8,128)} %product_sum.3.db_ref, bf16[256,2048]{1,0:T(8,128)(2,1)} %get-tuple-element.236.dy_ref, ...), custom_call_target="tpu_custom_call" | custom-call | flops 2147483648 | bytes 16777216 | tf_op jit(solution)/shard_map/middle_backward/pallas_call | solution.py:353
  639.3 8.3 convolution_convert_fusion
  647.6 4.2 all-to-all-start.4
  651.9 40.8 %attention_backward.2 = (bf16[2048,768]{1,0:T(8,128)(2,1)}, bf16[2048,768]{1,0:T(8,128)(2,1)}) custom-call(s32[10]{0:T(128)} %pad_add_fusion.4.span_ref, bf16[256,2048]{1,0:T(8,128)(2,1)} %get-tuple-element.172.refs_0_, bf16[256,2048]{1,0:T(8,128)(2,1)} %get-tuple-element.173.refs_1_, bf16[256,2048]{1,0:T(8,128)(2,1)} %get-tuple-element.174.refs_2_, ...), custom_call_target="tpu_custom_call" | custom-call | flops 21474836480 | bytes 20971520 | tf_op jit(solution)/shard_map/attention_backward/pallas_call | solution.py:269
  693.6 4.2 all-to-all-start.5
  697.8 42.4 %attention_backward.3 = (bf16[2048,768]{1,0:T(8,128)(2,1)}, bf16[2048,768]{1,0:T(8,128)(2,1)}) custom-call(s32[10]{0:T(128)} %pad_add_fusion.2.span_ref, bf16[256,2048]{1,0:T(8,128)(2,1)} %get-tuple-element.169.qT_ref, bf16[256,2048]{1,0:T(8,128)(2,1)} %get-tuple-element.170.kT_ref, ...), custom_call_target="tpu_custom_call", output_to_operand_aliasing={{0}: (9, {}), {1}: (10, {})} | custom-call | flops 21474836480 | bytes 20971520 | tf_op jit(solution)/shard_map/attention_backward/pallas_call | solution.py:269
  740.2 10.6 %fusion.58 = f32[2048,768]{1,0:T(8,128)S(1)} fusion(bf16[2048,2048]{1,0:T(8,128)(2,1)} %collective-permute-done.13, bf16[2048,768]{1,0:T(8,128)(2,1)} %get-tuple-element.203.x1_ref), kind=kOutput, calls=%fused_computation.225 | convolution fusion | flops 6442450944 | bytes 17825792 | tf_op jit(solution)/shard_map/td,tf->df/dot_general | solution.py:704
  750.8 10.9 %add_convert_fusion.2 = bf16[2048,768]{1,0:T(8,128)(2,1)} fusion(f32[2048,768]{1,0:T(8,128)S(1)} %fusion.58, bf16[2048,2048]{1,0:T(8,128)(2,1)} %constant_dynamic-update-slice_fusion.3, bf16[2048,768]{1,0:T(8,128)(2,1)S(1)} %copy-done.51), kind=kOutput, calls=%fused_computation.27 | convolution fusion | flops 6445596672 | bytes 20971520 | tf_op jit(solution)/shard_map/td,tf->df/dot_general | solution.py:704
  763.8 3.6 fusion.18
  773.0 87.1 %product_sum.4 = f32[512,2048]{1,0:T(8,128)} custom-call(bf16[2048,768]{1,0:T(8,128)(2,1)} %get-tuple-element.202.x0_ref, bf16[2048,768]{1,0:T(8,128)(2,1)} %get-tuple-element.203.x1_ref, bf16[2048,768]{1,0:T(8,128)(2,1)} %all-gather.5.cloned.1.call-done.w_ref), custom_call_target="tpu_custom_call" | custom-call | flops 51539607552 | bytes 20971520 | tf_op jit(solution)/shard_map/product_sum/pallas_call | solution.py:498
  860.1 3.6 all-to-all-start.6
  864.5 90.0 %product_sum.5 = f32[512,2048]{1,0:T(8,128)} custom-call(bf16[2048,1024]{1,0:T(8,128)(2,1)} %copy-done.14, bf16[2048,1024]{1,0:T(8,128)(2,1)} %copy-done.13, bf16[4,1024,1024]{2,1,0:T(8,128)(2,1)} %bitcast.244), custom_call_target="tpu_custom_call" | custom-call | flops 68719476736 | bytes 20971520 | tf_op jit(solution)/shard_map/product_sum/pallas_call | solution.py:498
  954.5 3.3 fusion.49
  960.2 2.8 maximum_add_fusion.1
  966.5 4.1 slice_reduce_fusion
  (316 shorter events, 108.3 us)
Async XLA Ops:
  7.2 122.9 %all-gather.5.cloned.1.call-start = ((), (), s32[]{:S(2)}) async-start(), calls=%async_computation.12 | async-start | bytes 3932160 | tf_op jit(solution)/shard_map/all_gather | solution.py:832
  9.6 17.5 %copy-start.48 = (bf16[64]{0:T(256)(128)(2,1)S(1)}, bf16[64]{0:T(256)(128)(2,1)}, u32[]{:S(2)}) copy-start(bf16[64]{0:T(256)(128)(2,1)} %param.26) | copy-start | bytes 388
  9.6 17.5 %copy-start.24 = (bf16[64,2048]{1,0:T(8,128)(2,1)S(1)}, bf16[64,2048]{1,0:T(8,128)(2,1)}, u32[]{:S(2)}) copy-start(bf16[64,2048]{1,0:T(8,128)(2,1)} %param.22) | copy-start | bytes 786436
  9.6 18.4 %copy-start = (bf16[2,256,2048]{2,1,0:T(8,128)(2,1)S(1)}, bf16[2,256,2048]{2,1,0:T(8,128)(2,1)}, u32[]{:S(2)}) copy-start(bf16[2,256,2048]{2,1,0:T(8,128)(2,1)} %param.17) | copy-start | bytes 6291460
  11.5 5.4 collective-permute-start
  12.0 7.5 collective-permute-start.1
  14.6 5.5 collective-permute-start.2
  14.8 5.3 collective-permute-start.3
  16.6 9.4 collective-permute-start.4
  16.8 9.2 collective-permute-start.5
  19.5 6.6 collective-permute-start.6
  27.0 145.9 %all-gather.7.cloned.1.call-start = ((), (), s32[]{:S(2)}) async-start(), calls=%async_computation.13 | async-start | bytes 8650752 | tf_op jit(solution)/shard_map/all_gather | solution.py:842
  29.1 30.3 %copy-start.10 = (bf16[64,8192]{1,0:T(8,128)(2,1)S(1)}, bf16[64,8192]{1,0:T(8,128)(2,1)}, u32[]{:S(2)}) copy-start(bf16[64,8192]{1,0:T(8,128)(2,1)} %param.23) | copy-start | bytes 3145732
  29.7 30.2 %copy-start.3 = (bf16[512,2048]{1,0:T(8,128)(2,1)}, bf16[512,2048]{1,0:T(8,128)(2,1)S(1)}, u32[]{:S(2)}) copy-start(bf16[512,2048]{1,0:T(8,128)(2,1)S(1)} %fusion.16) | copy-start | bytes 6291460
  31.8 26.3 %collective-permute-start.7 = (bf16[256,2048]{1,0:T(8,128)(2,1)}, bf16[256,2048]{1,0:T(8,128)(2,1)}, u32[]{:S(2)}, u32[]{:S(2)}) collective-permute-start(bf16[256,2048]{1,0:T(8,128)(2,1)} %get-tuple-element.246), channel_id=1, source_target_pairs={{0,2},{1,3},{2,0},{3,1},{4,6},{5,7},{6,4},{7,5},{8,10},{9,11},{10,... | collective-permute-start | bytes 3145736 | tf_op jit(solution)/shard_map/ppermute | solution.py:709
  33.3 52.1 %collective-permute-start.8 = (bf16[256,2048]{1,0:T(8,128)(2,1)}, bf16[256,2048]{1,0:T(8,128)(2,1)}, u32[]{:S(2)}, u32[]{:S(2)}) collective-permute-start(bf16[256,2048]{1,0:T(8,128)(2,1)} %get-tuple-element.246), channel_id=1, source_target_pairs={{0,4},{1,5},{2,6},{3,7},{4,0},{5,1},{6,2},{7,3},{8,12},{9,13},{10,... | collective-permute-start | bytes 3145736 | tf_op jit(solution)/shard_map/ppermute | solution.py:709
  34.6 80.9 %collective-permute-start.10 = (bf16[256,2048]{1,0:T(8,128)(2,1)}, bf16[256,2048]{1,0:T(8,128)(2,1)}, u32[]{:S(2)}, u32[]{:S(2)}) collective-permute-start(bf16[256,2048]{1,0:T(8,128)(2,1)} %get-tuple-element.244), channel_id=1, source_target_pairs={{0,2},{1,3},{2,0},{3,1},{4,6},{5,7},{6,4},{7,5},{8,10},{9,11},{10,... | collective-permute-start | bytes 3145736 | tf_op jit(solution)/shard_map/ppermute | solution.py:709
  35.1 47.0 %collective-permute-start.11 = (bf16[256,2048]{1,0:T(8,128)(2,1)}, bf16[256,2048]{1,0:T(8,128)(2,1)}, u32[]{:S(2)}, u32[]{:S(2)}) collective-permute-start(bf16[256,2048]{1,0:T(8,128)(2,1)} %get-tuple-element.244), channel_id=1, source_target_pairs={{0,4},{1,5},{2,6},{3,7},{4,0},{5,1},{6,2},{7,3},{8,12},{9,13},{10,... | collective-permute-start | bytes 3145736 | tf_op jit(solution)/shard_map/ppermute | solution.py:709
  35.9 24.0 %copy-start.45 = (f32[64]{0:T(128)}, f32[64]{0:T(128)S(1)}, u32[]{:S(2)}) copy-start(f32[64]{0:T(128)S(1)} %convert_element_type.150) | copy-start | bytes 772
  58.1 53.9 %collective-permute-start.9 = (bf16[256,2048]{1,0:T(8,128)(2,1)}, bf16[256,2048]{1,0:T(8,128)(2,1)}, u32[]{:S(2)}, u32[]{:S(2)}) collective-permute-start(bf16[256,2048]{1,0:T(8,128)(2,1)} %collective-permute-done.7), channel_id=1, source_target_pairs={{0,4},{1,5},{2,6},{3,7},{4,0},{5,1},{6,2},{7,3},{8,12},{9,13},{10,... | collective-permute-start | bytes 3145736 | tf_op jit(solution)/shard_map/ppermute | solution.py:709
  61.8 59.4 %all-to-all-start = ((bf16[8,64,1024]{2,1,0:T(8,128)(2,1)}), bf16[8,64,1024]{2,1,0:T(8,128)(2,1)S(1)}, u32[]{:S(2)}, u32[]{:S(2)}) async-start(bf16[8,64,1024]{2,1,0:T(8,128)(2,1)} %reshape.342), calls=%async_computation | async-start | bytes 2097152 | tf_op jit(solution)/shard_map/all_to_all | solution.py:834
  65.4 263.3 %all-gather.9.cloned.1.call-start = ((), (), s32[]{:S(2)}) async-start(), calls=%async_computation.19 | async-start | bytes 10485760 | tf_op jit(solution)/shard_map/all_gather | solution.py:850
  65.7 48.6 %copy-start.4 = (bf16[512,2048]{1,0:T(8,128)(2,1)S(1)}, bf16[512,2048]{1,0:T(8,128)(2,1)}, u32[]{:S(2)}) copy-start(bf16[512,2048]{1,0:T(8,128)(2,1)} %copy-done.3) | copy-start | bytes 6291460
  82.1 38.0 %collective-permute-start.12 = (bf16[256,2048]{1,0:T(8,128)(2,1)}, bf16[256,2048]{1,0:T(8,128)(2,1)S(1)}, u32[]{:S(2)}, u32[]{:S(2)}) collective-permute-start(bf16[256,2048]{1,0:T(8,128)(2,1)} %collective-permute-done.11), channel_id=1, source_target_pairs={{0,2},{1,3},{2,0},{3,1},{4,6},{5,7},{6,4},{7,5},{8,10},{9,11},{10,... | collective-permute-start | bytes 3145736 | tf_op jit(solution)/shard_map/ppermute | solution.py:709
  121.2 22.2 %collective-permute-start.13 = (bf16[2048,2048]{1,0:T(8,128)(2,1)}, bf16[2048,2048]{1,0:T(8,128)(2,1)}, u32[]{:S(2)}, u32[]{:S(2)}) collective-permute-start(bf16[2048,2048]{1,0:T(8,128)(2,1)} %constant_dynamic-update-slice_fusion.3), channel_id=1, source_target_pairs={{0,1},{1,0},{2,3},{3,2},{4,5},{5,4},{6,7},{7,6},{8,9},{9,8},{10,11... | collective-permute-start | bytes 25165832 | tf_op jit(solution)/shard_map/ppermute | solution.py:709
  176.2 32.9 %collective-permute-start.14 = (bf16[256,2048]{1,0:T(8,128)(2,1)}, bf16[256,2048]{1,0:T(8,128)(2,1)}, u32[]{:S(2)}, u32[]{:S(2)}) collective-permute-start(bf16[256,2048]{1,0:T(8,128)(2,1)} %get-tuple-element.150), channel_id=1, source_target_pairs={{0,2},{1,3},{2,0},{3,1},{4,6},{5,7},{6,4},{7,5},{8,10},{9,11},{10,... | collective-permute-start | bytes 3145736 | tf_op jit(solution)/shard_map/ppermute | solution.py:709
  177.6 31.5 %collective-permute-start.15 = (bf16[256,2048]{1,0:T(8,128)(2,1)}, bf16[256,2048]{1,0:T(8,128)(2,1)}, u32[]{:S(2)}, u32[]{:S(2)}) collective-permute-start(bf16[256,2048]{1,0:T(8,128)(2,1)} %get-tuple-element.154), channel_id=1, source_target_pairs={{0,4},{1,5},{2,6},{3,7},{4,0},{5,1},{6,2},{7,3},{8,12},{9,13},{10,... | collective-permute-start | bytes 3145736 | tf_op jit(solution)/shard_map/ppermute | solution.py:709
  209.1 37.4 %collective-permute-start.16 = (bf16[256,2048]{1,0:T(8,128)(2,1)}, bf16[256,2048]{1,0:T(8,128)(2,1)}, u32[]{:S(2)}, u32[]{:S(2)}) collective-permute-start(bf16[256,2048]{1,0:T(8,128)(2,1)} %get-tuple-element.150), channel_id=1, source_target_pairs={{0,4},{1,5},{2,6},{3,7},{4,0},{5,1},{6,2},{7,3},{8,12},{9,13},{10,... | collective-permute-start | bytes 3145736 | tf_op jit(solution)/shard_map/ppermute | solution.py:709
  210.7 35.9 %collective-permute-start.17 = (bf16[256,2048]{1,0:T(8,128)(2,1)}, bf16[256,2048]{1,0:T(8,128)(2,1)}, u32[]{:S(2)}, u32[]{:S(2)}) collective-permute-start(bf16[256,2048]{1,0:T(8,128)(2,1)} %get-tuple-element.154), channel_id=1, source_target_pairs={{0,2},{1,3},{2,0},{3,1},{4,6},{5,7},{6,4},{7,5},{8,10},{9,11},{10,... | collective-permute-start | bytes 3145736 | tf_op jit(solution)/shard_map/ppermute | solution.py:709
  211.2 35.3 %all-to-all-start.1 = ((bf16[8,256,256]{2,1,0:T(8,128)(2,1)}), bf16[8,256,256]{2,1,0:T(8,128)(2,1)S(1)}, u32[]{:S(2)}, u32[]{:S(2)}) async-start(bf16[8,256,256]{2,1,0:T(8,128)(2,1)} %bitcast.209), calls=%async_computation.1 | async-start | bytes 2097152 | tf_op jit(solution)/shard_map/all_to_all | solution.py:865
  246.5 20.2 %all-to-all-start.2 = ((bf16[8,256,256]{2,1,0:T(8,128)(2,1)}), bf16[8,256,256]{2,1,0:T(8,128)(2,1)}, u32[]{:S(2)}, u32[]{:S(2)}) async-start(bf16[8,256,256]{2,1,0:T(8,128)(2,1)} %bitcast.211), calls=%async_computation.2 | async-start | bytes 2097152 | tf_op jit(solution)/shard_map/all_to_all | solution.py:865
  250.8 351.5 %reduce-scatter.6.cloned.1.call-start = ((), (), s32[]{:S(2)}) async-start(), calls=%async_computation.14 | async-start | bytes 5242880 | tf_op jit(solution)/shard_map/reduce_scatter | solution.py:902
  250.8 36.9 %collective-permute-start.18 = (bf16[256,2048]{1,0:T(8,128)(2,1)}, bf16[256,2048]{1,0:T(8,128)(2,1)}, u32[]{:S(2)}, u32[]{:S(2)}) collective-permute-start(bf16[256,2048]{1,0:T(8,128)(2,1)} %collective-permute-done.14), channel_id=1, source_target_pairs={{0,4},{1,5},{2,6},{3,7},{4,0},{5,1},{6,2},{7,3},{8,12},{9,13},{10,... | collective-permute-start | bytes 3145736 | tf_op jit(solution)/shard_map/ppermute | solution.py:709
  252.7 35.1 %collective-permute-start.19 = (bf16[256,2048]{1,0:T(8,128)(2,1)}, bf16[256,2048]{1,0:T(8,128)(2,1)}, u32[]{:S(2)}, u32[]{:S(2)}) collective-permute-start(bf16[256,2048]{1,0:T(8,128)(2,1)} %collective-permute-done.15), channel_id=1, source_target_pairs={{0,2},{1,3},{2,0},{3,1},{4,6},{5,7},{6,4},{7,5},{8,10},{9,11},{10,... | collective-permute-start | bytes 3145736 | tf_op jit(solution)/shard_map/ppermute | solution.py:709
  298.7 13.4 %collective-permute-start.20 = (bf16[2048,2048]{1,0:T(8,128)(2,1)S(1)}, bf16[2048,2048]{1,0:T(8,128)(2,1)}, u32[]{:S(2)}, u32[]{:S(2)}) collective-permute-start(bf16[2048,2048]{1,0:T(8,128)(2,1)S(1)} %constant_dynamic-update-slice_fusion.11.dy0_ref), channel_id=1, source_target_pairs={{0,1},{1,0},{2,3},{3,2},{4,5},{5,4},{6,7},{7,6},{8,9},{9,8},{10,11... | collective-permute-start | bytes 25165832 | tf_op jit(solution)/shard_map/ppermute | solution.py:709
  447.9 23.8 %copy-start.13 = (bf16[2048,1024]{1,0:T(8,128)(2,1)}, bf16[2048,1024]{1,0:T(8,128)(2,1)S(1)}, u32[]{:S(2)}) copy-start(bf16[2048,1024]{1,0:T(8,128)(2,1)S(1)} %get-tuple-element.207.x1_ref) | copy-start | bytes 12582916
  464.4 20.5 %slice-start.4 = ((s8[8388608]{0:T(1024)(128)(4,1)}), s8[4194304]{0:T(1024)(128)(4,1)S(1)}, s32[]{:S(2)}) async-start(s8[8388608]{0:T(1024)(128)(4,1)} %bitcast.219), calls=%async_computation.24 | async-start | bytes 8388608
  511.5 181.2 %reduce-scatter.8.cloned.1.call-start = ((), (), s32[]{:S(2)}) async-start(), calls=%async_computation.15 | async-start | bytes 5242880 | tf_op jit(solution)/shard_map/reduce_scatter | solution.py:906
  622.7 24.9 %all-to-all-start.3 = ((bf16[8,256,256]{2,1,0:T(8,128)(2,1)}), bf16[8,256,256]{2,1,0:T(8,128)(2,1)S(1)}, u32[]{:S(2)}, u32[]{:S(2)}) async-start(bf16[8,256,256]{2,1,0:T(8,128)(2,1)} %get-tuple-element.180), calls=%async_computation.4 | async-start | bytes 2097152 | tf_op jit(solution)/shard_map/all_to_all | solution.py:909
  647.6 45.0 %all-to-all-start.4 = ((bf16[8,256,256]{2,1,0:T(8,128)(2,1)}), bf16[8,256,256]{2,1,0:T(8,128)(2,1)S(1)}, u32[]{:S(2)}, u32[]{:S(2)}) async-start(bf16[8,256,256]{2,1,0:T(8,128)(2,1)} %get-tuple-element.190), calls=%async_computation.5 | async-start | bytes 2097152 | tf_op jit(solution)/shard_map/all_to_all | solution.py:909
  651.8 111.9 %reduce-scatter.10.cloned.1.call-start = ((), (), s32[]{:S(2)}) async-start(), calls=%async_computation.16 | async-start | bytes 9437184 | tf_op jit(solution)/shard_map/reduce_scatter | solution.py:915
  693.6 68.1 %all-to-all-start.5 = ((bf16[8,64,1024]{2,1,0:T(8,128)(2,1)}), bf16[8,64,1024]{2,1,0:T(8,128)(2,1)S(1)}, u32[]{:S(2)}, u32[]{:S(2)}) async-start(bf16[8,64,1024]{2,1,0:T(8,128)(2,1)} %bitcast.47), calls=%async_computation.8 | async-start | bytes 2097152 | tf_op jit(solution)/shard_map/all_to_all | solution.py:916
  697.8 162.3 %reduce-scatter.12.cloned.1.call-start = ((), (), s32[]{:S(2)}) async-start(), calls=%async_computation.17 | async-start | bytes 3932160 | tf_op jit(solution)/shard_map/reduce_scatter | solution.py:922
  860.1 102.9 %all-to-all-start.6 = ((bf16[8,64,768]{2,1,0:T(8,128)(2,1)}), bf16[8,64,768]{2,1,0:T(8,128)(2,1)S(1)}, u32[]{:S(2)}, u32[]{:S(2)}) async-start(bf16[8,64,768]{2,1,0:T(8,128)(2,1)} %bitcast.218), calls=%async_computation.11 | async-start | bytes 1572864 | tf_op jit(solution)/shard_map/all_to_all | solution.py:927
  863.7 99.4 %reduce-scatter.14.cloned.1.call-start = ((), (), s32[]{:S(2)}) async-start(), calls=%async_computation.18 | async-start | bytes 1310720 | tf_op jit(solution)/shard_map/reduce_scatter | solution.py:925
  864.4 90.1 %copy-start.1 = (bf16[2,256,2048]{2,1,0:T(8,128)(2,1)S(1)}, bf16[2,256,2048]{2,1,0:T(8,128)(2,1)}, u32[]{:S(2)}) copy-start(bf16[2,256,2048]{2,1,0:T(8,128)(2,1)} %param.17) | copy-start | bytes 6291460
  864.4 90.1 %copy-start.35 = (f32[1,2,2,128]{3,1,2,0:T(2,128)S(1)}, f32[1,2,2,128]{3,1,2,0:T(2,128)}, u32[]{:S(2)}) copy-start(f32[1,2,2,128]{3,1,2,0:T(2,128)} %copy-done.34) | copy-start | bytes 6148
  864.5 90.1 %copy-start.37 = (f32[1,2,2,128]{3,1,2,0:T(2,128)S(1)}, f32[1,2,2,128]{3,1,2,0:T(2,128)}, u32[]{:S(2)}) copy-start(f32[1,2,2,128]{3,1,2,0:T(2,128)} %copy-done.36) | copy-start | bytes 6148
  (46 other events, 297.5 us)
Sparse Core Ops, SparseCore 0:
  27.1 64.5 all-gather.4
  95.2 77.6 all-gather.6
  180.4 148.2 all-gather.8
  511.6 74.0 reduce-scatter.5
  602.5 73.9 reduce-scatter.7
  692.8 70.8 reduce-scatter.9
  766.1 60.2 reduce-scatter.11
  866.9 27.8 reduce-scatter.13

commit v7 on v6

--- a/solution.py
+++ b/solution.py
@@ -821,6 +821,12 @@
     def scaled(w, gain):
         return (w.astype(f32) * gain.astype(f32)[:, None]).astype(bf16)
 
+    def against(w, raw):
+        return jnp.sum(w.astype(f32) * raw, axis=-1)
+
+    def grown(raw, gain):
+        return raw * gain.astype(f32)[:, None]
+
     x_own = inputs.reshape(tokens, width).astype(f32)
     x_hat, x_rstd = standardize(x_own)
     x_low = x_hat.astype(bf16)
@@ -918,12 +924,13 @@
         grads = attention_backward(r, rows, saved[r], do_heads[r], table[r], lowest[r], span[r], blk, local_len, grads)
     d0, d1 = grads
     qkv_part = (dot(xh0, d0, "td,tf->df") + dot(xh1, d1, "td,tf->df")).astype(bf16)
-    d0, d1, qkv_part, out_part, up_moved = lax.optimization_barrier((d0, d1, qkv_part, out_part, up_moved))
+    up_raw = up_moved.reshape(piece, n, m, unit).transpose(0, 2, 1, 3).reshape(piece, ff).astype(f32)
+    ffn_grads = (grown(up_raw, gain_ffn), against(w_up, up_raw), grown(down_raw, gain_ffn_sub), against(w_down, down_raw))
+    d0, d1, qkv_part, out_part, ffn_grads = lax.optimization_barrier((d0, d1, qkv_part, out_part, ffn_grads))
     qkv_part = lax.psum_scatter(qkv_part, "row", scatter_dimension=0, tiled=True)
     da = product_sum(d0, d1, w_qkv, rows, n, 2, True)
     e0, e1, da, qkv_part, out_part = lax.optimization_barrier((e0, e1, da, qkv_part, out_part))
     out_raw = lax.psum_scatter(out_part, "row", scatter_dimension=0, tiled=True).astype(f32)
-    up_raw = up_moved.reshape(piece, n, m, unit).transpose(0, 2, 1, 3).reshape(piece, ff).astype(f32)
     qkv_raw = lax.all_to_all(qkv_part.reshape(n, piece, 3 * heads_dim), "ctx", split_axis=0, concat_axis=2, tiled=True)
 
     ffn = product_sum(e0, e1, ffn_all, rows, n, 3, False, "down", width)
@@ -933,16 +940,10 @@
     query_raw, key_raw, value_raw = (qkv_raw[:, :, i].reshape(piece, width) for i in range(3))
     input_grad = jnp.stack(dx1) + standardize_back(x_hat, x_rstd, da).reshape(rows, local_len, width)
 
-    def against(w, raw):
-        return jnp.sum(w.astype(f32) * raw, axis=-1)
-
-    def grown(raw, gain):
-        return raw * gain.astype(f32)[:, None]
-
     gain_one = against(w_query, query_raw) + against(w_key, key_raw) + against(w_value, value_raw)
     return (output, input_grad, grown(query_raw, gain_attn), grown(key_raw, gain_attn), grown(value_raw, gain_attn),
-            grown(out_raw, gain_attn_sub), grown(up_raw, gain_ffn), grown(down_raw, gain_ffn_sub),
-            gain_one, against(w_out, out_raw), against(w_up, up_raw), against(w_down, down_raw))
+            grown(out_raw, gain_attn_sub), ffn_grads[0], ffn_grads[2],
+            gain_one, against(w_out, out_raw), ffn_grads[1], ffn_grads[3])
 
 
 def solution(mesh):

time: 991 us -> 994 us (level)
    unnamed x148 -> x150, local copies, waits for them, and re-layouts: 31.3 us -> 32.3 us
  transfers between devices with their start and end apart: 36 -> 36, of which waited for: 12 -> 11; matrix products, arithmetic and copies ran while one was open for 13% -> 13% of each run, Pallas kernels for 46% -> 46%
where the time goes in v7:
time: 994 us; the launch traced here: 987 us
  Pallas kernels  548 us (55%)
  waiting for transfers between devices  128 us (13%)
  matrix products  111 us (11%)
  local copies, waits for them, and re-layouts  70.4 us (7%)
  starting transfers between devices  52.6 us (5%)
  other arithmetic  52.2 us (5%)
  between operations  15.9 us (2%)
    pallas_call x3, Pallas kernels, product_sum(): pl.pallas_call(functools.partial(product_sum_kernel, n, rows, min(512, wi...  269 us
    dot_general x9, matrix products, dot(): return jnp.einsum(spec, a, b, preferred_element_type=f32).astype(kind)  111 us
    pallas_call x1, Pallas kernels, gather_product(): pl.pallas_call(functools.partial(gather_product_kernel, n, rows, min(256,...  95.2 us
    ppermute x21, waiting for transfers between devices, swap(): return lax.ppermute(x, 'ctx', [(i, i ^ bit) for i in range(n)])  88.4 us
    pallas_call x2, Pallas kernels, attention_backward(): pl.pallas_call(call, out_shape=(whole, whole), grid_spec=pltpu.PrefetchSc...  83.8 us
    pallas_call x2, Pallas kernels, attention_forward(): pl.pallas_call(functools.partial(forward_kernel, nh, blk, unit), out_shap...  58.1 us
    unnamed x150, local copies, waits for them, and re-layouts  32.3 us
    pallas_call x2, Pallas kernels, middle_backward(): pl.pallas_call(middle_backward_kernel, out_shape=(sds((size, width), f32)...  25.3 us
  transfers between devices with their start and end apart: 36, of which 11 were waited for; matrix products, arithmetic and copies ran while one was open for 13% of the time, Pallas kernels for 46%

profile of v7, /device:TPU:0, one launch (start us, length us, event | category | flops | bytes accessed | tf_op | source)
XLA Modules:
  0.0 987.3 jit_solution(2612815929871280964)
XLA Ops:
  16.8 2.6 collective-permute-start.5
  20.1 5.9 collective-permute-done.4
  35.9 22.3 %collective-permute-done.7 = bf16[256,2048]{1,0:T(8,128)(2,1)} collective-permute-done((bf16[256,2048]{1,0:T(8,128)(2,1)}, bf16[256,2048]{1,0:T(8,128)(2,1)}, u32[]{:S(2)}, u32[]{:S(2)}) %collective-permute-start.7) | collective-permute-done | bytes 1048608 | tf_op jit(solution)/shard_map/ppermute | solution.py:709
  61.8 3.6 all-to-all-start
  68.3 13.8 %collective-permute-done.11 = bf16[256,2048]{1,0:T(8,128)(2,1)} collective-permute-done((bf16[256,2048]{1,0:T(8,128)(2,1)}, bf16[256,2048]{1,0:T(8,128)(2,1)}, u32[]{:S(2)}, u32[]{:S(2)}) %collective-permute-start.11) | collective-permute-done | bytes 1048608 | tf_op jit(solution)/shard_map/ppermute | solution.py:709
  82.1 3.2 collective-permute-start.12
  87.7 24.4 %collective-permute-done.9 = bf16[256,2048]{1,0:T(8,128)(2,1)} collective-permute-done((bf16[256,2048]{1,0:T(8,128)(2,1)}, bf16[256,2048]{1,0:T(8,128)(2,1)}, u32[]{:S(2)}, u32[]{:S(2)}) %collective-permute-start.9) | collective-permute-done | bytes 1048608 | tf_op jit(solution)/shard_map/ppermute | solution.py:709
  125.3 3.1 power_multiply_fusion.3
  130.1 13.4 %fusion.54.q0_ref.k0_ref.v0_ref = f32[768,2048]{1,0:T(8,128)} fusion(bf16[2048,768]{1,0:T(8,128)(2,1)} %all-gather.5.cloned.1.call-done.w_ref, bf16[2048,2048]{1,0:T(8,128)(2,1)} %constant_dynamic-update-slice_fusion.3), kind=kOutput, calls=%fused_computation.222 | convolution fusion | flops 6442450944 | bytes 17825792 | tf_op jit(solution)/shard_map/df,td->ft/dot_general | solution.py:704
  143.5 11.4 %fusion.55.q1_ref.k1_ref.v1_ref = f32[768,2048]{1,0:T(8,128)} fusion(bf16[2048,768]{1,0:T(8,128)(2,1)S(1)} %copy-done.48, bf16[2048,2048]{1,0:T(8,128)(2,1)} %collective-permute-done.13), kind=kOutput, calls=%fused_computation.223 | convolution fusion | flops 6442450944 | bytes 17825792 | tf_op jit(solution)/shard_map/df,td->ft/dot_general | solution.py:704
  155.0 18.0 %all-gather.7.cloned.1.call-done.w_ref = bf16[2048,2048]{1,0:T(8,128)(2,1)} async-done(((bf16[64,2048]{1,0:T(8,128)(2,1)}), bf16[2048,2048]{1,0:T(8,128)(2,1)}) %all-gather.7.cloned.1.call-update) | async-done | bytes 8388624 | tf_op jit(solution)/shard_map/all_gather | solution.py:848
  172.9 3.3 slice_bitcast_fusion.6
  180.3 28.8 %attention_forward.2 = (bf16[2048,256]{1,0:T(8,128)(2,1)}, f32[256,2048]{1,0:T(8,128)}, f32[4,2048]{1,0:T(4,128)}, bf16[256,2048]{1,0:T(8,128)(2,1)}, bf16[256,2...) custom-call(s32[10]{0:T(128)} %pad_add_fusion.4.span_ref, f32[768,2048]{1,0:T(8,128)} %fusion.54.q0_ref.k0_ref.v0_ref, ...), custom_call_target="tpu_custom_call" | custom-call | flops 8589934592 | bytes 10485760 | tf_op jit(solution)/shard_map/attention_forward/pallas_call | solution.py:234
  211.5 3.7 all-to-all-start.1
  215.9 29.2 %attention_forward.3 = (bf16[2048,256]{1,0:T(8,128)(2,1)}, f32[256,2048]{1,0:T(8,128)}, f32[4,2048]{1,0:T(4,128)}, bf16[256,2048]{1,0:T(8,128)(2,1)}, bf16[256,2...) custom-call(s32[10]{0:T(128)} %pad_add_fusion.2.span_ref, f32[768,2048]{1,0:T(8,128)} %fusion.54.q0_ref.k0_ref.v0_ref, ...), custom_call_target="tpu_custom_call" | custom-call | flops 8589934592 | bytes 10485760 | tf_op jit(solution)/shard_map/attention_forward/pallas_call | solution.py:234
  246.6 4.3 all-to-all-start.2
  255.8 8.5 middle_forward.2
  264.2 2.6 all-to-all-done.2.o_ref
  266.8 8.5 middle_forward.3
  275.3 12.5 %collective-permute-done.18 = bf16[256,2048]{1,0:T(8,128)(2,1)} collective-permute-done((bf16[256,2048]{1,0:T(8,128)(2,1)}, bf16[256,2048]{1,0:T(8,128)(2,1)}, u32[]{:S(2)}, u32[]{:S(2)}) %collective-permute-start.18) | collective-permute-done | bytes 1048608 | tf_op jit(solution)/shard_map/ppermute | solution.py:709
  302.7 9.4 collective-permute-done.20.dy1_ref
  312.1 16.6 %all-gather.9.cloned.1.call-done = bf16[4096,1024]{1,0:T(8,128)(2,1)} async-done(((bf16[1024,1024]{1,0:T(8,128)(2,1)}), bf16[4096,1024]{1,0:T(8,128)(2,1)}) %all-gather.9.cloned.1.call-update) | async-done | bytes 8388624 | tf_op jit(solution)/shard_map/all_gather | solution.py:856
  328.7 95.2 %gather_product.1 = (bf16[2048,2048]{1,0:T(8,128)(2,1)}, bf16[2048,2048]{1,0:T(8,128)(2,1)}, f32[2048,1024]{1,0:T(8,128)}, f32[2048,1024]{1,0:T(8,128)}, f32[204...) custom-call(bf16[512,2048]{1,0:T(8,128)(2,1)} %pad_maximum_fusion.1.b_ref, ...), custom_call_target="tpu_custom_call" | custom-call | flops 68719476736 | bytes 73400320 | tf_op jit(solution)/shard_map/gather_product/pallas_call | solution.py:656
  427.7 9.7 all_gather.19
  439.9 8.0 fusion.11
  448.0 16.4 %fusion.57 = f32[2048,1024]{1,0:T(8,128)} fusion(bf16[2048,2048]{1,0:T(8,128)(2,1)} %get-tuple-element.169, bf16[2048,1024]{1,0:T(8,128)(2,1)S(1)} %get-tuple-element.179.x1_ref), kind=kOutput, calls=%fused_computation.225 | convolution fusion | flops 8589934592 | bytes 20971520 | tf_op jit(solution)/shard_map/td,tf->df/dot_general | solution.py:704
  464.5 7.3 fusion.5
  471.8 13.2 %fusion.56 = f32[1024,2048]{1,0:T(8,128)S(1)} fusion(bf16[2048,1024]{1,0:T(8,128)(2,1)S(1)} %get-tuple-element.211.x1_ref, bf16[2048,2048]{1,0:T(8,128)(2,1)} %collective-permute-done.20.dy1_ref), kind=kOutput, calls=%fused_computation.224 | convolution fusion | flops 8589934592 | bytes 20971520 | tf_op jit(solution)/shard_map/tf,td->fd/dot_general | solution.py:704
  485.0 11.2 %add_convert_fusion.1 = bf16[1024,2048]{1,0:T(8,128)(2,1)} fusion(f32[1024,2048]{1,0:T(8,128)S(1)} %fusion.56, bf16[2048,1024]{1,0:T(8,128)(2,1)S(1)} %get-tuple-element.210.x0_ref, bf16[2048,2048]{1,0:T(8,128)(2,1)S(1)} %bitcast.221), kind=kOutput, calls=%fused_computation.19 | convolution fusion | flops 8594128896 | bytes 25165824 | tf_op jit(solution)/shard_map/tf,td->fd/dot_general | solution.py:704
  496.2 15.3 %add_convert_fusion = bf16[2048,1024]{1,0:T(8,128)(2,1)} fusion(f32[2048,1024]{1,0:T(8,128)} %fusion.57, bf16[2048,2048]{1,0:T(8,128)(2,1)} %get-tuple-element.168, bf16[2048,1024]{1,0:T(8,128)(2,1)} %get-tuple-element.178.x0_ref), kind=kOutput, calls=%fused_computation.18 | convolution fusion | flops 8594128896 | bytes 25165824 | tf_op jit(solution)/shard_map/td,tf->df/dot_general | solution.py:704
  511.6 90.8 %product_sum.3.db_ref = f32[512,2048]{1,0:T(8,128)} custom-call(bf16[2048,1024]{1,0:T(8,128)(2,1)} %get-tuple-element.178.x0_ref, bf16[2048,1024]{1,0:T(8,128)(2,1)} %copy-done.15, bf16[4,1024,1024]{2,1,0:T(8,128)(2,1)} %bitcast.244), custom_call_target="tpu_custom_call" | custom-call | flops 68719476736 | bytes 20971520 | tf_op jit(solution)/shard_map/product_sum/pallas_call | solution.py:498
  610.1 12.7 %middle_backward.2 = (f32[256,2048]{1,0:T(8,128)}, bf16[256,2048]{1,0:T(8,128)(2,1)}, bf16[8,256,256]{2,1,0:T(8,128)(2,1)}) custom-call(bf16[8,256,256]{2,1,0:T(8,128)(2,1)} %copy-done.5, f32[256,2048]{1,0:T(8,128)} %get-tuple-element.140.x1_ref, f32[512,2048]{1,0:T(8,128)} %product_sum.3.db_ref, bf16[256,2048]{1,0:T(8,128)(2,1)} %get-tuple-element.243.dy_ref, ...), custom_call_target="tpu_custom_call" | custom-call | flops 2147483648 | bytes 16777216 | tf_op jit(solution)/shard_map/middle_backward/pallas_call | solution.py:353
  622.7 4.0 all-to-all-start.3
  626.7 12.7 %middle_backward.3 = (f32[256,2048]{1,0:T(8,128)}, bf16[256,2048]{1,0:T(8,128)(2,1)}, bf16[8,256,256]{2,1,0:T(8,128)(2,1)}) custom-call(bf16[8,256,256]{2,1,0:T(8,128)(2,1)} %all-to-all-done.2.o_ref, f32[256,2048]{1,0:T(8,128)} %get-tuple-element.142.x1_ref, f32[512,2048]{1,0:T(8,128)} %product_sum.3.db_ref, bf16[256,2048]{1,0:T(8,128)(2,1)} %get-tuple-element.242.dy_ref, ...), custom_call_target="tpu_custom_call" | custom-call | flops 2147483648 | bytes 16777216 | tf_op jit(solution)/shard_map/middle_backward/pallas_call | solution.py:353
  639.4 8.3 convolution_convert_fusion
  647.7 4.2 all-to-all-start.4
  651.9 40.8 %attention_backward.2 = (bf16[2048,768]{1,0:T(8,128)(2,1)}, bf16[2048,768]{1,0:T(8,128)(2,1)}) custom-call(s32[10]{0:T(128)} %pad_add_fusion.4.span_ref, bf16[256,2048]{1,0:T(8,128)(2,1)} %get-tuple-element.175.refs_0_, bf16[256,2048]{1,0:T(8,128)(2,1)} %get-tuple-element.176.refs_1_, bf16[256,2048]{1,0:T(8,128)(2,1)} %get-tuple-element.177.refs_2_, ...), custom_call_target="tpu_custom_call" | custom-call | flops 21474836480 | bytes 20971520 | tf_op jit(solution)/shard_map/attention_backward/pallas_call | solution.py:269
  696.9 4.2 all-to-all-start.5
  701.2 43.1 %attention_backward.3 = (bf16[2048,768]{1,0:T(8,128)(2,1)}, bf16[2048,768]{1,0:T(8,128)(2,1)}) custom-call(s32[10]{0:T(128)} %pad_add_fusion.2.span_ref, bf16[256,2048]{1,0:T(8,128)(2,1)} %get-tuple-element.172.qT_ref, bf16[256,2048]{1,0:T(8,128)(2,1)} %get-tuple-element.173.kT_ref, ...), custom_call_target="tpu_custom_call", output_to_operand_aliasing={{0}: (9, {}), {1}: (10, {})} | custom-call | flops 21474836480 | bytes 20971520 | tf_op jit(solution)/shard_map/attention_backward/pallas_call | solution.py:269
  744.2 10.6 %fusion.58 = f32[2048,768]{1,0:T(8,128)S(1)} fusion(bf16[2048,2048]{1,0:T(8,128)(2,1)} %collective-permute-done.13, bf16[2048,768]{1,0:T(8,128)(2,1)} %get-tuple-element.207.x1_ref), kind=kOutput, calls=%fused_computation.226 | convolution fusion | flops 6442450944 | bytes 17825792 | tf_op jit(solution)/shard_map/td,tf->df/dot_general | solution.py:704
  754.8 10.9 %add_convert_fusion.2 = bf16[2048,768]{1,0:T(8,128)(2,1)} fusion(f32[2048,768]{1,0:T(8,128)S(1)} %fusion.58, bf16[2048,2048]{1,0:T(8,128)(2,1)} %constant_dynamic-update-slice_fusion.3, bf16[2048,768]{1,0:T(8,128)(2,1)S(1)} %copy-done.52), kind=kOutput, calls=%fused_computation.27 | convolution fusion | flops 6445596672 | bytes 20971520 | tf_op jit(solution)/shard_map/td,tf->df/dot_general | solution.py:704
  768.0 2.9 copy.82
  774.3 87.7 %product_sum.4 = f32[512,2048]{1,0:T(8,128)} custom-call(bf16[2048,768]{1,0:T(8,128)(2,1)} %get-tuple-element.206.x0_ref, bf16[2048,768]{1,0:T(8,128)(2,1)} %get-tuple-element.207.x1_ref, bf16[2048,768]{1,0:T(8,128)(2,1)} %all-gather.5.cloned.1.call-done.w_ref), custom_call_target="tpu_custom_call" | custom-call | flops 51539607552 | bytes 20971520 | tf_op jit(solution)/shard_map/product_sum/pallas_call | solution.py:498
  862.1 3.6 all-to-all-start.6
  866.5 90.0 %product_sum.5 = f32[512,2048]{1,0:T(8,128)} custom-call(bf16[2048,1024]{1,0:T(8,128)(2,1)} %copy-done.14, bf16[2048,1024]{1,0:T(8,128)(2,1)} %copy-done.13, bf16[4,1024,1024]{2,1,0:T(8,128)(2,1)} %bitcast.245), custom_call_target="tpu_custom_call" | custom-call | flops 68719476736 | bytes 20971520 | tf_op jit(solution)/shard_map/product_sum/pallas_call | solution.py:498
  956.6 3.3 fusion.49
  962.2 2.8 maximum_add_fusion.1
  968.5 4.1 slice_reduce_fusion
  (318 shorter events, 109.5 us)
Async XLA Ops:
  7.2 122.9 %all-gather.5.cloned.1.call-start = ((), (), s32[]{:S(2)}) async-start(), calls=%async_computation.12 | async-start | bytes 3932160 | tf_op jit(solution)/shard_map/all_gather | solution.py:838
  9.6 17.5 %copy-start.49 = (bf16[64]{0:T(256)(128)(2,1)S(1)}, bf16[64]{0:T(256)(128)(2,1)}, u32[]{:S(2)}) copy-start(bf16[64]{0:T(256)(128)(2,1)} %param.26) | copy-start | bytes 388
  9.6 17.5 %copy-start.24 = (bf16[64,2048]{1,0:T(8,128)(2,1)S(1)}, bf16[64,2048]{1,0:T(8,128)(2,1)}, u32[]{:S(2)}) copy-start(bf16[64,2048]{1,0:T(8,128)(2,1)} %param.22) | copy-start | bytes 786436
  9.6 18.4 %copy-start = (bf16[2,256,2048]{2,1,0:T(8,128)(2,1)S(1)}, bf16[2,256,2048]{2,1,0:T(8,128)(2,1)}, u32[]{:S(2)}) copy-start(bf16[2,256,2048]{2,1,0:T(8,128)(2,1)} %param.17) | copy-start | bytes 6291460
  11.5 5.4 collective-permute-start
  12.0 7.5 collective-permute-start.1
  14.6 5.5 collective-permute-start.2
  14.8 5.3 collective-permute-start.3
  16.6 9.4 collective-permute-start.4
  16.8 9.2 collective-permute-start.5
  19.5 6.6 collective-permute-start.6
  27.0 145.9 %all-gather.7.cloned.1.call-start = ((), (), s32[]{:S(2)}) async-start(), calls=%async_computation.13 | async-start | bytes 8650752 | tf_op jit(solution)/shard_map/all_gather | solution.py:848
  29.1 30.3 %copy-start.10 = (bf16[64,8192]{1,0:T(8,128)(2,1)S(1)}, bf16[64,8192]{1,0:T(8,128)(2,1)}, u32[]{:S(2)}) copy-start(bf16[64,8192]{1,0:T(8,128)(2,1)} %param.23) | copy-start | bytes 3145732
  29.7 30.2 %copy-start.3 = (bf16[512,2048]{1,0:T(8,128)(2,1)}, bf16[512,2048]{1,0:T(8,128)(2,1)S(1)}, u32[]{:S(2)}) copy-start(bf16[512,2048]{1,0:T(8,128)(2,1)S(1)} %fusion.16) | copy-start | bytes 6291460
  31.8 26.3 %collective-permute-start.7 = (bf16[256,2048]{1,0:T(8,128)(2,1)}, bf16[256,2048]{1,0:T(8,128)(2,1)}, u32[]{:S(2)}, u32[]{:S(2)}) collective-permute-start(bf16[256,2048]{1,0:T(8,128)(2,1)} %get-tuple-element.252), channel_id=1, source_target_pairs={{0,2},{1,3},{2,0},{3,1},{4,6},{5,7},{6,4},{7,5},{8,10},{9,11},{10,... | collective-permute-start | bytes 3145736 | tf_op jit(solution)/shard_map/ppermute | solution.py:709
  33.3 52.1 %collective-permute-start.8 = (bf16[256,2048]{1,0:T(8,128)(2,1)}, bf16[256,2048]{1,0:T(8,128)(2,1)}, u32[]{:S(2)}, u32[]{:S(2)}) collective-permute-start(bf16[256,2048]{1,0:T(8,128)(2,1)} %get-tuple-element.252), channel_id=1, source_target_pairs={{0,4},{1,5},{2,6},{3,7},{4,0},{5,1},{6,2},{7,3},{8,12},{9,13},{10,... | collective-permute-start | bytes 3145736 | tf_op jit(solution)/shard_map/ppermute | solution.py:709
  34.6 80.9 %collective-permute-start.10 = (bf16[256,2048]{1,0:T(8,128)(2,1)}, bf16[256,2048]{1,0:T(8,128)(2,1)}, u32[]{:S(2)}, u32[]{:S(2)}) collective-permute-start(bf16[256,2048]{1,0:T(8,128)(2,1)} %get-tuple-element.250), channel_id=1, source_target_pairs={{0,2},{1,3},{2,0},{3,1},{4,6},{5,7},{6,4},{7,5},{8,10},{9,11},{10,... | collective-permute-start | bytes 3145736 | tf_op jit(solution)/shard_map/ppermute | solution.py:709
  35.1 47.0 %collective-permute-start.11 = (bf16[256,2048]{1,0:T(8,128)(2,1)}, bf16[256,2048]{1,0:T(8,128)(2,1)}, u32[]{:S(2)}, u32[]{:S(2)}) collective-permute-start(bf16[256,2048]{1,0:T(8,128)(2,1)} %get-tuple-element.250), channel_id=1, source_target_pairs={{0,4},{1,5},{2,6},{3,7},{4,0},{5,1},{6,2},{7,3},{8,12},{9,13},{10,... | collective-permute-start | bytes 3145736 | tf_op jit(solution)/shard_map/ppermute | solution.py:709
  35.9 24.0 %copy-start.46 = (f32[64]{0:T(128)}, f32[64]{0:T(128)S(1)}, u32[]{:S(2)}) copy-start(f32[64]{0:T(128)S(1)} %convert_element_type.153) | copy-start | bytes 772
  58.1 53.9 %collective-permute-start.9 = (bf16[256,2048]{1,0:T(8,128)(2,1)}, bf16[256,2048]{1,0:T(8,128)(2,1)}, u32[]{:S(2)}, u32[]{:S(2)}) collective-permute-start(bf16[256,2048]{1,0:T(8,128)(2,1)} %collective-permute-done.7), channel_id=1, source_target_pairs={{0,4},{1,5},{2,6},{3,7},{4,0},{5,1},{6,2},{7,3},{8,12},{9,13},{10,... | collective-permute-start | bytes 3145736 | tf_op jit(solution)/shard_map/ppermute | solution.py:709
  61.8 59.4 %all-to-all-start = ((bf16[8,64,1024]{2,1,0:T(8,128)(2,1)}), bf16[8,64,1024]{2,1,0:T(8,128)(2,1)S(1)}, u32[]{:S(2)}, u32[]{:S(2)}) async-start(bf16[8,64,1024]{2,1,0:T(8,128)(2,1)} %reshape.343), calls=%async_computation | async-start | bytes 2097152 | tf_op jit(solution)/shard_map/all_to_all | solution.py:840
  65.4 263.3 %all-gather.9.cloned.1.call-start = ((), (), s32[]{:S(2)}) async-start(), calls=%async_computation.19 | async-start | bytes 10485760 | tf_op jit(solution)/shard_map/all_gather | solution.py:856
  65.7 48.6 %copy-start.4 = (bf16[512,2048]{1,0:T(8,128)(2,1)S(1)}, bf16[512,2048]{1,0:T(8,128)(2,1)}, u32[]{:S(2)}) copy-start(bf16[512,2048]{1,0:T(8,128)(2,1)} %copy-done.3) | copy-start | bytes 6291460
  82.1 38.0 %collective-permute-start.12 = (bf16[256,2048]{1,0:T(8,128)(2,1)}, bf16[256,2048]{1,0:T(8,128)(2,1)S(1)}, u32[]{:S(2)}, u32[]{:S(2)}) collective-permute-start(bf16[256,2048]{1,0:T(8,128)(2,1)} %collective-permute-done.11), channel_id=1, source_target_pairs={{0,2},{1,3},{2,0},{3,1},{4,6},{5,7},{6,4},{7,5},{8,10},{9,11},{10,... | collective-permute-start | bytes 3145736 | tf_op jit(solution)/shard_map/ppermute | solution.py:709
  121.2 22.3 %collective-permute-start.13 = (bf16[2048,2048]{1,0:T(8,128)(2,1)}, bf16[2048,2048]{1,0:T(8,128)(2,1)}, u32[]{:S(2)}, u32[]{:S(2)}) collective-permute-start(bf16[2048,2048]{1,0:T(8,128)(2,1)} %constant_dynamic-update-slice_fusion.3), channel_id=1, source_target_pairs={{0,1},{1,0},{2,3},{3,2},{4,5},{5,4},{6,7},{7,6},{8,9},{9,8},{10,11... | collective-permute-start | bytes 25165832 | tf_op jit(solution)/shard_map/ppermute | solution.py:709
  176.2 33.0 %collective-permute-start.14 = (bf16[256,2048]{1,0:T(8,128)(2,1)}, bf16[256,2048]{1,0:T(8,128)(2,1)}, u32[]{:S(2)}, u32[]{:S(2)}) collective-permute-start(bf16[256,2048]{1,0:T(8,128)(2,1)} %get-tuple-element.153), channel_id=1, source_target_pairs={{0,2},{1,3},{2,0},{3,1},{4,6},{5,7},{6,4},{7,5},{8,10},{9,11},{10,... | collective-permute-start | bytes 3145736 | tf_op jit(solution)/shard_map/ppermute | solution.py:709
  177.6 31.6 %collective-permute-start.15 = (bf16[256,2048]{1,0:T(8,128)(2,1)}, bf16[256,2048]{1,0:T(8,128)(2,1)}, u32[]{:S(2)}, u32[]{:S(2)}) collective-permute-start(bf16[256,2048]{1,0:T(8,128)(2,1)} %get-tuple-element.157), channel_id=1, source_target_pairs={{0,4},{1,5},{2,6},{3,7},{4,0},{5,1},{6,2},{7,3},{8,12},{9,13},{10,... | collective-permute-start | bytes 3145736 | tf_op jit(solution)/shard_map/ppermute | solution.py:709
  209.2 37.4 %collective-permute-start.16 = (bf16[256,2048]{1,0:T(8,128)(2,1)}, bf16[256,2048]{1,0:T(8,128)(2,1)}, u32[]{:S(2)}, u32[]{:S(2)}) collective-permute-start(bf16[256,2048]{1,0:T(8,128)(2,1)} %get-tuple-element.153), channel_id=1, source_target_pairs={{0,4},{1,5},{2,6},{3,7},{4,0},{5,1},{6,2},{7,3},{8,12},{9,13},{10,... | collective-permute-start | bytes 3145736 | tf_op jit(solution)/shard_map/ppermute | solution.py:709
  210.8 35.8 %collective-permute-start.17 = (bf16[256,2048]{1,0:T(8,128)(2,1)}, bf16[256,2048]{1,0:T(8,128)(2,1)}, u32[]{:S(2)}, u32[]{:S(2)}) collective-permute-start(bf16[256,2048]{1,0:T(8,128)(2,1)} %get-tuple-element.157), channel_id=1, source_target_pairs={{0,2},{1,3},{2,0},{3,1},{4,6},{5,7},{6,4},{7,5},{8,10},{9,11},{10,... | collective-permute-start | bytes 3145736 | tf_op jit(solution)/shard_map/ppermute | solution.py:709
  211.5 35.2 %all-to-all-start.1 = ((bf16[8,256,256]{2,1,0:T(8,128)(2,1)}), bf16[8,256,256]{2,1,0:T(8,128)(2,1)S(1)}, u32[]{:S(2)}, u32[]{:S(2)}) async-start(bf16[8,256,256]{2,1,0:T(8,128)(2,1)} %bitcast.210), calls=%async_computation.1 | async-start | bytes 2097152 | tf_op jit(solution)/shard_map/all_to_all | solution.py:871
  246.6 20.2 %all-to-all-start.2 = ((bf16[8,256,256]{2,1,0:T(8,128)(2,1)}), bf16[8,256,256]{2,1,0:T(8,128)(2,1)}, u32[]{:S(2)}, u32[]{:S(2)}) async-start(bf16[8,256,256]{2,1,0:T(8,128)(2,1)} %bitcast.212), calls=%async_computation.2 | async-start | bytes 2097152 | tf_op jit(solution)/shard_map/all_to_all | solution.py:871
  250.9 351.5 %reduce-scatter.6.cloned.1.call-start = ((), (), s32[]{:S(2)}) async-start(), calls=%async_computation.14 | async-start | bytes 5242880 | tf_op jit(solution)/shard_map/reduce_scatter | solution.py:908
  250.9 36.9 %collective-permute-start.18 = (bf16[256,2048]{1,0:T(8,128)(2,1)}, bf16[256,2048]{1,0:T(8,128)(2,1)}, u32[]{:S(2)}, u32[]{:S(2)}) collective-permute-start(bf16[256,2048]{1,0:T(8,128)(2,1)} %collective-permute-done.14), channel_id=1, source_target_pairs={{0,4},{1,5},{2,6},{3,7},{4,0},{5,1},{6,2},{7,3},{8,12},{9,13},{10,... | collective-permute-start | bytes 3145736 | tf_op jit(solution)/shard_map/ppermute | solution.py:709
  252.8 35.1 %collective-permute-start.19 = (bf16[256,2048]{1,0:T(8,128)(2,1)}, bf16[256,2048]{1,0:T(8,128)(2,1)}, u32[]{:S(2)}, u32[]{:S(2)}) collective-permute-start(bf16[256,2048]{1,0:T(8,128)(2,1)} %collective-permute-done.15), channel_id=1, source_target_pairs={{0,2},{1,3},{2,0},{3,1},{4,6},{5,7},{6,4},{7,5},{8,10},{9,11},{10,... | collective-permute-start | bytes 3145736 | tf_op jit(solution)/shard_map/ppermute | solution.py:709
  298.8 13.4 %collective-permute-start.20 = (bf16[2048,2048]{1,0:T(8,128)(2,1)S(1)}, bf16[2048,2048]{1,0:T(8,128)(2,1)}, u32[]{:S(2)}, u32[]{:S(2)}) collective-permute-start(bf16[2048,2048]{1,0:T(8,128)(2,1)S(1)} %constant_dynamic-update-slice_fusion.11.dy0_ref), channel_id=1, source_target_pairs={{0,1},{1,0},{2,3},{3,2},{4,5},{5,4},{6,7},{7,6},{8,9},{9,8},{10,11... | collective-permute-start | bytes 25165832 | tf_op jit(solution)/shard_map/ppermute | solution.py:709
  447.9 23.8 %copy-start.13 = (bf16[2048,1024]{1,0:T(8,128)(2,1)}, bf16[2048,1024]{1,0:T(8,128)(2,1)S(1)}, u32[]{:S(2)}) copy-start(bf16[2048,1024]{1,0:T(8,128)(2,1)S(1)} %get-tuple-element.211.x1_ref) | copy-start | bytes 12582916
  464.5 20.5 %slice-start.4 = ((s8[8388608]{0:T(1024)(128)(4,1)}), s8[4194304]{0:T(1024)(128)(4,1)S(1)}, s32[]{:S(2)}) async-start(s8[8388608]{0:T(1024)(128)(4,1)} %bitcast.220), calls=%async_computation.24 | async-start | bytes 8388608
  511.5 181.2 %reduce-scatter.8.cloned.1.call-start = ((), (), s32[]{:S(2)}) async-start(), calls=%async_computation.15 | async-start | bytes 5242880 | tf_op jit(solution)/shard_map/reduce_scatter | solution.py:912
  622.7 24.9 %all-to-all-start.3 = ((bf16[8,256,256]{2,1,0:T(8,128)(2,1)}), bf16[8,256,256]{2,1,0:T(8,128)(2,1)S(1)}, u32[]{:S(2)}, u32[]{:S(2)}) async-start(bf16[8,256,256]{2,1,0:T(8,128)(2,1)} %get-tuple-element.183), calls=%async_computation.4 | async-start | bytes 2097152 | tf_op jit(solution)/shard_map/all_to_all | solution.py:915
  647.7 45.0 %all-to-all-start.4 = ((bf16[8,256,256]{2,1,0:T(8,128)(2,1)}), bf16[8,256,256]{2,1,0:T(8,128)(2,1)S(1)}, u32[]{:S(2)}, u32[]{:S(2)}) async-start(bf16[8,256,256]{2,1,0:T(8,128)(2,1)} %get-tuple-element.193), calls=%async_computation.5 | async-start | bytes 2097152 | tf_op jit(solution)/shard_map/all_to_all | solution.py:915
  651.9 122.5 %reduce-scatter.10.cloned.1.call-start = ((), (), s32[]{:S(2)}) async-start(), calls=%async_computation.16 | async-start | bytes 9437184 | tf_op jit(solution)/shard_map/reduce_scatter | solution.py:921
  696.9 68.8 %all-to-all-start.5 = ((bf16[8,64,1024]{2,1,0:T(8,128)(2,1)}), bf16[8,64,1024]{2,1,0:T(8,128)(2,1)S(1)}, u32[]{:S(2)}, u32[]{:S(2)}) async-start(bf16[8,64,1024]{2,1,0:T(8,128)(2,1)} %bitcast.47), calls=%async_computation.8 | async-start | bytes 2097152 | tf_op jit(solution)/shard_map/all_to_all | solution.py:922
  701.1 161.0 %reduce-scatter.12.cloned.1.call-start = ((), (), s32[]{:S(2)}) async-start(), calls=%async_computation.17 | async-start | bytes 3932160 | tf_op jit(solution)/shard_map/reduce_scatter | solution.py:930
  862.1 102.9 %all-to-all-start.6 = ((bf16[8,64,768]{2,1,0:T(8,128)(2,1)}), bf16[8,64,768]{2,1,0:T(8,128)(2,1)S(1)}, u32[]{:S(2)}, u32[]{:S(2)}) async-start(bf16[8,64,768]{2,1,0:T(8,128)(2,1)} %bitcast.219), calls=%async_computation.11 | async-start | bytes 1572864 | tf_op jit(solution)/shard_map/all_to_all | solution.py:934
  865.7 99.4 %reduce-scatter.14.cloned.1.call-start = ((), (), s32[]{:S(2)}) async-start(), calls=%async_computation.18 | async-start | bytes 1310720 | tf_op jit(solution)/shard_map/reduce_scatter | solution.py:933
  866.4 90.1 %copy-start.1 = (bf16[2,256,2048]{2,1,0:T(8,128)(2,1)S(1)}, bf16[2,256,2048]{2,1,0:T(8,128)(2,1)}, u32[]{:S(2)}) copy-start(bf16[2,256,2048]{2,1,0:T(8,128)(2,1)} %param.17) | copy-start | bytes 6291460
  866.4 90.1 %copy-start.36 = (f32[1,2,2,128]{3,1,2,0:T(2,128)S(1)}, f32[1,2,2,128]{3,1,2,0:T(2,128)}, u32[]{:S(2)}) copy-start(f32[1,2,2,128]{3,1,2,0:T(2,128)} %copy-done.35) | copy-start | bytes 6148
  866.5 90.1 %copy-start.38 = (f32[1,2,2,128]{3,1,2,0:T(2,128)S(1)}, f32[1,2,2,128]{3,1,2,0:T(2,128)}, u32[]{:S(2)}) copy-start(f32[1,2,2,128]{3,1,2,0:T(2,128)} %copy-done.37) | copy-start | bytes 6148
  (47 other events, 303.8 us)
Sparse Core Ops, SparseCore 0:
  27.2 64.5 all-gather.4
  95.2 77.6 all-gather.6
  180.4 148.2 all-gather.8
  511.6 74.0 reduce-scatter.5
  602.5 73.9 reduce-scatter.7
  692.9 70.0 reduce-scatter.9
  774.5 58.8 reduce-scatter.11
  868.9 25.7 reduce-scatter.13
